TPU v7x, 256 devices: a whole 4x4x8 slice. The times are simulated.
256 devices in a mesh: leaf: 64 (over z, x, core), col: 4 (over y).
Axes of the slice: x: 4, y: 4, z: 8, core: 2. Of those that a mesh axis runs over, the one named last changes fastest.
Arguments:
- points: float32 [65536, 128], P(('leaf', 'col')), may hold values from -6 to 6
- coefs: float32 [65536, 512], P(('leaf', 'col')), may hold values from -6 to 6
- targets: float32 [65536, 512], P(('leaf', 'col')), may hold values from -6 to 6
- ridge: float32 [1], replicated, may hold values from 0.5 to 2
- tile_mask: int32 [64, 5], P('leaf'), may hold values from 0 to 1, as said below
- cluster_perm: int32 [64, 1024], P('leaf'), may hold values from 0 to 1023, each once within a row
- leaf_map: int32 [64], replicated, may hold values from 0 to 63, as said below
- leaf_inverse: float32 [64, 1024, 1024], P('leaf'), may hold values from -0.25 to 1.3
- leaf_basis: float32 [64, 1024, 256], P('leaf'), may hold values from -0.1875 to 0.1875
- node_inverse: float32 [64, 336, 1024], P('leaf'), may hold values from -0.25 to 1.3
- node_transfer: float32 [64, 336, 256], P('leaf'), may hold values from -0.1875 to 0.1875
Outputs:
- residual: float32 [65536, 512], P(('leaf', 'col'))
- new_coef: float32 [65536, 512], P(('leaf', 'col'))
Inputs may be any that keep to these rules, and one draw needn't show every extreme that they name: `tile_mask`: entry k of row i is 1 when block i has a nonzero tile with block i + k - 2; entry 2 is always 1, entries naming a block outside 0 .. 63 are 0, and some row lists all 5 tiles. `cluster_perm`: each row is a permutation of 0 .. 1023. `leaf_map`: a permutation of 0 .. 63 that sends the tree leaves 4 n .. 4 n + 3 to the blocks 4 n .. 4 n + 3.
All inputs are finite; a program needn't handle non-finite values.
Results may differ from a plain program's by a relative error of at most 0.0003.
Values sent between devices are 32-bit elements; how exact they have to be, the bound alone decides.
No kernel may reach another device: no remote copies, remote signals or barrier semaphores. Data moves between devices by JAX's collectives and lax.ppermute only.
A program may use at most 128 MiB of HBM per device.

v0:
```python
import jax
import jax.numpy as jnp
from jax import lax
from jax.experimental import pallas as pl
from jax.experimental.pallas import tpu as pltpu
from jax.sharding import PartitionSpec as P


HIGH = lax.Precision.HIGH
F32 = jnp.float32
BF16 = jnp.bfloat16
Q = 256
RANK = 256
LEAVES = 64


def leaf_at(z, x_hi, kappa):
    x = 2 * x_hi + ((kappa >> 1) ^ x_hi)
    return z * 8 + x * 2 + (kappa & 1)


G4 = [[4 * n + k for k in range(4)] for n in range(16)]
GK = [[leaf_at(z, xh, k) for k in range(4)] for z in range(8) for xh in range(2)]


def facing(i, flip_x, flip_z):
    z, x, core = i // 8, i // 2 % 4, i % 2
    return (z ^ flip_z) * 8 + (3 - x if flip_x else x) * 2 + core


def leaf_route(value, target):
    return lax.ppermute(value, "leaf", [(i, target(i)) for i in range(LEAVES)])


def leaf_xor(value, bit):
    return leaf_route(value, lambda i: i ^ bit)


def leaf_from(value, step):
    return leaf_route(value, lambda i: (i - step) % LEAVES)


def siblings(value):
    return [value] + [
        leaf_route(value, lambda i, d=d: facing(i, d & 1, d >> 1)) for d in (1, 2, 3)
    ]


def z_from(value, even, odd):
    route = []
    for i in range(LEAVES):
        step = odd if i // 8 % 2 else even
        route.append(((i + 8 * step) % LEAVES, i))
    return lax.ppermute(value, "leaf", route)


def col_shift(value, step):
    return lax.ppermute(value, "col", [(i, (i + step) % 4) for i in range(4)])


def gather4(value, groups):
    return lax.all_gather(value, "leaf", axis=0, axis_index_groups=groups)


def mm(a, b, dims, precision=HIGH):
    return lax.dot_general(a, b, (dims, ((), ())), precision=precision, preferred_element_type=F32)


def halves(value):
    top = lax.reduce_precision(value, 8, 7)
    return top.astype(BF16), (value - top).astype(BF16)


def select(value, picks, dims):
    a, b = halves(value)
    return mm(a, picks, dims, None) + mm(b, picks, dims, None)


NN = ((1,), (0,))
NT = ((1,), (1,))


def dot(a, b, dims=NN):
    return lax.dot_general(a, b, (dims, ((), ())), preferred_element_type=F32)


def split(value):
    top = value.astype(BF16)
    return top, (value - top.astype(F32)).astype(BF16)


def dot3(a, b, dims=NN):
    at, al = split(a)
    bt, bl = split(b)
    return dot(at, bt, dims) + (dot(at, bl, dims) + dot(al, bt, dims))


SMEM = pl.BlockSpec(memory_space=pltpu.SMEM)


def whole(*shape):
    return pl.BlockSpec(shape, lambda *i: (0,) * len(shape))


def like(*shape, dtype=F32):
    return jax.ShapeDtypeStruct(shape, dtype)


CHUNK = 512


def two_part(value):
    top, low = split(value)
    return jnp.concatenate([top, low], axis=1), top.astype(F32) + low.astype(F32)


def tile_setup(place, xs, blocks, rows, norms, squares, others, tops, lows):
    for k, ref in enumerate(xs):
        at = (place[2] + 4 - k) % 4
        rows[at], exact = two_part(ref[...])
        norms[at] = jnp.sum(exact * exact, axis=1, keepdims=True)
    for k, (y, a) in enumerate(blocks):
        others[k], exact = two_part(y)
        total = jnp.sum(exact * exact, axis=1, keepdims=True)
        squares[k] = jnp.transpose(jnp.broadcast_to(total, (Q, 128)))[:8]
        tops[k], lows[k] = split(a)


def tile_sum(i, weights, rows, norms, squares, others, tops, lows):
    x = rows[pl.ds(2 * i, 2)].reshape(CHUNK, 256)
    own = norms[pl.ds(2 * i, 2)].reshape(CHUNK, 1)
    total = None
    for k, weight in enumerate(weights):
        top, low = others[k][:, :128], others[k][:, 128:]
        inner = dot(x, jnp.concatenate([top, top], axis=1), NT)
        inner = inner + dot(x, jnp.concatenate([low, low], axis=1), NT)
        distance = own + squares[k][:1] - 2.0 * inner
        top, low = split(jnp.exp(distance * (-2.0 / 128.0)) * weight)
        term = dot(top, tops[k]) + dot(top, lows[k]) + dot(low, tops[k])
        total = term if total is None else total + term
    return total


def near_kernel(place, mask, x0, x1, x2, x3, p0, p1, out, *scratch):
    i = pl.program_id(0)

    @pl.when(i == 0)
    def _():
        blocks = [(p[:, :128], p[:, 128:]) for p in (p0, p1)]
        tile_setup(place, (x0, x1, x2, x3), blocks, *scratch)

    weights = (mask[0, 2].astype(F32), mask[0, 3 - 2 * place[0]].astype(F32))
    out[...] = tile_sum(i, weights, *scratch)


def far_kernel(
    place, mask, ridge, x0, x1, x2, x3, p0, p1, p2, near, own_y, own_a, lead, out, led, *scratch
):
    i = pl.program_id(0)

    @pl.when(i == 0)
    def _():
        blocks = [(p[:, :128], p[:, 128:]) for p in (p0, p1, p2)]
        tile_setup(place, (x0, x1, x2, x3), blocks, *scratch)

    weights = (
        mask[0, 0].astype(F32),
        mask[0, 4].astype(F32),
        mask[0, 1 + 2 * place[0]].astype(F32),
    )
    total = near[...] + tile_sum(i, weights, *scratch)
    own = own_y[...] - ridge[0] * own_a[...]
    part = jnp.concatenate(
        [
            jnp.where(place[2] == 2 * i + h, own, 0.0) - total[h * Q : (h + 1) * Q]
            for h in range(2)
        ],
        axis=0,
    )
    product = dot3(lead[...], part)
    for k in range(4):
        out[k] = part[:, k * 128 : (k + 1) * 128]
        piece = product[:, k * 128 : (k + 1) * 128]
        led[k] = jnp.where(i == 0, piece, led[k] + piece)


def tile_scratch(count):
    return [
        pltpu.VMEM((4, Q, 256), BF16),
        pltpu.VMEM((4, Q, 1), F32),
        pltpu.VMEM((count, 8, Q), F32),
        pltpu.VMEM((count, Q, 256), BF16),
        pltpu.VMEM((count, Q, 512), BF16),
        pltpu.VMEM((count, Q, 512), BF16),
    ]


def near_call(place, mask, xs, blocks):
    return pl.pallas_call(
        near_kernel,
        grid=(2,),
        in_specs=[SMEM, SMEM] + [whole(Q, 128)] * 4 + [whole(Q, 640)] * 2,
        out_specs=pl.BlockSpec((CHUNK, 512), lambda i: (i, 0)),
        out_shape=like(1024, 512),
        scratch_shapes=tile_scratch(2),
        name="near",
    )(place, mask, *xs, *blocks)


def far_call(place, mask, ridge, xs, blocks, near, own_y, own_a, lead):
    return pl.pallas_call(
        far_kernel,
        grid=(2,),
        in_specs=[SMEM, SMEM, SMEM]
        + [whole(Q, 128)] * 4
        + [whole(Q, 640)] * 3
        + [pl.BlockSpec((CHUNK, 512), lambda i: (i, 0))]
        + [whole(Q, 512)] * 2
        + [pl.BlockSpec((RANK, CHUNK), lambda i: (0, i))],
        out_specs=[pl.BlockSpec((4, CHUNK, 128), lambda i: (0, i, 0)), whole(4, RANK, 128)],
        out_shape=[like(4, 1024, 128), like(4, RANK, 128)],
        scratch_shapes=tile_scratch(3),
        name="far",
    )(place, mask, ridge, *xs, *blocks, near, own_y, own_a, lead)


def pack_kernel(a, b, out):
    out[:, :128] = a[...]
    out[:, 128:] = b[...]


def pack_call(a, b):
    return pl.pallas_call(pack_kernel, out_shape=like(Q, 640), name="pack")(a, b)


def fill_slices(transfer, inverse, out, start):
    out[start : start + 64, :] = transfer[0, 256:320, :]
    for k in range(4):
        at = start + 64 + k * 16
        out[at : at + 16, :] = inverse[0, 320:336, k * 256 : (k + 1) * 256]


def slices_kernel(transfer, inverse, out):
    fill_slices(transfer, inverse, out, 0)


def pair_kernel(transfer, inverse, lower, out):
    fill_slices(transfer, inverse, out, 0)
    out[128:, :] = lower[...]


def held_kernel(transfer, inverse, lower, mirrored, out):
    out[:256, :] = transfer[0, :256, :]
    for k in range(4):
        at = 256 + k * 64
        out[at : at + 64, :] = inverse[0, 256:320, k * 256 : (k + 1) * 256]
    fill_slices(transfer, inverse, out, 512)
    out[640:768, :] = lower[...]
    out[768:, :] = mirrored[...]


def collect(body, rows, *parts):
    return pl.pallas_call(body, out_shape=like(rows, 256))(*parts)


def nodes_kernel(place, b0, b1, b2, b3, e1, m2, f2, m3, own_e2, e2):
    q = place[3] % 4
    child = place[3] // 4 % 4
    parent = place[3] // 16
    odd = place[3] // 8 % 2
    for d, block in enumerate((b0, b1, b2, b3)):
        at = q ^ d
        e1[pl.ds(pl.multiple_of(at * 256, 256), 256), :] = block[:256, :]
        rows = pl.ds(pl.multiple_of(at * 64, 64), 64)
        for k in range(4):
            source = pl.multiple_of(256 + (child ^ k) * 64, 64)
            m2[rows, k * 256 : (k + 1) * 256] = block[pl.ds(source, 64), :]
        for s, (start, flip) in enumerate(((512, 0), (768, 2), (640, 0), (896, 2))):
            held = at ^ flip
            e2[pl.ds(pl.multiple_of(s * 256 + held * 64, 64), 64), :] = block[
                start : start + 64, :
            ]
            rows = pl.ds(pl.multiple_of((child ^ s) * 64 + held * 16, 16), 16)
            for k in range(4):
                step = (0, 3, 1, 2)[k] + odd * (0, -2, 2, 0)[k]
                source = pl.multiple_of(start + 64 + (parent + step) % 4 * 16, 16)
                m3[rows, k * 256 : (k + 1) * 256] = block[pl.ds(source, 16), :]
    own_e2[...] = e2[:256, :]
    f2[...] = dot3(m2[...], e2[...])


def nodes_call(place, blocks):
    return pl.pallas_call(
        nodes_kernel,
        in_specs=[SMEM] + [whole(1024, 256)] * 4,
        out_specs=[whole(1024, 256), whole(256, 1024), whole(256, 256), whole(256, 1024), whole(256, 256)],
        out_shape=[like(1024, 256), like(256, 1024), like(256, 256), like(256, 1024), like(256, 256)],
        scratch_shapes=[pltpu.VMEM((1024, 256), F32)],
        grid=(1,),
        name="nodes",
    )(place, *blocks)


def level1_kernel(place, leaf_map, stacked, m1, e1, w1, p1):
    base = place[3] // 4 * 4
    total = None
    for k in range(4):
        term = dot3(m1[0, :, k * 256 : (k + 1) * 256], stacked[leaf_map[base + k] - base])
        total = term if total is None else total + term
    w1[...] = total
    p1[...] = dot3(jnp.transpose(total), e1[0])


def level1_call(place, leaf_map, stacked, node_inverse, node_transfer):
    return pl.pallas_call(
        level1_kernel,
        grid=(1,),
        in_specs=[SMEM, SMEM, whole(4, 256, 128), whole(1, 256, 1024), whole(1, 256, 256)],
        out_specs=[whole(256, 128), whole(128, 256)],
        out_shape=[like(256, 128), like(128, 256)],
        name="level1",
    )(place, leaf_map, stacked, node_inverse, node_transfer)


def row_blocks(parts, matrix):
    total = None
    for k, part in enumerate(parts):
        term = dot3(part[...], matrix[:, k * 256 : (k + 1) * 256], NT)
        total = term if total is None else total + term
    return total


def level2_kernel(r0, r1, r2, r3, m2, e2, w2, p2):
    total = row_blocks((r0, r1, r2, r3), m2)
    w2[...] = total
    p2[...] = dot3(total, e2[...])


def level2_call(parts, m2, e2):
    return pl.pallas_call(
        level2_kernel,
        out_shape=[like(32, 256), like(32, 256)],
        name="level2",
    )(*parts, m2, e2)


def upper_kernel(r0, r1, r2, r3, m3, f2, w2, g1):
    g2 = row_blocks((r0, r1, r2, r3), m3)
    g1[...] = w2[...] - dot3(g2, f2[...], NT)


def upper_call(parts, m3, f2, w2):
    return pl.pallas_call(upper_kernel, out_shape=like(32, 256), name="upper")(
        *parts, m3, f2, w2
    )


def down1_kernel(g1, e1, m1, w1, v1):
    g = g1[...].reshape(128, 256)
    lifted = dot3(g, e1[...], NT)
    v1[...] = w1[...] - dot3(m1[0], lifted, NT)


def down1_call(g1, e1, node_inverse, w1):
    return pl.pallas_call(
        down1_kernel,
        grid=(1,),
        in_specs=[whole(4, 32, 256), whole(1024, 256), whole(1, 256, 1024), whole(256, 128)],
        out_specs=whole(256, 128),
        out_shape=like(256, 128),
        name="down1",
    )(g1, e1, node_inverse, w1)


def residual_kernel(order, parts, res, ordered, picks):
    res_sum = parts[0] + parts[1] + (parts[2] + parts[3])
    res[...] = res_sum
    at = lax.broadcasted_iota(jnp.int32, (1024, 1024), 1)
    picks[...] = jnp.where(order[...] == at, 1.0, 0.0).astype(BF16)
    both = dot(picks[...], jnp.concatenate(split(res_sum), axis=1))
    ordered[...] = both[:, :128] + both[:, 128:]


def residual_call(order, parts):
    return pl.pallas_call(
        residual_kernel,
        out_shape=[like(1024, 128), like(1024, 128)],
        scratch_shapes=[pltpu.VMEM((1024, 1024), BF16)],
        name="residual",
    )(order, parts)


def finish_kernel(place, leaf_map, order, pieces, ordered, basis, solve, delta, picks, rhs):
    i = pl.program_id(0)

    @pl.when(i == 0)
    def _():
        base = place[3] // 4 * 4
        slot = jnp.int32(3)
        for k in range(3):
            slot = jnp.where(leaf_map[base + k] == place[3], k, slot)
        top, low = split(ordered[...] - dot3(basis[0], pieces[slot]))
        rhs[...] = jnp.concatenate([top, low], axis=1)

    a, b = split(solve[0])
    both = dot(a, rhs[...])
    y = both[:, :128] + (both[:, 128:] + dot(b, rhs[:, :128]))
    at = lax.broadcasted_iota(jnp.int32, (1024, Q), 0)
    picks[...] = jnp.where(order[...] == at, 1.0, 0.0).astype(BF16)
    both = dot(picks[...], jnp.concatenate(split(y), axis=1))
    term = both[:, :128] + both[:, 128:]
    delta[...] = jnp.where(i == 0, term, delta[...] + term)


def finish_call(place, leaf_map, order, pieces, ordered, leaf_basis, leaf_inverse):
    return pl.pallas_call(
        finish_kernel,
        grid=(4,),
        in_specs=[
            SMEM,
            SMEM,
            pl.BlockSpec((1, Q), lambda i: (0, i)),
            whole(4, 256, 128),
            whole(1024, 128),
            whole(1, 1024, 256),
            pl.BlockSpec((1, Q, 1024), lambda i: (0, i, 0)),
        ],
        out_specs=whole(1024, 128),
        out_shape=like(1024, 128),
        scratch_shapes=[
            pltpu.VMEM((1024, Q), BF16),
            pltpu.VMEM((1024, 256), BF16),
        ],
        name="finish",
    )(place, leaf_map, order, pieces, ordered, leaf_basis, leaf_inverse)


def outputs_kernel(res, delta, coefs, out_res, out_new):
    for k in range(4):
        at = slice(k * 128, (k + 1) * 128)
        out_res[:, at] = res[k]
        out_new[:, at] = coefs[:, at] + delta[k]


def outputs_call(res, delta, coefs):
    return pl.pallas_call(
        outputs_kernel, out_shape=[like(Q, 512), like(Q, 512)], name="outputs"
    )(res, delta, coefs)


def swap_cols(value):
    return lax.all_to_all(value, "col", 0, 0, tiled=True)


def step(
    points,
    coefs,
    targets,
    ridge,
    tile_mask,
    cluster_perm,
    leaf_map,
    leaf_inverse,
    leaf_basis,
    node_inverse,
    node_transfer,
):
    col = lax.axis_index("col")
    leaf = lax.axis_index("leaf")
    core = leaf % 2
    place = jnp.stack([core, leaf // 2 % 2, col, leaf]).astype(jnp.int32)

    xs = [points] + [col_shift(points, d) for d in (1, 2, 3)]
    packed = pack_call(points, coefs)
    left, right = leaf_from(packed, -2), leaf_from(packed, 2)
    partner = leaf_xor(packed, 1)
    relay = leaf_xor(jnp.where(core == 0, right, left), 1)

    nodes = (node_transfer, node_inverse)
    lower = leaf_route(collect(slices_kernel, 128, *nodes), lambda i: facing(i, 0, 1))
    mirrored = leaf_route(collect(pair_kernel, 256, *nodes, lower), lambda i: facing(i, 1, 0))
    held = collect(held_kernel, 1024, *nodes, lower, mirrored)

    order = cluster_perm[0]
    at = jnp.arange(1024, dtype=jnp.int32)
    pick = (order[:, None] == at[None, :]).astype(BF16)
    lead = select(mm(leaf_basis[0], leaf_inverse[0], ((0,), (0,))), pick, NN)

    near = near_call(place, tile_mask, xs, (packed, partner))
    near, held = lax.optimization_barrier((near, held))
    across = leaf_xor(held, 2)
    own_core = leaf_xor(held, 1)
    both_ways = leaf_xor(across, 1)
    partial, led = far_call(
        place, tile_mask, ridge, xs, (left, right, relay), near, targets, coefs, lead
    )
    reduced = swap_cols(led).sum(0)
    e1, m2, f2, m3, e2 = nodes_call(place, (held, own_core, across, both_ways))

    partial, _ = lax.optimization_barrier((partial, reduced))
    res, ordered = residual_call(order.reshape(1024, 1), swap_cols(partial))
    res_rows = swap_cols(res.reshape(4, Q, 128))

    w1, p1 = level1_call(place, leaf_map, gather4(reduced, G4), node_inverse, node_transfer)
    p1 = lax.all_to_all(p1, "leaf", 0, 0, axis_index_groups=GK, tiled=True)
    r1 = p1.reshape(4, 32, RANK).sum(0)
    w2, p2 = level2_call(siblings(r1), m2, e2)
    r2 = sum(siblings(p2))
    r2s = [r2, z_from(r2, -1, 1), z_from(r2, 2, -2), z_from(r2, -3, 3)]
    g1 = gather4(upper_call(r2s, m3, f2, w2), GK)
    pieces = gather4(down1_call(g1, e1, node_inverse, w1), G4)

    delta = finish_call(place, leaf_map, cluster_perm, pieces, ordered, leaf_basis, leaf_inverse)
    return outputs_call(res_rows, swap_cols(delta.reshape(4, Q, 128)), coefs)


def solution(mesh):
    return jax.shard_map(
        step,
        mesh=mesh,
        in_specs=(
            P(("leaf", "col"), None),
            P(("leaf", "col"), None),
            P(("leaf", "col"), None),
            P(),
            P("leaf", None),
            P("leaf", None),
            P(),
            P("leaf", None, None),
            P("leaf", None, None),
            P("leaf", None, None),
            P("leaf", None, None),
        ),
        out_specs=(P(("leaf", "col"), None), P(("leaf", "col"), None)),
        check_vma=False,
    )
```

profile of v0, /device:TPU:1, one launch (start us, length us, event | category | flops | bytes accessed | tf_op | source)
XLA Modules:
  0.0 204.0 jit_solution(7276715617410133917)
XLA Ops:
  0.6 2.0 pack.1.p0
  2.6 8.6 %collective-permute-start.4 = (f32[256,640]{1,0:T(8,128)}, f32[256,640]{1,0:T(8,128)S(1)}, u32[]{:S(2)}, u32[]{:S(2)}) collective-permute-start(f32[256,640]{1,0:T(8,128)} %pack.1.p0), channel_id=1, source_target_pairs={{0,248},{4,252},{8,0},{12,4},{16,8},{20,12},{24,16},{28,20},{32,24... | collective-permute-start | bytes 1966088 | tf_op jit(solution)/shard_map/ppermute | solution.py:32
  11.2 2.7 %collective-permute-start.2 = (f32[256,128]{1,0:T(8,128)}, f32[256,128]{1,0:T(8,128)S(1)}, u32[]{:S(2)}, u32[]{:S(2)}) collective-permute-start(f32[256,128]{1,0:T(8,128)} %x0.3), channel_id=1, source_target_pairs={{0,3},{1,0},{2,1},{3,2},{4,7},{5,4},{6,5},{7,6},{8,11},{9,8},{10,9... | collective-permute-start | bytes 393224 | tf_op jit(solution)/shard_map/ppermute | solution.py:58
  14.0 0.3 collective-permute-start.1
  14.3 2.1 %shard_map.122 = f32[128,256]{1,0:T(8,128)} custom-call(f32[1,336,256]{2,1,0:T(8,128)} %e1.1, f32[1,336,1024]{2,1,0:T(8,128)} %m1.3), custom_call_target="tpu_custom_call" | custom-call | tf_op jit(solution)/shard_map/pallas_call | solution.py:263
  16.4 4.5 %fusion = f32[256,1024]{1,0:T(8,128)S(1)} fusion(f32[1,1024,1024]{2,1,0:T(8,128)} %solve.1, f32[1,1024,256]{2,1,0:T(8,128)} %basis.1), kind=kOutput, calls=%fused_computation | convolution fusion | flops 1610612736 | bytes 6291456 | tf_op jit(solution)/shard_map/dot_general | solution.py:66
  20.9 0.0 copy-start.6
  20.9 3.4 %collective-permute-done.7.lower = f32[128,256]{1,0:T(8,128)S(1)} collective-permute-done((f32[128,256]{1,0:T(8,128)}, f32[128,256]{1,0:T(8,128)S(1)}, u32[]{:S(2)}, u32[]{:S(2)}) %collective-permute-start.7) | collective-permute-done | bytes 131104 | tf_op jit(solution)/shard_map/ppermute | solution.py:32
  24.3 1.5 collective-permute-start.6
  25.8 2.1 %shard_map.123 = f32[256,256]{1,0:T(8,128)} custom-call(f32[1,336,256]{2,1,0:T(8,128)} %e1.1, f32[1,336,1024]{2,1,0:T(8,128)} %m1.3, f32[128,256]{1,0:T(8,128)} %copy-done.9), custom_call_target="tpu_custom_call" | custom-call | tf_op jit(solution)/shard_map/pallas_call | solution.py:263
  28.0 1.8 collective-permute-start.8
  29.7 0.4 collective-permute-done.3.p0
  30.1 1.0 broadcast_select_fusion
  31.1 1.8 collective-permute-start.5
  32.9 1.1 fusion.2
  34.0 2.7 %collective-permute-done.8.mirrored = f32[256,256]{1,0:T(8,128)} collective-permute-done((f32[256,256]{1,0:T(8,128)}, f32[256,256]{1,0:T(8,128)}, u32[]{:S(2)}, u32[]{:S(2)}) %collective-permute-start.8) | collective-permute-done | bytes 262176 | tf_op jit(solution)/shard_map/ppermute | solution.py:32
  36.7 1.3 collective-permute-start
  38.0 2.1 %fusion.6.lead = f32[256,1024]{1,0:T(8,128)} fusion(f32[256,1024]{1,0:T(8,128)S(1)} %fusion.2, s32[1024]{0:T(1024)S(1)} %bitcast.25, f32[256,1024]{1,0:T(8,128)S(1)} %fusion), kind=kOutput, calls=%fused_computation.9 | convolution fusion | flops 538705920 | bytes 3149824 | tf_op jit(solution)/shard_map/dot_general | solution.py:66
  40.7 0.6 pad_add_fusion.place
  41.3 2.6 %shard_map.124.b0 = f32[1024,256]{1,0:T(8,128)} custom-call(f32[1,336,256]{2,1,0:T(8,128)} %e1.1, f32[1,336,1024]{2,1,0:T(8,128)} %m1.3, f32[128,256]{1,0:T(8,128)} %copy-done.9, f32[256,256]{1,0:T(8,128)} %collective-permute-done.8.mirrored), custom_call_target="tpu_custom_call" | custom-call | tf_op jit(solution)/shard_map/pallas_call | solution.py:263
  43.9 0.0 copy-start.10
  43.9 0.6 copy-done.7
  44.5 0.1 copy-done.8
  44.6 0.0 copy-done.10
  44.6 6.8 %near.1 = f32[1024,512]{1,0:T(8,128)} custom-call(s32[4]{0:T(128)} %pad_add_fusion.place, s32[1,5]{1,0:T(1,128)} %mask.3, f32[256,128]{1,0:T(8,128)} %x0.3, f32[256,128]{1,0:T(8,128)} %copy-done.10, f32[256,128]{1,0:T(8,128)} %copy-done.8, f32[256,128]{1,0:T(8,128)} %copy-done.7, f32[256,640]{1,0:T(8,128)} %pack.1.p0, f32[256,640]{1,0:T(8,128)} %collective-permute-done.6.p1), custom_call_target="tpu_custom_call" | custom-call | tf_op jit(solution)/shard_map/near/pallas_call | solution.py:199
  51.4 11.3 %far.1 = (f32[4,1024,128]{2,1,0:T(8,128)}, f32[4,256,128]{2,1,0:T(8,128)}) custom-call(s32[4]{0:T(128)} %pad_add_fusion.place, s32[1,5]{1,0:T(1,128)} %mask.3, f32[1]{0:T(128)S(6)} %copy.14.ridge, f32[256,128]{1,0:T(8,128)} %x0.3, f32[256,128]{1,0:T(8,128)} %copy-done.10, f32[256,128]{1,0:T(8,128)} %copy-done.8, f32[256,128]{1,0:T(8,128)} %copy-done.7, ...), custom_call_target="tpu_custom_call" | custom-call | tf_op jit(solution)/shard_map/far/pallas_call | solution.py:211
  62.7 3.9 %all-to-all-start = ((f32[4,256,128]{2,1,0:T(8,128)}), f32[4,256,128]{2,1,0:T(8,128)S(1)}, u32[]{:S(2)}, u32[]{:S(2)}) async-start(f32[4,256,128]{2,1,0:T(8,128)} %get-tuple-element.20), calls=%async_computation | async-start | bytes 1048576 | tf_op jit(solution)/shard_map/all_to_all | solution.py:452
  66.6 7.2 %all-to-all-done = f32[4,256,128]{2,1,0:T(8,128)S(1)} async-done(((f32[4,256,128]{2,1,0:T(8,128)}), f32[4,256,128]{2,1,0:T(8,128)S(1)}, u32[]{:S(2)}, u32[]{:S(2)}) %all-to-all-start) | async-done | bytes 524320 | tf_op jit(solution)/shard_map/all_to_all | solution.py:452
  73.8 22.3 %all-gather = f32[1024,128]{1,0:T(8,128)} all-gather(f32[256,128]{1,0:T(8,128)S(1)} %reduce_sum.18), channel_id=2, replica_groups={{0,4,8,12},{16,20,24,28},{32,36,40,44},{48,52,56,60},{64,68,72,76},{80,..., dimensions={0}, use_global_device_ids=true | all-gather | bytes 655360 | tf_op jit(solution)/shard_map/all_gather | solution.py:62
  96.1 3.0 %level1.1 = (f32[256,128]{1,0:T(8,128)}, f32[128,256]{1,0:T(8,128)}) custom-call(s32[4]{0:T(128)} %pad_add_fusion.place, s32[64]{0:T(128)} %leaf_map.3, f32[4,256,128]{2,1,0:T(8,128)} %bitcast.20, f32[1,336,1024]{2,1,0:T(8,128)} %m1.3, f32[1,336,256]{2,1,0:T(8,128)} %e1.1), custom_call_target="tpu_custom_call" | custom-call | tf_op jit(solution)/shard_map/level1/pallas_call | solution.py:315
  99.1 3.5 %all-to-all-start.3 = ((f32[4,32,256]{2,1,0:T(8,128)}), f32[4,32,256]{2,1,0:T(8,128)S(1)}, u32[]{:S(2)}, u32[]{:S(2)}) async-start(f32[4,32,256]{2,1,0:T(8,128)} %bitcast.23), calls=%async_computation.3 | async-start | bytes 262144 | tf_op jit(solution)/shard_map/all_to_all | solution.py:505
  102.6 3.6 %all-to-all-done.3 = f32[4,32,256]{2,1,0:T(8,128)S(1)} async-done(((f32[4,32,256]{2,1,0:T(8,128)}), f32[4,32,256]{2,1,0:T(8,128)S(1)}, u32[]{:S(2)}, u32[]{:S(2)}) %all-to-all-start.3) | async-done | bytes 131104 | tf_op jit(solution)/shard_map/all_to_all | solution.py:505
  106.1 4.2 %all-to-all-start.1 = ((f32[4,1024,128]{2,1,0:T(8,128)}), f32[4,1024,128]{2,1,0:T(8,128)S(1)}, u32[]{:S(2)}, u32[]{:S(2)}) async-start(f32[4,1024,128]{2,1,0:T(8,128)} %get-tuple-element.21), calls=%async_computation.1 | async-start | bytes 4194304 | tf_op jit(solution)/shard_map/all_to_all | solution.py:452
  110.4 1.3 collective-permute-start.12
  111.7 0.1 collective-permute-start.14
  111.8 0.0 copy-start.11
  111.8 3.7 %collective-permute-start.11 = (f32[32,256]{1,0:T(8,128)S(1)}, f32[32,256]{1,0:T(8,128)S(1)}, u32[]{:S(2)}, u32[]{:S(2)}) collective-permute-start(f32[32,256]{1,0:T(8,128)S(1)} %reduce_sum.19.r0), channel_id=1, source_target_pairs={{0,56},{4,60},{8,48},{12,52},{16,40},{20,44},{24,32},{28,36},{32,2... | collective-permute-start | bytes 98312 | tf_op jit(solution)/shard_map/ppermute | solution.py:32
  115.5 0.4 collective-permute-start.9
  115.9 4.2 %nodes.1 = (f32[1024,256]{1,0:T(8,128)}, f32[256,1024]{1,0:T(8,128)}, f32[256,256]{1,0:T(8,128)}, f32[256,1024]{1,0:T(8,128)}, f32[256,256]{1,0:T(8,128)}) custom-call(s32[4]{0:T(128)} %pad_add_fusion.place, f32[1024,256]{1,0:T(8,128)} %shard_map.124.b0, f32[1024,256]{1,0:T(8,128)} %collective-permute-done.12.b1, f32[1024,256]{1,0:T(8,128)} %collective-permute-done.13.b2, ...), custom_call_target="tpu_custom_call" | custom-call | tf_op jit(solution)/shard_map/nodes/pallas_call | solution.py:293
  120.2 0.5 copy-done.14
  120.7 0.0 copy-done.15
  120.7 0.0 copy-done.16
  120.8 2.8 %level2.1 = (f32[32,256]{1,0:T(8,128)}, f32[32,256]{1,0:T(8,128)}) custom-call(f32[32,256]{1,0:T(8,128)} %copy-done.11, f32[32,256]{1,0:T(8,128)} %copy-done.16, f32[32,256]{1,0:T(8,128)} %copy-done.15, f32[32,256]{1,0:T(8,128)} %copy-done.14, f32[256,1024]{1,0:T(8,128)} %get-tuple-element.25.m2, f32[256,256]{1,0:T(8,128)} %get-tuple-element.26.e2), custom_call_target="tpu_custom_call" | custom-call | tf_op jit(solution)/shard_map/level2/pallas_call | solution.py:340
  123.5 3.5 %collective-permute-start.17 = (f32[32,256]{1,0:T(8,128)}, f32[32,256]{1,0:T(8,128)S(1)}, u32[]{:S(2)}, u32[]{:S(2)}) collective-permute-start(f32[32,256]{1,0:T(8,128)} %get-tuple-element.27), channel_id=1, source_target_pairs={{0,56},{4,60},{8,48},{12,52},{16,40},{20,44},{24,32},{28,36},{32,2... | collective-permute-start | bytes 98312 | tf_op jit(solution)/shard_map/ppermute | solution.py:32
  127.0 0.4 collective-permute-start.15
  127.4 1.0 copy.13.order
  128.4 7.0 %all-to-all-done.1.parts = f32[4,1024,128]{2,1,0:T(8,128)S(1)} async-done(((f32[4,1024,128]{2,1,0:T(8,128)}), f32[4,1024,128]{2,1,0:T(8,128)S(1)}, u32[]{:S(2)}, u32[]{:S(2)}) %all-to-all-start.1) | async-done | bytes 2097184 | tf_op jit(solution)/shard_map/all_to_all | solution.py:452
  135.5 1.3 copy-done
  136.8 3.3 %residual.1 = (f32[1024,128]{1,0:T(8,128)}, f32[1024,128]{1,0:T(8,128)}) custom-call(s32[1024,1]{1,0:T(8,128)} %copy.13.order, f32[4,1024,128]{2,1,0:T(8,128)} %copy-done), custom_call_target="tpu_custom_call" | custom-call | tf_op jit(solution)/shard_map/residual/pallas_call | solution.py:385
  140.1 3.5 %all-to-all-start.2 = ((f32[4,256,128]{2,1,0:T(8,128)}), f32[4,256,128]{2,1,0:T(8,128)S(1)}, u32[]{:S(2)}, u32[]{:S(2)}) async-start(f32[4,256,128]{2,1,0:T(8,128)} %bitcast.22), calls=%async_computation.2 | async-start | bytes 1048576 | tf_op jit(solution)/shard_map/all_to_all | solution.py:452
  143.7 0.0 copy-start.12
  143.7 7.3 %collective-permute-start.20 = (f32[32,256]{1,0:T(8,128)S(1)}, f32[32,256]{1,0:T(8,128)S(1)}, u32[]{:S(2)}, u32[]{:S(2)}) collective-permute-start(f32[32,256]{1,0:T(8,128)S(1)} %add_add_fusion.r0), channel_id=1, source_target_pairs={{160,0},{164,4},{168,8},{172,12},{176,16},{180,20},{184,24},{188,2... | collective-permute-start | bytes 98312 | tf_op jit(solution)/shard_map/ppermute | solution.py:54
  151.0 2.4 %collective-permute-start.18 = (f32[32,256]{1,0:T(8,128)S(1)}, f32[32,256]{1,0:T(8,128)S(1)}, u32[]{:S(2)}, u32[]{:S(2)}) collective-permute-start(f32[32,256]{1,0:T(8,128)S(1)} %add_add_fusion.r0), channel_id=1, source_target_pairs={{224,0},{228,4},{232,8},{236,12},{240,16},{244,20},{248,24},{252,2... | collective-permute-start | bytes 98312 | tf_op jit(solution)/shard_map/ppermute | solution.py:54
  153.4 1.6 collective-permute-done.19.r2
  154.9 0.4 collective-permute-done.18.r1
  155.3 0.2 copy-done.18
  155.5 0.4 copy-done.19
  155.9 2.9 %upper.1 = f32[32,256]{1,0:T(8,128)} custom-call(f32[32,256]{1,0:T(8,128)} %copy-done.12, f32[32,256]{1,0:T(8,128)} %copy-done.19, f32[32,256]{1,0:T(8,128)} %copy-done.18, f32[32,256]{1,0:T(8,128)} %copy-done.17, f32[256,1024]{1,0:T(8,128)} %get-tuple-element.28.m3, f32[256,256]{1,0:T(8,128)} %get-tuple-element.29.f2, f32[32,256]{1,0:T(8,128)} %get-tuple-element.30.w2), custom_call_target="tpu_custom_call" | custom-call | tf_op jit(solution)/shard_map/upper/pallas_call | solution.py:353
  158.8 9.3 %all-gather.1 = f32[128,256]{1,0:T(8,128)} all-gather(f32[32,256]{1,0:T(8,128)} %upper.1), channel_id=3, replica_groups={{0,4,8,12},{24,28,16,20},{32,36,40,44},{56,60,48,52},{64,68,72,76},{88,..., dimensions={0}, use_global_device_ids=true | all-gather | bytes 163840 | tf_op jit(solution)/shard_map/all_gather | solution.py:62
  168.2 4.0 %down1.1 = f32[256,128]{1,0:T(8,128)} custom-call(f32[4,32,256]{2,1,0:T(8,128)} %bitcast.21, f32[1024,256]{1,0:T(8,128)} %get-tuple-element.31.e1, f32[1,336,1024]{2,1,0:T(8,128)} %m1.3, f32[256,128]{1,0:T(8,128)} %get-tuple-element.32.w1), custom_call_target="tpu_custom_call" | custom-call | tf_op jit(solution)/shard_map/down1/pallas_call | solution.py:365
  172.1 8.9 %all-gather.2 = f32[1024,128]{1,0:T(8,128)} all-gather(f32[256,128]{1,0:T(8,128)} %down1.1), channel_id=4, replica_groups={{0,4,8,12},{16,20,24,28},{32,36,40,44},{48,52,56,60},{64,68,72,76},{80,..., dimensions={0}, use_global_device_ids=true | all-gather | bytes 655360 | tf_op jit(solution)/shard_map/all_gather | solution.py:62
  181.1 6.8 %finish.1 = f32[1024,128]{1,0:T(8,128)} custom-call(s32[4]{0:T(128)} %pad_add_fusion.place, s32[64]{0:T(128)} %leaf_map.3, s32[1,1024]{1,0:T(1,128)} %order.1, f32[4,256,128]{2,1,0:T(8,128)} %bitcast.18, f32[1024,128]{1,0:T(8,128)} %get-tuple-element.33.ordered, f32[1,1024,256]{2,1,0:T(8,128)} %basis.1, f32[1,1024,1024]{2,1,0:T(8,128)} %solve.1), custom_call_target="tpu_custom_call" | custom-call | tf_op jit(solution)/shard_map/finish/pallas_call | solution.py:416
  187.9 13.7 %all_to_all.29.delta = f32[4,256,128]{2,1,0:T(8,128)} all-to-all(f32[4,256,128]{2,1,0:T(8,128)} %bitcast.19), channel_id=1, replica_groups=mesh['leaf'=64,'col'=4] {'col'}, dimensions={0} | all-to-all | bytes 1048576 | tf_op jit(solution)/shard_map/all_to_all | solution.py:452
  201.6 2.4 %outputs.1 = (f32[256,512]{1,0:T(8,128)}, f32[256,512]{1,0:T(8,128)}) custom-call(f32[4,256,128]{2,1,0:T(8,128)} %copy-done.5, f32[4,256,128]{2,1,0:T(8,128)} %all_to_all.29.delta, f32[256,512]{1,0:T(8,128)} %coefs.1), custom_call_target="tpu_custom_call" | custom-call | tf_op jit(solution)/shard_map/outputs/pallas_call | solution.py:446
  (55 shorter events, 0.2 us)
Async XLA Ops:
  2.6 21.7 %copy-start.4 = (f32[256,640]{1,0:T(8,128)S(1)}, f32[256,640]{1,0:T(8,128)}, u32[]{:S(2)}) copy-start(f32[256,640]{1,0:T(8,128)} %pack.1.p0) | copy-start | bytes 1966084
  2.6 25.3 %collective-permute-start.4 = (f32[256,640]{1,0:T(8,128)}, f32[256,640]{1,0:T(8,128)S(1)}, u32[]{:S(2)}, u32[]{:S(2)}) collective-permute-start(f32[256,640]{1,0:T(8,128)} %pack.1.p0), channel_id=1, source_target_pairs={{0,248},{4,252},{8,0},{12,4},{16,8},{20,12},{24,16},{28,20},{32,24... | collective-permute-start | bytes 1966088 | tf_op jit(solution)/shard_map/ppermute | solution.py:32
  11.2 18.9 %collective-permute-start.3 = (f32[256,640]{1,0:T(8,128)}, f32[256,640]{1,0:T(8,128)S(1)}, u32[]{:S(2)}, u32[]{:S(2)}) collective-permute-start(f32[256,640]{1,0:T(8,128)} %pack.1.p0), channel_id=1, source_target_pairs={{0,8},{4,12},{8,16},{12,20},{16,24},{20,28},{24,32},{28,36},{32,40... | collective-permute-start | bytes 1966088 | tf_op jit(solution)/shard_map/ppermute | solution.py:32
  11.2 32.6 %collective-permute-start.2 = (f32[256,128]{1,0:T(8,128)}, f32[256,128]{1,0:T(8,128)S(1)}, u32[]{:S(2)}, u32[]{:S(2)}) collective-permute-start(f32[256,128]{1,0:T(8,128)} %x0.3), channel_id=1, source_target_pairs={{0,3},{1,0},{2,1},{3,2},{4,7},{5,4},{6,5},{7,6},{8,11},{9,8},{10,9... | collective-permute-start | bytes 393224 | tf_op jit(solution)/shard_map/ppermute | solution.py:58
  14.0 29.9 %collective-permute-start.1 = (f32[256,128]{1,0:T(8,128)}, f32[256,128]{1,0:T(8,128)S(1)}, u32[]{:S(2)}, u32[]{:S(2)}) collective-permute-start(f32[256,128]{1,0:T(8,128)} %x0.3), channel_id=1, source_target_pairs={{0,2},{1,3},{2,0},{3,1},{4,6},{5,7},{6,4},{7,5},{8,10},{9,11},{10,... | collective-permute-start | bytes 393224 | tf_op jit(solution)/shard_map/ppermute | solution.py:58
  16.4 16.5 %copy-start.20 = (s32[1,1024]{1,0:T(1,128)S(1)}, s32[1,1024]{1,0:T(1,128)}, u32[]{:S(2)}) copy-start(s32[1,1024]{1,0:T(1,128)} %order.1) | copy-start | bytes 12292
  16.4 7.9 %collective-permute-start.7 = (f32[128,256]{1,0:T(8,128)}, f32[128,256]{1,0:T(8,128)S(1)}, u32[]{:S(2)}, u32[]{:S(2)}) collective-permute-start(f32[128,256]{1,0:T(8,128)} %shard_map.122), channel_id=1, source_target_pairs={{0,32},{4,36},{8,40},{12,44},{16,48},{20,52},{24,56},{28,60},{32,0... | collective-permute-start | bytes 393224 | tf_op jit(solution)/shard_map/ppermute | solution.py:32
  20.9 15.8 %copy-start.6 = (f32[256,128]{1,0:T(8,128)S(1)}, f32[256,128]{1,0:T(8,128)}, u32[]{:S(2)}) copy-start(f32[256,128]{1,0:T(8,128)} %x0.3) | copy-start | bytes 393220
  24.3 1.5 copy-start.9
  24.3 19.6 %collective-permute-start.6 = (f32[256,640]{1,0:T(8,128)S(1)}, f32[256,640]{1,0:T(8,128)}, u32[]{:S(2)}, u32[]{:S(2)}) collective-permute-start(f32[256,640]{1,0:T(8,128)S(1)} %copy-done.4), channel_id=1, source_target_pairs={{0,4},{4,0},{8,12},{12,8},{16,20},{20,16},{24,28},{28,24},{32,36},... | collective-permute-start | bytes 1966088 | tf_op jit(solution)/shard_map/ppermute | solution.py:32
  28.0 12.1 %copy-start.2 = (f32[256,640]{1,0:T(8,128)}, f32[256,640]{1,0:T(8,128)S(1)}, u32[]{:S(2)}) copy-start(f32[256,640]{1,0:T(8,128)S(1)} %collective-permute-done.4.p1) | copy-start | bytes 1966084
  28.0 8.7 %collective-permute-start.8 = (f32[256,256]{1,0:T(8,128)}, f32[256,256]{1,0:T(8,128)}, u32[]{:S(2)}, u32[]{:S(2)}) collective-permute-start(f32[256,256]{1,0:T(8,128)} %shard_map.123), channel_id=1, source_target_pairs={{0,24},{4,28},{8,16},{12,20},{16,8},{20,12},{24,0},{28,4},{32,56},... | collective-permute-start | bytes 786440 | tf_op jit(solution)/shard_map/ppermute | solution.py:32
  30.1 10.0 %copy-start.3 = (f32[256,640]{1,0:T(8,128)}, f32[256,640]{1,0:T(8,128)S(1)}, u32[]{:S(2)}) copy-start(f32[256,640]{1,0:T(8,128)S(1)} %collective-permute-done.3.p0) | copy-start | bytes 1966084
  31.1 20.3 %collective-permute-start.5 = (f32[256,640]{1,0:T(8,128)}, f32[256,640]{1,0:T(8,128)}, u32[]{:S(2)}, u32[]{:S(2)}) collective-permute-start(f32[256,640]{1,0:T(8,128)} %broadcast_select_fusion), channel_id=1, source_target_pairs={{0,4},{4,0},{8,12},{12,8},{16,20},{20,16},{24,28},{28,24},{32,36},... | collective-permute-start | bytes 1966088 | tf_op jit(solution)/shard_map/ppermute | solution.py:32
  36.7 7.2 %collective-permute-start = (f32[256,128]{1,0:T(8,128)S(1)}, f32[256,128]{1,0:T(8,128)S(1)}, u32[]{:S(2)}, u32[]{:S(2)}) collective-permute-start(f32[256,128]{1,0:T(8,128)S(1)} %copy-done.6), channel_id=1, source_target_pairs={{0,1},{1,2},{2,3},{3,0},{4,5},{5,6},{6,7},{7,4},{8,9},{9,10},{10,1... | collective-permute-start | bytes 393224 | tf_op jit(solution)/shard_map/ppermute | solution.py:58
  43.9 0.7 copy-start.7
  43.9 0.7 copy-start.8
  43.9 0.7 copy-start.10
  51.4 15.2 %copy-start.1 = (f32[1024,256]{1,0:T(8,128)S(1)}, f32[1024,256]{1,0:T(8,128)}, u32[]{:S(2)}) copy-start(f32[1024,256]{1,0:T(8,128)} %shard_map.124.b0) | copy-start | bytes 3145732
  62.7 11.1 %all-to-all-start = ((f32[4,256,128]{2,1,0:T(8,128)}), f32[4,256,128]{2,1,0:T(8,128)S(1)}, u32[]{:S(2)}, u32[]{:S(2)}) async-start(f32[4,256,128]{2,1,0:T(8,128)} %get-tuple-element.20), calls=%async_computation | async-start | bytes 1048576 | tf_op jit(solution)/shard_map/all_to_all | solution.py:452
  66.6 45.1 %collective-permute-start.13 = (f32[1024,256]{1,0:T(8,128)S(1)}, f32[1024,256]{1,0:T(8,128)}, u32[]{:S(2)}, u32[]{:S(2)}) collective-permute-start(f32[1024,256]{1,0:T(8,128)S(1)} %copy-done.1), channel_id=1, source_target_pairs={{0,8},{4,12},{8,0},{12,4},{16,24},{20,28},{24,16},{28,20},{32,40},... | collective-permute-start | bytes 3145736 | tf_op jit(solution)/shard_map/ppermute | solution.py:32
  99.1 7.0 %all-to-all-start.3 = ((f32[4,32,256]{2,1,0:T(8,128)}), f32[4,32,256]{2,1,0:T(8,128)S(1)}, u32[]{:S(2)}, u32[]{:S(2)}) async-start(f32[4,32,256]{2,1,0:T(8,128)} %bitcast.23), calls=%async_computation.3 | async-start | bytes 262144 | tf_op jit(solution)/shard_map/all_to_all | solution.py:505
  106.1 29.3 %all-to-all-start.1 = ((f32[4,1024,128]{2,1,0:T(8,128)}), f32[4,1024,128]{2,1,0:T(8,128)S(1)}, u32[]{:S(2)}, u32[]{:S(2)}) async-start(f32[4,1024,128]{2,1,0:T(8,128)} %get-tuple-element.21), calls=%async_computation.1 | async-start | bytes 4194304 | tf_op jit(solution)/shard_map/all_to_all | solution.py:452
  110.4 5.5 %collective-permute-start.12 = (f32[1024,256]{1,0:T(8,128)S(1)}, f32[1024,256]{1,0:T(8,128)}, u32[]{:S(2)}, u32[]{:S(2)}) collective-permute-start(f32[1024,256]{1,0:T(8,128)S(1)} %copy-done.1), channel_id=1, source_target_pairs={{0,4},{4,0},{8,12},{12,8},{16,20},{20,16},{24,28},{28,24},{32,36},... | collective-permute-start | bytes 3145736 | tf_op jit(solution)/shard_map/ppermute | solution.py:32
  111.7 4.2 %collective-permute-start.14 = (f32[1024,256]{1,0:T(8,128)}, f32[1024,256]{1,0:T(8,128)}, u32[]{:S(2)}, u32[]{:S(2)}) collective-permute-start(f32[1024,256]{1,0:T(8,128)} %collective-permute-done.13.b2), channel_id=1, source_target_pairs={{0,4},{4,0},{8,12},{12,8},{16,20},{20,16},{24,28},{28,24},{32,36},... | collective-permute-start | bytes 3145736 | tf_op jit(solution)/shard_map/ppermute | solution.py:32
  111.8 8.4 %copy-start.11 = (f32[32,256]{1,0:T(8,128)}, f32[32,256]{1,0:T(8,128)S(1)}, u32[]{:S(2)}) copy-start(f32[32,256]{1,0:T(8,128)S(1)} %reduce_sum.19.r0) | copy-start | bytes 98308
  111.8 8.3 %collective-permute-start.11 = (f32[32,256]{1,0:T(8,128)S(1)}, f32[32,256]{1,0:T(8,128)S(1)}, u32[]{:S(2)}, u32[]{:S(2)}) collective-permute-start(f32[32,256]{1,0:T(8,128)S(1)} %reduce_sum.19.r0), channel_id=1, source_target_pairs={{0,56},{4,60},{8,48},{12,52},{16,40},{20,44},{24,32},{28,36},{32,2... | collective-permute-start | bytes 98312 | tf_op jit(solution)/shard_map/ppermute | solution.py:32
  115.5 4.7 %collective-permute-start.10 = (f32[32,256]{1,0:T(8,128)S(1)}, f32[32,256]{1,0:T(8,128)S(1)}, u32[]{:S(2)}, u32[]{:S(2)}) collective-permute-start(f32[32,256]{1,0:T(8,128)S(1)} %reduce_sum.19.r0), channel_id=1, source_target_pairs={{0,32},{4,36},{8,40},{12,44},{16,48},{20,52},{24,56},{28,60},{32,0... | collective-permute-start | bytes 98312 | tf_op jit(solution)/shard_map/ppermute | solution.py:32
  115.5 4.7 %collective-permute-start.9 = (f32[32,256]{1,0:T(8,128)S(1)}, f32[32,256]{1,0:T(8,128)S(1)}, u32[]{:S(2)}, u32[]{:S(2)}) collective-permute-start(f32[32,256]{1,0:T(8,128)S(1)} %reduce_sum.19.r0), channel_id=1, source_target_pairs={{0,24},{4,28},{8,16},{12,20},{16,8},{20,12},{24,0},{28,4},{32,56},... | collective-permute-start | bytes 98312 | tf_op jit(solution)/shard_map/ppermute | solution.py:32
  120.1 0.6 copy-start.14
  120.1 0.6 copy-start.15
  120.2 0.6 copy-start.16
  123.5 20.1 %copy-start.13 = (f32[32,256]{1,0:T(8,128)S(1)}, f32[32,256]{1,0:T(8,128)}, u32[]{:S(2)}) copy-start(f32[32,256]{1,0:T(8,128)} %get-tuple-element.27) | copy-start | bytes 98308
  123.5 20.1 %collective-permute-start.17 = (f32[32,256]{1,0:T(8,128)}, f32[32,256]{1,0:T(8,128)S(1)}, u32[]{:S(2)}, u32[]{:S(2)}) collective-permute-start(f32[32,256]{1,0:T(8,128)} %get-tuple-element.27), channel_id=1, source_target_pairs={{0,56},{4,60},{8,48},{12,52},{16,40},{20,44},{24,32},{28,36},{32,2... | collective-permute-start | bytes 98312 | tf_op jit(solution)/shard_map/ppermute | solution.py:32
  127.0 16.6 %collective-permute-start.16 = (f32[32,256]{1,0:T(8,128)}, f32[32,256]{1,0:T(8,128)S(1)}, u32[]{:S(2)}, u32[]{:S(2)}) collective-permute-start(f32[32,256]{1,0:T(8,128)} %get-tuple-element.27), channel_id=1, source_target_pairs={{0,32},{4,36},{8,40},{12,44},{16,48},{20,52},{24,56},{28,60},{32,0... | collective-permute-start | bytes 98312 | tf_op jit(solution)/shard_map/ppermute | solution.py:32
  127.0 16.6 %collective-permute-start.15 = (f32[32,256]{1,0:T(8,128)}, f32[32,256]{1,0:T(8,128)S(1)}, u32[]{:S(2)}, u32[]{:S(2)}) collective-permute-start(f32[32,256]{1,0:T(8,128)} %get-tuple-element.27), channel_id=1, source_target_pairs={{0,24},{4,28},{8,16},{12,20},{16,8},{20,12},{24,0},{28,4},{32,56},... | collective-permute-start | bytes 98312 | tf_op jit(solution)/shard_map/ppermute | solution.py:32
  135.5 1.3 copy-start
  140.1 47.7 %all-to-all-start.2 = ((f32[4,256,128]{2,1,0:T(8,128)}), f32[4,256,128]{2,1,0:T(8,128)S(1)}, u32[]{:S(2)}, u32[]{:S(2)}) async-start(f32[4,256,128]{2,1,0:T(8,128)} %bitcast.22), calls=%async_computation.2 | async-start | bytes 1048576 | tf_op jit(solution)/shard_map/all_to_all | solution.py:452
  143.7 11.7 %copy-start.12 = (f32[32,256]{1,0:T(8,128)}, f32[32,256]{1,0:T(8,128)S(1)}, u32[]{:S(2)}) copy-start(f32[32,256]{1,0:T(8,128)S(1)} %add_add_fusion.r0) | copy-start | bytes 98308
  143.7 9.7 %collective-permute-start.20 = (f32[32,256]{1,0:T(8,128)S(1)}, f32[32,256]{1,0:T(8,128)S(1)}, u32[]{:S(2)}, u32[]{:S(2)}) collective-permute-start(f32[32,256]{1,0:T(8,128)S(1)} %add_add_fusion.r0), channel_id=1, source_target_pairs={{160,0},{164,4},{168,8},{172,12},{176,16},{180,20},{184,24},{188,2... | collective-permute-start | bytes 98312 | tf_op jit(solution)/shard_map/ppermute | solution.py:54
  151.0 4.0 %collective-permute-start.19 = (f32[32,256]{1,0:T(8,128)S(1)}, f32[32,256]{1,0:T(8,128)S(1)}, u32[]{:S(2)}, u32[]{:S(2)}) collective-permute-start(f32[32,256]{1,0:T(8,128)S(1)} %add_add_fusion.r0), channel_id=1, source_target_pairs={{64,0},{68,4},{72,8},{76,12},{80,16},{84,20},{88,24},{92,28},{224,... | collective-permute-start | bytes 98312 | tf_op jit(solution)/shard_map/ppermute | solution.py:54
  151.0 4.4 %collective-permute-start.18 = (f32[32,256]{1,0:T(8,128)S(1)}, f32[32,256]{1,0:T(8,128)S(1)}, u32[]{:S(2)}, u32[]{:S(2)}) collective-permute-start(f32[32,256]{1,0:T(8,128)S(1)} %add_add_fusion.r0), channel_id=1, source_target_pairs={{224,0},{228,4},{232,8},{236,12},{240,16},{244,20},{248,24},{252,2... | collective-permute-start | bytes 98312 | tf_op jit(solution)/shard_map/ppermute | solution.py:54
  153.4 2.0 copy-start.17
  154.9 0.6 copy-start.18
  155.3 0.6 copy-start.19
  187.9 13.7 %copy-start.5 = (f32[4,256,128]{2,1,0:T(8,128)}, f32[4,256,128]{2,1,0:T(8,128)S(1)}, u32[]{:S(2)}) copy-start(f32[4,256,128]{2,1,0:T(8,128)S(1)} %all-to-all-done.2.res) | copy-start | bytes 1572868
where the time goes:
time: 205 us; the launch traced here: 204 us
  Pallas kernels  56.3 us (27%)
  blocking collectives  54.3 us (26%)
  starting transfers between devices  52.1 us (25%)
  waiting for transfers between devices  26.3 us (13%)
  matrix products  7.61 us (4%)
  local copies, waits for them, and re-layouts  4.29 us (2%)
    all_gather x3, blocking collectives, gather4(): return lax.all_gather(value, 'leaf', axis=0, axis_index_groups=groups)  40.6 us
    ppermute x15, starting transfers between devices, leaf_route(): return lax.ppermute(value, 'leaf', [(i, target(i)) for i in range(LEAVES)])  23 us
    all_to_all x3, waiting for transfers between devices, swap_cols(): return lax.all_to_all(value, 'col', 0, 0, tiled=True)  14.3 us
    all_to_all x1, blocking collectives, swap_cols(): return lax.all_to_all(value, 'col', 0, 0, tiled=True)  13.7 us
    all_to_all x3, starting transfers between devices, swap_cols(): return lax.all_to_all(value, 'col', 0, 0, tiled=True)  11.6 us
    pallas_call x1, Pallas kernels, far_call(): pl.pallas_call(far_kernel, grid=(2,), in_specs=[SMEM, SMEM, SMEM] + [whol...  11.3 us
    ppermute x3, starting transfers between devices, z_from(): return lax.ppermute(value, 'leaf', route)  9.67 us
    dot_general x3, matrix products, mm(): lax.dot_general(a, b, (dims, ((), ())), precision=precision, preferred_el...  7.61 us
  transfers between devices with their start and end apart: 25, of which 8 were waited for; matrix products, arithmetic and copies ran while one was open for 5% of the time, Pallas kernels for 20%

commit v1 on v0

--- a/solution.py
+++ b/solution.py
@@ -6,7 +6,6 @@
 from jax.sharding import PartitionSpec as P
 
 
-HIGH = lax.Precision.HIGH
 F32 = jnp.float32
 BF16 = jnp.bfloat16
 Q = 256
@@ -62,20 +61,6 @@
     return lax.all_gather(value, "leaf", axis=0, axis_index_groups=groups)
 
 
-def mm(a, b, dims, precision=HIGH):
-    return lax.dot_general(a, b, (dims, ((), ())), precision=precision, preferred_element_type=F32)
-
-
-def halves(value):
-    top = lax.reduce_precision(value, 8, 7)
-    return top.astype(BF16), (value - top).astype(BF16)
-
-
-def select(value, picks, dims):
-    a, b = halves(value)
-    return mm(a, picks, dims, None) + mm(b, picks, dims, None)
-
-
 NN = ((1,), (0,))
 NT = ((1,), (1,))
 
@@ -96,10 +81,23 @@
 
 
 SMEM = pl.BlockSpec(memory_space=pltpu.SMEM)
-
-
-def whole(*shape):
-    return pl.BlockSpec(shape, lambda *i: (0,) * len(shape))
+VMEM = pl.BlockSpec(memory_space=pltpu.VMEM)
+
+
+def near_memory(value):
+    return pltpu.with_memory_space_constraint(value, pltpu.VMEM)
+
+
+def kernel(body, outs, values, scalars=(), scratch=()):
+    result = pl.pallas_call(
+        body,
+        in_specs=[SMEM] * len(scalars) + [VMEM] * len(values),
+        out_specs=[VMEM] * len(outs),
+        out_shape=[pltpu.VMEM(shape, F32) for shape in outs],
+        scratch_shapes=list(scratch),
+        compiler_params=pltpu.CompilerParams(vmem_limit_bytes=20 << 20),
+    )(*scalars, *[near_memory(value) for value in values])
+    return result if len(outs) > 1 else result[0]
 
 
 def like(*shape, dtype=F32):
@@ -142,46 +140,44 @@
 
 
 def near_kernel(place, mask, x0, x1, x2, x3, p0, p1, out, *scratch):
-    i = pl.program_id(0)
-
-    @pl.when(i == 0)
-    def _():
-        blocks = [(p[:, :128], p[:, 128:]) for p in (p0, p1)]
-        tile_setup(place, (x0, x1, x2, x3), blocks, *scratch)
-
+    blocks = [(p[:, :128], p[:, 128:]) for p in (p0, p1)]
+    tile_setup(place, (x0, x1, x2, x3), blocks, *scratch)
     weights = (mask[0, 2].astype(F32), mask[0, 3 - 2 * place[0]].astype(F32))
-    out[...] = tile_sum(i, weights, *scratch)
+
+    @pl.loop(0, 2)
+    def _(i):
+        out[pl.ds(pl.multiple_of(i * CHUNK, CHUNK), CHUNK), :] = tile_sum(i, weights, *scratch)
 
 
 def far_kernel(
     place, mask, ridge, x0, x1, x2, x3, p0, p1, p2, near, own_y, own_a, lead, out, led, *scratch
 ):
-    i = pl.program_id(0)
-
-    @pl.when(i == 0)
-    def _():
-        blocks = [(p[:, :128], p[:, 128:]) for p in (p0, p1, p2)]
-        tile_setup(place, (x0, x1, x2, x3), blocks, *scratch)
-
+    blocks = [(p[:, :128], p[:, 128:]) for p in (p0, p1, p2)]
+    tile_setup(place, (x0, x1, x2, x3), blocks, *scratch)
     weights = (
         mask[0, 0].astype(F32),
         mask[0, 4].astype(F32),
         mask[0, 1 + 2 * place[0]].astype(F32),
     )
-    total = near[...] + tile_sum(i, weights, *scratch)
-    own = own_y[...] - ridge[0] * own_a[...]
-    part = jnp.concatenate(
-        [
-            jnp.where(place[2] == 2 * i + h, own, 0.0) - total[h * Q : (h + 1) * Q]
-            for h in range(2)
-        ],
-        axis=0,
-    )
-    product = dot3(lead[...], part)
     for k in range(4):
-        out[k] = part[:, k * 128 : (k + 1) * 128]
-        piece = product[:, k * 128 : (k + 1) * 128]
-        led[k] = jnp.where(i == 0, piece, led[k] + piece)
+        led[k] = jnp.zeros((RANK, 128), F32)
+
+    @pl.loop(0, 2)
+    def _(i):
+        rows = pl.ds(pl.multiple_of(i * CHUNK, CHUNK), CHUNK)
+        total = near[rows, :] + tile_sum(i, weights, *scratch)
+        own = own_y[...] - ridge[0] * own_a[...]
+        part = jnp.concatenate(
+            [
+                jnp.where(place[2] == 2 * i + h, own, 0.0) - total[h * Q : (h + 1) * Q]
+                for h in range(2)
+            ],
+            axis=0,
+        )
+        product = dot3(lead[:, rows], part)
+        for k in range(4):
+            out[k, rows, :] = part[:, k * 128 : (k + 1) * 128]
+            led[k] += product[:, k * 128 : (k + 1) * 128]
 
 
 def tile_scratch(count):
@@ -196,32 +192,39 @@
 
 
 def near_call(place, mask, xs, blocks):
-    return pl.pallas_call(
-        near_kernel,
-        grid=(2,),
-        in_specs=[SMEM, SMEM] + [whole(Q, 128)] * 4 + [whole(Q, 640)] * 2,
-        out_specs=pl.BlockSpec((CHUNK, 512), lambda i: (i, 0)),
-        out_shape=like(1024, 512),
-        scratch_shapes=tile_scratch(2),
-        name="near",
-    )(place, mask, *xs, *blocks)
+    return kernel(near_kernel, [(1024, 512)], [*xs, *blocks], (place, mask), tile_scratch(2))
 
 
 def far_call(place, mask, ridge, xs, blocks, near, own_y, own_a, lead):
-    return pl.pallas_call(
+    return kernel(
         far_kernel,
-        grid=(2,),
-        in_specs=[SMEM, SMEM, SMEM]
-        + [whole(Q, 128)] * 4
-        + [whole(Q, 640)] * 3
-        + [pl.BlockSpec((CHUNK, 512), lambda i: (i, 0))]
-        + [whole(Q, 512)] * 2
-        + [pl.BlockSpec((RANK, CHUNK), lambda i: (0, i))],
-        out_specs=[pl.BlockSpec((4, CHUNK, 128), lambda i: (0, i, 0)), whole(4, RANK, 128)],
-        out_shape=[like(4, 1024, 128), like(4, RANK, 128)],
-        scratch_shapes=tile_scratch(3),
-        name="far",
-    )(place, mask, ridge, *xs, *blocks, near, own_y, own_a, lead)
+        [(4, 1024, 128), (4, RANK, 128)],
+        [*xs, *blocks, near, own_y, own_a, lead],
+        (place, mask, ridge),
+        tile_scratch(3),
+    )
+
+
+def picks_by_row(order, picks):
+    at = lax.broadcasted_iota(jnp.int32, picks.shape, 0)
+    picks[...] = jnp.where(order == at, 1.0, 0.0).astype(BF16)
+
+
+def lead_kernel(order, basis, solve, lead, picks):
+    picks_by_row(order[...], picks)
+    turned = jnp.transpose(basis[0])
+    both = jnp.concatenate(split(dot3(turned, solve[0])), axis=0)
+    chosen = dot(both, picks[...], NT)
+    lead[...] = chosen[:RANK] + chosen[RANK:]
+
+
+def lead_call(order, leaf_basis, leaf_inverse):
+    return kernel(
+        lead_kernel,
+        [(RANK, 1024)],
+        [order, leaf_basis, leaf_inverse],
+        scratch=[pltpu.VMEM((1024, 1024), BF16)],
+    )
 
 
 def pack_kernel(a, b, out):
@@ -230,7 +233,7 @@
 
 
 def pack_call(a, b):
-    return pl.pallas_call(pack_kernel, out_shape=like(Q, 640), name="pack")(a, b)
+    return kernel(pack_kernel, [(Q, 640)], [a, b])
 
 
 def fill_slices(transfer, inverse, out, start):
@@ -260,7 +263,7 @@
 
 
 def collect(body, rows, *parts):
-    return pl.pallas_call(body, out_shape=like(rows, 256))(*parts)
+    return kernel(body, [(rows, 256)], parts)
 
 
 def nodes_kernel(place, b0, b1, b2, b3, e1, m2, f2, m3, own_e2, e2):
@@ -290,36 +293,32 @@
 
 
 def nodes_call(place, blocks):
-    return pl.pallas_call(
+    return kernel(
         nodes_kernel,
-        in_specs=[SMEM] + [whole(1024, 256)] * 4,
-        out_specs=[whole(1024, 256), whole(256, 1024), whole(256, 256), whole(256, 1024), whole(256, 256)],
-        out_shape=[like(1024, 256), like(256, 1024), like(256, 256), like(256, 1024), like(256, 256)],
-        scratch_shapes=[pltpu.VMEM((1024, 256), F32)],
-        grid=(1,),
-        name="nodes",
-    )(place, *blocks)
+        [(1024, 256), (256, 1024), (256, 256), (256, 1024), (256, 256)],
+        blocks,
+        (place,),
+        [pltpu.VMEM((1024, 256), F32)],
+    )
 
 
 def level1_kernel(place, leaf_map, stacked, m1, e1, w1, p1):
     base = place[3] // 4 * 4
     total = None
     for k in range(4):
-        term = dot3(m1[0, :, k * 256 : (k + 1) * 256], stacked[leaf_map[base + k] - base])
+        term = dot3(m1[0, :256, k * 256 : (k + 1) * 256], stacked[leaf_map[base + k] - base])
         total = term if total is None else total + term
     w1[...] = total
-    p1[...] = dot3(jnp.transpose(total), e1[0])
+    p1[...] = dot3(jnp.transpose(total), e1[0, :256, :])
 
 
 def level1_call(place, leaf_map, stacked, node_inverse, node_transfer):
-    return pl.pallas_call(
+    return kernel(
         level1_kernel,
-        grid=(1,),
-        in_specs=[SMEM, SMEM, whole(4, 256, 128), whole(1, 256, 1024), whole(1, 256, 256)],
-        out_specs=[whole(256, 128), whole(128, 256)],
-        out_shape=[like(256, 128), like(128, 256)],
-        name="level1",
-    )(place, leaf_map, stacked, node_inverse, node_transfer)
+        [(256, 128), (128, 256)],
+        [stacked, node_inverse, node_transfer],
+        (place, leaf_map),
+    )
 
 
 def row_blocks(parts, matrix):
@@ -337,11 +336,7 @@
 
 
 def level2_call(parts, m2, e2):
-    return pl.pallas_call(
-        level2_kernel,
-        out_shape=[like(32, 256), like(32, 256)],
-        name="level2",
-    )(*parts, m2, e2)
+    return kernel(level2_kernel, [(32, 256), (32, 256)], [*parts, m2, e2])
 
 
 def upper_kernel(r0, r1, r2, r3, m3, f2, w2, g1):
@@ -350,89 +345,76 @@
 
 
 def upper_call(parts, m3, f2, w2):
-    return pl.pallas_call(upper_kernel, out_shape=like(32, 256), name="upper")(
-        *parts, m3, f2, w2
-    )
+    return kernel(upper_kernel, [(32, 256)], [*parts, m3, f2, w2])
 
 
 def down1_kernel(g1, e1, m1, w1, v1):
     g = g1[...].reshape(128, 256)
     lifted = dot3(g, e1[...], NT)
-    v1[...] = w1[...] - dot3(m1[0], lifted, NT)
+    v1[...] = w1[...] - dot3(m1[0, :256, :], lifted, NT)
 
 
 def down1_call(g1, e1, node_inverse, w1):
-    return pl.pallas_call(
-        down1_kernel,
-        grid=(1,),
-        in_specs=[whole(4, 32, 256), whole(1024, 256), whole(1, 256, 1024), whole(256, 128)],
-        out_specs=whole(256, 128),
-        out_shape=like(256, 128),
-        name="down1",
-    )(g1, e1, node_inverse, w1)
+    return kernel(down1_kernel, [(256, 128)], [g1, e1, node_inverse, w1])
 
 
 def residual_kernel(order, parts, res, ordered, picks):
     res_sum = parts[0] + parts[1] + (parts[2] + parts[3])
     res[...] = res_sum
+    rows = jnp.broadcast_to(order[...].astype(F32), (128, 1024))
+    holds = jnp.transpose(rows)[:, :1].astype(jnp.int32)
     at = lax.broadcasted_iota(jnp.int32, (1024, 1024), 1)
-    picks[...] = jnp.where(order[...] == at, 1.0, 0.0).astype(BF16)
+    picks[...] = jnp.where(holds == at, 1.0, 0.0).astype(BF16)
     both = dot(picks[...], jnp.concatenate(split(res_sum), axis=1))
     ordered[...] = both[:, :128] + both[:, 128:]
 
 
 def residual_call(order, parts):
-    return pl.pallas_call(
+    return kernel(
         residual_kernel,
-        out_shape=[like(1024, 128), like(1024, 128)],
-        scratch_shapes=[pltpu.VMEM((1024, 1024), BF16)],
-        name="residual",
-    )(order, parts)
-
-
-def finish_kernel(place, leaf_map, order, pieces, ordered, basis, solve, delta, picks, rhs):
-    i = pl.program_id(0)
-
-    @pl.when(i == 0)
-    def _():
-        base = place[3] // 4 * 4
-        slot = jnp.int32(3)
-        for k in range(3):
-            slot = jnp.where(leaf_map[base + k] == place[3], k, slot)
-        top, low = split(ordered[...] - dot3(basis[0], pieces[slot]))
-        rhs[...] = jnp.concatenate([top, low], axis=1)
-
-    a, b = split(solve[0])
-    both = dot(a, rhs[...])
-    y = both[:, :128] + (both[:, 128:] + dot(b, rhs[:, :128]))
-    at = lax.broadcasted_iota(jnp.int32, (1024, Q), 0)
-    picks[...] = jnp.where(order[...] == at, 1.0, 0.0).astype(BF16)
-    both = dot(picks[...], jnp.concatenate(split(y), axis=1))
-    term = both[:, :128] + both[:, 128:]
-    delta[...] = jnp.where(i == 0, term, delta[...] + term)
+        [(1024, 128), (1024, 128)],
+        [order, parts],
+        scratch=[pltpu.VMEM((1024, 1024), BF16)],
+    )
+
+
+def finish_kernel(place, leaf_map, order, pieces, ordered, basis, solve, delta, picks, rhs, sides):
+    base = place[3] // 4 * 4
+    slot = jnp.int32(3)
+    for k in range(3):
+        slot = jnp.where(leaf_map[base + k] == place[3], k, slot)
+    rhs[...] = jnp.concatenate(
+        split(ordered[...] - dot3(basis[0], pieces[slot])), axis=1
+    )
+    picks_by_row(order[...], picks)
+
+    @pl.loop(0, 2)
+    def _(i):
+        rows = pl.ds(pl.multiple_of(i * CHUNK, CHUNK), CHUNK)
+        a, b = split(solve[0, rows, :])
+        both = dot(a, rhs[...])
+        y = both[:, :128] + (both[:, 128:] + dot(b, rhs[:, :128]))
+        sides[rows, :] = jnp.concatenate(split(y), axis=1)
+
+    @pl.loop(0, 2)
+    def _(i):
+        rows = pl.ds(pl.multiple_of(i * CHUNK, CHUNK), CHUNK)
+        both = dot(picks[rows, :], sides[...])
+        delta[rows, :] = both[:, :128] + both[:, 128:]
 
 
 def finish_call(place, leaf_map, order, pieces, ordered, leaf_basis, leaf_inverse):
-    return pl.pallas_call(
+    return kernel(
         finish_kernel,
-        grid=(4,),
-        in_specs=[
-            SMEM,
-            SMEM,
-            pl.BlockSpec((1, Q), lambda i: (0, i)),
-            whole(4, 256, 128),
-            whole(1024, 128),
-            whole(1, 1024, 256),
-            pl.BlockSpec((1, Q, 1024), lambda i: (0, i, 0)),
-        ],
-        out_specs=whole(1024, 128),
-        out_shape=like(1024, 128),
-        scratch_shapes=[
-            pltpu.VMEM((1024, Q), BF16),
+        [(1024, 128)],
+        [order, pieces, ordered, leaf_basis, leaf_inverse],
+        (place, leaf_map),
+        [
+            pltpu.VMEM((1024, 1024), BF16),
+            pltpu.VMEM((1024, 256), BF16),
             pltpu.VMEM((1024, 256), BF16),
         ],
-        name="finish",
-    )(place, leaf_map, order, pieces, ordered, leaf_basis, leaf_inverse)
+    )
 
 
 def outputs_kernel(res, delta, coefs, out_res, out_new):
@@ -444,8 +426,12 @@
 
 def outputs_call(res, delta, coefs):
     return pl.pallas_call(
-        outputs_kernel, out_shape=[like(Q, 512), like(Q, 512)], name="outputs"
-    )(res, delta, coefs)
+        outputs_kernel,
+        in_specs=[VMEM] * 3,
+        out_shape=[like(Q, 512), like(Q, 512)],
+        compiler_params=pltpu.CompilerParams(vmem_limit_bytes=8 << 20),
+        name="outputs",
+    )(*[near_memory(value) for value in (res, delta, coefs)])
 
 
 def swap_cols(value):
@@ -481,10 +467,7 @@
     mirrored = leaf_route(collect(pair_kernel, 256, *nodes, lower), lambda i: facing(i, 1, 0))
     held = collect(held_kernel, 1024, *nodes, lower, mirrored)
 
-    order = cluster_perm[0]
-    at = jnp.arange(1024, dtype=jnp.int32)
-    pick = (order[:, None] == at[None, :]).astype(BF16)
-    lead = select(mm(leaf_basis[0], leaf_inverse[0], ((0,), (0,))), pick, NN)
+    lead = lead_call(cluster_perm, leaf_basis, leaf_inverse)
 
     near = near_call(place, tile_mask, xs, (packed, partner))
     near, held = lax.optimization_barrier((near, held))
@@ -498,8 +481,7 @@
     e1, m2, f2, m3, e2 = nodes_call(place, (held, own_core, across, both_ways))
 
     partial, _ = lax.optimization_barrier((partial, reduced))
-    res, ordered = residual_call(order.reshape(1024, 1), swap_cols(partial))
-    res_rows = swap_cols(res.reshape(4, Q, 128))
+    columns = swap_cols(partial)
 
     w1, p1 = level1_call(place, leaf_map, gather4(reduced, G4), node_inverse, node_transfer)
     p1 = lax.all_to_all(p1, "leaf", 0, 0, axis_index_groups=GK, tiled=True)
@@ -507,7 +489,11 @@
     w2, p2 = level2_call(siblings(r1), m2, e2)
     r2 = sum(siblings(p2))
     r2s = [r2, z_from(r2, -1, 1), z_from(r2, 2, -2), z_from(r2, -3, 3)]
-    g1 = gather4(upper_call(r2s, m3, f2, w2), GK)
+    g1 = upper_call(r2s, m3, f2, w2)
+    columns, g1 = lax.optimization_barrier((columns, g1))
+    res, ordered = residual_call(cluster_perm, columns)
+    res_rows = swap_cols(res.reshape(4, Q, 128))
+    g1 = gather4(g1, GK)
     pieces = gather4(down1_call(g1, e1, node_inverse, w1), G4)
 
     delta = finish_call(place, leaf_map, cluster_perm, pieces, ordered, leaf_basis, leaf_inverse)

time: 205 us -> 183 us (0.89)
  Pallas kernels: 56.3 us -> 34.8 us
  waiting for transfers between devices: 26.3 us -> 39 us
  starting transfers between devices: 52.1 us -> 40.5 us
  local copies, waits for them, and re-layouts: 4.29 us -> 12.6 us
  matrix products: 7.61 us -> 0 us
  blocking collectives: 54.3 us -> 51.7 us
    ppermute x15, waiting for transfers between devices: 6.46 us -> 30.7 us  [leaf_route(): return lax.ppermute(value, 'leaf', [(i, target(i)) for i in range(LEAVES)])]
    pallas_call x14 -> x15, Pallas kernels: 56.3 us -> 34.8 us  [the longest x14 33.7 us: kernel(): pl.pallas_call(body, in_specs=[SMEM] * len(scalars) + [VMEM] * len(values...]
    all_gather x3, blocking collectives: 40.6 us -> 27.8 us  [gather4(): return lax.all_gather(value, 'leaf', axis=0, axis_index_groups=groups)]
    all_to_all x3 -> x2, waiting for transfers between devices: 14.3 us -> 1.84 us  [swap_cols(): return lax.all_to_all(value, 'col', 0, 0, tiled=True)]
    all_to_all x1 -> x2, blocking collectives: 13.7 us -> 23.9 us  [swap_cols(): return lax.all_to_all(value, 'col', 0, 0, tiled=True)]
    unnamed x42 -> x60, local copies, waits for them, and re-layouts: 3.27 us -> 12.6 us
    dot_general x3 -> x0, matrix products: 7.61 us -> none  [mm(): lax.dot_general(a, b, (dims, ((), ())), precision=precision, preferred_el...]
    ppermute x3, starting transfers between devices: 9.67 us -> 3.92 us  [z_from(): return lax.ppermute(value, 'leaf', route)]
  transfers between devices with their start and end apart: 25 -> 24, of which waited for: 8 -> 10; matrix products, arithmetic and copies ran while one was open for 5% -> 1% of each run, Pallas kernels for 20% -> 17%
where the time goes in v1:
time: 183 us; the launch traced here: 182 us
  blocking collectives  51.7 us (28%)
  starting transfers between devices  40.5 us (22%)
  waiting for transfers between devices  39 us (21%)
  Pallas kernels  34.8 us (19%)
  local copies, waits for them, and re-layouts  12.6 us (7%)
  other arithmetic  1.96 us (1%)
    pallas_call x14, Pallas kernels, kernel(): pl.pallas_call(body, in_specs=[SMEM] * len(scalars) + [VMEM] * len(values...  33.7 us
    ppermute x15, waiting for transfers between devices, leaf_route(): return lax.ppermute(value, 'leaf', [(i, target(i)) for i in range(LEAVES)])  30.7 us
    all_gather x3, blocking collectives, gather4(): return lax.all_gather(value, 'leaf', axis=0, axis_index_groups=groups)  27.8 us
    all_to_all x2, blocking collectives, swap_cols(): return lax.all_to_all(value, 'col', 0, 0, tiled=True)  23.9 us
    ppermute x15, starting transfers between devices, leaf_route(): return lax.ppermute(value, 'leaf', [(i, target(i)) for i in range(LEAVES)])  20.9 us
    unnamed x60, local copies, waits for them, and re-layouts  12.6 us
    all_to_all x2, starting transfers between devices, swap_cols(): return lax.all_to_all(value, 'col', 0, 0, tiled=True)  7.21 us
    ppermute x3, starting transfers between devices, col_shift(): return lax.ppermute(value, 'col', [(i, (i + step) % 4) for i in range(4)])  4.46 us
  transfers between devices with their start and end apart: 24, of which 10 were waited for; matrix products, arithmetic and copies ran while one was open for 1% of the time, Pallas kernels for 17%

profile of v1, /device:TPU:1, one launch (start us, length us, event | category | flops | bytes accessed | tf_op | source)
XLA Modules:
  0.0 182.2 jit_solution(16419731989836416617)
XLA Ops:
  0.7 1.2 copy-done.4
  1.8 0.9 copy-done.10
  2.7 0.9 shard_map.122.p0
  3.6 8.6 %collective-permute-start.4 = (f32[256,640]{1,0:T(8,128)}, f32[256,640]{1,0:T(8,128)S(1)}, u32[]{:S(2)}, u32[]{:S(2)}) collective-permute-start(f32[256,640]{1,0:T(8,128)} %shard_map.122.p0), channel_id=1, source_target_pairs={{0,248},{4,252},{8,0},{12,4},{16,8},{20,12},{24,16},{28,20},{32,24... | collective-permute-start | bytes 1966088 | tf_op jit(solution)/shard_map/ppermute | solution.py:31
  12.2 1.0 collective-permute-start.6
  13.2 12.8 %collective-permute-done.4.p1 = f32[256,640]{1,0:T(8,128)S(1)} collective-permute-done((f32[256,640]{1,0:T(8,128)}, f32[256,640]{1,0:T(8,128)S(1)}, u32[]{:S(2)}, u32[]{:S(2)}) %collective-permute-start.4) | collective-permute-done | bytes 655392 | tf_op jit(solution)/shard_map/ppermute | solution.py:31
  26.0 5.1 %collective-permute-done.3.p0 = f32[256,640]{1,0:T(8,128)S(1)} collective-permute-done((f32[256,640]{1,0:T(8,128)}, f32[256,640]{1,0:T(8,128)S(1)}, u32[]{:S(2)}, u32[]{:S(2)}) %collective-permute-start.3) | collective-permute-done | bytes 655392 | tf_op jit(solution)/shard_map/ppermute | solution.py:31
  31.1 0.9 broadcast_select_fusion
  32.0 1.8 collective-permute-start.5
  33.9 0.1 collective-permute-start.7
  34.0 5.0 %collective-permute-done.7.lower = f32[128,256]{1,0:T(8,128)S(1)} collective-permute-done((f32[128,256]{1,0:T(8,128)S(1)}, f32[128,256]{1,0:T(8,128)S(1)}, u32[]{:S(2)}, u32[]{:S(2)}) %collective-permute-start.7) | collective-permute-done | bytes 131104 | tf_op jit(solution)/shard_map/ppermute | solution.py:31
  39.0 0.1 collective-permute-start.8
  39.1 2.8 %collective-permute-start.2 = (f32[256,128]{1,0:T(8,128)S(1)}, f32[256,128]{1,0:T(8,128)S(1)}, u32[]{:S(2)}, u32[]{:S(2)}) collective-permute-start(f32[256,128]{1,0:T(8,128)S(1)} %copy-done.11), channel_id=1, source_target_pairs={{0,3},{1,0},{2,1},{3,2},{4,7},{5,4},{6,5},{7,6},{8,11},{9,8},{10,9... | collective-permute-start | bytes 393224 | tf_op jit(solution)/shard_map/ppermute | solution.py:57
  41.9 0.3 collective-permute-start.1
  42.3 5.0 %collective-permute-done.8.mirrored = f32[256,256]{1,0:T(8,128)S(1)} collective-permute-done((f32[256,256]{1,0:T(8,128)S(1)}, f32[256,256]{1,0:T(8,128)S(1)}, u32[]{:S(2)}, u32[]{:S(2)}) %collective-permute-start.8) | collective-permute-done | bytes 262176 | tf_op jit(solution)/shard_map/ppermute | solution.py:31
  47.3 0.7 copy-done.20
  48.0 1.3 collective-permute-start
  49.4 0.9 copy-done.18
  50.3 0.9 copy-done.21
  51.2 1.1 shard_map.126.b0
  52.3 0.8 collective-permute-done.x1
  53.1 5.6 %shard_map.123.near = f32[1024,512]{1,0:T(8,128)S(1)} custom-call(s32[4]{0:T(128)S(1)} %pad_add_fusion.place, s32[1,5]{1,0:T(1,128)S(1)} %copy-done.28, f32[256,128]{1,0:T(8,128)S(1)} %copy-done.11, f32[256,128]{1,0:T(8,128)S(1)} %collective-permute-done.x1, f32[256,128]{1,0:T(8,128)S(1)} %collective-permute-done.1.x2, ...), custom_call_target="tpu_custom_call" | custom-call | tf_op jit(solution)/shard_map/pallas_call | solution.py:92
  58.7 0.3 collective-permute-start.13
  59.7 3.1 %shard_map.127.lead = f32[256,1024]{1,0:T(8,128)S(1)} custom-call(s32[1,1024]{1,0:T(1,128)S(1)} %copy-done.24, f32[1,1024,256]{2,1,0:T(8,128)S(1)} %copy-done.7, f32[1,1024,1024]{2,1,0:T(8,128)S(1)} %copy-done.1), custom_call_target="tpu_custom_call" | custom-call | tf_op jit(solution)/shard_map/pallas_call | solution.py:92
  62.9 8.8 %shard_map.128 = (f32[4,1024,128]{2,1,0:T(8,128)S(1)}, f32[4,256,128]{2,1,0:T(8,128)S(1)}) custom-call(s32[4]{0:T(128)S(1)} %pad_add_fusion.place, s32[1,5]{1,0:T(1,128)S(1)} %copy-done.28, f32[1]{0:T(128)S(6)} %copy.13.ridge, f32[256,128]{1,0:T(8,128)S(1)} %copy-done.11, f32[256,128]{1,0:T(8,128)S(1)} %collective-permute-done.x1, ...), custom_call_target="tpu_custom_call" | custom-call | tf_op jit(solution)/shard_map/pallas_call | solution.py:92
  71.7 1.3 copy-done.9
  73.0 10.5 %all_to_all.29 = f32[4,256,128]{2,1,0:T(8,128)S(1)} all-to-all(f32[4,256,128]{2,1,0:T(8,128)S(1)} %get-tuple-element.22), channel_id=1, replica_groups=mesh['leaf'=64,'col'=4] {'col'}, dimensions={0} | all-to-all | bytes 1048576 | tf_op jit(solution)/shard_map/all_to_all | solution.py:438
  83.5 11.2 %all-gather = f32[1024,128]{1,0:T(8,128)S(1)} all-gather(f32[256,128]{1,0:T(8,128)S(1)} %reduce_sum.18), channel_id=2, replica_groups={{0,4,8,12},{16,20,24,28},{32,36,40,44},{48,52,56,60},{64,68,72,76},{80,..., dimensions={0}, use_global_device_ids=true | all-gather | bytes 655360 | tf_op jit(solution)/shard_map/all_gather | solution.py:61
  94.8 2.1 %shard_map.129 = (f32[256,128]{1,0:T(8,128)S(1)}, f32[128,256]{1,0:T(8,128)}) custom-call(s32[4]{0:T(128)S(1)} %copy-done.27, s32[64]{0:T(128)S(1)} %copy-done.29, f32[4,256,128]{2,1,0:T(8,128)S(1)} %bitcast.12, f32[1,336,1024]{2,1,0:T(8,128)S(1)} %copy-done, f32[1,336,256]{2,1,0:T(8,128)S(1)} %copy-done.3), custom_call_target="tpu_custom_call" | custom-call | tf_op jit(solution)/shard_map/pallas_call | solution.py:92
  96.9 0.7 copy-done.22
  97.5 4.1 %all-to-all-start.2 = ((f32[4,32,256]{2,1,0:T(8,128)}), f32[4,32,256]{2,1,0:T(8,128)}, u32[]{:S(2)}, u32[]{:S(2)}) async-start(f32[4,32,256]{2,1,0:T(8,128)} %bitcast.5), calls=%async_computation.2 | async-start | bytes 262144 | tf_op jit(solution)/shard_map/all_to_all | solution.py:487
  101.6 3.7 %all-to-all-done.2 = f32[4,32,256]{2,1,0:T(8,128)} async-done(((f32[4,32,256]{2,1,0:T(8,128)}), f32[4,32,256]{2,1,0:T(8,128)}, u32[]{:S(2)}, u32[]{:S(2)}) %all-to-all-start.2) | async-done | bytes 131104 | tf_op jit(solution)/shard_map/all_to_all | solution.py:487
  105.3 3.6 %all-to-all-start.1 = ((f32[4,1024,128]{2,1,0:T(8,128)}), f32[4,1024,128]{2,1,0:T(8,128)S(1)}, u32[]{:S(2)}, u32[]{:S(2)}) async-start(f32[4,1024,128]{2,1,0:T(8,128)} %copy-done.9), calls=%async_computation.1 | async-start | bytes 4194304 | tf_op jit(solution)/shard_map/all_to_all | solution.py:438
  108.9 1.1 collective-permute-start.12
  110.0 0.1 collective-permute-start.14
  110.1 0.9 reduce_sum.19.r0
  111.0 0.2 collective-permute-start.11
  111.2 1.1 collective-permute-start.10
  112.3 2.7 %collective-permute-start.9 = (f32[32,256]{1,0:T(8,128)S(1)}, f32[32,256]{1,0:T(8,128)S(1)}, u32[]{:S(2)}, u32[]{:S(2)}) collective-permute-start(f32[32,256]{1,0:T(8,128)S(1)} %reduce_sum.19.r0), channel_id=1, source_target_pairs={{0,24},{4,28},{8,16},{12,20},{16,8},{20,12},{24,0},{28,4},{32,56},... | collective-permute-start | bytes 98312 | tf_op jit(solution)/shard_map/ppermute | solution.py:31
  115.0 3.1 %shard_map.130 = (f32[1024,256]{1,0:T(8,128)S(1)}, f32[256,1024]{1,0:T(8,128)S(1)}, f32[256,256]{1,0:T(8,128)S(1)}, f32[256,1024]{1,0:T(8,128)S(1)}, f32[256,256]{1,0:T(8,128)S(1)}) custom-call(s32[4]{0:T(128)S(1)} %copy-done.27, f32[1024,256]{1,0:T(8,128)} %shard_map.126.b0, f32[1024,256]{1,0:T(8,128)} %collective-permute-done.12.b1, ...), custom_call_target="tpu_custom_call" | custom-call | tf_op jit(solution)/shard_map/pallas_call | solution.py:92
  118.1 0.8 shard_map.131
  119.0 1.1 collective-permute-start.17
  120.1 1.2 collective-permute-start.16
  121.3 1.6 collective-permute-start.15
  122.8 1.0 collective-permute-done.17
  123.8 1.7 collective-permute-done.15
  125.6 0.5 collective-permute-start.20
  126.0 3.4 %collective-permute-start.18 = (f32[32,256]{1,0:T(8,128)S(1)}, f32[32,256]{1,0:T(8,128)S(1)}, u32[]{:S(2)}, u32[]{:S(2)}) collective-permute-start(f32[32,256]{1,0:T(8,128)S(1)} %add_add_fusion.r0), channel_id=1, source_target_pairs={{224,0},{228,4},{232,8},{236,12},{240,16},{244,20},{248,24},{252,2... | collective-permute-start | bytes 98312 | tf_op jit(solution)/shard_map/ppermute | solution.py:53
  129.5 2.0 %collective-permute-done.20.r3 = f32[32,256]{1,0:T(8,128)S(1)} collective-permute-done((f32[32,256]{1,0:T(8,128)S(1)}, f32[32,256]{1,0:T(8,128)S(1)}, u32[]{:S(2)}, u32[]{:S(2)}) %collective-permute-start.20) | collective-permute-done | bytes 32800 | tf_op jit(solution)/shard_map/ppermute | solution.py:53
  131.5 0.9 shard_map.132
  132.4 1.8 %all-to-all-done.1.parts = f32[4,1024,128]{2,1,0:T(8,128)S(1)} async-done(((f32[4,1024,128]{2,1,0:T(8,128)}), f32[4,1024,128]{2,1,0:T(8,128)S(1)}, u32[]{:S(2)}, u32[]{:S(2)}) %all-to-all-start.1) | async-done | bytes 2097184 | tf_op jit(solution)/shard_map/all_to_all | solution.py:438
  134.2 1.2 shard_map.133
  135.4 0.8 copy-done.15
  136.2 0.8 copy-done.19
  137.0 3.6 %all-to-all-start.3 = ((f32[4,256,128]{2,1,0:T(8,128)}), f32[4,256,128]{2,1,0:T(8,128)S(1)}, u32[]{:S(2)}, u32[]{:S(2)}) async-start(f32[4,256,128]{2,1,0:T(8,128)} %bitcast.14), calls=%async_computation.3 | async-start | bytes 1048576 | tf_op jit(solution)/shard_map/all_to_all | solution.py:438
  140.6 9.3 %all-gather.1 = f32[128,256]{1,0:T(8,128)S(1)} all-gather(f32[32,256]{1,0:T(8,128)S(1)} %shard_map.132), channel_id=3, replica_groups={{0,4,8,12},{24,28,16,20},{32,36,40,44},{56,60,48,52},{64,68,72,76},{88,..., dimensions={0}, use_global_device_ids=true | all-gather | bytes 163840 | tf_op jit(solution)/shard_map/all_gather | solution.py:61
  149.9 1.2 copy-done.13
  151.1 0.9 copy-done.23
  152.0 1.7 shard_map.134
  153.8 7.3 %all-gather.2 = f32[1024,128]{1,0:T(8,128)S(1)} all-gather(f32[256,128]{1,0:T(8,128)S(1)} %shard_map.134), channel_id=4, replica_groups={{0,4,8,12},{16,20,24,28},{32,36,40,44},{48,52,56,60},{64,68,72,76},{80,..., dimensions={0}, use_global_device_ids=true | all-gather | bytes 655360 | tf_op jit(solution)/shard_map/all_gather | solution.py:61
  161.0 2.2 %copy-done.2 = f32[1,1024,1024]{2,1,0:T(8,128)S(1)} copy-done((f32[1,1024,1024]{2,1,0:T(8,128)S(1)}, f32[1,1024,1024]{2,1,0:T(8,128)}, u32[]{:S(2)}) %copy-start.2) | copy-done | bytes 4194328
  163.2 4.4 %shard_map.135 = f32[1024,128]{1,0:T(8,128)S(1)} custom-call(s32[4]{0:T(128)S(1)} %copy-done.27, s32[64]{0:T(128)S(1)} %copy-done.29, s32[1,1024]{1,0:T(1,128)S(1)} %copy-done.25, f32[4,256,128]{2,1,0:T(8,128)S(1)} %bitcast.10, f32[1024,128]{1,0:T(8,128)S(1)} %copy-done.16, f32[1,1024,256]{2,1,0:T(8,128)S(1)} %copy-done.8, f32[1,1024,1024]{2,1,0:T(8,128)S(1)} %copy-done.2), custom_call_target="tpu_custom_call" | custom-call | tf_op jit(solution)/shard_map/pallas_call | solution.py:92
  167.6 13.4 %all_to_all.30.delta = f32[4,256,128]{2,1,0:T(8,128)S(1)} all-to-all(f32[4,256,128]{2,1,0:T(8,128)S(1)} %bitcast.11), channel_id=1, replica_groups=mesh['leaf'=64,'col'=4] {'col'}, dimensions={0} | all-to-all | bytes 1048576 | tf_op jit(solution)/shard_map/all_to_all | solution.py:438
  181.1 1.1 outputs.1
  (69 shorter events, 0.3 us)
Async XLA Ops:
  0.6 33.2 %copy-start = (f32[1,336,1024]{2,1,0:T(8,128)S(1)}, f32[1,336,1024]{2,1,0:T(8,128)}, u32[]{:S(2)}) copy-start(f32[1,336,1024]{2,1,0:T(8,128)} %m1.3) | copy-start | bytes 4128772
  0.6 33.2 %copy-start.3 = (f32[1,336,256]{2,1,0:T(8,128)S(1)}, f32[1,336,256]{2,1,0:T(8,128)}, u32[]{:S(2)}) copy-start(f32[1,336,256]{2,1,0:T(8,128)} %e1.1) | copy-start | bytes 1032196
  0.6 1.2 copy-start.4
  1.8 0.9 copy-start.10
  3.6 22.3 %collective-permute-start.4 = (f32[256,640]{1,0:T(8,128)}, f32[256,640]{1,0:T(8,128)S(1)}, u32[]{:S(2)}, u32[]{:S(2)}) collective-permute-start(f32[256,640]{1,0:T(8,128)} %shard_map.122.p0), channel_id=1, source_target_pairs={{0,248},{4,252},{8,0},{12,4},{16,8},{20,12},{24,16},{28,20},{32,24... | collective-permute-start | bytes 1966088 | tf_op jit(solution)/shard_map/ppermute | solution.py:31
  12.2 18.9 %collective-permute-start.3 = (f32[256,640]{1,0:T(8,128)}, f32[256,640]{1,0:T(8,128)S(1)}, u32[]{:S(2)}, u32[]{:S(2)}) collective-permute-start(f32[256,640]{1,0:T(8,128)} %shard_map.122.p0), channel_id=1, source_target_pairs={{0,8},{4,12},{8,16},{12,20},{16,24},{20,28},{24,32},{28,36},{32,40... | collective-permute-start | bytes 1966088 | tf_op jit(solution)/shard_map/ppermute | solution.py:31
  12.2 40.9 %collective-permute-start.6 = (f32[256,640]{1,0:T(8,128)}, f32[256,640]{1,0:T(8,128)}, u32[]{:S(2)}, u32[]{:S(2)}) collective-permute-start(f32[256,640]{1,0:T(8,128)} %shard_map.122.p0), channel_id=1, source_target_pairs={{0,4},{4,0},{8,12},{12,8},{16,20},{20,16},{24,28},{28,24},{32,36},... | collective-permute-start | bytes 1966088 | tf_op jit(solution)/shard_map/ppermute | solution.py:31
  32.0 7.1 %copy-start.11 = (f32[256,128]{1,0:T(8,128)S(1)}, f32[256,128]{1,0:T(8,128)}, u32[]{:S(2)}) copy-start(f32[256,128]{1,0:T(8,128)} %x0.3) | copy-start | bytes 393220
  32.0 30.8 %collective-permute-start.5 = (f32[256,640]{1,0:T(8,128)}, f32[256,640]{1,0:T(8,128)}, u32[]{:S(2)}, u32[]{:S(2)}) collective-permute-start(f32[256,640]{1,0:T(8,128)} %broadcast_select_fusion), channel_id=1, source_target_pairs={{0,4},{4,0},{8,12},{12,8},{16,20},{20,16},{24,28},{28,24},{32,36},... | collective-permute-start | bytes 1966088 | tf_op jit(solution)/shard_map/ppermute | solution.py:31
  33.9 5.1 %collective-permute-start.7 = (f32[128,256]{1,0:T(8,128)S(1)}, f32[128,256]{1,0:T(8,128)S(1)}, u32[]{:S(2)}, u32[]{:S(2)}) collective-permute-start(f32[128,256]{1,0:T(8,128)S(1)} %shard_map.124), channel_id=1, source_target_pairs={{0,32},{4,36},{8,40},{12,44},{16,48},{20,52},{24,56},{28,60},{32,0... | collective-permute-start | bytes 393224 | tf_op jit(solution)/shard_map/ppermute | solution.py:31
  39.0 3.3 %copy-start.17 = (f32[128,256]{1,0:T(8,128)}, f32[128,256]{1,0:T(8,128)S(1)}, u32[]{:S(2)}) copy-start(f32[128,256]{1,0:T(8,128)S(1)} %collective-permute-done.7.lower) | copy-start | bytes 393220
  39.0 8.3 %collective-permute-start.8 = (f32[256,256]{1,0:T(8,128)S(1)}, f32[256,256]{1,0:T(8,128)S(1)}, u32[]{:S(2)}, u32[]{:S(2)}) collective-permute-start(f32[256,256]{1,0:T(8,128)S(1)} %shard_map.125), channel_id=1, source_target_pairs={{0,24},{4,28},{8,16},{12,20},{16,8},{20,12},{24,0},{28,4},{32,56},... | collective-permute-start | bytes 786440 | tf_op jit(solution)/shard_map/ppermute | solution.py:31
  39.1 13.2 %collective-permute-start.2 = (f32[256,128]{1,0:T(8,128)S(1)}, f32[256,128]{1,0:T(8,128)S(1)}, u32[]{:S(2)}, u32[]{:S(2)}) collective-permute-start(f32[256,128]{1,0:T(8,128)S(1)} %copy-done.11), channel_id=1, source_target_pairs={{0,3},{1,0},{2,1},{3,2},{4,7},{5,4},{6,5},{7,6},{8,11},{9,8},{10,9... | collective-permute-start | bytes 393224 | tf_op jit(solution)/shard_map/ppermute | solution.py:57
  41.9 10.4 %collective-permute-start.1 = (f32[256,128]{1,0:T(8,128)S(1)}, f32[256,128]{1,0:T(8,128)S(1)}, u32[]{:S(2)}, u32[]{:S(2)}) collective-permute-start(f32[256,128]{1,0:T(8,128)S(1)} %copy-done.11), channel_id=1, source_target_pairs={{0,2},{1,3},{2,0},{3,1},{4,6},{5,7},{6,4},{7,5},{8,10},{9,11},{10,... | collective-permute-start | bytes 393224 | tf_op jit(solution)/shard_map/ppermute | solution.py:57
  47.3 0.7 copy-start.20
  48.0 5.1 %collective-permute-start = (f32[256,128]{1,0:T(8,128)S(1)}, f32[256,128]{1,0:T(8,128)S(1)}, u32[]{:S(2)}, u32[]{:S(2)}) collective-permute-start(f32[256,128]{1,0:T(8,128)S(1)} %copy-done.11), channel_id=1, source_target_pairs={{0,1},{1,2},{2,3},{3,0},{4,5},{5,6},{6,7},{7,4},{8,9},{9,10},{10,1... | collective-permute-start | bytes 393224 | tf_op jit(solution)/shard_map/ppermute | solution.py:57
  49.3 3.8 %copy-start.28 = (s32[1,5]{1,0:T(1,128)S(1)}, s32[1,5]{1,0:T(1,128)}, u32[]{:S(2)}) copy-start(s32[1,5]{1,0:T(1,128)} %mask.3) | copy-start | bytes 64
  49.4 0.9 copy-start.18
  50.3 0.9 copy-start.21
  51.2 11.6 %copy-start.26 = (s32[4]{0:T(128)}, s32[4]{0:T(128)S(1)}, u32[]{:S(2)}) copy-start(s32[4]{0:T(128)S(1)} %pad_add_fusion.place) | copy-start | bytes 52
  51.2 8.4 %copy-start.1 = (f32[1,1024,1024]{2,1,0:T(8,128)S(1)}, f32[1,1024,1024]{2,1,0:T(8,128)}, u32[]{:S(2)}) copy-start(f32[1,1024,1024]{2,1,0:T(8,128)} %solve.3) | copy-start | bytes 12582916
  52.3 7.4 %copy-start.7 = (f32[1,1024,256]{2,1,0:T(8,128)S(1)}, f32[1,1024,256]{2,1,0:T(8,128)}, u32[]{:S(2)}) copy-start(f32[1,1024,256]{2,1,0:T(8,128)} %basis.3) | copy-start | bytes 3145732
  52.3 7.4 %copy-start.24 = (s32[1,1024]{1,0:T(1,128)S(1)}, s32[1,1024]{1,0:T(1,128)}, u32[]{:S(2)}) copy-start(s32[1,1024]{1,0:T(1,128)} %order.5) | copy-start | bytes 12292
  58.7 51.3 %collective-permute-start.13 = (f32[1024,256]{1,0:T(8,128)}, f32[1024,256]{1,0:T(8,128)}, u32[]{:S(2)}, u32[]{:S(2)}) collective-permute-start(f32[1024,256]{1,0:T(8,128)} %shard_map.126.b0), channel_id=1, source_target_pairs={{0,8},{4,12},{8,0},{12,4},{16,24},{20,28},{24,16},{28,20},{32,40},... | collective-permute-start | bytes 3145736 | tf_op jit(solution)/shard_map/ppermute | solution.py:31
  59.7 3.1 %copy-start.5 = (f32[256,512]{1,0:T(8,128)S(1)}, f32[256,512]{1,0:T(8,128)}, u32[]{:S(2)}) copy-start(f32[256,512]{1,0:T(8,128)} %coefs.1) | copy-start | bytes 1572868
  59.7 3.1 %copy-start.14 = (f32[256,512]{1,0:T(8,128)S(1)}, f32[256,512]{1,0:T(8,128)}, u32[]{:S(2)}) copy-start(f32[256,512]{1,0:T(8,128)} %own_y.1) | copy-start | bytes 1572868
  71.7 1.4 copy-start.9
  73.0 21.7 %copy-start.27 = (s32[4]{0:T(128)S(1)}, s32[4]{0:T(128)}, u32[]{:S(2)}) copy-start(s32[4]{0:T(128)} %copy-done.26) | copy-start | bytes 52
  73.0 21.7 %copy-start.29 = (s32[64]{0:T(128)S(1)}, s32[64]{0:T(128)}, u32[]{:S(2)}) copy-start(s32[64]{0:T(128)} %leaf_map.3) | copy-start | bytes 772
  96.9 0.7 copy-start.22
  97.5 7.7 %all-to-all-start.2 = ((f32[4,32,256]{2,1,0:T(8,128)}), f32[4,32,256]{2,1,0:T(8,128)}, u32[]{:S(2)}, u32[]{:S(2)}) async-start(f32[4,32,256]{2,1,0:T(8,128)} %bitcast.5), calls=%async_computation.2 | async-start | bytes 262144 | tf_op jit(solution)/shard_map/all_to_all | solution.py:487
  105.3 29.0 %all-to-all-start.1 = ((f32[4,1024,128]{2,1,0:T(8,128)}), f32[4,1024,128]{2,1,0:T(8,128)S(1)}, u32[]{:S(2)}, u32[]{:S(2)}) async-start(f32[4,1024,128]{2,1,0:T(8,128)} %copy-done.9), calls=%async_computation.1 | async-start | bytes 4194304 | tf_op jit(solution)/shard_map/all_to_all | solution.py:438
  108.9 6.1 %collective-permute-start.12 = (f32[1024,256]{1,0:T(8,128)}, f32[1024,256]{1,0:T(8,128)}, u32[]{:S(2)}, u32[]{:S(2)}) collective-permute-start(f32[1024,256]{1,0:T(8,128)} %shard_map.126.b0), channel_id=1, source_target_pairs={{0,4},{4,0},{8,12},{12,8},{16,20},{20,16},{24,28},{28,24},{32,36},... | collective-permute-start | bytes 3145736 | tf_op jit(solution)/shard_map/ppermute | solution.py:31
  110.0 5.0 %collective-permute-start.14 = (f32[1024,256]{1,0:T(8,128)}, f32[1024,256]{1,0:T(8,128)}, u32[]{:S(2)}, u32[]{:S(2)}) collective-permute-start(f32[1024,256]{1,0:T(8,128)} %collective-permute-done.13.b2), channel_id=1, source_target_pairs={{0,4},{4,0},{8,12},{12,8},{16,20},{20,16},{24,28},{28,24},{32,36},... | collective-permute-start | bytes 3145736 | tf_op jit(solution)/shard_map/ppermute | solution.py:31
  111.0 7.1 %collective-permute-start.11 = (f32[32,256]{1,0:T(8,128)S(1)}, f32[32,256]{1,0:T(8,128)S(1)}, u32[]{:S(2)}, u32[]{:S(2)}) collective-permute-start(f32[32,256]{1,0:T(8,128)S(1)} %reduce_sum.19.r0), channel_id=1, source_target_pairs={{0,56},{4,60},{8,48},{12,52},{16,40},{20,44},{24,32},{28,36},{32,2... | collective-permute-start | bytes 98312 | tf_op jit(solution)/shard_map/ppermute | solution.py:31
  111.2 6.9 %collective-permute-start.10 = (f32[32,256]{1,0:T(8,128)S(1)}, f32[32,256]{1,0:T(8,128)S(1)}, u32[]{:S(2)}, u32[]{:S(2)}) collective-permute-start(f32[32,256]{1,0:T(8,128)S(1)} %reduce_sum.19.r0), channel_id=1, source_target_pairs={{0,32},{4,36},{8,40},{12,44},{16,48},{20,52},{24,56},{28,60},{32,0... | collective-permute-start | bytes 98312 | tf_op jit(solution)/shard_map/ppermute | solution.py:31
  112.3 5.8 %collective-permute-start.9 = (f32[32,256]{1,0:T(8,128)S(1)}, f32[32,256]{1,0:T(8,128)S(1)}, u32[]{:S(2)}, u32[]{:S(2)}) collective-permute-start(f32[32,256]{1,0:T(8,128)S(1)} %reduce_sum.19.r0), channel_id=1, source_target_pairs={{0,24},{4,28},{8,16},{12,20},{16,8},{20,12},{24,0},{28,4},{32,56},... | collective-permute-start | bytes 98312 | tf_op jit(solution)/shard_map/ppermute | solution.py:31
  118.1 13.4 %copy-start.12 = (f32[1024,256]{1,0:T(8,128)}, f32[1024,256]{1,0:T(8,128)S(1)}, u32[]{:S(2)}) copy-start(f32[1024,256]{1,0:T(8,128)S(1)} %get-tuple-element.35.e1) | copy-start | bytes 3145732
  118.1 16.1 %copy-start.25 = (s32[1,1024]{1,0:T(1,128)S(1)}, s32[1,1024]{1,0:T(1,128)}, u32[]{:S(2)}) copy-start(s32[1,1024]{1,0:T(1,128)} %order.5) | copy-start | bytes 12292
  119.0 4.9 %collective-permute-start.17 = (f32[32,256]{1,0:T(8,128)S(1)}, f32[32,256]{1,0:T(8,128)S(1)}, u32[]{:S(2)}, u32[]{:S(2)}) collective-permute-start(f32[32,256]{1,0:T(8,128)S(1)} %get-tuple-element.28), channel_id=1, source_target_pairs={{0,56},{4,60},{8,48},{12,52},{16,40},{20,44},{24,32},{28,36},{32,2... | collective-permute-start | bytes 98312 | tf_op jit(solution)/shard_map/ppermute | solution.py:31
  120.1 3.8 %collective-permute-start.16 = (f32[32,256]{1,0:T(8,128)S(1)}, f32[32,256]{1,0:T(8,128)S(1)}, u32[]{:S(2)}, u32[]{:S(2)}) collective-permute-start(f32[32,256]{1,0:T(8,128)S(1)} %get-tuple-element.28), channel_id=1, source_target_pairs={{0,32},{4,36},{8,40},{12,44},{16,48},{20,52},{24,56},{28,60},{32,0... | collective-permute-start | bytes 98312 | tf_op jit(solution)/shard_map/ppermute | solution.py:31
  121.3 4.3 %collective-permute-start.15 = (f32[32,256]{1,0:T(8,128)S(1)}, f32[32,256]{1,0:T(8,128)S(1)}, u32[]{:S(2)}, u32[]{:S(2)}) collective-permute-start(f32[32,256]{1,0:T(8,128)S(1)} %get-tuple-element.28), channel_id=1, source_target_pairs={{0,24},{4,28},{8,16},{12,20},{16,8},{20,12},{24,0},{28,4},{32,56},... | collective-permute-start | bytes 98312 | tf_op jit(solution)/shard_map/ppermute | solution.py:31
  125.6 5.9 %collective-permute-start.20 = (f32[32,256]{1,0:T(8,128)S(1)}, f32[32,256]{1,0:T(8,128)S(1)}, u32[]{:S(2)}, u32[]{:S(2)}) collective-permute-start(f32[32,256]{1,0:T(8,128)S(1)} %add_add_fusion.r0), channel_id=1, source_target_pairs={{160,0},{164,4},{168,8},{172,12},{176,16},{180,20},{184,24},{188,2... | collective-permute-start | bytes 98312 | tf_op jit(solution)/shard_map/ppermute | solution.py:53
  126.0 5.4 %collective-permute-start.19 = (f32[32,256]{1,0:T(8,128)S(1)}, f32[32,256]{1,0:T(8,128)S(1)}, u32[]{:S(2)}, u32[]{:S(2)}) collective-permute-start(f32[32,256]{1,0:T(8,128)S(1)} %add_add_fusion.r0), channel_id=1, source_target_pairs={{64,0},{68,4},{72,8},{76,12},{80,16},{84,20},{88,24},{92,28},{224,... | collective-permute-start | bytes 98312 | tf_op jit(solution)/shard_map/ppermute | solution.py:53
  126.0 5.4 %collective-permute-start.18 = (f32[32,256]{1,0:T(8,128)S(1)}, f32[32,256]{1,0:T(8,128)S(1)}, u32[]{:S(2)}, u32[]{:S(2)}) collective-permute-start(f32[32,256]{1,0:T(8,128)S(1)} %add_add_fusion.r0), channel_id=1, source_target_pairs={{224,0},{228,4},{232,8},{236,12},{240,16},{244,20},{248,24},{252,2... | collective-permute-start | bytes 98312 | tf_op jit(solution)/shard_map/ppermute | solution.py:53
  135.4 0.8 copy-start.15
  136.2 0.8 copy-start.19
  137.0 24.0 %copy-start.8 = (f32[1,1024,256]{2,1,0:T(8,128)S(1)}, f32[1,1024,256]{2,1,0:T(8,128)}, u32[]{:S(2)}) copy-start(f32[1,1024,256]{2,1,0:T(8,128)} %basis.3) | copy-start | bytes 3145732
  137.0 30.6 %all-to-all-start.3 = ((f32[4,256,128]{2,1,0:T(8,128)}), f32[4,256,128]{2,1,0:T(8,128)S(1)}, u32[]{:S(2)}, u32[]{:S(2)}) async-start(f32[4,256,128]{2,1,0:T(8,128)} %bitcast.14), calls=%async_computation.3 | async-start | bytes 1048576 | tf_op jit(solution)/shard_map/all_to_all | solution.py:438
  149.9 1.2 copy-start.13
  151.1 0.9 copy-start.23
  152.0 9.0 %copy-start.16 = (f32[1024,128]{1,0:T(8,128)S(1)}, f32[1024,128]{1,0:T(8,128)}, u32[]{:S(2)}) copy-start(f32[1024,128]{1,0:T(8,128)} %copy-done.15) | copy-start | bytes 1572868
  161.0 2.2 %copy-start.2 = (f32[1,1024,1024]{2,1,0:T(8,128)S(1)}, f32[1,1024,1024]{2,1,0:T(8,128)}, u32[]{:S(2)}) copy-start(f32[1,1024,1024]{2,1,0:T(8,128)} %solve.3) | copy-start | bytes 12582916
  163.2 17.8 %copy-start.6 = (f32[256,512]{1,0:T(8,128)S(1)}, f32[256,512]{1,0:T(8,128)}, u32[]{:S(2)}) copy-start(f32[256,512]{1,0:T(8,128)} %coefs.1) | copy-start | bytes 1572868

commit v2 on v1

--- a/solution.py
+++ b/solution.py
@@ -82,22 +82,28 @@
 
 SMEM = pl.BlockSpec(memory_space=pltpu.SMEM)
 VMEM = pl.BlockSpec(memory_space=pltpu.VMEM)
+HBM = pl.BlockSpec(memory_space=pltpu.HBM)
 
 
 def near_memory(value):
     return pltpu.with_memory_space_constraint(value, pltpu.VMEM)
 
 
-def kernel(body, outs, values, scalars=(), scratch=()):
+def far_memory(value):
+    return pltpu.with_memory_space_constraint(value, pltpu.HBM)
+
+
+def kernel(body, outs, values, scalars=(), scratch=(), far_values=(), far_outs=()):
     result = pl.pallas_call(
         body,
-        in_specs=[SMEM] * len(scalars) + [VMEM] * len(values),
-        out_specs=[VMEM] * len(outs),
-        out_shape=[pltpu.VMEM(shape, F32) for shape in outs],
+        in_specs=[SMEM] * len(scalars) + [VMEM] * len(values) + [HBM] * len(far_values),
+        out_specs=[VMEM] * len(outs) + [HBM] * len(far_outs),
+        out_shape=[pltpu.VMEM(shape, F32) for shape in outs]
+        + [pltpu.HBM(shape, F32) for shape in far_outs],
         scratch_shapes=list(scratch),
         compiler_params=pltpu.CompilerParams(vmem_limit_bytes=20 << 20),
-    )(*scalars, *[near_memory(value) for value in values])
-    return result if len(outs) > 1 else result[0]
+    )(*scalars, *[near_memory(value) for value in values], *[far_memory(value) for value in far_values])
+    return result if len(outs) + len(far_outs) > 1 else result[0]
 
 
 def like(*shape, dtype=F32):
@@ -150,7 +156,8 @@
 
 
 def far_kernel(
-    place, mask, ridge, x0, x1, x2, x3, p0, p1, p2, near, own_y, own_a, lead, out, led, *scratch
+    place, mask, ridge, x0, x1, x2, x3, p0, p1, p2, near, own_y, own_a, lead,
+    led, out, parts, sems, *scratch
 ):
     blocks = [(p[:, :128], p[:, 128:]) for p in (p0, p1, p2)]
     tile_setup(place, (x0, x1, x2, x3), blocks, *scratch)
@@ -161,6 +168,10 @@
     )
     for k in range(4):
         led[k] = jnp.zeros((RANK, 128), F32)
+
+    def sent(i):
+        rows = pl.ds(pl.multiple_of(i * CHUNK, CHUNK), CHUNK)
+        return pltpu.make_async_copy(parts.at[i], out.at[:, rows, :], sems.at[i])
 
     @pl.loop(0, 2)
     def _(i):
@@ -176,8 +187,12 @@
         )
         product = dot3(lead[:, rows], part)
         for k in range(4):
-            out[k, rows, :] = part[:, k * 128 : (k + 1) * 128]
+            parts[i, k] = part[:, k * 128 : (k + 1) * 128]
             led[k] += product[:, k * 128 : (k + 1) * 128]
+        sent(i).start()
+
+    for i in range(2):
+        sent(i).wait()
 
 
 def tile_scratch(count):
@@ -198,10 +213,11 @@
 def far_call(place, mask, ridge, xs, blocks, near, own_y, own_a, lead):
     return kernel(
         far_kernel,
-        [(4, 1024, 128), (4, RANK, 128)],
+        [(4, RANK, 128)],
         [*xs, *blocks, near, own_y, own_a, lead],
         (place, mask, ridge),
-        tile_scratch(3),
+        [pltpu.VMEM((2, 4, CHUNK, 128), F32), pltpu.SemaphoreType.DMA((2,))] + tile_scratch(3),
+        far_outs=[(4, 1024, 128)],
     )
 
 
@@ -210,10 +226,39 @@
     picks[...] = jnp.where(order == at, 1.0, 0.0).astype(BF16)
 
 
-def lead_kernel(order, basis, solve, lead, picks):
+def load_solve(basis, solve, basis_in, solve_in, sems):
+    copies = [pltpu.make_async_copy(basis.at[0], basis_in, sems.at[4])]
+    for k in range(4):
+        rows = pl.ds(k * Q, Q)
+        copies.append(
+            pltpu.make_async_copy(solve.at[0, rows, :], solve_in.at[rows, :], sems.at[k])
+        )
+    for copy in copies:
+        copy.start()
+    return copies
+
+
+SOLVE_SCRATCH = [
+    pltpu.VMEM((1024, RANK), F32),
+    pltpu.VMEM((1024, 1024), F32),
+    pltpu.SemaphoreType.DMA((5,)),
+]
+
+
+def lead_kernel(order, basis, solve, lead, basis_in, solve_in, sems, picks, turned):
+    first, *rest = load_solve(basis, solve, basis_in, solve_in, sems)
     picks_by_row(order[...], picks)
-    turned = jnp.transpose(basis[0])
-    both = jnp.concatenate(split(dot3(turned, solve[0])), axis=0)
+    first.wait()
+    turned[...] = jnp.transpose(basis_in[...])
+    for k in range(4):
+        rest[k].wait()
+        rows = slice(k * Q, (k + 1) * Q)
+        term = dot3(turned[:, rows], solve_in[rows, :])
+        if k:
+            lead[...] += term
+        else:
+            lead[...] = term
+    both = jnp.concatenate(split(lead[...]), axis=0)
     chosen = dot(both, picks[...], NT)
     lead[...] = chosen[:RANK] + chosen[RANK:]
 
@@ -222,48 +267,65 @@
     return kernel(
         lead_kernel,
         [(RANK, 1024)],
-        [order, leaf_basis, leaf_inverse],
-        scratch=[pltpu.VMEM((1024, 1024), BF16)],
-    )
-
-
-def pack_kernel(a, b, out):
-    out[:, :128] = a[...]
-    out[:, 128:] = b[...]
-
-
-def pack_call(a, b):
-    return kernel(pack_kernel, [(Q, 640)], [a, b])
-
-
-def fill_slices(transfer, inverse, out, start):
-    out[start : start + 64, :] = transfer[0, 256:320, :]
-    for k in range(4):
-        at = start + 64 + k * 16
-        out[at : at + 16, :] = inverse[0, 320:336, k * 256 : (k + 1) * 256]
-
-
-def slices_kernel(transfer, inverse, out):
-    fill_slices(transfer, inverse, out, 0)
-
-
-def pair_kernel(transfer, inverse, lower, out):
-    fill_slices(transfer, inverse, out, 0)
-    out[128:, :] = lower[...]
-
-
-def held_kernel(transfer, inverse, lower, mirrored, out):
-    out[:256, :] = transfer[0, :256, :]
-    for k in range(4):
-        at = 256 + k * 64
-        out[at : at + 64, :] = inverse[0, 256:320, k * 256 : (k + 1) * 256]
-    fill_slices(transfer, inverse, out, 512)
-    out[640:768, :] = lower[...]
-    out[768:, :] = mirrored[...]
-
-
-def collect(body, rows, *parts):
-    return kernel(body, [(rows, 256)], parts)
+        [order],
+        scratch=SOLVE_SCRATCH
+        + [pltpu.VMEM((1024, 1024), BF16), pltpu.VMEM((RANK, 1024), F32)],
+        far_values=[leaf_basis, leaf_inverse],
+    )
+
+
+def run_copies(sems, moves):
+    copies = [
+        pltpu.make_async_copy(source, target, sems.at[k])
+        for k, (source, target) in enumerate(moves)
+    ]
+    for copy in copies:
+        copy.start()
+    for copy in copies:
+        copy.wait()
+
+
+def mover(body, shape, count, *parts):
+    return pl.pallas_call(
+        body,
+        in_specs=[HBM] * len(parts),
+        out_specs=HBM,
+        out_shape=like(*shape),
+        scratch_shapes=[pltpu.SemaphoreType.DMA((count,))],
+        compiler_params=pltpu.CompilerParams(vmem_limit_bytes=4 << 20),
+    )(*[far_memory(part) for part in parts])
+
+
+def pack_kernel(a, b, out, sems):
+    run_copies(sems, [(a, out.at[:, pl.ds(0, 128)]), (b, out.at[:, pl.ds(128, 512)])])
+
+
+def slice_moves(transfer, inverse, out, start):
+    moves = [(transfer.at[0, pl.ds(256, 64), :], out.at[pl.ds(start, 64), :])]
+    for k in range(4):
+        source = inverse.at[0, pl.ds(320, 16), pl.ds(k * 256, 256)]
+        moves.append((source, out.at[pl.ds(start + 64 + k * 16, 16), :]))
+    return moves
+
+
+def slices_kernel(transfer, inverse, out, sems):
+    run_copies(sems, slice_moves(transfer, inverse, out, 0))
+
+
+def pair_kernel(slices, lower, out, sems):
+    run_copies(sems, [(slices, out.at[pl.ds(0, 128), :]), (lower, out.at[pl.ds(128, 128), :])])
+
+
+def held_kernel(transfer, inverse, pair, mirrored, out, sems):
+    moves = [
+        (transfer.at[0, pl.ds(0, 256), :], out.at[pl.ds(0, 256), :]),
+        (pair, out.at[pl.ds(512, 256), :]),
+        (mirrored, out.at[pl.ds(768, 256), :]),
+    ]
+    for k in range(4):
+        source = inverse.at[0, pl.ds(256, 64), pl.ds(k * 256, 256)]
+        moves.append((source, out.at[pl.ds(256 + k * 64, 64), :]))
+    run_copies(sems, moves)
 
 
 def nodes_kernel(place, b0, b1, b2, b3, e1, m2, f2, m3, own_e2, e2):
@@ -358,7 +420,7 @@
     return kernel(down1_kernel, [(256, 128)], [g1, e1, node_inverse, w1])
 
 
-def residual_kernel(order, parts, res, ordered, picks):
+def residual_kernel(order, parts, res_out, ordered_out, picks, res, ordered, sems):
     res_sum = parts[0] + parts[1] + (parts[2] + parts[3])
     res[...] = res_sum
     rows = jnp.broadcast_to(order[...].astype(F32), (128, 1024))
@@ -367,31 +429,42 @@
     picks[...] = jnp.where(holds == at, 1.0, 0.0).astype(BF16)
     both = dot(picks[...], jnp.concatenate(split(res_sum), axis=1))
     ordered[...] = both[:, :128] + both[:, 128:]
+    run_copies(sems, [(res, res_out), (ordered, ordered_out)])
 
 
 def residual_call(order, parts):
     return kernel(
         residual_kernel,
-        [(1024, 128), (1024, 128)],
+        [],
         [order, parts],
-        scratch=[pltpu.VMEM((1024, 1024), BF16)],
-    )
-
-
-def finish_kernel(place, leaf_map, order, pieces, ordered, basis, solve, delta, picks, rhs, sides):
+        scratch=[
+            pltpu.VMEM((1024, 1024), BF16),
+            pltpu.VMEM((1024, 128), F32),
+            pltpu.VMEM((1024, 128), F32),
+            pltpu.SemaphoreType.DMA((2,)),
+        ],
+        far_outs=[(1024, 128), (1024, 128)],
+    )
+
+
+def finish_kernel(
+    place, leaf_map, order, pieces, ordered, basis, solve, delta,
+    basis_in, solve_in, sems, picks, rhs, sides,
+):
+    first, *rest = load_solve(basis, solve, basis_in, solve_in, sems)
     base = place[3] // 4 * 4
     slot = jnp.int32(3)
     for k in range(3):
         slot = jnp.where(leaf_map[base + k] == place[3], k, slot)
+    picks_by_row(order[...], picks)
+    first.wait()
     rhs[...] = jnp.concatenate(
-        split(ordered[...] - dot3(basis[0], pieces[slot])), axis=1
-    )
-    picks_by_row(order[...], picks)
-
-    @pl.loop(0, 2)
-    def _(i):
-        rows = pl.ds(pl.multiple_of(i * CHUNK, CHUNK), CHUNK)
-        a, b = split(solve[0, rows, :])
+        split(ordered[...] - dot3(basis_in[...], pieces[slot])), axis=1
+    )
+    for k in range(4):
+        rest[k].wait()
+        rows = slice(k * Q, (k + 1) * Q)
+        a, b = split(solve_in[rows, :])
         both = dot(a, rhs[...])
         y = both[:, :128] + (both[:, 128:] + dot(b, rhs[:, :128]))
         sides[rows, :] = jnp.concatenate(split(y), axis=1)
@@ -407,13 +480,15 @@
     return kernel(
         finish_kernel,
         [(1024, 128)],
-        [order, pieces, ordered, leaf_basis, leaf_inverse],
+        [order, pieces, ordered],
         (place, leaf_map),
-        [
+        SOLVE_SCRATCH
+        + [
             pltpu.VMEM((1024, 1024), BF16),
             pltpu.VMEM((1024, 256), BF16),
             pltpu.VMEM((1024, 256), BF16),
         ],
+        [leaf_basis, leaf_inverse],
     )
 
 
@@ -457,15 +532,17 @@
     place = jnp.stack([core, leaf // 2 % 2, col, leaf]).astype(jnp.int32)
 
     xs = [points] + [col_shift(points, d) for d in (1, 2, 3)]
-    packed = pack_call(points, coefs)
+    packed = mover(pack_kernel, (Q, 640), 2, points, coefs)
     left, right = leaf_from(packed, -2), leaf_from(packed, 2)
     partner = leaf_xor(packed, 1)
     relay = leaf_xor(jnp.where(core == 0, right, left), 1)
 
     nodes = (node_transfer, node_inverse)
-    lower = leaf_route(collect(slices_kernel, 128, *nodes), lambda i: facing(i, 0, 1))
-    mirrored = leaf_route(collect(pair_kernel, 256, *nodes, lower), lambda i: facing(i, 1, 0))
-    held = collect(held_kernel, 1024, *nodes, lower, mirrored)
+    slices = mover(slices_kernel, (128, 256), 5, *nodes)
+    lower = leaf_route(slices, lambda i: facing(i, 0, 1))
+    pair = mover(pair_kernel, (256, 256), 2, slices, lower)
+    mirrored = leaf_route(pair, lambda i: facing(i, 1, 0))
+    held = mover(held_kernel, (1024, 256), 7, *nodes, pair, mirrored)
 
     lead = lead_call(cluster_perm, leaf_basis, leaf_inverse)
 
@@ -474,13 +551,13 @@
     across = leaf_xor(held, 2)
     own_core = leaf_xor(held, 1)
     both_ways = leaf_xor(across, 1)
-    partial, led = far_call(
+    led, partial = far_call(
         place, tile_mask, ridge, xs, (left, right, relay), near, targets, coefs, lead
     )
-    reduced = swap_cols(led).sum(0)
+    led = swap_cols(led)
+    reduced = led.sum(0)
     e1, m2, f2, m3, e2 = nodes_call(place, (held, own_core, across, both_ways))
 
-    partial, _ = lax.optimization_barrier((partial, reduced))
     columns = swap_cols(partial)
 
     w1, p1 = level1_call(place, leaf_map, gather4(reduced, G4), node_inverse, node_transfer)

time: 183 us -> 209 us (1.14)
  Pallas kernels: 34.8 us -> 71.4 us
  local copies, waits for them, and re-layouts: 12.6 us -> 4.2 us
  blocking collectives: 51.7 us -> 58.7 us
  waiting for transfers between devices: 39 us -> 34.2 us
  starting transfers between devices: 40.5 us -> 36.7 us
    pallas_call x0 -> x4, Pallas kernels: none -> 35.9 us  [mover(): pl.pallas_call(body, in_specs=[HBM] * len(parts), out_specs=HBM, out_shap...]
    unnamed x60 -> x36, local copies, waits for them, and re-layouts: 12.6 us -> 4.2 us
    all_to_all x0 -> x1, blocking collectives: none -> 6.76 us  [step(): p1 = lax.all_to_all(p1, 'leaf', 0, 0, axis_index_groups=GK, tiled=True)]
    all_to_all x1 -> x0, starting transfers between devices: 4.06 us -> none  [step(): p1 = lax.all_to_all(p1, 'leaf', 0, 0, axis_index_groups=GK, tiled=True)]
    all_to_all x1 -> x0, waiting for transfers between devices: 3.67 us -> none  [step(): p1 = lax.all_to_all(p1, 'leaf', 0, 0, axis_index_groups=GK, tiled=True)]
    pallas_call x14 -> x10, Pallas kernels: 33.7 us -> 34.4 us  [kernel(): pl.pallas_call(body, in_specs=[SMEM] * len(scalars) + [VMEM] * len(values...]
  transfers between devices with their start and end apart: 24 -> 23, of which waited for: 10 -> 8; matrix products, arithmetic and copies ran while one was open for 1% -> 1% of each run, Pallas kernels for 17% -> 32%
where the time goes in v2:
time: 209 us
  Pallas kernels  71.4 us (34%)
  blocking collectives  58.7 us (28%)
  starting transfers between devices  36.7 us (18%)
  waiting for transfers between devices  34.2 us (16%)
  local copies, waits for them, and re-layouts  4.2 us (2%)
    pallas_call x4, Pallas kernels, mover(): pl.pallas_call(body, in_specs=[HBM] * len(parts), out_specs=HBM, out_shap...  35.9 us
    pallas_call x10, Pallas kernels, kernel(): pl.pallas_call(body, in_specs=[SMEM] * len(scalars) + [VMEM] * len(values...  34.4 us
    ppermute x15, waiting for transfers between devices, leaf_route(): return lax.ppermute(value, 'leaf', [(i, target(i)) for i in range(LEAVES)])  30.6 us
    all_gather x3, blocking collectives, gather4(): return lax.all_gather(value, 'leaf', axis=0, axis_index_groups=groups)  27.6 us
    all_to_all x2, blocking collectives, swap_cols(): return lax.all_to_all(value, 'col', 0, 0, tiled=True)  24.3 us
    ppermute x15, starting transfers between devices, leaf_route(): return lax.ppermute(value, 'leaf', [(i, target(i)) for i in range(LEAVES)])  21.1 us
    all_to_all x2, starting transfers between devices, swap_cols(): return lax.all_to_all(value, 'col', 0, 0, tiled=True)  7.22 us
    all_to_all x1, blocking collectives, step(): p1 = lax.all_to_all(p1, 'leaf', 0, 0, axis_index_groups=GK, tiled=True)  6.76 us
  transfers between devices with their start and end apart: 23, of which 8 were waited for; matrix products, arithmetic and copies ran while one was open for 1% of the time, Pallas kernels for 32%

profile of v2, /device:TPU:1, one launch (start us, length us, event | category | flops | bytes accessed | tf_op | source)
XLA Modules:
  0.0 208.9 jit_solution(1818751959606463832)
XLA Ops:
  0.6 1.1 shard_map.122.p0
  1.8 8.7 %collective-permute-start.4 = (f32[256,640]{1,0:T(8,128)S(1)}, f32[256,640]{1,0:T(8,128)S(1)}, u32[]{:S(2)}, u32[]{:S(2)}) collective-permute-start(f32[256,640]{1,0:T(8,128)S(1)} %shard_map.122.p0), channel_id=1, source_target_pairs={{0,248},{4,252},{8,0},{12,4},{16,8},{20,12},{24,16},{28,20},{32,24... | collective-permute-start | bytes 1966088 | tf_op jit(solution)/shard_map/ppermute | solution.py:31
  10.4 1.0 collective-permute-start.6
  11.4 12.5 %collective-permute-done.4.p1 = f32[256,640]{1,0:T(8,128)S(1)} collective-permute-done((f32[256,640]{1,0:T(8,128)S(1)}, f32[256,640]{1,0:T(8,128)S(1)}, u32[]{:S(2)}, u32[]{:S(2)}) %collective-permute-start.4) | collective-permute-done | bytes 655392 | tf_op jit(solution)/shard_map/ppermute | solution.py:31
  23.9 5.2 %collective-permute-done.3.p0 = f32[256,640]{1,0:T(8,128)S(1)} collective-permute-done((f32[256,640]{1,0:T(8,128)S(1)}, f32[256,640]{1,0:T(8,128)S(1)}, u32[]{:S(2)}, u32[]{:S(2)}) %collective-permute-start.3) | collective-permute-done | bytes 655392 | tf_op jit(solution)/shard_map/ppermute | solution.py:31
  29.1 1.0 broadcast_select_fusion
  30.1 1.8 collective-permute-start.5
  31.9 0.9 shard_map.124.slices
  32.8 0.0 copy-start.8
  32.8 0.1 collective-permute-start.7
  32.9 5.0 %collective-permute-done.7.lower = f32[128,256]{1,0:T(8,128)S(1)} collective-permute-done((f32[128,256]{1,0:T(8,128)S(1)}, f32[128,256]{1,0:T(8,128)S(1)}, u32[]{:S(2)}, u32[]{:S(2)}) %collective-permute-start.7) | collective-permute-done | bytes 131104 | tf_op jit(solution)/shard_map/ppermute | solution.py:31
  37.9 0.7 copy-done.17
  38.6 1.0 shard_map.125.pair
  39.6 0.0 copy-start.5
  39.6 0.1 collective-permute-start.8
  39.7 2.8 %collective-permute-start.2 = (f32[256,128]{1,0:T(8,128)S(1)}, f32[256,128]{1,0:T(8,128)S(1)}, u32[]{:S(2)}, u32[]{:S(2)}) collective-permute-start(f32[256,128]{1,0:T(8,128)S(1)} %copy-done.4), channel_id=1, source_target_pairs={{0,3},{1,0},{2,1},{3,2},{4,7},{5,4},{6,5},{7,6},{8,11},{9,8},{10,9... | collective-permute-start | bytes 393224 | tf_op jit(solution)/shard_map/ppermute | solution.py:57
  42.5 0.3 collective-permute-start.1
  42.9 5.0 %collective-permute-done.8.mirrored = f32[256,256]{1,0:T(8,128)S(1)} collective-permute-done((f32[256,256]{1,0:T(8,128)S(1)}, f32[256,256]{1,0:T(8,128)S(1)}, u32[]{:S(2)}, u32[]{:S(2)}) %collective-permute-start.8) | collective-permute-done | bytes 262176 | tf_op jit(solution)/shard_map/ppermute | solution.py:31
  47.9 0.7 copy-done.16
  48.6 1.3 collective-permute-start
  49.9 0.1 pad_add_fusion.place
  50.0 32.9 %shard_map.126.b0 = f32[1024,256]{1,0:T(8,128)} custom-call(f32[1,336,256]{2,1,0:T(8,128)} %e1.1, f32[1,336,1024]{2,1,0:T(8,128)} %m1.3, f32[256,256]{1,0:T(8,128)} %copy-done.5, f32[256,256]{1,0:T(8,128)} %copy-done.16), custom_call_target="tpu_custom_call" | custom-call | tf_op jit(solution)/shard_map/pallas_call | solution.py:289
  83.0 5.3 %shard_map.123.near = f32[1024,512]{1,0:T(8,128)S(1)} custom-call(s32[4]{0:T(128)S(1)} %pad_add_fusion.place, s32[1,5]{1,0:T(1,128)S(1)} %copy-done.14, f32[256,128]{1,0:T(8,128)S(1)} %copy-done.4, f32[256,128]{1,0:T(8,128)S(1)} %collective-permute-done.x1, f32[256,128]{1,0:T(8,128)S(1)} %collective-permute-done.1.x2, ...), custom_call_target="tpu_custom_call" | custom-call | tf_op jit(solution)/shard_map/pallas_call | solution.py:97
  88.3 0.3 collective-permute-start.13
  89.2 0.0 copy-start.1
  89.3 0.0 copy-start.9
  89.3 4.8 %shard_map.127.lead = f32[256,1024]{1,0:T(8,128)S(1)} custom-call(s32[1,1024]{1,0:T(1,128)S(1)} %copy-done.13, f32[1,1024,256]{2,1,0:T(8,128)} %basis.3, f32[1,1024,1024]{2,1,0:T(8,128)} %solve.3), custom_call_target="tpu_custom_call" | custom-call | tf_op jit(solution)/shard_map/pallas_call | solution.py:97
  94.1 8.6 %shard_map.128 = (f32[4,256,128]{2,1,0:T(8,128)S(1)}, f32[4,1024,128]{2,1,0:T(8,128)}) custom-call(s32[4]{0:T(128)S(1)} %pad_add_fusion.place, s32[1,5]{1,0:T(1,128)S(1)} %copy-done.14, f32[1]{0:T(128)S(6)} %copy.13.ridge, f32[256,128]{1,0:T(8,128)S(1)} %copy-done.4, f32[256,128]{1,0:T(8,128)S(1)} %collective-permute-done.x1, ...), custom_call_target="tpu_custom_call" | custom-call | tf_op jit(solution)/shard_map/pallas_call | solution.py:97
  102.7 0.0 copy-start.3
  102.7 0.0 copy-start.15
  102.7 10.8 %all_to_all.29 = f32[4,256,128]{2,1,0:T(8,128)S(1)} all-to-all(f32[4,256,128]{2,1,0:T(8,128)S(1)} %get-tuple-element.21), channel_id=1, replica_groups=mesh['leaf'=64,'col'=4] {'col'}, dimensions={0} | all-to-all | bytes 1048576 | tf_op jit(solution)/shard_map/all_to_all | solution.py:513
  113.6 10.9 %all-gather = f32[1024,128]{1,0:T(8,128)S(1)} all-gather(f32[256,128]{1,0:T(8,128)S(1)} %reduce_sum.18), channel_id=2, replica_groups={{0,4,8,12},{16,20,24,28},{32,36,40,44},{48,52,56,60},{64,68,72,76},{80,..., dimensions={0}, use_global_device_ids=true | all-gather | bytes 655360 | tf_op jit(solution)/shard_map/all_gather | solution.py:61
  124.5 1.4 shard_map.129
  125.9 0.6 copy-done.11
  126.6 6.8 %all_to_all.30 = f32[4,32,256]{2,1,0:T(8,128)} all-to-all(f32[4,32,256]{2,1,0:T(8,128)S(1)} %bitcast.14), channel_id=1, replica_groups={{0,4,8,12},{24,28,16,20},{32,36,40,44},{56,60,48,52},{64,68,72,76},{88,..., dimensions={0} | all-to-all | bytes 262144 | tf_op jit(solution)/shard_map/all_to_all | solution.py:564
  133.3 3.6 %all-to-all-start = ((f32[4,1024,128]{2,1,0:T(8,128)}), f32[4,1024,128]{2,1,0:T(8,128)S(1)}, u32[]{:S(2)}, u32[]{:S(2)}) async-start(f32[4,1024,128]{2,1,0:T(8,128)} %get-tuple-element.20), calls=%async_computation | async-start | bytes 4194304 | tf_op jit(solution)/shard_map/all_to_all | solution.py:513
  137.0 1.1 collective-permute-start.12
  138.1 0.1 collective-permute-start.14
  138.2 0.9 reduce_sum.19.r0
  139.1 0.4 collective-permute-start.11
  139.6 0.9 collective-permute-start.10
  140.5 2.6 %collective-permute-start.9 = (f32[32,256]{1,0:T(8,128)S(1)}, f32[32,256]{1,0:T(8,128)S(1)}, u32[]{:S(2)}, u32[]{:S(2)}) collective-permute-start(f32[32,256]{1,0:T(8,128)S(1)} %reduce_sum.19.r0), channel_id=1, source_target_pairs={{0,24},{4,28},{8,16},{12,20},{16,8},{20,12},{24,0},{28,4},{32,56},... | collective-permute-start | bytes 98312 | tf_op jit(solution)/shard_map/ppermute | solution.py:31
  143.1 3.0 %shard_map.130 = (f32[1024,256]{1,0:T(8,128)S(1)}, f32[256,1024]{1,0:T(8,128)S(1)}, f32[256,256]{1,0:T(8,128)S(1)}, f32[256,1024]{1,0:T(8,128)S(1)}, f32[256,256]{1,0:T(8,128)S(1)}) custom-call(s32[4]{0:T(128)S(1)} %pad_add_fusion.place, f32[1024,256]{1,0:T(8,128)} %shard_map.126.b0, f32[1024,256]{1,0:T(8,128)} %collective-permute-done.12.b1, ...), custom_call_target="tpu_custom_call" | custom-call | tf_op jit(solution)/shard_map/pallas_call | solution.py:97
  146.2 0.8 shard_map.131
  147.0 1.4 collective-permute-start.17
  148.4 1.1 collective-permute-start.16
  149.5 1.5 collective-permute-start.15
  151.0 1.0 collective-permute-done.17
  152.1 1.8 collective-permute-done.15
  153.8 0.5 collective-permute-start.20
  154.3 3.4 %collective-permute-start.18 = (f32[32,256]{1,0:T(8,128)S(1)}, f32[32,256]{1,0:T(8,128)S(1)}, u32[]{:S(2)}, u32[]{:S(2)}) collective-permute-start(f32[32,256]{1,0:T(8,128)S(1)} %add_add_fusion.r0), channel_id=1, source_target_pairs={{224,0},{228,4},{232,8},{236,12},{240,16},{244,20},{248,24},{252,2... | collective-permute-start | bytes 98312 | tf_op jit(solution)/shard_map/ppermute | solution.py:53
  157.8 2.0 collective-permute-done.20.r3
  159.8 0.9 shard_map.132
  160.7 1.6 all-to-all-done.parts
  162.3 2.0 shard_map.133
  164.3 3.6 %all-to-all-start.3 = ((f32[4,256,128]{2,1,0:T(8,128)}), f32[4,256,128]{2,1,0:T(8,128)S(1)}, u32[]{:S(2)}, u32[]{:S(2)}) async-start(f32[4,256,128]{2,1,0:T(8,128)} %bitcast.15), calls=%async_computation.3 | async-start | bytes 1048576 | tf_op jit(solution)/shard_map/all_to_all | solution.py:513
  168.0 9.5 %all-gather.1 = f32[128,256]{1,0:T(8,128)S(1)} all-gather(f32[32,256]{1,0:T(8,128)S(1)} %shard_map.132), channel_id=3, replica_groups={{0,4,8,12},{24,28,16,20},{32,36,40,44},{56,60,48,52},{64,68,72,76},{88,..., dimensions={0}, use_global_device_ids=true | all-gather | bytes 163840 | tf_op jit(solution)/shard_map/all_gather | solution.py:61
  177.4 1.2 copy-done.7
  178.7 0.9 copy-done.12
  179.6 1.7 shard_map.134
  181.3 7.3 %all-gather.2 = f32[1024,128]{1,0:T(8,128)S(1)} all-gather(f32[256,128]{1,0:T(8,128)S(1)} %shard_map.134), channel_id=4, replica_groups={{0,4,8,12},{16,20,24,28},{32,36,40,44},{48,52,56,60},{64,68,72,76},{80,..., dimensions={0}, use_global_device_ids=true | all-gather | bytes 655360 | tf_op jit(solution)/shard_map/all_gather | solution.py:61
  188.6 5.8 %shard_map.135 = f32[1024,128]{1,0:T(8,128)S(1)} custom-call(s32[4]{0:T(128)S(1)} %pad_add_fusion.place, s32[64]{0:T(128)S(1)} %copy-done.15, s32[1,1024]{1,0:T(1,128)S(1)} %copy-done.13, f32[4,256,128]{2,1,0:T(8,128)S(1)} %bitcast.10, f32[1024,128]{1,0:T(8,128)S(1)} %copy-done.10, f32[1,1024,256]{2,1,0:T(8,128)} %basis.3, f32[1,1024,1024]{2,1,0:T(8,128)} %solve.3), custom_call_target="tpu_custom_call" | custom-call | tf_op jit(solution)/shard_map/pallas_call | solution.py:97
  194.4 13.4 %all_to_all.31.delta = f32[4,256,128]{2,1,0:T(8,128)S(1)} all-to-all(f32[4,256,128]{2,1,0:T(8,128)S(1)} %bitcast.11), channel_id=1, replica_groups=mesh['leaf'=64,'col'=4] {'col'}, dimensions={0} | all-to-all | bytes 1048576 | tf_op jit(solution)/shard_map/all_to_all | solution.py:513
  207.8 1.1 outputs.1
  (44 shorter events, 0.1 us)
Async XLA Ops:
  1.8 22.1 %collective-permute-start.4 = (f32[256,640]{1,0:T(8,128)S(1)}, f32[256,640]{1,0:T(8,128)S(1)}, u32[]{:S(2)}, u32[]{:S(2)}) collective-permute-start(f32[256,640]{1,0:T(8,128)S(1)} %shard_map.122.p0), channel_id=1, source_target_pairs={{0,248},{4,252},{8,0},{12,4},{16,8},{20,12},{24,16},{28,20},{32,24... | collective-permute-start | bytes 1966088 | tf_op jit(solution)/shard_map/ppermute | solution.py:31
  10.4 18.7 %collective-permute-start.3 = (f32[256,640]{1,0:T(8,128)S(1)}, f32[256,640]{1,0:T(8,128)S(1)}, u32[]{:S(2)}, u32[]{:S(2)}) collective-permute-start(f32[256,640]{1,0:T(8,128)S(1)} %shard_map.122.p0), channel_id=1, source_target_pairs={{0,8},{4,12},{8,16},{12,20},{16,24},{20,28},{24,32},{28,36},{32,40... | collective-permute-start | bytes 1966088 | tf_op jit(solution)/shard_map/ppermute | solution.py:31
  10.4 72.5 %collective-permute-start.6 = (f32[256,640]{1,0:T(8,128)S(1)}, f32[256,640]{1,0:T(8,128)}, u32[]{:S(2)}, u32[]{:S(2)}) collective-permute-start(f32[256,640]{1,0:T(8,128)S(1)} %shard_map.122.p0), channel_id=1, source_target_pairs={{0,4},{4,0},{8,12},{12,8},{16,20},{20,16},{24,28},{28,24},{32,36},... | collective-permute-start | bytes 1966088 | tf_op jit(solution)/shard_map/ppermute | solution.py:31
  11.4 28.3 %copy-start.4 = (f32[256,128]{1,0:T(8,128)S(1)}, f32[256,128]{1,0:T(8,128)}, u32[]{:S(2)}) copy-start(f32[256,128]{1,0:T(8,128)} %x0.3) | copy-start | bytes 393220
  30.1 64.0 %collective-permute-start.5 = (f32[256,640]{1,0:T(8,128)}, f32[256,640]{1,0:T(8,128)S(1)}, u32[]{:S(2)}, u32[]{:S(2)}) collective-permute-start(f32[256,640]{1,0:T(8,128)} %broadcast_select_fusion), channel_id=1, source_target_pairs={{0,4},{4,0},{8,12},{12,8},{16,20},{20,16},{24,28},{28,24},{32,36},... | collective-permute-start | bytes 1966088 | tf_op jit(solution)/shard_map/ppermute | solution.py:31
  32.8 5.2 %copy-start.8 = (f32[128,256]{1,0:T(8,128)}, f32[128,256]{1,0:T(8,128)S(1)}, u32[]{:S(2)}) copy-start(f32[128,256]{1,0:T(8,128)S(1)} %shard_map.124.slices) | copy-start | bytes 393220
  32.8 50.2 %copy-start.14 = (s32[1,5]{1,0:T(1,128)S(1)}, s32[1,5]{1,0:T(1,128)}, u32[]{:S(2)}) copy-start(s32[1,5]{1,0:T(1,128)} %mask.3) | copy-start | bytes 64
  32.8 5.1 %collective-permute-start.7 = (f32[128,256]{1,0:T(8,128)S(1)}, f32[128,256]{1,0:T(8,128)S(1)}, u32[]{:S(2)}, u32[]{:S(2)}) collective-permute-start(f32[128,256]{1,0:T(8,128)S(1)} %shard_map.124.slices), channel_id=1, source_target_pairs={{0,32},{4,36},{8,40},{12,44},{16,48},{20,52},{24,56},{28,60},{32,0... | collective-permute-start | bytes 393224 | tf_op jit(solution)/shard_map/ppermute | solution.py:31
  37.9 0.7 copy-start.17
  39.6 10.4 %copy-start.5 = (f32[256,256]{1,0:T(8,128)}, f32[256,256]{1,0:T(8,128)S(1)}, u32[]{:S(2)}) copy-start(f32[256,256]{1,0:T(8,128)S(1)} %shard_map.125.pair) | copy-start | bytes 786436
  39.6 8.3 %collective-permute-start.8 = (f32[256,256]{1,0:T(8,128)S(1)}, f32[256,256]{1,0:T(8,128)S(1)}, u32[]{:S(2)}, u32[]{:S(2)}) collective-permute-start(f32[256,256]{1,0:T(8,128)S(1)} %shard_map.125.pair), channel_id=1, source_target_pairs={{0,24},{4,28},{8,16},{12,20},{16,8},{20,12},{24,0},{28,4},{32,56},... | collective-permute-start | bytes 786440 | tf_op jit(solution)/shard_map/ppermute | solution.py:31
  39.7 43.2 %collective-permute-start.2 = (f32[256,128]{1,0:T(8,128)S(1)}, f32[256,128]{1,0:T(8,128)S(1)}, u32[]{:S(2)}, u32[]{:S(2)}) collective-permute-start(f32[256,128]{1,0:T(8,128)S(1)} %copy-done.4), channel_id=1, source_target_pairs={{0,3},{1,0},{2,1},{3,2},{4,7},{5,4},{6,5},{7,6},{8,11},{9,8},{10,9... | collective-permute-start | bytes 393224 | tf_op jit(solution)/shard_map/ppermute | solution.py:57
  42.5 40.4 %collective-permute-start.1 = (f32[256,128]{1,0:T(8,128)S(1)}, f32[256,128]{1,0:T(8,128)S(1)}, u32[]{:S(2)}, u32[]{:S(2)}) collective-permute-start(f32[256,128]{1,0:T(8,128)S(1)} %copy-done.4), channel_id=1, source_target_pairs={{0,2},{1,3},{2,0},{3,1},{4,6},{5,7},{6,4},{7,5},{8,10},{9,11},{10,... | collective-permute-start | bytes 393224 | tf_op jit(solution)/shard_map/ppermute | solution.py:57
  47.9 0.7 copy-start.16
  48.6 34.3 %collective-permute-start = (f32[256,128]{1,0:T(8,128)S(1)}, f32[256,128]{1,0:T(8,128)S(1)}, u32[]{:S(2)}, u32[]{:S(2)}) collective-permute-start(f32[256,128]{1,0:T(8,128)S(1)} %copy-done.4), channel_id=1, source_target_pairs={{0,1},{1,2},{2,3},{3,0},{4,5},{5,6},{6,7},{7,4},{8,9},{9,10},{10,1... | collective-permute-start | bytes 393224 | tf_op jit(solution)/shard_map/ppermute | solution.py:57
  82.9 6.3 %copy-start.13 = (s32[1,1024]{1,0:T(1,128)S(1)}, s32[1,1024]{1,0:T(1,128)}, u32[]{:S(2)}) copy-start(s32[1,1024]{1,0:T(1,128)} %order.5) | copy-start | bytes 12292
  88.3 49.8 %collective-permute-start.13 = (f32[1024,256]{1,0:T(8,128)}, f32[1024,256]{1,0:T(8,128)}, u32[]{:S(2)}, u32[]{:S(2)}) collective-permute-start(f32[1024,256]{1,0:T(8,128)} %shard_map.126.b0), channel_id=1, source_target_pairs={{0,8},{4,12},{8,0},{12,4},{16,24},{20,28},{24,16},{28,20},{32,40},... | collective-permute-start | bytes 3145736 | tf_op jit(solution)/shard_map/ppermute | solution.py:31
  89.2 4.8 %copy-start.1 = (f32[256,512]{1,0:T(8,128)S(1)}, f32[256,512]{1,0:T(8,128)}, u32[]{:S(2)}) copy-start(f32[256,512]{1,0:T(8,128)} %coefs.1) | copy-start | bytes 1572868
  89.3 4.8 %copy-start.9 = (f32[256,512]{1,0:T(8,128)S(1)}, f32[256,512]{1,0:T(8,128)}, u32[]{:S(2)}) copy-start(f32[256,512]{1,0:T(8,128)} %own_y.1) | copy-start | bytes 1572868
  102.7 21.8 %copy-start = (f32[1,336,1024]{2,1,0:T(8,128)S(1)}, f32[1,336,1024]{2,1,0:T(8,128)}, u32[]{:S(2)}) copy-start(f32[1,336,1024]{2,1,0:T(8,128)} %m1.3) | copy-start | bytes 4128772
  102.7 21.8 %copy-start.3 = (f32[1,336,256]{2,1,0:T(8,128)S(1)}, f32[1,336,256]{2,1,0:T(8,128)}, u32[]{:S(2)}) copy-start(f32[1,336,256]{2,1,0:T(8,128)} %e1.1) | copy-start | bytes 1032196
  102.7 21.8 %copy-start.15 = (s32[64]{0:T(128)S(1)}, s32[64]{0:T(128)}, u32[]{:S(2)}) copy-start(s32[64]{0:T(128)} %leaf_map.3) | copy-start | bytes 772
  125.9 0.6 copy-start.11
  133.3 29.0 %all-to-all-start = ((f32[4,1024,128]{2,1,0:T(8,128)}), f32[4,1024,128]{2,1,0:T(8,128)S(1)}, u32[]{:S(2)}, u32[]{:S(2)}) async-start(f32[4,1024,128]{2,1,0:T(8,128)} %get-tuple-element.20), calls=%async_computation | async-start | bytes 4194304 | tf_op jit(solution)/shard_map/all_to_all | solution.py:513
  137.0 6.1 %collective-permute-start.12 = (f32[1024,256]{1,0:T(8,128)}, f32[1024,256]{1,0:T(8,128)}, u32[]{:S(2)}, u32[]{:S(2)}) collective-permute-start(f32[1024,256]{1,0:T(8,128)} %shard_map.126.b0), channel_id=1, source_target_pairs={{0,4},{4,0},{8,12},{12,8},{16,20},{20,16},{24,28},{28,24},{32,36},... | collective-permute-start | bytes 3145736 | tf_op jit(solution)/shard_map/ppermute | solution.py:31
  138.1 5.0 %collective-permute-start.14 = (f32[1024,256]{1,0:T(8,128)}, f32[1024,256]{1,0:T(8,128)}, u32[]{:S(2)}, u32[]{:S(2)}) collective-permute-start(f32[1024,256]{1,0:T(8,128)} %collective-permute-done.13.b2), channel_id=1, source_target_pairs={{0,4},{4,0},{8,12},{12,8},{16,20},{20,16},{24,28},{28,24},{32,36},... | collective-permute-start | bytes 3145736 | tf_op jit(solution)/shard_map/ppermute | solution.py:31
  139.1 7.0 %collective-permute-start.11 = (f32[32,256]{1,0:T(8,128)S(1)}, f32[32,256]{1,0:T(8,128)S(1)}, u32[]{:S(2)}, u32[]{:S(2)}) collective-permute-start(f32[32,256]{1,0:T(8,128)S(1)} %reduce_sum.19.r0), channel_id=1, source_target_pairs={{0,56},{4,60},{8,48},{12,52},{16,40},{20,44},{24,32},{28,36},{32,2... | collective-permute-start | bytes 98312 | tf_op jit(solution)/shard_map/ppermute | solution.py:31
  139.6 6.6 %collective-permute-start.10 = (f32[32,256]{1,0:T(8,128)S(1)}, f32[32,256]{1,0:T(8,128)S(1)}, u32[]{:S(2)}, u32[]{:S(2)}) collective-permute-start(f32[32,256]{1,0:T(8,128)S(1)} %reduce_sum.19.r0), channel_id=1, source_target_pairs={{0,32},{4,36},{8,40},{12,44},{16,48},{20,52},{24,56},{28,60},{32,0... | collective-permute-start | bytes 98312 | tf_op jit(solution)/shard_map/ppermute | solution.py:31
  140.5 5.7 %collective-permute-start.9 = (f32[32,256]{1,0:T(8,128)S(1)}, f32[32,256]{1,0:T(8,128)S(1)}, u32[]{:S(2)}, u32[]{:S(2)}) collective-permute-start(f32[32,256]{1,0:T(8,128)S(1)} %reduce_sum.19.r0), channel_id=1, source_target_pairs={{0,24},{4,28},{8,16},{12,20},{16,8},{20,12},{24,0},{28,4},{32,56},... | collective-permute-start | bytes 98312 | tf_op jit(solution)/shard_map/ppermute | solution.py:31
  146.1 13.7 %copy-start.6 = (f32[1024,256]{1,0:T(8,128)}, f32[1024,256]{1,0:T(8,128)S(1)}, u32[]{:S(2)}) copy-start(f32[1024,256]{1,0:T(8,128)S(1)} %get-tuple-element.33.e1) | copy-start | bytes 3145732
  147.0 5.1 %collective-permute-start.17 = (f32[32,256]{1,0:T(8,128)S(1)}, f32[32,256]{1,0:T(8,128)S(1)}, u32[]{:S(2)}, u32[]{:S(2)}) collective-permute-start(f32[32,256]{1,0:T(8,128)S(1)} %get-tuple-element.26), channel_id=1, source_target_pairs={{0,56},{4,60},{8,48},{12,52},{16,40},{20,44},{24,32},{28,36},{32,2... | collective-permute-start | bytes 98312 | tf_op jit(solution)/shard_map/ppermute | solution.py:31
  148.4 3.6 %collective-permute-start.16 = (f32[32,256]{1,0:T(8,128)S(1)}, f32[32,256]{1,0:T(8,128)S(1)}, u32[]{:S(2)}, u32[]{:S(2)}) collective-permute-start(f32[32,256]{1,0:T(8,128)S(1)} %get-tuple-element.26), channel_id=1, source_target_pairs={{0,32},{4,36},{8,40},{12,44},{16,48},{20,52},{24,56},{28,60},{32,0... | collective-permute-start | bytes 98312 | tf_op jit(solution)/shard_map/ppermute | solution.py:31
  149.5 4.3 %collective-permute-start.15 = (f32[32,256]{1,0:T(8,128)S(1)}, f32[32,256]{1,0:T(8,128)S(1)}, u32[]{:S(2)}, u32[]{:S(2)}) collective-permute-start(f32[32,256]{1,0:T(8,128)S(1)} %get-tuple-element.26), channel_id=1, source_target_pairs={{0,24},{4,28},{8,16},{12,20},{16,8},{20,12},{24,0},{28,4},{32,56},... | collective-permute-start | bytes 98312 | tf_op jit(solution)/shard_map/ppermute | solution.py:31
  153.8 5.9 %collective-permute-start.20 = (f32[32,256]{1,0:T(8,128)S(1)}, f32[32,256]{1,0:T(8,128)S(1)}, u32[]{:S(2)}, u32[]{:S(2)}) collective-permute-start(f32[32,256]{1,0:T(8,128)S(1)} %add_add_fusion.r0), channel_id=1, source_target_pairs={{160,0},{164,4},{168,8},{172,12},{176,16},{180,20},{184,24},{188,2... | collective-permute-start | bytes 98312 | tf_op jit(solution)/shard_map/ppermute | solution.py:53
  154.3 5.4 %collective-permute-start.19 = (f32[32,256]{1,0:T(8,128)S(1)}, f32[32,256]{1,0:T(8,128)S(1)}, u32[]{:S(2)}, u32[]{:S(2)}) collective-permute-start(f32[32,256]{1,0:T(8,128)S(1)} %add_add_fusion.r0), channel_id=1, source_target_pairs={{64,0},{68,4},{72,8},{76,12},{80,16},{84,20},{88,24},{92,28},{224,... | collective-permute-start | bytes 98312 | tf_op jit(solution)/shard_map/ppermute | solution.py:53
  154.3 5.4 %collective-permute-start.18 = (f32[32,256]{1,0:T(8,128)S(1)}, f32[32,256]{1,0:T(8,128)S(1)}, u32[]{:S(2)}, u32[]{:S(2)}) collective-permute-start(f32[32,256]{1,0:T(8,128)S(1)} %add_add_fusion.r0), channel_id=1, source_target_pairs={{224,0},{228,4},{232,8},{236,12},{240,16},{244,20},{248,24},{252,2... | collective-permute-start | bytes 98312 | tf_op jit(solution)/shard_map/ppermute | solution.py:53
  164.3 24.2 %copy-start.10 = (f32[1024,128]{1,0:T(8,128)S(1)}, f32[1024,128]{1,0:T(8,128)}, u32[]{:S(2)}) copy-start(f32[1024,128]{1,0:T(8,128)} %get-tuple-element.35.ordered) | copy-start | bytes 1572868
  164.3 30.0 %all-to-all-start.3 = ((f32[4,256,128]{2,1,0:T(8,128)}), f32[4,256,128]{2,1,0:T(8,128)S(1)}, u32[]{:S(2)}, u32[]{:S(2)}) async-start(f32[4,256,128]{2,1,0:T(8,128)} %bitcast.15), calls=%async_computation.3 | async-start | bytes 1048576 | tf_op jit(solution)/shard_map/all_to_all | solution.py:513
  177.4 1.2 copy-start.7
  178.7 0.9 copy-start.12
  188.6 19.3 %copy-start.2 = (f32[256,512]{1,0:T(8,128)S(1)}, f32[256,512]{1,0:T(8,128)}, u32[]{:S(2)}) copy-start(f32[256,512]{1,0:T(8,128)} %coefs.1) | copy-start | bytes 1572868

commit v3 on v2

--- a/solution.py
+++ b/solution.py
@@ -157,7 +157,7 @@
 
 def far_kernel(
     place, mask, ridge, x0, x1, x2, x3, p0, p1, p2, near, own_y, own_a, lead,
-    led, out, parts, sems, *scratch
+    led, out0, out1, out2, out3, parts, sems, *scratch
 ):
     blocks = [(p[:, :128], p[:, 128:]) for p in (p0, p1, p2)]
     tile_setup(place, (x0, x1, x2, x3), blocks, *scratch)
@@ -171,7 +171,12 @@
 
     def sent(i):
         rows = pl.ds(pl.multiple_of(i * CHUNK, CHUNK), CHUNK)
-        return pltpu.make_async_copy(parts.at[i], out.at[:, rows, :], sems.at[i])
+        return [
+            pltpu.make_async_copy(
+                parts.at[i, (place[2] + d) % 4], out.at[rows, :], sems.at[i, d]
+            )
+            for d, out in enumerate((out0, out1, out2, out3))
+        ]
 
     @pl.loop(0, 2)
     def _(i):
@@ -189,10 +194,12 @@
         for k in range(4):
             parts[i, k] = part[:, k * 128 : (k + 1) * 128]
             led[k] += product[:, k * 128 : (k + 1) * 128]
-        sent(i).start()
+        for copy in sent(i):
+            copy.start()
 
     for i in range(2):
-        sent(i).wait()
+        for copy in sent(i):
+            copy.wait()
 
 
 def tile_scratch(count):
@@ -207,7 +214,9 @@
 
 
 def near_call(place, mask, xs, blocks):
-    return kernel(near_kernel, [(1024, 512)], [*xs, *blocks], (place, mask), tile_scratch(2))
+    return kernel(
+        near_kernel, [(1024, 512)], [*xs, *blocks], (place, mask), tile_scratch(2)
+    )
 
 
 def far_call(place, mask, ridge, xs, blocks, near, own_y, own_a, lead):
@@ -216,8 +225,8 @@
         [(4, RANK, 128)],
         [*xs, *blocks, near, own_y, own_a, lead],
         (place, mask, ridge),
-        [pltpu.VMEM((2, 4, CHUNK, 128), F32), pltpu.SemaphoreType.DMA((2,))] + tile_scratch(3),
-        far_outs=[(4, 1024, 128)],
+        [pltpu.VMEM((2, 4, CHUNK, 128), F32), pltpu.SemaphoreType.DMA((2, 4))] + tile_scratch(3),
+        far_outs=[(1024, 128)] * 4,
     )
 
 
@@ -316,16 +325,28 @@
     run_copies(sems, [(slices, out.at[pl.ds(0, 128), :]), (lower, out.at[pl.ds(128, 128), :])])
 
 
-def held_kernel(transfer, inverse, pair, mirrored, out, sems):
+def held_kernel(transfer, inverse, pair, mirrored, out, buffer, sems):
     moves = [
-        (transfer.at[0, pl.ds(0, 256), :], out.at[pl.ds(0, 256), :]),
-        (pair, out.at[pl.ds(512, 256), :]),
-        (mirrored, out.at[pl.ds(768, 256), :]),
+        (transfer.at[0, pl.ds(0, 256), :], buffer.at[pl.ds(0, 256), :]),
+        (pair, buffer.at[pl.ds(512, 256), :]),
+        (mirrored, buffer.at[pl.ds(768, 256), :]),
     ]
     for k in range(4):
         source = inverse.at[0, pl.ds(256, 64), pl.ds(k * 256, 256)]
-        moves.append((source, out.at[pl.ds(256 + k * 64, 64), :]))
+        moves.append((source, buffer.at[pl.ds(256 + k * 64, 64), :]))
     run_copies(sems, moves)
+    run_copies(sems, [(buffer, out)])
+
+
+def held_call(*parts):
+    return kernel(
+        held_kernel,
+        [],
+        [],
+        scratch=[pltpu.VMEM((1024, 256), F32), pltpu.SemaphoreType.DMA((7,))],
+        far_values=parts,
+        far_outs=[(1024, 256)],
+    )
 
 
 def nodes_kernel(place, b0, b1, b2, b3, e1, m2, f2, m3, own_e2, e2):
@@ -410,18 +431,41 @@
     return kernel(upper_kernel, [(32, 256)], [*parts, m3, f2, w2])
 
 
-def down1_kernel(g1, e1, m1, w1, v1):
+def down1_kernel(g1, e1, m1, w1, v1, e1_in, m1_in, w1_in, sems):
+    copies = [
+        pltpu.make_async_copy(e1, e1_in, sems.at[0]),
+        pltpu.make_async_copy(m1.at[0, pl.ds(0, 256), :], m1_in, sems.at[1]),
+        pltpu.make_async_copy(w1, w1_in, sems.at[2]),
+    ]
+    for copy in copies:
+        copy.start()
     g = g1[...].reshape(128, 256)
-    lifted = dot3(g, e1[...], NT)
-    v1[...] = w1[...] - dot3(m1[0, :256, :], lifted, NT)
+    copies[0].wait()
+    lifted = dot3(g, e1_in[...], NT)
+    copies[1].wait()
+    copies[2].wait()
+    v1[...] = w1_in[...] - dot3(m1_in[...], lifted, NT)
 
 
 def down1_call(g1, e1, node_inverse, w1):
-    return kernel(down1_kernel, [(256, 128)], [g1, e1, node_inverse, w1])
-
-
-def residual_kernel(order, parts, res_out, ordered_out, picks, res, ordered, sems):
-    res_sum = parts[0] + parts[1] + (parts[2] + parts[3])
+    return kernel(
+        down1_kernel,
+        [(256, 128)],
+        [g1],
+        scratch=[
+            pltpu.VMEM((1024, 256), F32),
+            pltpu.VMEM((256, 1024), F32),
+            pltpu.VMEM((256, 128), F32),
+            pltpu.SemaphoreType.DMA((3,)),
+        ],
+        far_values=[e1, node_inverse, w1],
+    )
+
+
+def residual_kernel(
+    place, order, p0, p1, p2, p3, ordered_out, out0, out1, out2, out3, picks, res, ordered, sems
+):
+    res_sum = p0[...] + p1[...] + (p2[...] + p3[...])
     res[...] = res_sum
     rows = jnp.broadcast_to(order[...].astype(F32), (128, 1024))
     holds = jnp.transpose(rows)[:, :1].astype(jnp.int32)
@@ -429,21 +473,26 @@
     picks[...] = jnp.where(holds == at, 1.0, 0.0).astype(BF16)
     both = dot(picks[...], jnp.concatenate(split(res_sum), axis=1))
     ordered[...] = both[:, :128] + both[:, 128:]
-    run_copies(sems, [(res, res_out), (ordered, ordered_out)])
-
-
-def residual_call(order, parts):
+    moves = [(ordered, ordered_out)]
+    for k, out in enumerate((out0, out1, out2, out3)):
+        rows = pl.ds(pl.multiple_of((place[2] + k) % 4 * Q, Q), Q)
+        moves.append((res.at[rows, :], out))
+    run_copies(sems, moves)
+
+
+def residual_call(place, order, parts):
     return kernel(
         residual_kernel,
         [],
-        [order, parts],
-        scratch=[
+        [order, *parts],
+        (place,),
+        [
             pltpu.VMEM((1024, 1024), BF16),
             pltpu.VMEM((1024, 128), F32),
             pltpu.VMEM((1024, 128), F32),
-            pltpu.SemaphoreType.DMA((2,)),
+            pltpu.SemaphoreType.DMA((5,)),
         ],
-        far_outs=[(1024, 128), (1024, 128)],
+        far_outs=[(1024, 128)] + [(Q, 128)] * 4,
     )
 
 
@@ -492,21 +541,22 @@
     )
 
 
-def outputs_kernel(res, delta, coefs, out_res, out_new):
-    for k in range(4):
+def outputs_kernel(place, r0, r1, r2, r3, delta, coefs, out_res, out_new):
+    for k, res in enumerate((r0, r1, r2, r3)):
         at = slice(k * 128, (k + 1) * 128)
-        out_res[:, at] = res[k]
         out_new[:, at] = coefs[:, at] + delta[k]
-
-
-def outputs_call(res, delta, coefs):
+        source = pl.multiple_of((place[2] + 4 - k) % 4 * 128, 128)
+        out_res[:, pl.ds(source, 128)] = res[...]
+
+
+def outputs_call(place, res, delta, coefs):
     return pl.pallas_call(
         outputs_kernel,
-        in_specs=[VMEM] * 3,
+        in_specs=[SMEM] + [VMEM] * 6,
         out_shape=[like(Q, 512), like(Q, 512)],
         compiler_params=pltpu.CompilerParams(vmem_limit_bytes=8 << 20),
         name="outputs",
-    )(*[near_memory(value) for value in (res, delta, coefs)])
+    )(place, *[near_memory(value) for value in (*res, delta, coefs)])
 
 
 def swap_cols(value):
@@ -542,7 +592,7 @@
     lower = leaf_route(slices, lambda i: facing(i, 0, 1))
     pair = mover(pair_kernel, (256, 256), 2, slices, lower)
     mirrored = leaf_route(pair, lambda i: facing(i, 1, 0))
-    held = mover(held_kernel, (1024, 256), 7, *nodes, pair, mirrored)
+    held = held_call(*nodes, pair, mirrored)
 
     lead = lead_call(cluster_perm, leaf_basis, leaf_inverse)
 
@@ -551,30 +601,31 @@
     across = leaf_xor(held, 2)
     own_core = leaf_xor(held, 1)
     both_ways = leaf_xor(across, 1)
-    led, partial = far_call(
+    led, *partial = far_call(
         place, tile_mask, ridge, xs, (left, right, relay), near, targets, coefs, lead
     )
     led = swap_cols(led)
-    reduced = led.sum(0)
+    reduced = led[0] + led[1] + (led[2] + led[3])
     e1, m2, f2, m3, e2 = nodes_call(place, (held, own_core, across, both_ways))
 
-    columns = swap_cols(partial)
+    columns = [partial[0]] + [col_shift(partial[d], d) for d in (1, 2, 3)]
 
     w1, p1 = level1_call(place, leaf_map, gather4(reduced, G4), node_inverse, node_transfer)
     p1 = lax.all_to_all(p1, "leaf", 0, 0, axis_index_groups=GK, tiled=True)
-    r1 = p1.reshape(4, 32, RANK).sum(0)
+    p1 = p1.reshape(4, 32, RANK)
+    r1 = p1[0] + p1[1] + (p1[2] + p1[3])
     w2, p2 = level2_call(siblings(r1), m2, e2)
     r2 = sum(siblings(p2))
     r2s = [r2, z_from(r2, -1, 1), z_from(r2, 2, -2), z_from(r2, -3, 3)]
     g1 = upper_call(r2s, m3, f2, w2)
     columns, g1 = lax.optimization_barrier((columns, g1))
-    res, ordered = residual_call(cluster_perm, columns)
-    res_rows = swap_cols(res.reshape(4, Q, 128))
+    ordered, *pieces = residual_call(place, cluster_perm, columns)
+    res_rows = [pieces[0]] + [col_shift(pieces[k], k) for k in (1, 2, 3)]
     g1 = gather4(g1, GK)
     pieces = gather4(down1_call(g1, e1, node_inverse, w1), G4)
 
     delta = finish_call(place, leaf_map, cluster_perm, pieces, ordered, leaf_basis, leaf_inverse)
-    return outputs_call(res_rows, swap_cols(delta.reshape(4, Q, 128)), coefs)
+    return outputs_call(place, res_rows, swap_cols(delta.reshape(4, Q, 128)), coefs)
 
 
 def solution(mesh):

time: 209 us -> 206 us (0.986)
  blocking collectives: 58.7 us -> 27.4 us
  starting transfers between devices: 36.7 us -> 59.8 us
  waiting for transfers between devices: 34.2 us -> 46.9 us
  Pallas kernels: 71.4 us -> 64.5 us
    all_to_all x3 -> x0, blocking collectives: 31 us -> none  [the longest x2 24.3 us: swap_cols(): return lax.all_to_all(value, 'col', 0, 0, tiled=True)]
    ppermute x3 -> x9, waiting for transfers between devices: 0.01 us -> 14.7 us  [col_shift(): return lax.ppermute(value, 'col', [(i, (i + step) % 4) for i in range(4)])]
    pallas_call x4 -> x3, Pallas kernels: 35.9 us -> 22.8 us  [mover(): pl.pallas_call(body, in_specs=[HBM] * len(parts), out_specs=HBM, out_shap...]
    ppermute x3 -> x9, starting transfers between devices: 4.46 us -> 14.1 us  [col_shift(): return lax.ppermute(value, 'col', [(i, (i + step) % 4) for i in range(4)])]
    ppermute x15, waiting for transfers between devices: 30.6 us -> 24.1 us  [leaf_route(): return lax.ppermute(value, 'leaf', [(i, target(i)) for i in range(LEAVES)])]
    ppermute x3, starting transfers between devices: 3.92 us -> 10.1 us  [z_from(): return lax.ppermute(value, 'leaf', route)]
    pallas_call x10 -> x11, Pallas kernels: 34.4 us -> 40 us  [kernel(): pl.pallas_call(body, in_specs=[SMEM] * len(scalars) + [VMEM] * len(values...]
    all_to_all x0 -> x1, starting transfers between devices: none -> 3.45 us  [step(): p1 = lax.all_to_all(p1, 'leaf', 0, 0, axis_index_groups=GK, tiled=True)]
  transfers between devices with their start and end apart: 23 -> 30, of which waited for: 8 -> 15; matrix products, arithmetic and copies ran while one was open for 1% -> 1% of each run, Pallas kernels for 32% -> 14%
where the time goes in v3:
time: 206 us
  Pallas kernels  64.5 us (31%)
  starting transfers between devices  59.8 us (29%)
  waiting for transfers between devices  46.9 us (23%)
  blocking collectives  27.4 us (13%)
  local copies, waits for them, and re-layouts  4.24 us (2%)
    pallas_call x11, Pallas kernels, kernel(): pl.pallas_call(body, in_specs=[SMEM] * len(scalars) + [VMEM] * len(values...  40 us
    all_gather x3, blocking collectives, gather4(): return lax.all_gather(value, 'leaf', axis=0, axis_index_groups=groups)  27.4 us
    ppermute x15, starting transfers between devices, leaf_route(): return lax.ppermute(value, 'leaf', [(i, target(i)) for i in range(LEAVES)])  24.3 us
    ppermute x15, waiting for transfers between devices, leaf_route(): return lax.ppermute(value, 'leaf', [(i, target(i)) for i in range(LEAVES)])  24.1 us
    pallas_call x3, Pallas kernels, mover(): pl.pallas_call(body, in_specs=[HBM] * len(parts), out_specs=HBM, out_shap...  22.8 us
    ppermute x9, waiting for transfers between devices, col_shift(): return lax.ppermute(value, 'col', [(i, (i + step) % 4) for i in range(4)])  14.7 us
    ppermute x9, starting transfers between devices, col_shift(): return lax.ppermute(value, 'col', [(i, (i + step) % 4) for i in range(4)])  14.1 us
    ppermute x3, starting transfers between devices, z_from(): return lax.ppermute(value, 'leaf', route)  10.1 us
  transfers between devices with their start and end apart: 30, of which 15 were waited for; matrix products, arithmetic and copies ran while one was open for 1% of the time, Pallas kernels for 14%

profile of v3, /device:TPU:1, one launch (start us, length us, event | category | flops | bytes accessed | tf_op | source)
XLA Modules:
  0.0 205.9 jit_solution(5470021345115553467)
XLA Ops:
  0.6 21.0 %shard_map.122.p0 = f32[256,640]{1,0:T(8,128)} custom-call(f32[256,128]{1,0:T(8,128)} %x0.3, f32[256,512]{1,0:T(8,128)} %coefs.1), custom_call_target="tpu_custom_call" | custom-call | tf_op jit(solution)/shard_map/pallas_call | solution.py:298
  21.6 3.3 %collective-permute-start.6 = (f32[256,640]{1,0:T(8,128)}, f32[256,640]{1,0:T(8,128)}, u32[]{:S(2)}, u32[]{:S(2)}) collective-permute-start(f32[256,640]{1,0:T(8,128)} %shard_map.122.p0), channel_id=1, source_target_pairs={{0,4},{4,0},{8,12},{12,8},{16,20},{20,16},{24,28},{28,24},{32,36},... | collective-permute-start | bytes 1966088 | tf_op jit(solution)/shard_map/ppermute | solution.py:31
  24.9 6.1 %collective-permute-start.4 = (f32[256,640]{1,0:T(8,128)}, f32[256,640]{1,0:T(8,128)S(1)}, u32[]{:S(2)}, u32[]{:S(2)}) collective-permute-start(f32[256,640]{1,0:T(8,128)} %shard_map.122.p0), channel_id=1, source_target_pairs={{0,248},{4,252},{8,0},{12,4},{16,8},{20,12},{24,16},{28,20},{32,24... | collective-permute-start | bytes 1966088 | tf_op jit(solution)/shard_map/ppermute | solution.py:31
  31.0 0.9 shard_map.124.slices
  32.0 12.6 %collective-permute-done.7.lower = f32[128,256]{1,0:T(8,128)S(1)} collective-permute-done((f32[128,256]{1,0:T(8,128)S(1)}, f32[128,256]{1,0:T(8,128)S(1)}, u32[]{:S(2)}, u32[]{:S(2)}) %collective-permute-start.7) | collective-permute-done | bytes 131104 | tf_op jit(solution)/shard_map/ppermute | solution.py:31
  44.6 0.7 copy-done.18
  45.3 1.0 shard_map.125.pair
  46.3 1.5 collective-permute-start.8
  47.7 2.7 %collective-permute-start.2 = (f32[256,128]{1,0:T(8,128)S(1)}, f32[256,128]{1,0:T(8,128)S(1)}, u32[]{:S(2)}, u32[]{:S(2)}) collective-permute-start(f32[256,128]{1,0:T(8,128)S(1)} %copy-done.4), channel_id=1, source_target_pairs={{0,3},{1,0},{2,1},{3,2},{4,7},{5,4},{6,5},{7,6},{8,11},{9,8},{10,9... | collective-permute-start | bytes 393224 | tf_op jit(solution)/shard_map/ppermute | solution.py:57
  50.5 1.9 collective-permute-done.2.x3
  52.4 2.3 %collective-permute-start.1 = (f32[256,128]{1,0:T(8,128)S(1)}, f32[256,128]{1,0:T(8,128)S(1)}, u32[]{:S(2)}, u32[]{:S(2)}) collective-permute-start(f32[256,128]{1,0:T(8,128)S(1)} %copy-done.4), channel_id=1, source_target_pairs={{0,2},{1,3},{2,0},{3,1},{4,6},{5,7},{6,4},{7,5},{8,10},{9,11},{10,... | collective-permute-start | bytes 393224 | tf_op jit(solution)/shard_map/ppermute | solution.py:57
  54.8 1.7 collective-permute-done.8.mirrored
  56.4 1.3 collective-permute-start
  57.8 2.2 %shard_map.126.b0 = f32[1024,256]{1,0:T(8,128)} custom-call(f32[1,336,256]{2,1,0:T(8,128)} %e1.1, f32[1,336,1024]{2,1,0:T(8,128)} %m1.3, f32[256,256]{1,0:T(8,128)} %copy-done.5, f32[256,256]{1,0:T(8,128)} %copy-done.17), custom_call_target="tpu_custom_call" | custom-call | tf_op jit(solution)/shard_map/pallas_call | solution.py:97
  60.1 2.7 %collective-permute-done.x1 = f32[256,128]{1,0:T(8,128)S(1)} collective-permute-done((f32[256,128]{1,0:T(8,128)S(1)}, f32[256,128]{1,0:T(8,128)S(1)}, u32[]{:S(2)}, u32[]{:S(2)}) %collective-permute-start) | collective-permute-done | bytes 131104 | tf_op jit(solution)/shard_map/ppermute | solution.py:57
  62.7 5.5 %shard_map.123.near = f32[1024,512]{1,0:T(8,128)S(1)} custom-call(s32[4]{0:T(128)S(1)} %pad_add_fusion.place, s32[1,5]{1,0:T(1,128)S(1)} %copy-done.15, f32[256,128]{1,0:T(8,128)S(1)} %copy-done.4, f32[256,128]{1,0:T(8,128)S(1)} %collective-permute-done.x1, f32[256,128]{1,0:T(8,128)S(1)} %collective-permute-done.1.x2, ...), custom_call_target="tpu_custom_call" | custom-call | tf_op jit(solution)/shard_map/pallas_call | solution.py:97
  68.5 1.6 collective-permute-start.5
  70.8 4.8 %shard_map.127.lead = f32[256,1024]{1,0:T(8,128)S(1)} custom-call(s32[1,1024]{1,0:T(1,128)S(1)} %copy-done.14, f32[1,1024,256]{2,1,0:T(8,128)} %basis.3, f32[1,1024,1024]{2,1,0:T(8,128)} %solve.3), custom_call_target="tpu_custom_call" | custom-call | tf_op jit(solution)/shard_map/pallas_call | solution.py:97
  75.6 8.4 %shard_map.128 = (f32[4,256,128]{2,1,0:T(8,128)S(1)}, f32[1024,128]{1,0:T(8,128)}, f32[1024,128]{1,0:T(8,128)}, f32[1024,128]{1,0:T(8,128)}, f32[1024,128]{1,0:T(8,128)}) custom-call(s32[4]{0:T(128)S(1)} %pad_add_fusion.place, s32[1,5]{1,0:T(1,128)S(1)} %copy-done.15, f32[1]{0:T(128)S(6)} %copy.13.ridge, f32[256,128]{1,0:T(8,128)S(1)} %copy-done.4, ...), custom_call_target="tpu_custom_call" | custom-call | tf_op jit(solution)/shard_map/pallas_call | solution.py:97
  84.0 0.8 copy-done.11
  84.8 4.3 %all-to-all-start = ((f32[4,256,128]{2,1,0:T(8,128)}), f32[4,256,128]{2,1,0:T(8,128)}, u32[]{:S(2)}, u32[]{:S(2)}) async-start(f32[4,256,128]{2,1,0:T(8,128)} %copy-done.11), calls=%async_computation | async-start | bytes 1048576 | tf_op jit(solution)/shard_map/all_to_all | solution.py:563
  89.2 2.6 %collective-permute-done.16.b2 = f32[1024,256]{1,0:T(8,128)} collective-permute-done((f32[1024,256]{1,0:T(8,128)S(1)}, f32[1024,256]{1,0:T(8,128)}, u32[]{:S(2)}, u32[]{:S(2)}) %collective-permute-start.16) | collective-permute-done | bytes 1048608 | tf_op jit(solution)/shard_map/ppermute | solution.py:31
  91.9 2.2 %collective-permute-start.17 = (f32[1024,256]{1,0:T(8,128)}, f32[1024,256]{1,0:T(8,128)}, u32[]{:S(2)}, u32[]{:S(2)}) collective-permute-start(f32[1024,256]{1,0:T(8,128)} %collective-permute-done.16.b2), channel_id=1, source_target_pairs={{0,4},{4,0},{8,12},{12,8},{16,20},{20,16},{24,28},{28,24},{32,36},... | collective-permute-start | bytes 3145736 | tf_op jit(solution)/shard_map/ppermute | solution.py:31
  94.1 4.7 %all-to-all-done = f32[4,256,128]{2,1,0:T(8,128)} async-done(((f32[4,256,128]{2,1,0:T(8,128)}), f32[4,256,128]{2,1,0:T(8,128)}, u32[]{:S(2)}, u32[]{:S(2)}) %all-to-all-start) | async-done | bytes 524320 | tf_op jit(solution)/shard_map/all_to_all | solution.py:563
  98.8 1.1 fusion
  99.9 8.4 %all_gather.16.stacked = f32[4,256,128]{2,1,0:T(8,128)S(1)} all-gather(f32[1,256,128]{2,1,0:T(8,128)S(1)} %fusion), channel_id=1, replica_groups={{0,4,8,12},{16,20,24,28},{32,36,40,44},{48,52,56,60},{64,68,72,76},{80,..., dimensions={0}, use_global_device_ids=true | all-gather | bytes 655360 | tf_op jit(solution)/shard_map/all_gather | solution.py:61
  108.3 2.1 %shard_map.129 = (f32[256,128]{1,0:T(8,128)S(1)}, f32[128,256]{1,0:T(8,128)}) custom-call(s32[4]{0:T(128)S(1)} %pad_add_fusion.place, s32[64]{0:T(128)S(1)} %copy-done.16, f32[4,256,128]{2,1,0:T(8,128)S(1)} %all_gather.16.stacked, f32[1,336,1024]{2,1,0:T(8,128)S(1)} %copy-done, f32[1,336,256]{2,1,0:T(8,128)S(1)} %copy-done.3), custom_call_target="tpu_custom_call" | custom-call | tf_op jit(solution)/shard_map/pallas_call | solution.py:97
  110.4 0.7 copy-done.12
  111.0 3.5 %all-to-all-start.1 = ((f32[4,32,256]{2,1,0:T(8,128)}), f32[4,32,256]{2,1,0:T(8,128)S(1)}, u32[]{:S(2)}, u32[]{:S(2)}) async-start(f32[4,32,256]{2,1,0:T(8,128)} %bitcast.4), calls=%async_computation.1 | async-start | bytes 262144 | tf_op jit(solution)/shard_map/all_to_all | solution.py:614
  114.5 0.3 collective-permute-start.9
  114.8 1.8 collective-permute-start.10
  116.5 0.7 collective-permute-start.11
  117.2 0.8 all-to-all-done.1
  118.1 1.8 collective-permute-start.14
  119.9 3.1 %collective-permute-done.14.r3 = f32[32,256]{1,0:T(8,128)S(1)} collective-permute-done((f32[32,256]{1,0:T(8,128)S(1)}, f32[32,256]{1,0:T(8,128)S(1)}, u32[]{:S(2)}, u32[]{:S(2)}) %collective-permute-start.14) | collective-permute-done | bytes 32800 | tf_op jit(solution)/shard_map/ppermute | solution.py:31
  123.0 1.7 collective-permute-start.13
  124.8 0.3 collective-permute-start.12
  125.1 2.8 %shard_map.130 = (f32[1024,256]{1,0:T(8,128)S(1)}, f32[256,1024]{1,0:T(8,128)S(1)}, f32[256,256]{1,0:T(8,128)S(1)}, f32[256,1024]{1,0:T(8,128)S(1)}, f32[256,256]{1,0:T(8,128)S(1)}) custom-call(s32[4]{0:T(128)S(1)} %pad_add_fusion.place, f32[1024,256]{1,0:T(8,128)S(1)} %copy-done.2, f32[1024,256]{1,0:T(8,128)} %collective-permute-done.15.b1, ...), custom_call_target="tpu_custom_call" | custom-call | tf_op jit(solution)/shard_map/pallas_call | solution.py:97
  127.8 1.0 copy-done.6
  129.0 0.8 shard_map.131
  129.9 1.9 collective-permute-start.20
  131.8 1.5 collective-permute-start.19
  133.3 1.8 collective-permute-done.20
  135.0 2.2 %collective-permute-start.18 = (f32[32,256]{1,0:T(8,128)S(1)}, f32[32,256]{1,0:T(8,128)S(1)}, u32[]{:S(2)}, u32[]{:S(2)}) collective-permute-start(f32[32,256]{1,0:T(8,128)S(1)} %get-tuple-element.38), channel_id=1, source_target_pairs={{0,24},{4,28},{8,16},{12,20},{16,8},{20,12},{24,0},{28,4},{32,56},... | collective-permute-start | bytes 98312 | tf_op jit(solution)/shard_map/ppermute | solution.py:31
  137.2 2.1 %collective-permute-done.18 = f32[32,256]{1,0:T(8,128)S(1)} collective-permute-done((f32[32,256]{1,0:T(8,128)S(1)}, f32[32,256]{1,0:T(8,128)S(1)}, u32[]{:S(2)}, u32[]{:S(2)}) %collective-permute-start.18) | collective-permute-done | bytes 32800 | tf_op jit(solution)/shard_map/ppermute | solution.py:31
  139.3 5.8 %collective-permute-start.23 = (f32[32,256]{1,0:T(8,128)S(1)}, f32[32,256]{1,0:T(8,128)S(1)}, u32[]{:S(2)}, u32[]{:S(2)}) collective-permute-start(f32[32,256]{1,0:T(8,128)S(1)} %add_add_fusion.r0), channel_id=1, source_target_pairs={{160,0},{164,4},{168,8},{172,12},{176,16},{180,20},{184,24},{188,2... | collective-permute-start | bytes 98312 | tf_op jit(solution)/shard_map/ppermute | solution.py:53
  145.1 0.4 collective-permute-start.22
  145.5 0.9 collective-permute-done.23.r3
  146.4 3.9 %collective-permute-start.21 = (f32[32,256]{1,0:T(8,128)S(1)}, f32[32,256]{1,0:T(8,128)S(1)}, u32[]{:S(2)}, u32[]{:S(2)}) collective-permute-start(f32[32,256]{1,0:T(8,128)S(1)} %add_add_fusion.r0), channel_id=1, source_target_pairs={{224,0},{228,4},{232,8},{236,12},{240,16},{244,20},{248,24},{252,2... | collective-permute-start | bytes 98312 | tf_op jit(solution)/shard_map/ppermute | solution.py:53
  150.4 1.7 collective-permute-done.21.r1
  152.1 0.9 shard_map.132
  153.0 11.7 %all-gather = f32[128,256]{1,0:T(8,128)S(1)} all-gather(f32[32,256]{1,0:T(8,128)S(1)} %shard_map.132), channel_id=2, replica_groups={{0,4,8,12},{24,28,16,20},{32,36,40,44},{56,60,48,52},{64,68,72,76},{88,..., dimensions={0}, use_global_device_ids=true | all-gather | bytes 163840 | tf_op jit(solution)/shard_map/all_gather | solution.py:61
  164.8 3.2 %shard_map.134 = f32[256,128]{1,0:T(8,128)S(1)} custom-call(f32[4,32,256]{2,1,0:T(8,128)S(1)} %bitcast.11, f32[1024,256]{1,0:T(8,128)} %copy-done.6, f32[1,336,1024]{2,1,0:T(8,128)} %m1.3, f32[256,128]{1,0:T(8,128)} %copy-done.12), custom_call_target="tpu_custom_call" | custom-call | tf_op jit(solution)/shard_map/pallas_call | solution.py:97
  168.0 7.3 %all-gather.1 = f32[1024,128]{1,0:T(8,128)S(1)} all-gather(f32[256,128]{1,0:T(8,128)S(1)} %shard_map.134), channel_id=3, replica_groups={{0,4,8,12},{16,20,24,28},{32,36,40,44},{48,52,56,60},{64,68,72,76},{80,..., dimensions={0}, use_global_device_ids=true | all-gather | bytes 655360 | tf_op jit(solution)/shard_map/all_gather | solution.py:61
  175.3 2.7 %shard_map.133 = (f32[1024,128]{1,0:T(8,128)}, f32[256,128]{1,0:T(8,128)}, f32[256,128]{1,0:T(8,128)}, f32[256,128]{1,0:T(8,128)}, f32[256,128]{1,0:T(8,128)}) custom-call(s32[4]{0:T(128)S(1)} %pad_add_fusion.place, s32[1,1024]{1,0:T(1,128)S(1)} %copy-done.14, f32[1024,128]{1,0:T(8,128)S(1)} %copy-done.9, f32[1024,128]{1,0:T(8,128)S(1)} %collective-permute-done.9.p1, ...), custom_call_target="tpu_custom_call" | custom-call | tf_op jit(solution)/shard_map/pallas_call | solution.py:97
  178.0 1.0 copy-done.10
  179.1 6.6 %shard_map.135 = f32[1024,128]{1,0:T(8,128)} custom-call(s32[4]{0:T(128)S(1)} %pad_add_fusion.place, s32[64]{0:T(128)S(1)} %copy-done.16, s32[1,1024]{1,0:T(1,128)S(1)} %copy-done.14, f32[4,256,128]{2,1,0:T(8,128)S(1)} %bitcast.10, f32[1024,128]{1,0:T(8,128)S(1)} %copy-done.10, f32[1,1024,256]{2,1,0:T(8,128)} %basis.3, f32[1,1024,1024]{2,1,0:T(8,128)} %solve.3), custom_call_target="tpu_custom_call" | custom-call | tf_op jit(solution)/shard_map/pallas_call | solution.py:97
  185.7 3.5 %all-to-all-start.2 = ((f32[4,256,128]{2,1,0:T(8,128)}), f32[4,256,128]{2,1,0:T(8,128)S(1)}, u32[]{:S(2)}, u32[]{:S(2)}) async-start(f32[4,256,128]{2,1,0:T(8,128)} %bitcast.8), calls=%async_computation.2 | async-start | bytes 1048576 | tf_op jit(solution)/shard_map/all_to_all | solution.py:563
  189.2 1.4 collective-permute-start.24
  190.6 2.4 %collective-permute-start.25 = (f32[256,128]{1,0:T(8,128)S(1)}, f32[256,128]{1,0:T(8,128)S(1)}, u32[]{:S(2)}, u32[]{:S(2)}) collective-permute-start(f32[256,128]{1,0:T(8,128)S(1)} %copy-done.20), channel_id=1, source_target_pairs={{0,2},{1,3},{2,0},{3,1},{4,6},{5,7},{6,4},{7,5},{8,10},{9,11},{10,... | collective-permute-start | bytes 393224 | tf_op jit(solution)/shard_map/ppermute | solution.py:57
  193.0 1.2 collective-permute-start.26
  194.2 6.9 %collective-permute-done.24.r1 = f32[256,128]{1,0:T(8,128)S(1)} collective-permute-done((f32[256,128]{1,0:T(8,128)S(1)}, f32[256,128]{1,0:T(8,128)S(1)}, u32[]{:S(2)}, u32[]{:S(2)}) %collective-permute-start.24) | collective-permute-done | bytes 131104 | tf_op jit(solution)/shard_map/ppermute | solution.py:57
  201.1 3.1 %collective-permute-done.25.r2 = f32[256,128]{1,0:T(8,128)S(1)} collective-permute-done((f32[256,128]{1,0:T(8,128)S(1)}, f32[256,128]{1,0:T(8,128)S(1)}, u32[]{:S(2)}, u32[]{:S(2)}) %collective-permute-start.25) | collective-permute-done | bytes 131104 | tf_op jit(solution)/shard_map/ppermute | solution.py:57
  204.2 1.7 outputs.1
  (63 shorter events, 0.8 us)
Async XLA Ops:
  0.6 47.1 %copy-start.4 = (f32[256,128]{1,0:T(8,128)S(1)}, f32[256,128]{1,0:T(8,128)}, u32[]{:S(2)}) copy-start(f32[256,128]{1,0:T(8,128)} %x0.3) | copy-start | bytes 393220
  21.6 41.1 %collective-permute-start.6 = (f32[256,640]{1,0:T(8,128)}, f32[256,640]{1,0:T(8,128)}, u32[]{:S(2)}, u32[]{:S(2)}) collective-permute-start(f32[256,640]{1,0:T(8,128)} %shard_map.122.p0), channel_id=1, source_target_pairs={{0,4},{4,0},{8,12},{12,8},{16,20},{20,16},{24,28},{28,24},{32,36},... | collective-permute-start | bytes 1966088 | tf_op jit(solution)/shard_map/ppermute | solution.py:31
  24.9 43.5 %collective-permute-start.4 = (f32[256,640]{1,0:T(8,128)}, f32[256,640]{1,0:T(8,128)S(1)}, u32[]{:S(2)}, u32[]{:S(2)}) collective-permute-start(f32[256,640]{1,0:T(8,128)} %shard_map.122.p0), channel_id=1, source_target_pairs={{0,248},{4,252},{8,0},{12,4},{16,8},{20,12},{24,16},{28,20},{32,24... | collective-permute-start | bytes 1966088 | tf_op jit(solution)/shard_map/ppermute | solution.py:31
  31.0 37.4 %collective-permute-start.3 = (f32[256,640]{1,0:T(8,128)}, f32[256,640]{1,0:T(8,128)S(1)}, u32[]{:S(2)}, u32[]{:S(2)}) collective-permute-start(f32[256,640]{1,0:T(8,128)} %shard_map.122.p0), channel_id=1, source_target_pairs={{0,8},{4,12},{8,16},{12,20},{16,24},{20,28},{24,32},{28,36},{32,40... | collective-permute-start | bytes 1966088 | tf_op jit(solution)/shard_map/ppermute | solution.py:31
  31.9 12.7 %copy-start.7 = (f32[128,256]{1,0:T(8,128)}, f32[128,256]{1,0:T(8,128)S(1)}, u32[]{:S(2)}) copy-start(f32[128,256]{1,0:T(8,128)S(1)} %shard_map.124.slices) | copy-start | bytes 393220
  31.9 30.9 %copy-start.15 = (s32[1,5]{1,0:T(1,128)S(1)}, s32[1,5]{1,0:T(1,128)}, u32[]{:S(2)}) copy-start(s32[1,5]{1,0:T(1,128)} %mask.3) | copy-start | bytes 64
  31.9 12.7 %collective-permute-start.7 = (f32[128,256]{1,0:T(8,128)S(1)}, f32[128,256]{1,0:T(8,128)S(1)}, u32[]{:S(2)}, u32[]{:S(2)}) collective-permute-start(f32[128,256]{1,0:T(8,128)S(1)} %shard_map.124.slices), channel_id=1, source_target_pairs={{0,32},{4,36},{8,40},{12,44},{16,48},{20,52},{24,56},{28,60},{32,0... | collective-permute-start | bytes 393224 | tf_op jit(solution)/shard_map/ppermute | solution.py:31
  44.6 0.7 copy-start.18
  46.3 11.5 %copy-start.5 = (f32[256,256]{1,0:T(8,128)}, f32[256,256]{1,0:T(8,128)S(1)}, u32[]{:S(2)}) copy-start(f32[256,256]{1,0:T(8,128)S(1)} %shard_map.125.pair) | copy-start | bytes 786436
  46.3 10.2 %collective-permute-start.8 = (f32[256,256]{1,0:T(8,128)S(1)}, f32[256,256]{1,0:T(8,128)S(1)}, u32[]{:S(2)}, u32[]{:S(2)}) collective-permute-start(f32[256,256]{1,0:T(8,128)S(1)} %shard_map.125.pair), channel_id=1, source_target_pairs={{0,24},{4,28},{8,16},{12,20},{16,8},{20,12},{24,0},{28,4},{32,56},... | collective-permute-start | bytes 786440 | tf_op jit(solution)/shard_map/ppermute | solution.py:31
  47.7 4.7 %collective-permute-start.2 = (f32[256,128]{1,0:T(8,128)S(1)}, f32[256,128]{1,0:T(8,128)S(1)}, u32[]{:S(2)}, u32[]{:S(2)}) collective-permute-start(f32[256,128]{1,0:T(8,128)S(1)} %copy-done.4), channel_id=1, source_target_pairs={{0,3},{1,0},{2,1},{3,2},{4,7},{5,4},{6,5},{7,6},{8,11},{9,8},{10,9... | collective-permute-start | bytes 393224 | tf_op jit(solution)/shard_map/ppermute | solution.py:57
  52.4 7.6 %collective-permute-start.1 = (f32[256,128]{1,0:T(8,128)S(1)}, f32[256,128]{1,0:T(8,128)S(1)}, u32[]{:S(2)}, u32[]{:S(2)}) collective-permute-start(f32[256,128]{1,0:T(8,128)S(1)} %copy-done.4), channel_id=1, source_target_pairs={{0,2},{1,3},{2,0},{3,1},{4,6},{5,7},{6,4},{7,5},{8,10},{9,11},{10,... | collective-permute-start | bytes 393224 | tf_op jit(solution)/shard_map/ppermute | solution.py:57
  56.4 1.4 copy-start.17
  56.4 6.3 %collective-permute-start = (f32[256,128]{1,0:T(8,128)S(1)}, f32[256,128]{1,0:T(8,128)S(1)}, u32[]{:S(2)}, u32[]{:S(2)}) collective-permute-start(f32[256,128]{1,0:T(8,128)S(1)} %copy-done.4), channel_id=1, source_target_pairs={{0,1},{1,2},{2,3},{3,0},{4,5},{5,6},{6,7},{7,4},{8,9},{9,10},{10,1... | collective-permute-start | bytes 393224 | tf_op jit(solution)/shard_map/ppermute | solution.py:57
  60.0 8.2 %copy-start.2 = (f32[1024,256]{1,0:T(8,128)S(1)}, f32[1024,256]{1,0:T(8,128)}, u32[]{:S(2)}) copy-start(f32[1024,256]{1,0:T(8,128)} %shard_map.126.b0) | copy-start | bytes 3145732
  60.0 10.7 %copy-start.14 = (s32[1,1024]{1,0:T(1,128)S(1)}, s32[1,1024]{1,0:T(1,128)}, u32[]{:S(2)}) copy-start(s32[1,1024]{1,0:T(1,128)} %order.5) | copy-start | bytes 12292
  68.3 23.6 %collective-permute-start.16 = (f32[1024,256]{1,0:T(8,128)S(1)}, f32[1024,256]{1,0:T(8,128)}, u32[]{:S(2)}, u32[]{:S(2)}) collective-permute-start(f32[1024,256]{1,0:T(8,128)S(1)} %copy-done.2), channel_id=1, source_target_pairs={{0,8},{4,12},{8,0},{12,4},{16,24},{20,28},{24,16},{28,20},{32,40},... | collective-permute-start | bytes 3145736 | tf_op jit(solution)/shard_map/ppermute | solution.py:31
  68.5 7.1 %collective-permute-start.5 = (f32[256,640]{1,0:T(8,128)S(1)}, f32[256,640]{1,0:T(8,128)S(1)}, u32[]{:S(2)}, u32[]{:S(2)}) collective-permute-start(f32[256,640]{1,0:T(8,128)S(1)} %broadcast_select_fusion), channel_id=1, source_target_pairs={{0,4},{4,0},{8,12},{12,8},{16,20},{20,16},{24,28},{28,24},{32,36},... | collective-permute-start | bytes 1966088 | tf_op jit(solution)/shard_map/ppermute | solution.py:31
  70.7 4.8 %copy-start.1 = (f32[256,512]{1,0:T(8,128)S(1)}, f32[256,512]{1,0:T(8,128)}, u32[]{:S(2)}) copy-start(f32[256,512]{1,0:T(8,128)} %coefs.1) | copy-start | bytes 1572868
  70.8 4.8 %copy-start.8 = (f32[256,512]{1,0:T(8,128)S(1)}, f32[256,512]{1,0:T(8,128)}, u32[]{:S(2)}) copy-start(f32[256,512]{1,0:T(8,128)} %own_y.1) | copy-start | bytes 1572868
  84.0 0.8 copy-start.11
  84.8 23.4 %copy-start = (f32[1,336,1024]{2,1,0:T(8,128)S(1)}, f32[1,336,1024]{2,1,0:T(8,128)}, u32[]{:S(2)}) copy-start(f32[1,336,1024]{2,1,0:T(8,128)} %m1.3) | copy-start | bytes 4128772
  84.8 23.4 %copy-start.3 = (f32[1,336,256]{2,1,0:T(8,128)S(1)}, f32[1,336,256]{2,1,0:T(8,128)}, u32[]{:S(2)}) copy-start(f32[1,336,256]{2,1,0:T(8,128)} %e1.1) | copy-start | bytes 1032196
  84.8 23.4 %copy-start.16 = (s32[64]{0:T(128)S(1)}, s32[64]{0:T(128)}, u32[]{:S(2)}) copy-start(s32[64]{0:T(128)} %leaf_map.3) | copy-start | bytes 772
  84.8 13.9 %all-to-all-start = ((f32[4,256,128]{2,1,0:T(8,128)}), f32[4,256,128]{2,1,0:T(8,128)}, u32[]{:S(2)}, u32[]{:S(2)}) async-start(f32[4,256,128]{2,1,0:T(8,128)} %copy-done.11), calls=%async_computation | async-start | bytes 1048576 | tf_op jit(solution)/shard_map/all_to_all | solution.py:563
  89.1 28.9 %collective-permute-start.15 = (f32[1024,256]{1,0:T(8,128)S(1)}, f32[1024,256]{1,0:T(8,128)}, u32[]{:S(2)}, u32[]{:S(2)}) collective-permute-start(f32[1024,256]{1,0:T(8,128)S(1)} %copy-done.2), channel_id=1, source_target_pairs={{0,4},{4,0},{8,12},{12,8},{16,20},{20,16},{24,28},{28,24},{32,36},... | collective-permute-start | bytes 3145736 | tf_op jit(solution)/shard_map/ppermute | solution.py:31
  91.9 32.9 %collective-permute-start.17 = (f32[1024,256]{1,0:T(8,128)}, f32[1024,256]{1,0:T(8,128)}, u32[]{:S(2)}, u32[]{:S(2)}) collective-permute-start(f32[1024,256]{1,0:T(8,128)} %collective-permute-done.16.b2), channel_id=1, source_target_pairs={{0,4},{4,0},{8,12},{12,8},{16,20},{20,16},{24,28},{28,24},{32,36},... | collective-permute-start | bytes 3145736 | tf_op jit(solution)/shard_map/ppermute | solution.py:31
  110.4 0.7 copy-start.12
  111.0 7.0 %all-to-all-start.1 = ((f32[4,32,256]{2,1,0:T(8,128)}), f32[4,32,256]{2,1,0:T(8,128)S(1)}, u32[]{:S(2)}, u32[]{:S(2)}) async-start(f32[4,32,256]{2,1,0:T(8,128)} %bitcast.4), calls=%async_computation.1 | async-start | bytes 262144 | tf_op jit(solution)/shard_map/all_to_all | solution.py:614
  114.5 38.5 %collective-permute-start.9 = (f32[1024,128]{1,0:T(8,128)}, f32[1024,128]{1,0:T(8,128)S(1)}, u32[]{:S(2)}, u32[]{:S(2)}) collective-permute-start(f32[1024,128]{1,0:T(8,128)} %get-tuple-element.30), channel_id=1, source_target_pairs={{0,1},{1,2},{2,3},{3,0},{4,5},{5,6},{6,7},{7,4},{8,9},{9,10},{10,1... | collective-permute-start | bytes 1572872 | tf_op jit(solution)/shard_map/ppermute | solution.py:57
  114.8 38.3 %collective-permute-start.10 = (f32[1024,128]{1,0:T(8,128)}, f32[1024,128]{1,0:T(8,128)S(1)}, u32[]{:S(2)}, u32[]{:S(2)}) collective-permute-start(f32[1024,128]{1,0:T(8,128)} %get-tuple-element.31), channel_id=1, source_target_pairs={{0,2},{1,3},{2,0},{3,1},{4,6},{5,7},{6,4},{7,5},{8,10},{9,11},{10,... | collective-permute-start | bytes 1572872 | tf_op jit(solution)/shard_map/ppermute | solution.py:57
  116.5 36.5 %collective-permute-start.11 = (f32[1024,128]{1,0:T(8,128)}, f32[1024,128]{1,0:T(8,128)S(1)}, u32[]{:S(2)}, u32[]{:S(2)}) collective-permute-start(f32[1024,128]{1,0:T(8,128)} %get-tuple-element.32), channel_id=1, source_target_pairs={{0,3},{1,0},{2,1},{3,2},{4,7},{5,4},{6,5},{7,6},{8,11},{9,8},{10,9... | collective-permute-start | bytes 1572872 | tf_op jit(solution)/shard_map/ppermute | solution.py:57
  118.1 5.0 %collective-permute-start.14 = (f32[32,256]{1,0:T(8,128)S(1)}, f32[32,256]{1,0:T(8,128)S(1)}, u32[]{:S(2)}, u32[]{:S(2)}) collective-permute-start(f32[32,256]{1,0:T(8,128)S(1)} %fusion.2.r0), channel_id=1, source_target_pairs={{0,56},{4,60},{8,48},{12,52},{16,40},{20,44},{24,32},{28,36},{32,2... | collective-permute-start | bytes 98312 | tf_op jit(solution)/shard_map/ppermute | solution.py:31
  123.0 5.8 %collective-permute-start.13 = (f32[32,256]{1,0:T(8,128)S(1)}, f32[32,256]{1,0:T(8,128)S(1)}, u32[]{:S(2)}, u32[]{:S(2)}) collective-permute-start(f32[32,256]{1,0:T(8,128)S(1)} %fusion.2.r0), channel_id=1, source_target_pairs={{0,32},{4,36},{8,40},{12,44},{16,48},{20,52},{24,56},{28,60},{32,0... | collective-permute-start | bytes 98312 | tf_op jit(solution)/shard_map/ppermute | solution.py:31
  124.8 4.3 %collective-permute-start.12 = (f32[32,256]{1,0:T(8,128)S(1)}, f32[32,256]{1,0:T(8,128)S(1)}, u32[]{:S(2)}, u32[]{:S(2)}) collective-permute-start(f32[32,256]{1,0:T(8,128)S(1)} %fusion.2.r0), channel_id=1, source_target_pairs={{0,24},{4,28},{8,16},{12,20},{16,8},{20,12},{24,0},{28,4},{32,56},... | collective-permute-start | bytes 98312 | tf_op jit(solution)/shard_map/ppermute | solution.py:31
  127.8 1.0 copy-start.6
  129.9 5.2 %collective-permute-start.20 = (f32[32,256]{1,0:T(8,128)S(1)}, f32[32,256]{1,0:T(8,128)S(1)}, u32[]{:S(2)}, u32[]{:S(2)}) collective-permute-start(f32[32,256]{1,0:T(8,128)S(1)} %get-tuple-element.38), channel_id=1, source_target_pairs={{0,56},{4,60},{8,48},{12,52},{16,40},{20,44},{24,32},{28,36},{32,2... | collective-permute-start | bytes 98312 | tf_op jit(solution)/shard_map/ppermute | solution.py:31
  131.8 5.4 %collective-permute-start.19 = (f32[32,256]{1,0:T(8,128)S(1)}, f32[32,256]{1,0:T(8,128)S(1)}, u32[]{:S(2)}, u32[]{:S(2)}) collective-permute-start(f32[32,256]{1,0:T(8,128)S(1)} %get-tuple-element.38), channel_id=1, source_target_pairs={{0,32},{4,36},{8,40},{12,44},{16,48},{20,52},{24,56},{28,60},{32,0... | collective-permute-start | bytes 98312 | tf_op jit(solution)/shard_map/ppermute | solution.py:31
  135.0 4.3 %collective-permute-start.18 = (f32[32,256]{1,0:T(8,128)S(1)}, f32[32,256]{1,0:T(8,128)S(1)}, u32[]{:S(2)}, u32[]{:S(2)}) collective-permute-start(f32[32,256]{1,0:T(8,128)S(1)} %get-tuple-element.38), channel_id=1, source_target_pairs={{0,24},{4,28},{8,16},{12,20},{16,8},{20,12},{24,0},{28,4},{32,56},... | collective-permute-start | bytes 98312 | tf_op jit(solution)/shard_map/ppermute | solution.py:31
  139.3 7.1 %collective-permute-start.23 = (f32[32,256]{1,0:T(8,128)S(1)}, f32[32,256]{1,0:T(8,128)S(1)}, u32[]{:S(2)}, u32[]{:S(2)}) collective-permute-start(f32[32,256]{1,0:T(8,128)S(1)} %add_add_fusion.r0), channel_id=1, source_target_pairs={{160,0},{164,4},{168,8},{172,12},{176,16},{180,20},{184,24},{188,2... | collective-permute-start | bytes 98312 | tf_op jit(solution)/shard_map/ppermute | solution.py:53
  145.1 5.2 %collective-permute-start.22 = (f32[32,256]{1,0:T(8,128)S(1)}, f32[32,256]{1,0:T(8,128)S(1)}, u32[]{:S(2)}, u32[]{:S(2)}) collective-permute-start(f32[32,256]{1,0:T(8,128)S(1)} %add_add_fusion.r0), channel_id=1, source_target_pairs={{64,0},{68,4},{72,8},{76,12},{80,16},{84,20},{88,24},{92,28},{224,... | collective-permute-start | bytes 98312 | tf_op jit(solution)/shard_map/ppermute | solution.py:53
  146.4 5.6 %collective-permute-start.21 = (f32[32,256]{1,0:T(8,128)S(1)}, f32[32,256]{1,0:T(8,128)S(1)}, u32[]{:S(2)}, u32[]{:S(2)}) collective-permute-start(f32[32,256]{1,0:T(8,128)S(1)} %add_add_fusion.r0), channel_id=1, source_target_pairs={{224,0},{228,4},{232,8},{236,12},{240,16},{244,20},{248,24},{252,2... | collective-permute-start | bytes 98312 | tf_op jit(solution)/shard_map/ppermute | solution.py:53
  153.0 22.3 %copy-start.9 = (f32[1024,128]{1,0:T(8,128)S(1)}, f32[1024,128]{1,0:T(8,128)}, u32[]{:S(2)}) copy-start(f32[1024,128]{1,0:T(8,128)} %get-tuple-element.42.p0) | copy-start | bytes 1572868
  178.0 1.0 copy-start.10
  179.1 10.1 %copy-start.21 = (f32[256,128]{1,0:T(8,128)S(1)}, f32[256,128]{1,0:T(8,128)}, u32[]{:S(2)}) copy-start(f32[256,128]{1,0:T(8,128)} %get-tuple-element.47) | copy-start | bytes 393220
  179.1 11.5 %copy-start.20 = (f32[256,128]{1,0:T(8,128)S(1)}, f32[256,128]{1,0:T(8,128)}, u32[]{:S(2)}) copy-start(f32[256,128]{1,0:T(8,128)} %get-tuple-element.48) | copy-start | bytes 393220
  179.1 13.9 %copy-start.19 = (f32[256,128]{1,0:T(8,128)S(1)}, f32[256,128]{1,0:T(8,128)}, u32[]{:S(2)}) copy-start(f32[256,128]{1,0:T(8,128)} %get-tuple-element.49) | copy-start | bytes 393220
  179.1 25.2 %copy-start.13 = (f32[256,128]{1,0:T(8,128)S(1)}, f32[256,128]{1,0:T(8,128)}, u32[]{:S(2)}) copy-start(f32[256,128]{1,0:T(8,128)} %get-tuple-element.46.r0) | copy-start | bytes 393220
  185.7 18.5 %all-to-all-start.2 = ((f32[4,256,128]{2,1,0:T(8,128)}), f32[4,256,128]{2,1,0:T(8,128)S(1)}, u32[]{:S(2)}, u32[]{:S(2)}) async-start(f32[4,256,128]{2,1,0:T(8,128)} %bitcast.8), calls=%async_computation.2 | async-start | bytes 1048576 | tf_op jit(solution)/shard_map/all_to_all | solution.py:563
  189.2 11.9 %collective-permute-start.24 = (f32[256,128]{1,0:T(8,128)S(1)}, f32[256,128]{1,0:T(8,128)S(1)}, u32[]{:S(2)}, u32[]{:S(2)}) collective-permute-start(f32[256,128]{1,0:T(8,128)S(1)} %copy-done.21), channel_id=1, source_target_pairs={{0,1},{1,2},{2,3},{3,0},{4,5},{5,6},{6,7},{7,4},{8,9},{9,10},{10,1... | collective-permute-start | bytes 393224 | tf_op jit(solution)/shard_map/ppermute | solution.py:57
  190.6 13.6 %collective-permute-start.25 = (f32[256,128]{1,0:T(8,128)S(1)}, f32[256,128]{1,0:T(8,128)S(1)}, u32[]{:S(2)}, u32[]{:S(2)}) collective-permute-start(f32[256,128]{1,0:T(8,128)S(1)} %copy-done.20), channel_id=1, source_target_pairs={{0,2},{1,3},{2,0},{3,1},{4,6},{5,7},{6,4},{7,5},{8,10},{9,11},{10,... | collective-permute-start | bytes 393224 | tf_op jit(solution)/shard_map/ppermute | solution.py:57
  193.0 11.2 %collective-permute-start.26 = (f32[256,128]{1,0:T(8,128)S(1)}, f32[256,128]{1,0:T(8,128)S(1)}, u32[]{:S(2)}, u32[]{:S(2)}) collective-permute-start(f32[256,128]{1,0:T(8,128)S(1)} %copy-done.19), channel_id=1, source_target_pairs={{0,3},{1,0},{2,1},{3,2},{4,7},{5,4},{6,5},{7,6},{8,11},{9,8},{10,9... | collective-permute-start | bytes 393224 | tf_op jit(solution)/shard_map/ppermute | solution.py:57

commit v4 on v3

--- a/solution.py
+++ b/solution.py
@@ -118,19 +118,25 @@
     return jnp.concatenate([top, low], axis=1), top.astype(F32) + low.astype(F32)
 
 
-def tile_setup(place, xs, blocks, rows, norms, squares, others, tops, lows):
-    for k, ref in enumerate(xs):
-        at = (place[2] + 4 - k) % 4
-        rows[at], exact = two_part(ref[...])
-        norms[at] = jnp.sum(exact * exact, axis=1, keepdims=True)
+def tile_setup(place, xs, blocks, loaded, arrived, rows, norms, squares, others, tops, lows):
+    copies = [
+        pltpu.make_async_copy(ref, loaded.at[k], arrived.at[k]) for k, ref in enumerate(xs)
+    ]
+    for copy in copies:
+        copy.start()
     for k, (y, a) in enumerate(blocks):
         others[k], exact = two_part(y)
         total = jnp.sum(exact * exact, axis=1, keepdims=True)
         squares[k] = jnp.transpose(jnp.broadcast_to(total, (Q, 128)))[:8]
         tops[k], lows[k] = split(a)
-
-
-def tile_sum(i, weights, rows, norms, squares, others, tops, lows):
+    for k, copy in enumerate(copies):
+        copy.wait()
+        at = (place[2] + 4 - k) % 4
+        rows[at], exact = two_part(loaded[k])
+        norms[at] = jnp.sum(exact * exact, axis=1, keepdims=True)
+
+
+def tile_sum(i, weights, loaded, arrived, rows, norms, squares, others, tops, lows):
     x = rows[pl.ds(2 * i, 2)].reshape(CHUNK, 256)
     own = norms[pl.ds(2 * i, 2)].reshape(CHUNK, 1)
     total = None
@@ -145,7 +151,7 @@
     return total
 
 
-def near_kernel(place, mask, x0, x1, x2, x3, p0, p1, out, *scratch):
+def near_kernel(place, mask, p0, p1, x0, x1, x2, x3, out, *scratch):
     blocks = [(p[:, :128], p[:, 128:]) for p in (p0, p1)]
     tile_setup(place, (x0, x1, x2, x3), blocks, *scratch)
     weights = (mask[0, 2].astype(F32), mask[0, 3 - 2 * place[0]].astype(F32))
@@ -156,7 +162,7 @@
 
 
 def far_kernel(
-    place, mask, ridge, x0, x1, x2, x3, p0, p1, p2, near, own_y, own_a, lead,
+    place, mask, ridge, p0, p1, p2, near, own_y, own_a, lead, x0, x1, x2, x3,
     led, out0, out1, out2, out3, parts, sems, *scratch
 ):
     blocks = [(p[:, :128], p[:, 128:]) for p in (p0, p1, p2)]
@@ -204,6 +210,8 @@
 
 def tile_scratch(count):
     return [
+        pltpu.VMEM((4, Q, 128), F32),
+        pltpu.SemaphoreType.DMA((4,)),
         pltpu.VMEM((4, Q, 256), BF16),
         pltpu.VMEM((4, Q, 1), F32),
         pltpu.VMEM((count, 8, Q), F32),
@@ -214,19 +222,18 @@
 
 
 def near_call(place, mask, xs, blocks):
-    return kernel(
-        near_kernel, [(1024, 512)], [*xs, *blocks], (place, mask), tile_scratch(2)
-    )
+    return kernel(near_kernel, [(1024, 512)], blocks, (place, mask), tile_scratch(2), xs)
 
 
 def far_call(place, mask, ridge, xs, blocks, near, own_y, own_a, lead):
     return kernel(
         far_kernel,
         [(4, RANK, 128)],
-        [*xs, *blocks, near, own_y, own_a, lead],
+        [*blocks, near, own_y, own_a, lead],
         (place, mask, ridge),
         [pltpu.VMEM((2, 4, CHUNK, 128), F32), pltpu.SemaphoreType.DMA((2, 4))] + tile_scratch(3),
-        far_outs=[(1024, 128)] * 4,
+        xs,
+        [(1024, 128)] * 4,
     )
 
 
@@ -321,8 +328,9 @@
     run_copies(sems, slice_moves(transfer, inverse, out, 0))
 
 
-def pair_kernel(slices, lower, out, sems):
-    run_copies(sems, [(slices, out.at[pl.ds(0, 128), :]), (lower, out.at[pl.ds(128, 128), :])])
+def pair_kernel(slices, lower, out):
+    out[:128, :] = slices[...]
+    out[128:, :] = lower[...]
 
 
 def held_kernel(transfer, inverse, pair, mirrored, out, buffer, sems):
@@ -590,7 +598,7 @@
     nodes = (node_transfer, node_inverse)
     slices = mover(slices_kernel, (128, 256), 5, *nodes)
     lower = leaf_route(slices, lambda i: facing(i, 0, 1))
-    pair = mover(pair_kernel, (256, 256), 2, slices, lower)
+    pair = kernel(pair_kernel, [(256, 256)], [slices, lower])
     mirrored = leaf_route(pair, lambda i: facing(i, 1, 0))
     held = held_call(*nodes, pair, mirrored)
 
@@ -605,7 +613,7 @@
         place, tile_mask, ridge, xs, (left, right, relay), near, targets, coefs, lead
     )
     led = swap_cols(led)
-    reduced = led[0] + led[1] + (led[2] + led[3])
+    reduced = led.sum(0)
     e1, m2, f2, m3, e2 = nodes_call(place, (held, own_core, across, both_ways))
 
     columns = [partial[0]] + [col_shift(partial[d], d) for d in (1, 2, 3)]

time: 206 us -> 225 us (1.092)
  waiting for transfers between devices: 46.9 us -> 63.6 us
  blocking collectives: 27.4 us -> 39.1 us
  starting transfers between devices: 59.8 us -> 49.6 us
    ppermute x15, waiting for transfers between devices: 24.1 us -> 45.9 us  [leaf_route(): return lax.ppermute(value, 'leaf', [(i, target(i)) for i in range(LEAVES)])]
    all_to_all x0 -> x1, blocking collectives: none -> 12.1 us  [swap_cols(): return lax.all_to_all(value, 'col', 0, 0, tiled=True)]
    all_to_all x2 -> x1, waiting for transfers between devices: 4.71 us -> 0.01 us  [swap_cols(): return lax.all_to_all(value, 'col', 0, 0, tiled=True)]
    ppermute x15, starting transfers between devices: 24.3 us -> 20 us  [leaf_route(): return lax.ppermute(value, 'leaf', [(i, target(i)) for i in range(LEAVES)])]
    all_to_all x2 -> x1, starting transfers between devices: 7.77 us -> 3.48 us  [swap_cols(): return lax.all_to_all(value, 'col', 0, 0, tiled=True)]
    pallas_call x11 -> x12, Pallas kernels: 40 us -> 42.2 us  [kernel(): pl.pallas_call(body, in_specs=[SMEM] * len(scalars) + [VMEM] * len(values...]
    pallas_call x3 -> x2, Pallas kernels: 22.8 us -> 21.9 us  [mover(): pl.pallas_call(body, in_specs=[HBM] * len(parts), out_specs=HBM, out_shap...]
  transfers between devices with their start and end apart: 30 -> 29, of which waited for: 15 -> 13; matrix products, arithmetic and copies ran while one was open for 1% -> 1% of each run, Pallas kernels for 14% -> 14%
where the time goes in v4:
time: 225 us
  Pallas kernels  65.7 us (29%)
  waiting for transfers between devices  63.6 us (28%)
  starting transfers between devices  49.6 us (22%)
  blocking collectives  39.1 us (17%)
  local copies, waits for them, and re-layouts  3.69 us (2%)
    ppermute x15, waiting for transfers between devices, leaf_route(): return lax.ppermute(value, 'leaf', [(i, target(i)) for i in range(LEAVES)])  45.9 us
    pallas_call x12, Pallas kernels, kernel(): pl.pallas_call(body, in_specs=[SMEM] * len(scalars) + [VMEM] * len(values...  42.2 us
    all_gather x3, blocking collectives, gather4(): return lax.all_gather(value, 'leaf', axis=0, axis_index_groups=groups)  26.9 us
    pallas_call x2, Pallas kernels, mover(): pl.pallas_call(body, in_specs=[HBM] * len(parts), out_specs=HBM, out_shap...  21.9 us
    ppermute x15, starting transfers between devices, leaf_route(): return lax.ppermute(value, 'leaf', [(i, target(i)) for i in range(LEAVES)])  20 us
    ppermute x9, starting transfers between devices, col_shift(): return lax.ppermute(value, 'col', [(i, (i + step) % 4) for i in range(4)])  14.2 us
    ppermute x9, waiting for transfers between devices, col_shift(): return lax.ppermute(value, 'col', [(i, (i + step) % 4) for i in range(4)])  13.8 us
    all_to_all x1, blocking collectives, swap_cols(): return lax.all_to_all(value, 'col', 0, 0, tiled=True)  12.1 us
  transfers between devices with their start and end apart: 29, of which 13 were waited for; matrix products, arithmetic and copies ran while one was open for 1% of the time, Pallas kernels for 14%

profile of v4, /device:TPU:1, one launch (start us, length us, event | category | flops | bytes accessed | tf_op | source)
XLA Modules:
  0.0 224.6 jit_solution(1881840194998183423)
XLA Ops:
  0.6 21.0 %shard_map.122.p0 = f32[256,640]{1,0:T(8,128)} custom-call(f32[256,128]{1,0:T(8,128)} %x0.3, f32[256,512]{1,0:T(8,128)} %coefs.1), custom_call_target="tpu_custom_call" | custom-call | tf_op jit(solution)/shard_map/pallas_call | solution.py:305
  21.6 3.3 %collective-permute-start.3 = (f32[256,640]{1,0:T(8,128)}, f32[256,640]{1,0:T(8,128)S(1)}, u32[]{:S(2)}, u32[]{:S(2)}) collective-permute-start(f32[256,640]{1,0:T(8,128)} %shard_map.122.p0), channel_id=1, source_target_pairs={{0,4},{4,0},{8,12},{12,8},{16,20},{20,16},{24,28},{28,24},{32,36},... | collective-permute-start | bytes 1966088 | tf_op jit(solution)/shard_map/ppermute | solution.py:31
  24.9 0.9 shard_map.124.slices
  25.8 0.1 collective-permute-start.7
  25.9 6.8 %collective-permute-start.1 = (f32[256,640]{1,0:T(8,128)}, f32[256,640]{1,0:T(8,128)S(1)}, u32[]{:S(2)}, u32[]{:S(2)}) collective-permute-start(f32[256,640]{1,0:T(8,128)} %shard_map.122.p0), channel_id=1, source_target_pairs={{0,248},{4,252},{8,0},{12,4},{16,8},{20,12},{24,16},{28,20},{32,24... | collective-permute-start | bytes 1966088 | tf_op jit(solution)/shard_map/ppermute | solution.py:31
  32.7 0.1 collective-permute-start.8
  32.8 2.8 %collective-permute-start.6 = (f32[256,128]{1,0:T(8,128)S(1)}, f32[256,128]{1,0:T(8,128)S(1)}, u32[]{:S(2)}, u32[]{:S(2)}) collective-permute-start(f32[256,128]{1,0:T(8,128)S(1)} %copy-done.15), channel_id=1, source_target_pairs={{0,3},{1,0},{2,1},{3,2},{4,7},{5,4},{6,5},{7,6},{8,11},{9,8},{10,9... | collective-permute-start | bytes 393224 | tf_op jit(solution)/shard_map/ppermute | solution.py:57
  35.7 2.3 %collective-permute-done.6.x3 = f32[256,128]{1,0:T(8,128)S(1)} collective-permute-done((f32[256,128]{1,0:T(8,128)S(1)}, f32[256,128]{1,0:T(8,128)S(1)}, u32[]{:S(2)}, u32[]{:S(2)}) %collective-permute-start.6) | collective-permute-done | bytes 131104 | tf_op jit(solution)/shard_map/ppermute | solution.py:57
  37.9 2.4 %collective-permute-start.5 = (f32[256,128]{1,0:T(8,128)S(1)}, f32[256,128]{1,0:T(8,128)S(1)}, u32[]{:S(2)}, u32[]{:S(2)}) collective-permute-start(f32[256,128]{1,0:T(8,128)S(1)} %copy-done.15), channel_id=1, source_target_pairs={{0,2},{1,3},{2,0},{3,1},{4,6},{5,7},{6,4},{7,5},{8,10},{9,11},{10,... | collective-permute-start | bytes 393224 | tf_op jit(solution)/shard_map/ppermute | solution.py:57
  40.3 15.0 %collective-permute-done.8.mirrored = f32[256,256]{1,0:T(8,128)S(1)} collective-permute-done((f32[256,256]{1,0:T(8,128)S(1)}, f32[256,256]{1,0:T(8,128)S(1)}, u32[]{:S(2)}, u32[]{:S(2)}) %collective-permute-start.8) | collective-permute-done | bytes 262176 | tf_op jit(solution)/shard_map/ppermute | solution.py:31
  55.4 1.3 collective-permute-start.4
  56.7 0.1 pad_add_fusion.place
  56.7 2.2 shard_map.126.b0
  59.0 1.5 collective-permute-done.4.x1
  60.5 0.6 copy-done.18
  61.1 0.8 copy-done.5
  61.9 1.1 copy-done.6
  63.0 6.2 %shard_map.123.near = f32[1024,512]{1,0:T(8,128)S(1)} custom-call(s32[4]{0:T(128)S(1)} %pad_add_fusion.place, s32[1,5]{1,0:T(1,128)S(1)} %copy-done.13, f32[256,640]{1,0:T(8,128)} %shard_map.122.p0, f32[256,640]{1,0:T(8,128)S(1)} %copy-done.6, f32[256,128]{1,0:T(8,128)} %x0.3, f32[256,128]{1,0:T(8,128)} %copy-done.18, f32[256,128]{1,0:T(8,128)} %copy-done.17, ...), custom_call_target="tpu_custom_call" | custom-call | tf_op jit(solution)/shard_map/pallas_call | solution.py:97
  69.2 0.1 collective-permute-start.16
  69.4 1.2 broadcast_select_fusion
  70.5 1.5 collective-permute-start.2
  72.1 0.1 collective-permute-start.15
  72.2 19.7 %collective-permute-done.16.b2 = f32[1024,256]{1,0:T(8,128)} collective-permute-done((f32[1024,256]{1,0:T(8,128)}, f32[1024,256]{1,0:T(8,128)}, u32[]{:S(2)}, u32[]{:S(2)}) %collective-permute-start.16) | collective-permute-done | bytes 1048608 | tf_op jit(solution)/shard_map/ppermute | solution.py:31
  91.8 3.4 %collective-permute-start.17 = (f32[1024,256]{1,0:T(8,128)}, f32[1024,256]{1,0:T(8,128)}, u32[]{:S(2)}, u32[]{:S(2)}) collective-permute-start(f32[1024,256]{1,0:T(8,128)} %collective-permute-done.16.b2), channel_id=1, source_target_pairs={{0,4},{4,0},{8,12},{12,8},{16,20},{20,16},{24,28},{28,24},{32,36},... | collective-permute-start | bytes 3145736 | tf_op jit(solution)/shard_map/ppermute | solution.py:31
  95.9 4.8 %shard_map.127.lead = f32[256,1024]{1,0:T(8,128)S(1)} custom-call(s32[1,1024]{1,0:T(1,128)S(1)} %copy-done.12, f32[1,1024,256]{2,1,0:T(8,128)} %basis.3, f32[1,1024,1024]{2,1,0:T(8,128)} %solve.3), custom_call_target="tpu_custom_call" | custom-call | tf_op jit(solution)/shard_map/pallas_call | solution.py:97
  100.7 9.5 %shard_map.128 = (f32[4,256,128]{2,1,0:T(8,128)S(1)}, f32[1024,128]{1,0:T(8,128)}, f32[1024,128]{1,0:T(8,128)}, f32[1024,128]{1,0:T(8,128)}, f32[1024,128]{1,0:T(8,128)}) custom-call(s32[4]{0:T(128)S(1)} %pad_add_fusion.place, s32[1,5]{1,0:T(1,128)S(1)} %copy-done.13, f32[1]{0:T(128)S(6)} %copy.13.ridge, f32[256,640]{1,0:T(8,128)} %collective-permute-done.p0, ...), custom_call_target="tpu_custom_call" | custom-call | tf_op jit(solution)/shard_map/pallas_call | solution.py:97
  110.3 12.1 %all_to_all.19 = f32[4,256,128]{2,1,0:T(8,128)S(1)} all-to-all(f32[4,256,128]{2,1,0:T(8,128)S(1)} %get-tuple-element.33), channel_id=1, replica_groups=mesh['leaf'=64,'col'=4] {'col'}, dimensions={0} | all-to-all | bytes 1048576 | tf_op jit(solution)/shard_map/all_to_all | solution.py:571
  122.5 7.6 %all-gather = f32[1024,128]{1,0:T(8,128)S(1)} all-gather(f32[256,128]{1,0:T(8,128)S(1)} %reduce_sum.9), channel_id=2, replica_groups={{0,4,8,12},{16,20,24,28},{32,36,40,44},{48,52,56,60},{64,68,72,76},{80,..., dimensions={0}, use_global_device_ids=true | all-gather | bytes 655360 | tf_op jit(solution)/shard_map/all_gather | solution.py:61
  130.1 2.1 shard_map.129
  132.2 3.4 %all-to-all-start.1 = ((f32[4,32,256]{2,1,0:T(8,128)}), f32[4,32,256]{2,1,0:T(8,128)S(1)}, u32[]{:S(2)}, u32[]{:S(2)}) async-start(f32[4,32,256]{2,1,0:T(8,128)} %bitcast.5), calls=%async_computation.1 | async-start | bytes 262144 | tf_op jit(solution)/shard_map/all_to_all | solution.py:622
  135.6 0.3 collective-permute-start.9
  135.9 1.8 collective-permute-start.10
  137.7 0.7 collective-permute-start.11
  138.4 0.8 all-to-all-done.1
  139.2 0.1 collective-permute-start.14
  139.3 4.9 %collective-permute-done.14.r3 = f32[32,256]{1,0:T(8,128)S(1)} collective-permute-done((f32[32,256]{1,0:T(8,128)S(1)}, f32[32,256]{1,0:T(8,128)S(1)}, u32[]{:S(2)}, u32[]{:S(2)}) %collective-permute-start.14) | collective-permute-done | bytes 32800 | tf_op jit(solution)/shard_map/ppermute | solution.py:31
  144.2 0.3 collective-permute-start.12
  144.5 3.1 %shard_map.130 = (f32[1024,256]{1,0:T(8,128)S(1)}, f32[256,1024]{1,0:T(8,128)S(1)}, f32[256,256]{1,0:T(8,128)S(1)}, f32[256,1024]{1,0:T(8,128)S(1)}, f32[256,256]{1,0:T(8,128)S(1)}) custom-call(s32[4]{0:T(128)S(1)} %pad_add_fusion.place, f32[1024,256]{1,0:T(8,128)} %shard_map.126.b0, f32[1024,256]{1,0:T(8,128)} %collective-permute-done.15.b1, ...), custom_call_target="tpu_custom_call" | custom-call | tf_op jit(solution)/shard_map/pallas_call | solution.py:97
  147.6 1.1 collective-permute-done.12.r1
  148.8 0.8 shard_map.131
  149.6 2.4 %collective-permute-start.20 = (f32[32,256]{1,0:T(8,128)S(1)}, f32[32,256]{1,0:T(8,128)S(1)}, u32[]{:S(2)}, u32[]{:S(2)}) collective-permute-start(f32[32,256]{1,0:T(8,128)S(1)} %get-tuple-element.38), channel_id=1, source_target_pairs={{0,56},{4,60},{8,48},{12,52},{16,40},{20,44},{24,32},{28,36},{32,2... | collective-permute-start | bytes 98312 | tf_op jit(solution)/shard_map/ppermute | solution.py:31
  152.0 0.3 collective-permute-start.19
  152.3 2.5 %collective-permute-done.20 = f32[32,256]{1,0:T(8,128)S(1)} collective-permute-done((f32[32,256]{1,0:T(8,128)S(1)}, f32[32,256]{1,0:T(8,128)S(1)}, u32[]{:S(2)}, u32[]{:S(2)}) %collective-permute-start.20) | collective-permute-done | bytes 32800 | tf_op jit(solution)/shard_map/ppermute | solution.py:31
  154.8 1.5 collective-permute-start.18
  156.3 2.7 %collective-permute-done.18 = f32[32,256]{1,0:T(8,128)S(1)} collective-permute-done((f32[32,256]{1,0:T(8,128)S(1)}, f32[32,256]{1,0:T(8,128)S(1)}, u32[]{:S(2)}, u32[]{:S(2)}) %collective-permute-start.18) | collective-permute-done | bytes 32800 | tf_op jit(solution)/shard_map/ppermute | solution.py:31
  159.1 4.5 %collective-permute-start.23 = (f32[32,256]{1,0:T(8,128)S(1)}, f32[32,256]{1,0:T(8,128)S(1)}, u32[]{:S(2)}, u32[]{:S(2)}) collective-permute-start(f32[32,256]{1,0:T(8,128)S(1)} %add_add_fusion.r0), channel_id=1, source_target_pairs={{160,0},{164,4},{168,8},{172,12},{176,16},{180,20},{184,24},{188,2... | collective-permute-start | bytes 98312 | tf_op jit(solution)/shard_map/ppermute | solution.py:53
  163.5 0.2 collective-permute-start.22
  163.7 1.2 collective-permute-done.23.r3
  165.0 3.8 %collective-permute-start.21 = (f32[32,256]{1,0:T(8,128)S(1)}, f32[32,256]{1,0:T(8,128)S(1)}, u32[]{:S(2)}, u32[]{:S(2)}) collective-permute-start(f32[32,256]{1,0:T(8,128)S(1)} %add_add_fusion.r0), channel_id=1, source_target_pairs={{224,0},{228,4},{232,8},{236,12},{240,16},{244,20},{248,24},{252,2... | collective-permute-start | bytes 98312 | tf_op jit(solution)/shard_map/ppermute | solution.py:53
  168.7 1.8 collective-permute-done.21.r1
  170.5 0.9 shard_map.132
  171.5 12.0 %all-gather.1 = f32[128,256]{1,0:T(8,128)S(1)} all-gather(f32[32,256]{1,0:T(8,128)S(1)} %shard_map.132), channel_id=3, replica_groups={{0,4,8,12},{24,28,16,20},{32,36,40,44},{56,60,48,52},{64,68,72,76},{88,..., dimensions={0}, use_global_device_ids=true | all-gather | bytes 163840 | tf_op jit(solution)/shard_map/all_gather | solution.py:61
  183.5 3.2 %shard_map.134 = f32[256,128]{1,0:T(8,128)S(1)} custom-call(f32[4,32,256]{2,1,0:T(8,128)S(1)} %bitcast.13, f32[1024,256]{1,0:T(8,128)} %copy-done.4, f32[1,336,1024]{2,1,0:T(8,128)} %m1.3, f32[256,128]{1,0:T(8,128)} %copy-done.10), custom_call_target="tpu_custom_call" | custom-call | tf_op jit(solution)/shard_map/pallas_call | solution.py:97
  186.7 7.3 %all-gather.2 = f32[1024,128]{1,0:T(8,128)S(1)} all-gather(f32[256,128]{1,0:T(8,128)S(1)} %shard_map.134), channel_id=4, replica_groups={{0,4,8,12},{16,20,24,28},{32,36,40,44},{48,52,56,60},{64,68,72,76},{80,..., dimensions={0}, use_global_device_ids=true | all-gather | bytes 655360 | tf_op jit(solution)/shard_map/all_gather | solution.py:61
  194.0 2.8 %shard_map.133 = (f32[1024,128]{1,0:T(8,128)}, f32[256,128]{1,0:T(8,128)}, f32[256,128]{1,0:T(8,128)}, f32[256,128]{1,0:T(8,128)}, f32[256,128]{1,0:T(8,128)}) custom-call(s32[4]{0:T(128)S(1)} %pad_add_fusion.place, s32[1,1024]{1,0:T(1,128)S(1)} %copy-done.12, f32[1024,128]{1,0:T(8,128)S(1)} %copy-done.8, f32[1024,128]{1,0:T(8,128)S(1)} %collective-permute-done.9.p1, ...), custom_call_target="tpu_custom_call" | custom-call | tf_op jit(solution)/shard_map/pallas_call | solution.py:97
  196.8 1.0 copy-done.9
  197.8 6.6 %shard_map.135 = f32[1024,128]{1,0:T(8,128)} custom-call(s32[4]{0:T(128)S(1)} %pad_add_fusion.place, s32[64]{0:T(128)S(1)} %copy-done.14, s32[1,1024]{1,0:T(1,128)S(1)} %copy-done.12, f32[4,256,128]{2,1,0:T(8,128)S(1)} %bitcast.11, f32[1024,128]{1,0:T(8,128)S(1)} %copy-done.9, f32[1,1024,256]{2,1,0:T(8,128)} %basis.3, f32[1,1024,1024]{2,1,0:T(8,128)} %solve.3), custom_call_target="tpu_custom_call" | custom-call | tf_op jit(solution)/shard_map/pallas_call | solution.py:97
  204.4 3.5 %all-to-all-start.2 = ((f32[4,256,128]{2,1,0:T(8,128)}), f32[4,256,128]{2,1,0:T(8,128)S(1)}, u32[]{:S(2)}, u32[]{:S(2)}) async-start(f32[4,256,128]{2,1,0:T(8,128)} %bitcast.9), calls=%async_computation.2 | async-start | bytes 1048576 | tf_op jit(solution)/shard_map/all_to_all | solution.py:571
  207.9 1.4 collective-permute-start.24
  209.4 2.4 %collective-permute-start.25 = (f32[256,128]{1,0:T(8,128)S(1)}, f32[256,128]{1,0:T(8,128)S(1)}, u32[]{:S(2)}, u32[]{:S(2)}) collective-permute-start(f32[256,128]{1,0:T(8,128)S(1)} %copy-done.22), channel_id=1, source_target_pairs={{0,2},{1,3},{2,0},{3,1},{4,6},{5,7},{6,4},{7,5},{8,10},{9,11},{10,... | collective-permute-start | bytes 393224 | tf_op jit(solution)/shard_map/ppermute | solution.py:57
  211.8 1.2 collective-permute-start.26
  212.9 6.9 %collective-permute-done.24.r1 = f32[256,128]{1,0:T(8,128)S(1)} collective-permute-done((f32[256,128]{1,0:T(8,128)S(1)}, f32[256,128]{1,0:T(8,128)S(1)}, u32[]{:S(2)}, u32[]{:S(2)}) %collective-permute-start.24) | collective-permute-done | bytes 131104 | tf_op jit(solution)/shard_map/ppermute | solution.py:57
  219.8 3.1 %collective-permute-done.25.r2 = f32[256,128]{1,0:T(8,128)S(1)} collective-permute-done((f32[256,128]{1,0:T(8,128)S(1)}, f32[256,128]{1,0:T(8,128)S(1)}, u32[]{:S(2)}, u32[]{:S(2)}) %collective-permute-start.25) | collective-permute-done | bytes 131104 | tf_op jit(solution)/shard_map/ppermute | solution.py:57
  223.0 1.6 outputs.1
  (66 shorter events, 0.2 us)
Async XLA Ops:
  0.6 32.2 %copy-start.15 = (f32[256,128]{1,0:T(8,128)S(1)}, f32[256,128]{1,0:T(8,128)}, u32[]{:S(2)}) copy-start(f32[256,128]{1,0:T(8,128)} %x0.3) | copy-start | bytes 393220
  21.6 38.8 %collective-permute-start.3 = (f32[256,640]{1,0:T(8,128)}, f32[256,640]{1,0:T(8,128)S(1)}, u32[]{:S(2)}, u32[]{:S(2)}) collective-permute-start(f32[256,640]{1,0:T(8,128)} %shard_map.122.p0), channel_id=1, source_target_pairs={{0,4},{4,0},{8,12},{12,8},{16,20},{20,16},{24,28},{28,24},{32,36},... | collective-permute-start | bytes 1966088 | tf_op jit(solution)/shard_map/ppermute | solution.py:31
  25.8 36.1 %copy-start.13 = (s32[1,5]{1,0:T(1,128)S(1)}, s32[1,5]{1,0:T(1,128)}, u32[]{:S(2)}) copy-start(s32[1,5]{1,0:T(1,128)} %mask.3) | copy-start | bytes 64
  25.8 6.9 %collective-permute-start.7 = (f32[128,256]{1,0:T(8,128)S(1)}, f32[128,256]{1,0:T(8,128)S(1)}, u32[]{:S(2)}, u32[]{:S(2)}) collective-permute-start(f32[128,256]{1,0:T(8,128)S(1)} %shard_map.124.slices), channel_id=1, source_target_pairs={{0,32},{4,36},{8,40},{12,44},{16,48},{20,52},{24,56},{28,60},{32,0... | collective-permute-start | bytes 393224 | tf_op jit(solution)/shard_map/ppermute | solution.py:31
  25.9 43.4 %collective-permute-start.1 = (f32[256,640]{1,0:T(8,128)}, f32[256,640]{1,0:T(8,128)S(1)}, u32[]{:S(2)}, u32[]{:S(2)}) collective-permute-start(f32[256,640]{1,0:T(8,128)} %shard_map.122.p0), channel_id=1, source_target_pairs={{0,248},{4,252},{8,0},{12,4},{16,8},{20,12},{24,16},{28,20},{32,24... | collective-permute-start | bytes 1966088 | tf_op jit(solution)/shard_map/ppermute | solution.py:31
  32.7 36.7 %collective-permute-start = (f32[256,640]{1,0:T(8,128)}, f32[256,640]{1,0:T(8,128)}, u32[]{:S(2)}, u32[]{:S(2)}) collective-permute-start(f32[256,640]{1,0:T(8,128)} %shard_map.122.p0), channel_id=1, source_target_pairs={{0,8},{4,12},{8,16},{12,20},{16,24},{20,28},{24,32},{28,36},{32,40... | collective-permute-start | bytes 1966088 | tf_op jit(solution)/shard_map/ppermute | solution.py:31
  32.7 24.0 %copy-start.3 = (f32[256,256]{1,0:T(8,128)}, f32[256,256]{1,0:T(8,128)S(1)}, u32[]{:S(2)}) copy-start(f32[256,256]{1,0:T(8,128)S(1)} %shard_map.125.pair) | copy-start | bytes 786436
  32.7 22.6 %collective-permute-start.8 = (f32[256,256]{1,0:T(8,128)S(1)}, f32[256,256]{1,0:T(8,128)S(1)}, u32[]{:S(2)}, u32[]{:S(2)}) collective-permute-start(f32[256,256]{1,0:T(8,128)S(1)} %shard_map.125.pair), channel_id=1, source_target_pairs={{0,24},{4,28},{8,16},{12,20},{16,8},{20,12},{24,0},{28,4},{32,56},... | collective-permute-start | bytes 786440 | tf_op jit(solution)/shard_map/ppermute | solution.py:31
  32.8 5.1 %collective-permute-start.6 = (f32[256,128]{1,0:T(8,128)S(1)}, f32[256,128]{1,0:T(8,128)S(1)}, u32[]{:S(2)}, u32[]{:S(2)}) collective-permute-start(f32[256,128]{1,0:T(8,128)S(1)} %copy-done.15), channel_id=1, source_target_pairs={{0,3},{1,0},{2,1},{3,2},{4,7},{5,4},{6,5},{7,6},{8,11},{9,8},{10,9... | collective-permute-start | bytes 393224 | tf_op jit(solution)/shard_map/ppermute | solution.py:57
  37.9 22.5 %copy-start.16 = (f32[256,128]{1,0:T(8,128)}, f32[256,128]{1,0:T(8,128)S(1)}, u32[]{:S(2)}) copy-start(f32[256,128]{1,0:T(8,128)S(1)} %collective-permute-done.6.x3) | copy-start | bytes 393220
  37.9 21.0 %collective-permute-start.5 = (f32[256,128]{1,0:T(8,128)S(1)}, f32[256,128]{1,0:T(8,128)S(1)}, u32[]{:S(2)}, u32[]{:S(2)}) collective-permute-start(f32[256,128]{1,0:T(8,128)S(1)} %copy-done.15), channel_id=1, source_target_pairs={{0,2},{1,3},{2,0},{3,1},{4,6},{5,7},{6,4},{7,5},{8,10},{9,11},{10,... | collective-permute-start | bytes 393224 | tf_op jit(solution)/shard_map/ppermute | solution.py:57
  55.4 1.4 copy-start.19
  55.4 5.1 %collective-permute-start.4 = (f32[256,128]{1,0:T(8,128)S(1)}, f32[256,128]{1,0:T(8,128)S(1)}, u32[]{:S(2)}, u32[]{:S(2)}) collective-permute-start(f32[256,128]{1,0:T(8,128)S(1)} %copy-done.15), channel_id=1, source_target_pairs={{0,1},{1,2},{2,3},{3,0},{4,5},{5,6},{6,7},{7,4},{8,9},{9,10},{10,1... | collective-permute-start | bytes 393224 | tf_op jit(solution)/shard_map/ppermute | solution.py:57
  56.7 39.1 %copy-start.12 = (s32[1,1024]{1,0:T(1,128)S(1)}, s32[1,1024]{1,0:T(1,128)}, u32[]{:S(2)}) copy-start(s32[1,1024]{1,0:T(1,128)} %order.5) | copy-start | bytes 12292
  59.0 1.5 copy-start.17
  60.5 0.7 copy-start.18
  61.1 0.8 copy-start.5
  61.9 1.1 copy-start.6
  69.2 22.6 %collective-permute-start.16 = (f32[1024,256]{1,0:T(8,128)}, f32[1024,256]{1,0:T(8,128)}, u32[]{:S(2)}, u32[]{:S(2)}) collective-permute-start(f32[1024,256]{1,0:T(8,128)} %shard_map.126.b0), channel_id=1, source_target_pairs={{0,8},{4,12},{8,0},{12,4},{16,24},{20,28},{24,16},{28,20},{32,40},... | collective-permute-start | bytes 3145736 | tf_op jit(solution)/shard_map/ppermute | solution.py:31
  70.5 30.2 %collective-permute-start.2 = (f32[256,640]{1,0:T(8,128)S(1)}, f32[256,640]{1,0:T(8,128)S(1)}, u32[]{:S(2)}, u32[]{:S(2)}) collective-permute-start(f32[256,640]{1,0:T(8,128)S(1)} %broadcast_select_fusion), channel_id=1, source_target_pairs={{0,4},{4,0},{8,12},{12,8},{16,20},{20,16},{24,28},{28,24},{32,36},... | collective-permute-start | bytes 1966088 | tf_op jit(solution)/shard_map/ppermute | solution.py:31
  72.1 67.1 %collective-permute-start.15 = (f32[1024,256]{1,0:T(8,128)}, f32[1024,256]{1,0:T(8,128)}, u32[]{:S(2)}, u32[]{:S(2)}) collective-permute-start(f32[1024,256]{1,0:T(8,128)} %shard_map.126.b0), channel_id=1, source_target_pairs={{0,4},{4,0},{8,12},{12,8},{16,20},{20,16},{24,28},{28,24},{32,36},... | collective-permute-start | bytes 3145736 | tf_op jit(solution)/shard_map/ppermute | solution.py:31
  91.8 52.4 %collective-permute-start.17 = (f32[1024,256]{1,0:T(8,128)}, f32[1024,256]{1,0:T(8,128)}, u32[]{:S(2)}, u32[]{:S(2)}) collective-permute-start(f32[1024,256]{1,0:T(8,128)} %collective-permute-done.16.b2), channel_id=1, source_target_pairs={{0,4},{4,0},{8,12},{12,8},{16,20},{20,16},{24,28},{28,24},{32,36},... | collective-permute-start | bytes 3145736 | tf_op jit(solution)/shard_map/ppermute | solution.py:31
  95.9 4.8 %copy-start.1 = (f32[256,512]{1,0:T(8,128)S(1)}, f32[256,512]{1,0:T(8,128)}, u32[]{:S(2)}) copy-start(f32[256,512]{1,0:T(8,128)} %coefs.1) | copy-start | bytes 1572868
  95.9 4.8 %copy-start.7 = (f32[256,512]{1,0:T(8,128)S(1)}, f32[256,512]{1,0:T(8,128)}, u32[]{:S(2)}) copy-start(f32[256,512]{1,0:T(8,128)} %own_y.1) | copy-start | bytes 1572868
  110.3 19.8 %copy-start = (f32[1,336,1024]{2,1,0:T(8,128)S(1)}, f32[1,336,1024]{2,1,0:T(8,128)}, u32[]{:S(2)}) copy-start(f32[1,336,1024]{2,1,0:T(8,128)} %m1.3) | copy-start | bytes 4128772
  110.3 19.8 %copy-start.2 = (f32[1,336,256]{2,1,0:T(8,128)S(1)}, f32[1,336,256]{2,1,0:T(8,128)}, u32[]{:S(2)}) copy-start(f32[1,336,256]{2,1,0:T(8,128)} %e1.1) | copy-start | bytes 1032196
  110.3 19.8 %copy-start.14 = (s32[64]{0:T(128)S(1)}, s32[64]{0:T(128)}, u32[]{:S(2)}) copy-start(s32[64]{0:T(128)} %leaf_map.3) | copy-start | bytes 772
  122.5 15.2 %copy-start.20 = (f32[1024,128]{1,0:T(8,128)S(1)}, f32[1024,128]{1,0:T(8,128)}, u32[]{:S(2)}) copy-start(f32[1024,128]{1,0:T(8,128)} %get-tuple-element.32) | copy-start | bytes 1572868
  132.2 12.0 %copy-start.10 = (f32[256,128]{1,0:T(8,128)}, f32[256,128]{1,0:T(8,128)S(1)}, u32[]{:S(2)}) copy-start(f32[256,128]{1,0:T(8,128)S(1)} %get-tuple-element.52.w1) | copy-start | bytes 393220
  132.2 7.0 %all-to-all-start.1 = ((f32[4,32,256]{2,1,0:T(8,128)}), f32[4,32,256]{2,1,0:T(8,128)S(1)}, u32[]{:S(2)}, u32[]{:S(2)}) async-start(f32[4,32,256]{2,1,0:T(8,128)} %bitcast.5), calls=%async_computation.1 | async-start | bytes 262144 | tf_op jit(solution)/shard_map/all_to_all | solution.py:622
  135.6 35.8 %collective-permute-start.9 = (f32[1024,128]{1,0:T(8,128)}, f32[1024,128]{1,0:T(8,128)S(1)}, u32[]{:S(2)}, u32[]{:S(2)}) collective-permute-start(f32[1024,128]{1,0:T(8,128)} %get-tuple-element.30), channel_id=1, source_target_pairs={{0,1},{1,2},{2,3},{3,0},{4,5},{5,6},{6,7},{7,4},{8,9},{9,10},{10,1... | collective-permute-start | bytes 1572872 | tf_op jit(solution)/shard_map/ppermute | solution.py:57
  135.9 35.5 %collective-permute-start.10 = (f32[1024,128]{1,0:T(8,128)}, f32[1024,128]{1,0:T(8,128)S(1)}, u32[]{:S(2)}, u32[]{:S(2)}) collective-permute-start(f32[1024,128]{1,0:T(8,128)} %get-tuple-element.31), channel_id=1, source_target_pairs={{0,2},{1,3},{2,0},{3,1},{4,6},{5,7},{6,4},{7,5},{8,10},{9,11},{10,... | collective-permute-start | bytes 1572872 | tf_op jit(solution)/shard_map/ppermute | solution.py:57
  137.7 33.8 %collective-permute-start.11 = (f32[1024,128]{1,0:T(8,128)S(1)}, f32[1024,128]{1,0:T(8,128)S(1)}, u32[]{:S(2)}, u32[]{:S(2)}) collective-permute-start(f32[1024,128]{1,0:T(8,128)S(1)} %copy-done.20), channel_id=1, source_target_pairs={{0,3},{1,0},{2,1},{3,2},{4,7},{5,4},{6,5},{7,6},{8,11},{9,8},{10,9... | collective-permute-start | bytes 1572872 | tf_op jit(solution)/shard_map/ppermute | solution.py:57
  139.2 5.0 %collective-permute-start.14 = (f32[32,256]{1,0:T(8,128)S(1)}, f32[32,256]{1,0:T(8,128)S(1)}, u32[]{:S(2)}, u32[]{:S(2)}) collective-permute-start(f32[32,256]{1,0:T(8,128)S(1)} %fusion.1.r0), channel_id=1, source_target_pairs={{0,56},{4,60},{8,48},{12,52},{16,40},{20,44},{24,32},{28,36},{32,2... | collective-permute-start | bytes 98312 | tf_op jit(solution)/shard_map/ppermute | solution.py:31
  144.2 3.4 %collective-permute-start.13 = (f32[32,256]{1,0:T(8,128)S(1)}, f32[32,256]{1,0:T(8,128)S(1)}, u32[]{:S(2)}, u32[]{:S(2)}) collective-permute-start(f32[32,256]{1,0:T(8,128)S(1)} %fusion.1.r0), channel_id=1, source_target_pairs={{0,32},{4,36},{8,40},{12,44},{16,48},{20,52},{24,56},{28,60},{32,0... | collective-permute-start | bytes 98312 | tf_op jit(solution)/shard_map/ppermute | solution.py:31
  144.2 4.6 %collective-permute-start.12 = (f32[32,256]{1,0:T(8,128)S(1)}, f32[32,256]{1,0:T(8,128)S(1)}, u32[]{:S(2)}, u32[]{:S(2)}) collective-permute-start(f32[32,256]{1,0:T(8,128)S(1)} %fusion.1.r0), channel_id=1, source_target_pairs={{0,24},{4,28},{8,16},{12,20},{16,8},{20,12},{24,0},{28,4},{32,56},... | collective-permute-start | bytes 98312 | tf_op jit(solution)/shard_map/ppermute | solution.py:31
  147.6 35.9 %copy-start.4 = (f32[1024,256]{1,0:T(8,128)}, f32[1024,256]{1,0:T(8,128)S(1)}, u32[]{:S(2)}) copy-start(f32[1024,256]{1,0:T(8,128)S(1)} %get-tuple-element.51.e1) | copy-start | bytes 3145732
  149.6 5.2 %collective-permute-start.20 = (f32[32,256]{1,0:T(8,128)S(1)}, f32[32,256]{1,0:T(8,128)S(1)}, u32[]{:S(2)}, u32[]{:S(2)}) collective-permute-start(f32[32,256]{1,0:T(8,128)S(1)} %get-tuple-element.38), channel_id=1, source_target_pairs={{0,56},{4,60},{8,48},{12,52},{16,40},{20,44},{24,32},{28,36},{32,2... | collective-permute-start | bytes 98312 | tf_op jit(solution)/shard_map/ppermute | solution.py:31
  152.0 4.3 %collective-permute-start.19 = (f32[32,256]{1,0:T(8,128)S(1)}, f32[32,256]{1,0:T(8,128)S(1)}, u32[]{:S(2)}, u32[]{:S(2)}) collective-permute-start(f32[32,256]{1,0:T(8,128)S(1)} %get-tuple-element.38), channel_id=1, source_target_pairs={{0,32},{4,36},{8,40},{12,44},{16,48},{20,52},{24,56},{28,60},{32,0... | collective-permute-start | bytes 98312 | tf_op jit(solution)/shard_map/ppermute | solution.py:31
  154.8 4.3 %collective-permute-start.18 = (f32[32,256]{1,0:T(8,128)S(1)}, f32[32,256]{1,0:T(8,128)S(1)}, u32[]{:S(2)}, u32[]{:S(2)}) collective-permute-start(f32[32,256]{1,0:T(8,128)S(1)} %get-tuple-element.38), channel_id=1, source_target_pairs={{0,24},{4,28},{8,16},{12,20},{16,8},{20,12},{24,0},{28,4},{32,56},... | collective-permute-start | bytes 98312 | tf_op jit(solution)/shard_map/ppermute | solution.py:31
  159.1 5.9 %collective-permute-start.23 = (f32[32,256]{1,0:T(8,128)S(1)}, f32[32,256]{1,0:T(8,128)S(1)}, u32[]{:S(2)}, u32[]{:S(2)}) collective-permute-start(f32[32,256]{1,0:T(8,128)S(1)} %add_add_fusion.r0), channel_id=1, source_target_pairs={{160,0},{164,4},{168,8},{172,12},{176,16},{180,20},{184,24},{188,2... | collective-permute-start | bytes 98312 | tf_op jit(solution)/shard_map/ppermute | solution.py:53
  163.5 5.2 %collective-permute-start.22 = (f32[32,256]{1,0:T(8,128)S(1)}, f32[32,256]{1,0:T(8,128)S(1)}, u32[]{:S(2)}, u32[]{:S(2)}) collective-permute-start(f32[32,256]{1,0:T(8,128)S(1)} %add_add_fusion.r0), channel_id=1, source_target_pairs={{64,0},{68,4},{72,8},{76,12},{80,16},{84,20},{88,24},{92,28},{224,... | collective-permute-start | bytes 98312 | tf_op jit(solution)/shard_map/ppermute | solution.py:53
  165.0 5.6 %collective-permute-start.21 = (f32[32,256]{1,0:T(8,128)S(1)}, f32[32,256]{1,0:T(8,128)S(1)}, u32[]{:S(2)}, u32[]{:S(2)}) collective-permute-start(f32[32,256]{1,0:T(8,128)S(1)} %add_add_fusion.r0), channel_id=1, source_target_pairs={{224,0},{228,4},{232,8},{236,12},{240,16},{244,20},{248,24},{252,2... | collective-permute-start | bytes 98312 | tf_op jit(solution)/shard_map/ppermute | solution.py:53
  171.4 22.6 %copy-start.8 = (f32[1024,128]{1,0:T(8,128)S(1)}, f32[1024,128]{1,0:T(8,128)}, u32[]{:S(2)}) copy-start(f32[1024,128]{1,0:T(8,128)} %get-tuple-element.42.p0) | copy-start | bytes 1572868
  196.8 1.0 copy-start.9
  197.8 10.1 %copy-start.23 = (f32[256,128]{1,0:T(8,128)S(1)}, f32[256,128]{1,0:T(8,128)}, u32[]{:S(2)}) copy-start(f32[256,128]{1,0:T(8,128)} %get-tuple-element.47) | copy-start | bytes 393220
  197.8 11.5 %copy-start.22 = (f32[256,128]{1,0:T(8,128)S(1)}, f32[256,128]{1,0:T(8,128)}, u32[]{:S(2)}) copy-start(f32[256,128]{1,0:T(8,128)} %get-tuple-element.48) | copy-start | bytes 393220
  197.8 13.9 %copy-start.21 = (f32[256,128]{1,0:T(8,128)S(1)}, f32[256,128]{1,0:T(8,128)}, u32[]{:S(2)}) copy-start(f32[256,128]{1,0:T(8,128)} %get-tuple-element.49) | copy-start | bytes 393220
  197.8 25.1 %copy-start.11 = (f32[256,128]{1,0:T(8,128)S(1)}, f32[256,128]{1,0:T(8,128)}, u32[]{:S(2)}) copy-start(f32[256,128]{1,0:T(8,128)} %get-tuple-element.46.r0) | copy-start | bytes 393220
  204.4 18.5 %all-to-all-start.2 = ((f32[4,256,128]{2,1,0:T(8,128)}), f32[4,256,128]{2,1,0:T(8,128)S(1)}, u32[]{:S(2)}, u32[]{:S(2)}) async-start(f32[4,256,128]{2,1,0:T(8,128)} %bitcast.9), calls=%async_computation.2 | async-start | bytes 1048576 | tf_op jit(solution)/shard_map/all_to_all | solution.py:571
  207.9 11.9 %collective-permute-start.24 = (f32[256,128]{1,0:T(8,128)S(1)}, f32[256,128]{1,0:T(8,128)S(1)}, u32[]{:S(2)}, u32[]{:S(2)}) collective-permute-start(f32[256,128]{1,0:T(8,128)S(1)} %copy-done.23), channel_id=1, source_target_pairs={{0,1},{1,2},{2,3},{3,0},{4,5},{5,6},{6,7},{7,4},{8,9},{9,10},{10,1... | collective-permute-start | bytes 393224 | tf_op jit(solution)/shard_map/ppermute | solution.py:57
  209.4 13.6 %collective-permute-start.25 = (f32[256,128]{1,0:T(8,128)S(1)}, f32[256,128]{1,0:T(8,128)S(1)}, u32[]{:S(2)}, u32[]{:S(2)}) collective-permute-start(f32[256,128]{1,0:T(8,128)S(1)} %copy-done.22), channel_id=1, source_target_pairs={{0,2},{1,3},{2,0},{3,1},{4,6},{5,7},{6,4},{7,5},{8,10},{9,11},{10,... | collective-permute-start | bytes 393224 | tf_op jit(solution)/shard_map/ppermute | solution.py:57
  211.8 11.2 %collective-permute-start.26 = (f32[256,128]{1,0:T(8,128)S(1)}, f32[256,128]{1,0:T(8,128)S(1)}, u32[]{:S(2)}, u32[]{:S(2)}) collective-permute-start(f32[256,128]{1,0:T(8,128)S(1)} %copy-done.21), channel_id=1, source_target_pairs={{0,3},{1,0},{2,1},{3,2},{4,7},{5,4},{6,5},{7,6},{8,11},{9,8},{10,9... | collective-permute-start | bytes 393224 | tf_op jit(solution)/shard_map/ppermute | solution.py:57

commit v5 on v3

--- a/solution.py
+++ b/solution.py
@@ -99,7 +99,10 @@
         in_specs=[SMEM] * len(scalars) + [VMEM] * len(values) + [HBM] * len(far_values),
         out_specs=[VMEM] * len(outs) + [HBM] * len(far_outs),
         out_shape=[pltpu.VMEM(shape, F32) for shape in outs]
-        + [pltpu.HBM(shape, F32) for shape in far_outs],
+        + [
+            pltpu.HBM(*shape) if isinstance(shape[0], tuple) else pltpu.HBM(shape, F32)
+            for shape in far_outs
+        ],
         scratch_shapes=list(scratch),
         compiler_params=pltpu.CompilerParams(vmem_limit_bytes=20 << 20),
     )(*scalars, *[near_memory(value) for value in values], *[far_memory(value) for value in far_values])
@@ -118,11 +121,15 @@
     return jnp.concatenate([top, low], axis=1), top.astype(F32) + low.astype(F32)
 
 
-def tile_setup(place, xs, blocks, rows, norms, squares, others, tops, lows):
+def row_setup(place, xs, loaded, arrived, rows, norms):
     for k, ref in enumerate(xs):
+        pltpu.make_async_copy(ref, loaded.at[k], arrived.at[k]).wait()
         at = (place[2] + 4 - k) % 4
-        rows[at], exact = two_part(ref[...])
+        rows[at], exact = two_part(loaded[k])
         norms[at] = jnp.sum(exact * exact, axis=1, keepdims=True)
+
+
+def block_setup(blocks, squares, others, tops, lows):
     for k, (y, a) in enumerate(blocks):
         others[k], exact = two_part(y)
         total = jnp.sum(exact * exact, axis=1, keepdims=True)
@@ -145,22 +152,36 @@
     return total
 
 
-def near_kernel(place, mask, x0, x1, x2, x3, p0, p1, out, *scratch):
-    blocks = [(p[:, :128], p[:, 128:]) for p in (p0, p1)]
-    tile_setup(place, (x0, x1, x2, x3), blocks, *scratch)
+def near_kernel(
+    place, mask, p0, p1, x0, x1, x2, x3, out, rows_out, norms_out, loaded, arrived, rows, norms, *scratch
+):
+    xs = (x0, x1, x2, x3)
+    for k, ref in enumerate(xs):
+        pltpu.make_async_copy(ref, loaded.at[k], arrived.at[k]).start()
+    block_setup([(p[:, :128], p[:, 128:]) for p in (p0, p1)], *scratch)
+    row_setup(place, xs, loaded, arrived, rows, norms)
+    copies = [
+        pltpu.make_async_copy(rows, rows_out, arrived.at[4]),
+        pltpu.make_async_copy(norms, norms_out, arrived.at[5]),
+    ]
+    for copy in copies:
+        copy.start()
     weights = (mask[0, 2].astype(F32), mask[0, 3 - 2 * place[0]].astype(F32))
 
     @pl.loop(0, 2)
     def _(i):
-        out[pl.ds(pl.multiple_of(i * CHUNK, CHUNK), CHUNK), :] = tile_sum(i, weights, *scratch)
+        at = pl.ds(pl.multiple_of(i * CHUNK, CHUNK), CHUNK)
+        out[at, :] = tile_sum(i, weights, rows, norms, *scratch)
+
+    for copy in copies:
+        copy.wait()
 
 
 def far_kernel(
-    place, mask, ridge, x0, x1, x2, x3, p0, p1, p2, near, own_y, own_a, lead,
+    place, mask, ridge, p0, p1, p2, near, own_y, own_a, lead, split_rows, norms,
     led, out0, out1, out2, out3, parts, sems, *scratch
 ):
-    blocks = [(p[:, :128], p[:, 128:]) for p in (p0, p1, p2)]
-    tile_setup(place, (x0, x1, x2, x3), blocks, *scratch)
+    block_setup([(p[:, :128], p[:, 128:]) for p in (p0, p1, p2)], *scratch)
     weights = (
         mask[0, 0].astype(F32),
         mask[0, 4].astype(F32),
@@ -181,7 +202,7 @@
     @pl.loop(0, 2)
     def _(i):
         rows = pl.ds(pl.multiple_of(i * CHUNK, CHUNK), CHUNK)
-        total = near[rows, :] + tile_sum(i, weights, *scratch)
+        total = near[rows, :] + tile_sum(i, weights, split_rows, norms, *scratch)
         own = own_y[...] - ridge[0] * own_a[...]
         part = jnp.concatenate(
             [
@@ -202,10 +223,8 @@
             copy.wait()
 
 
-def tile_scratch(count):
+def block_scratch(count):
     return [
-        pltpu.VMEM((4, Q, 256), BF16),
-        pltpu.VMEM((4, Q, 1), F32),
         pltpu.VMEM((count, 8, Q), F32),
         pltpu.VMEM((count, Q, 256), BF16),
         pltpu.VMEM((count, Q, 512), BF16),
@@ -215,17 +234,31 @@
 
 def near_call(place, mask, xs, blocks):
     return kernel(
-        near_kernel, [(1024, 512)], [*xs, *blocks], (place, mask), tile_scratch(2)
-    )
-
-
-def far_call(place, mask, ridge, xs, blocks, near, own_y, own_a, lead):
+        near_kernel,
+        [(1024, 512)],
+        blocks,
+        (place, mask),
+        [
+            pltpu.VMEM((4, Q, 128), F32),
+            pltpu.SemaphoreType.DMA((6,)),
+            pltpu.VMEM((4, Q, 256), BF16),
+            pltpu.VMEM((4, Q, 1), F32),
+        ]
+        + block_scratch(2),
+        xs,
+        [((4, Q, 256), BF16), (4, Q, 1)],
+    )
+
+
+def far_call(place, mask, ridge, blocks, near, own_y, own_a, lead):
+    near, rows, norms = near
     return kernel(
         far_kernel,
         [(4, RANK, 128)],
-        [*xs, *blocks, near, own_y, own_a, lead],
+        [*blocks, near, own_y, own_a, lead, rows, norms],
         (place, mask, ridge),
-        [pltpu.VMEM((2, 4, CHUNK, 128), F32), pltpu.SemaphoreType.DMA((2, 4))] + tile_scratch(3),
+        [pltpu.VMEM((2, 4, CHUNK, 128), F32), pltpu.SemaphoreType.DMA((2, 4))]
+        + block_scratch(3),
         far_outs=[(1024, 128)] * 4,
     )
 
@@ -294,35 +327,34 @@
         copy.wait()
 
 
-def mover(body, shape, count, *parts):
-    return pl.pallas_call(
-        body,
-        in_specs=[HBM] * len(parts),
-        out_specs=HBM,
-        out_shape=like(*shape),
-        scratch_shapes=[pltpu.SemaphoreType.DMA((count,))],
-        compiler_params=pltpu.CompilerParams(vmem_limit_bytes=4 << 20),
-    )(*[far_memory(part) for part in parts])
-
-
-def pack_kernel(a, b, out, sems):
-    run_copies(sems, [(a, out.at[:, pl.ds(0, 128)]), (b, out.at[:, pl.ds(128, 512)])])
-
-
-def slice_moves(transfer, inverse, out, start):
-    moves = [(transfer.at[0, pl.ds(256, 64), :], out.at[pl.ds(start, 64), :])]
+def pack_kernel(a, b, out, buffer, sems):
+    run_copies(sems, [(a, buffer.at[:, pl.ds(0, 128)]), (b, buffer.at[:, pl.ds(128, 512)])])
+    run_copies(sems, [(buffer, out)])
+
+
+def slices_kernel(transfer, inverse, out, buffer, sems):
+    moves = [(transfer.at[0, pl.ds(256, 64), :], buffer.at[pl.ds(0, 64), :])]
     for k in range(4):
         source = inverse.at[0, pl.ds(320, 16), pl.ds(k * 256, 256)]
-        moves.append((source, out.at[pl.ds(start + 64 + k * 16, 16), :]))
-    return moves
-
-
-def slices_kernel(transfer, inverse, out, sems):
-    run_copies(sems, slice_moves(transfer, inverse, out, 0))
-
-
-def pair_kernel(slices, lower, out, sems):
-    run_copies(sems, [(slices, out.at[pl.ds(0, 128), :]), (lower, out.at[pl.ds(128, 128), :])])
+        moves.append((source, buffer.at[pl.ds(64 + k * 16, 16), :]))
+    run_copies(sems, moves)
+    run_copies(sems, [(buffer, out)])
+
+
+def assemble(body, shape, count, *parts):
+    return kernel(
+        body,
+        [],
+        [],
+        scratch=[pltpu.VMEM(shape, F32), pltpu.SemaphoreType.DMA((count,))],
+        far_values=parts,
+        far_outs=[shape],
+    )
+
+
+def pair_kernel(slices, lower, out):
+    out[:128, :] = slices[...]
+    out[128:, :] = lower[...]
 
 
 def held_kernel(transfer, inverse, pair, mirrored, out, buffer, sems):
@@ -336,17 +368,6 @@
         moves.append((source, buffer.at[pl.ds(256 + k * 64, 64), :]))
     run_copies(sems, moves)
     run_copies(sems, [(buffer, out)])
-
-
-def held_call(*parts):
-    return kernel(
-        held_kernel,
-        [],
-        [],
-        scratch=[pltpu.VMEM((1024, 256), F32), pltpu.SemaphoreType.DMA((7,))],
-        far_values=parts,
-        far_outs=[(1024, 256)],
-    )
 
 
 def nodes_kernel(place, b0, b1, b2, b3, e1, m2, f2, m3, own_e2, e2):
@@ -582,17 +603,17 @@
     place = jnp.stack([core, leaf // 2 % 2, col, leaf]).astype(jnp.int32)
 
     xs = [points] + [col_shift(points, d) for d in (1, 2, 3)]
-    packed = mover(pack_kernel, (Q, 640), 2, points, coefs)
+    packed = assemble(pack_kernel, (Q, 640), 2, points, coefs)
     left, right = leaf_from(packed, -2), leaf_from(packed, 2)
     partner = leaf_xor(packed, 1)
     relay = leaf_xor(jnp.where(core == 0, right, left), 1)
 
     nodes = (node_transfer, node_inverse)
-    slices = mover(slices_kernel, (128, 256), 5, *nodes)
+    slices = assemble(slices_kernel, (128, 256), 5, *nodes)
     lower = leaf_route(slices, lambda i: facing(i, 0, 1))
-    pair = mover(pair_kernel, (256, 256), 2, slices, lower)
+    pair = kernel(pair_kernel, [(256, 256)], [slices, lower])
     mirrored = leaf_route(pair, lambda i: facing(i, 1, 0))
-    held = held_call(*nodes, pair, mirrored)
+    held = assemble(held_kernel, (1024, 256), 7, *nodes, pair, mirrored)
 
     lead = lead_call(cluster_perm, leaf_basis, leaf_inverse)
 
@@ -602,10 +623,10 @@
     own_core = leaf_xor(held, 1)
     both_ways = leaf_xor(across, 1)
     led, *partial = far_call(
-        place, tile_mask, ridge, xs, (left, right, relay), near, targets, coefs, lead
+        place, tile_mask, ridge, (left, right, relay), near, targets, coefs, lead
     )
     led = swap_cols(led)
-    reduced = led[0] + led[1] + (led[2] + led[3])
+    reduced = led.sum(0)
     e1, m2, f2, m3, e2 = nodes_call(place, (held, own_core, across, both_ways))
 
     columns = [partial[0]] + [col_shift(partial[d], d) for d in (1, 2, 3)]

time: 206 us -> 207 us (level)
  waiting for transfers between devices: 46.9 us -> 66.4 us
  Pallas kernels: 64.5 us -> 45.9 us
  blocking collectives: 27.4 us -> 39.6 us
  starting transfers between devices: 59.8 us -> 47.6 us
    ppermute x15, waiting for transfers between devices: 24.1 us -> 48.7 us  [leaf_route(): return lax.ppermute(value, 'leaf', [(i, target(i)) for i in range(LEAVES)])]
    pallas_call x3 -> x0, Pallas kernels: 22.8 us -> none  [mover(): pl.pallas_call(body, in_specs=[HBM] * len(parts), out_specs=HBM, out_shap...]
    all_to_all x0 -> x1, blocking collectives: none -> 13.3 us  [swap_cols(): return lax.all_to_all(value, 'col', 0, 0, tiled=True)]
    ppermute x15, starting transfers between devices: 24.3 us -> 18.8 us  [leaf_route(): return lax.ppermute(value, 'leaf', [(i, target(i)) for i in range(LEAVES)])]
    all_to_all x2 -> x1, waiting for transfers between devices: 4.71 us -> 0.01 us  [swap_cols(): return lax.all_to_all(value, 'col', 0, 0, tiled=True)]
    all_to_all x2 -> x1, starting transfers between devices: 7.77 us -> 3.48 us  [swap_cols(): return lax.all_to_all(value, 'col', 0, 0, tiled=True)]
    pallas_call x11 -> x14, Pallas kernels: 40 us -> 44.3 us  [kernel(): pl.pallas_call(body, in_specs=[SMEM] * len(scalars) + [VMEM] * len(values...]
    ppermute x3, starting transfers between devices: 10.1 us -> 7.08 us  [z_from(): return lax.ppermute(value, 'leaf', route)]
  transfers between devices with their start and end apart: 30 -> 29, of which waited for: 15 -> 13; matrix products, arithmetic and copies ran while one was open for 1% -> 1% of each run, Pallas kernels for 14% -> 14%
where the time goes in v5:
time: 207 us
  waiting for transfers between devices  66.4 us (32%)
  starting transfers between devices  47.6 us (23%)
  Pallas kernels  45.9 us (22%)
  blocking collectives  39.6 us (19%)
  local copies, waits for them, and re-layouts  4.05 us (2%)
    ppermute x15, waiting for transfers between devices, leaf_route(): return lax.ppermute(value, 'leaf', [(i, target(i)) for i in range(LEAVES)])  48.7 us
    pallas_call x14, Pallas kernels, kernel(): pl.pallas_call(body, in_specs=[SMEM] * len(scalars) + [VMEM] * len(values...  44.3 us
    all_gather x3, blocking collectives, gather4(): return lax.all_gather(value, 'leaf', axis=0, axis_index_groups=groups)  26.3 us
    ppermute x15, starting transfers between devices, leaf_route(): return lax.ppermute(value, 'leaf', [(i, target(i)) for i in range(LEAVES)])  18.8 us
    ppermute x9, starting transfers between devices, col_shift(): return lax.ppermute(value, 'col', [(i, (i + step) % 4) for i in range(4)])  14.8 us
    all_to_all x1, blocking collectives, swap_cols(): return lax.all_to_all(value, 'col', 0, 0, tiled=True)  13.3 us
    ppermute x9, waiting for transfers between devices, col_shift(): return lax.ppermute(value, 'col', [(i, (i + step) % 4) for i in range(4)])  13.1 us
    ppermute x3, starting transfers between devices, z_from(): return lax.ppermute(value, 'leaf', route)  7.08 us
  transfers between devices with their start and end apart: 29, of which 13 were waited for; matrix products, arithmetic and copies ran while one was open for 1% of the time, Pallas kernels for 14%

profile of v5, /device:TPU:1, one launch (start us, length us, event | category | flops | bytes accessed | tf_op | source)
XLA Modules:
  0.0 206.7 jit_solution(7353401824589638294)
XLA Ops:
  0.6 0.0 copy-start.21
  0.6 2.0 shard_map.122.p0
  2.7 3.3 %collective-permute-start.3 = (f32[256,640]{1,0:T(8,128)}, f32[256,640]{1,0:T(8,128)}, u32[]{:S(2)}, u32[]{:S(2)}) collective-permute-start(f32[256,640]{1,0:T(8,128)} %shard_map.122.p0), channel_id=1, source_target_pairs={{0,4},{4,0},{8,12},{12,8},{16,20},{20,16},{24,28},{28,24},{32,36},... | collective-permute-start | bytes 1966088 | tf_op jit(solution)/shard_map/ppermute | solution.py:31
  5.9 1.6 shard_map.124.slices
  7.5 0.1 collective-permute-start.7
  7.6 6.8 %collective-permute-start.1 = (f32[256,640]{1,0:T(8,128)}, f32[256,640]{1,0:T(8,128)S(1)}, u32[]{:S(2)}, u32[]{:S(2)}) collective-permute-start(f32[256,640]{1,0:T(8,128)} %shard_map.122.p0), channel_id=1, source_target_pairs={{0,248},{4,252},{8,0},{12,4},{16,8},{20,12},{24,16},{28,20},{32,24... | collective-permute-start | bytes 1966088 | tf_op jit(solution)/shard_map/ppermute | solution.py:31
  14.4 0.9 copy-done.9
  15.3 0.1 collective-permute-start.8
  15.5 3.0 %collective-permute-start.5 = (f32[256,128]{1,0:T(8,128)S(1)}, f32[256,128]{1,0:T(8,128)S(1)}, u32[]{:S(2)}, u32[]{:S(2)}) collective-permute-start(f32[256,128]{1,0:T(8,128)S(1)} %copy-done.21), channel_id=1, source_target_pairs={{0,2},{1,3},{2,0},{3,1},{4,6},{5,7},{6,4},{7,5},{8,10},{9,11},{10,... | collective-permute-start | bytes 393224 | tf_op jit(solution)/shard_map/ppermute | solution.py:57
  18.5 3.1 %collective-permute-done.5.x2 = f32[256,128]{1,0:T(8,128)S(1)} collective-permute-done((f32[256,128]{1,0:T(8,128)S(1)}, f32[256,128]{1,0:T(8,128)S(1)}, u32[]{:S(2)}, u32[]{:S(2)}) %collective-permute-start.5) | collective-permute-done | bytes 131104 | tf_op jit(solution)/shard_map/ppermute | solution.py:57
  21.5 1.3 collective-permute-start.4
  22.8 15.1 %collective-permute-done.8.mirrored = f32[256,256]{1,0:T(8,128)S(1)} collective-permute-done((f32[256,256]{1,0:T(8,128)S(1)}, f32[256,256]{1,0:T(8,128)S(1)}, u32[]{:S(2)}, u32[]{:S(2)}) %collective-permute-start.8) | collective-permute-done | bytes 262176 | tf_op jit(solution)/shard_map/ppermute | solution.py:31
  38.0 2.7 %collective-permute-start.6 = (f32[256,128]{1,0:T(8,128)S(1)}, f32[256,128]{1,0:T(8,128)}, u32[]{:S(2)}, u32[]{:S(2)}) collective-permute-start(f32[256,128]{1,0:T(8,128)S(1)} %copy-done.21), channel_id=1, source_target_pairs={{0,3},{1,0},{2,1},{3,2},{4,7},{5,4},{6,5},{7,6},{8,11},{9,8},{10,9... | collective-permute-start | bytes 393224 | tf_op jit(solution)/shard_map/ppermute | solution.py:57
  40.7 0.1 pad_add_fusion.place
  40.8 2.2 %shard_map.126.b0 = f32[1024,256]{1,0:T(8,128)} custom-call(f32[1,336,256]{2,1,0:T(8,128)} %e1.1, f32[1,336,1024]{2,1,0:T(8,128)} %m1.3, f32[256,256]{1,0:T(8,128)} %copy-done.7, f32[256,256]{1,0:T(8,128)} %copy-done.22), custom_call_target="tpu_custom_call" | custom-call | tf_op jit(solution)/shard_map/pallas_call | solution.py:97
  43.1 6.3 %shard_map.123 = (f32[1024,512]{1,0:T(8,128)S(1)}, bf16[4,256,256]{2,1,0:T(8,128)(2,1)}, f32[4,256,1]{2,1,0:T(8,128)}) custom-call(s32[4]{0:T(128)S(1)} %pad_add_fusion.place, s32[1,5]{1,0:T(1,128)S(1)} %copy-done.19, f32[256,640]{1,0:T(8,128)S(1)} %copy-done.4, f32[256,640]{1,0:T(8,128)} %collective-permute-done.3.p1, f32[256,128]{1,0:T(8,128)} %x0.1, ...), custom_call_target="tpu_custom_call" | custom-call | tf_op jit(solution)/shard_map/pallas_call | solution.py:97
  49.4 1.4 copy-done.5
  50.8 0.1 broadcast_select_fusion
  50.9 2.0 collective-permute-start.2
  52.8 0.1 collective-permute-start.15
  52.9 21.0 %collective-permute-done.16.b2 = f32[1024,256]{1,0:T(8,128)} collective-permute-done((f32[1024,256]{1,0:T(8,128)}, f32[1024,256]{1,0:T(8,128)}, u32[]{:S(2)}, u32[]{:S(2)}) %collective-permute-start.16) | collective-permute-done | bytes 1048608 | tf_op jit(solution)/shard_map/ppermute | solution.py:31
  73.9 2.7 %collective-permute-start.17 = (f32[1024,256]{1,0:T(8,128)}, f32[1024,256]{1,0:T(8,128)}, u32[]{:S(2)}, u32[]{:S(2)}) collective-permute-start(f32[1024,256]{1,0:T(8,128)} %collective-permute-done.16.b2), channel_id=1, source_target_pairs={{0,4},{4,0},{8,12},{12,8},{16,20},{20,16},{24,28},{28,24},{32,36},... | collective-permute-start | bytes 3145736 | tf_op jit(solution)/shard_map/ppermute | solution.py:31
  77.3 0.0 copy-start.1
  77.4 4.8 %shard_map.127.lead = f32[256,1024]{1,0:T(8,128)S(1)} custom-call(s32[1,1024]{1,0:T(1,128)S(1)} %copy-done.18, f32[1,1024,256]{2,1,0:T(8,128)} %basis.3, f32[1,1024,1024]{2,1,0:T(8,128)} %solve.3), custom_call_target="tpu_custom_call" | custom-call | tf_op jit(solution)/shard_map/pallas_call | solution.py:97
  82.3 8.1 %shard_map.128 = (f32[4,256,128]{2,1,0:T(8,128)S(1)}, f32[1024,128]{1,0:T(8,128)}, f32[1024,128]{1,0:T(8,128)}, f32[1024,128]{1,0:T(8,128)}, f32[1024,128]{1,0:T(8,128)}) custom-call(s32[4]{0:T(128)S(1)} %pad_add_fusion.place, s32[1,5]{1,0:T(1,128)S(1)} %copy-done.19, f32[1]{0:T(128)S(6)} %copy.13.ridge, f32[256,640]{1,0:T(8,128)S(1)} %collective-permute-done.p0, ...), custom_call_target="tpu_custom_call" | custom-call | tf_op jit(solution)/shard_map/pallas_call | solution.py:97
  90.5 13.3 %all_to_all.19 = f32[4,256,128]{2,1,0:T(8,128)} all-to-all(f32[4,256,128]{2,1,0:T(8,128)S(1)} %get-tuple-element.43), channel_id=1, replica_groups=mesh['leaf'=64,'col'=4] {'col'}, dimensions={0} | all-to-all | bytes 1048576 | tf_op jit(solution)/shard_map/all_to_all | solution.py:584
  103.8 1.1 reduce_sum.9
  104.9 7.5 %all-gather = f32[1024,128]{1,0:T(8,128)S(1)} all-gather(f32[256,128]{1,0:T(8,128)S(1)} %reduce_sum.9), channel_id=2, replica_groups={{0,4,8,12},{16,20,24,28},{32,36,40,44},{48,52,56,60},{64,68,72,76},{80,..., dimensions={0}, use_global_device_ids=true | all-gather | bytes 655360 | tf_op jit(solution)/shard_map/all_gather | solution.py:61
  112.3 1.4 shard_map.129
  113.8 0.6 copy-done.17
  114.4 3.5 %all-to-all-start.1 = ((f32[4,32,256]{2,1,0:T(8,128)}), f32[4,32,256]{2,1,0:T(8,128)S(1)}, u32[]{:S(2)}, u32[]{:S(2)}) async-start(f32[4,32,256]{2,1,0:T(8,128)} %bitcast.14), calls=%async_computation.1 | async-start | bytes 262144 | tf_op jit(solution)/shard_map/all_to_all | solution.py:635
  117.9 0.3 collective-permute-start.9
  118.2 1.8 collective-permute-start.10
  120.0 0.7 collective-permute-start.11
  120.6 0.8 all-to-all-done.1
  121.5 0.1 collective-permute-start.14
  121.6 4.9 %collective-permute-done.14.r3 = f32[32,256]{1,0:T(8,128)S(1)} collective-permute-done((f32[32,256]{1,0:T(8,128)S(1)}, f32[32,256]{1,0:T(8,128)S(1)}, u32[]{:S(2)}, u32[]{:S(2)}) %collective-permute-start.14) | collective-permute-done | bytes 32800 | tf_op jit(solution)/shard_map/ppermute | solution.py:31
  126.4 0.3 collective-permute-start.12
  126.7 2.7 %shard_map.130 = (f32[1024,256]{1,0:T(8,128)S(1)}, f32[256,1024]{1,0:T(8,128)S(1)}, f32[256,256]{1,0:T(8,128)S(1)}, f32[256,1024]{1,0:T(8,128)S(1)}, f32[256,256]{1,0:T(8,128)S(1)}) custom-call(s32[4]{0:T(128)S(1)} %pad_add_fusion.place, f32[1024,256]{1,0:T(8,128)S(1)} %copy-done.2, f32[1024,256]{1,0:T(8,128)} %collective-permute-done.15.b1, ...), custom_call_target="tpu_custom_call" | custom-call | tf_op jit(solution)/shard_map/pallas_call | solution.py:97
  129.5 0.1 collective-permute-done.13.r2
  129.6 1.2 collective-permute-done.12.r1
  130.8 0.8 shard_map.131
  131.6 2.3 %collective-permute-start.20 = (f32[32,256]{1,0:T(8,128)S(1)}, f32[32,256]{1,0:T(8,128)S(1)}, u32[]{:S(2)}, u32[]{:S(2)}) collective-permute-start(f32[32,256]{1,0:T(8,128)S(1)} %get-tuple-element.48), channel_id=1, source_target_pairs={{0,56},{4,60},{8,48},{12,52},{16,40},{20,44},{24,32},{28,36},{32,2... | collective-permute-start | bytes 98312 | tf_op jit(solution)/shard_map/ppermute | solution.py:31
  133.9 3.0 %collective-permute-done.20 = f32[32,256]{1,0:T(8,128)S(1)} collective-permute-done((f32[32,256]{1,0:T(8,128)S(1)}, f32[32,256]{1,0:T(8,128)S(1)}, u32[]{:S(2)}, u32[]{:S(2)}) %collective-permute-start.20) | collective-permute-done | bytes 32800 | tf_op jit(solution)/shard_map/ppermute | solution.py:31
  136.9 1.1 collective-permute-start.18
  138.0 3.3 %collective-permute-done.18 = f32[32,256]{1,0:T(8,128)S(1)} collective-permute-done((f32[32,256]{1,0:T(8,128)S(1)}, f32[32,256]{1,0:T(8,128)S(1)}, u32[]{:S(2)}, u32[]{:S(2)}) %collective-permute-start.18) | collective-permute-done | bytes 32800 | tf_op jit(solution)/shard_map/ppermute | solution.py:31
  141.3 3.9 %collective-permute-start.23 = (f32[32,256]{1,0:T(8,128)S(1)}, f32[32,256]{1,0:T(8,128)S(1)}, u32[]{:S(2)}, u32[]{:S(2)}) collective-permute-start(f32[32,256]{1,0:T(8,128)S(1)} %add_add_fusion.r0), channel_id=1, source_target_pairs={{160,0},{164,4},{168,8},{172,12},{176,16},{180,20},{184,24},{188,2... | collective-permute-start | bytes 98312 | tf_op jit(solution)/shard_map/ppermute | solution.py:53
  145.2 2.0 collective-permute-done.23.r3
  147.2 3.2 %collective-permute-start.21 = (f32[32,256]{1,0:T(8,128)S(1)}, f32[32,256]{1,0:T(8,128)S(1)}, u32[]{:S(2)}, u32[]{:S(2)}) collective-permute-start(f32[32,256]{1,0:T(8,128)S(1)} %add_add_fusion.r0), channel_id=1, source_target_pairs={{224,0},{228,4},{232,8},{236,12},{240,16},{244,20},{248,24},{252,2... | collective-permute-start | bytes 98312 | tf_op jit(solution)/shard_map/ppermute | solution.py:53
  150.4 1.8 collective-permute-done.21.r1
  152.2 0.9 shard_map.132
  153.2 11.6 %all-gather.1 = f32[128,256]{1,0:T(8,128)S(1)} all-gather(f32[32,256]{1,0:T(8,128)S(1)} %shard_map.132), channel_id=3, replica_groups={{0,4,8,12},{24,28,16,20},{32,36,40,44},{56,60,48,52},{64,68,72,76},{88,..., dimensions={0}, use_global_device_ids=true | all-gather | bytes 163840 | tf_op jit(solution)/shard_map/all_gather | solution.py:61
  164.8 3.2 %shard_map.134 = f32[256,128]{1,0:T(8,128)S(1)} custom-call(f32[4,32,256]{2,1,0:T(8,128)S(1)} %bitcast.13, f32[1024,256]{1,0:T(8,128)} %copy-done.8, f32[1,336,1024]{2,1,0:T(8,128)} %m1.3, f32[256,128]{1,0:T(8,128)} %copy-done.15), custom_call_target="tpu_custom_call" | custom-call | tf_op jit(solution)/shard_map/pallas_call | solution.py:97
  168.0 7.3 %all-gather.2 = f32[1024,128]{1,0:T(8,128)S(1)} all-gather(f32[256,128]{1,0:T(8,128)S(1)} %shard_map.134), channel_id=4, replica_groups={{0,4,8,12},{16,20,24,28},{32,36,40,44},{48,52,56,60},{64,68,72,76},{80,..., dimensions={0}, use_global_device_ids=true | all-gather | bytes 655360 | tf_op jit(solution)/shard_map/all_gather | solution.py:61
  175.3 3.6 %shard_map.133 = (f32[1024,128]{1,0:T(8,128)}, f32[256,128]{1,0:T(8,128)}, f32[256,128]{1,0:T(8,128)}, f32[256,128]{1,0:T(8,128)}, f32[256,128]{1,0:T(8,128)}) custom-call(s32[4]{0:T(128)S(1)} %pad_add_fusion.place, s32[1,1024]{1,0:T(1,128)S(1)} %copy-done.18, f32[1024,128]{1,0:T(8,128)S(1)} %copy-done.10, f32[1024,128]{1,0:T(8,128)} %collective-permute-done.9.p1, ...), custom_call_target="tpu_custom_call" | custom-call | tf_op jit(solution)/shard_map/pallas_call | solution.py:97
  178.8 1.0 copy-done.11
  179.9 6.6 %shard_map.135 = f32[1024,128]{1,0:T(8,128)} custom-call(s32[4]{0:T(128)S(1)} %pad_add_fusion.place, s32[64]{0:T(128)S(1)} %copy-done.20, s32[1,1024]{1,0:T(1,128)S(1)} %copy-done.18, f32[4,256,128]{2,1,0:T(8,128)S(1)} %bitcast.11, f32[1024,128]{1,0:T(8,128)S(1)} %copy-done.11, f32[1,1024,256]{2,1,0:T(8,128)} %basis.3, f32[1,1024,1024]{2,1,0:T(8,128)} %solve.3), custom_call_target="tpu_custom_call" | custom-call | tf_op jit(solution)/shard_map/pallas_call | solution.py:97
  186.5 3.5 %all-to-all-start.2 = ((f32[4,256,128]{2,1,0:T(8,128)}), f32[4,256,128]{2,1,0:T(8,128)S(1)}, u32[]{:S(2)}, u32[]{:S(2)}) async-start(f32[4,256,128]{2,1,0:T(8,128)} %bitcast.9), calls=%async_computation.2 | async-start | bytes 1048576 | tf_op jit(solution)/shard_map/all_to_all | solution.py:584
  190.0 1.4 collective-permute-start.24
  191.4 2.4 %collective-permute-start.25 = (f32[256,128]{1,0:T(8,128)S(1)}, f32[256,128]{1,0:T(8,128)S(1)}, u32[]{:S(2)}, u32[]{:S(2)}) collective-permute-start(f32[256,128]{1,0:T(8,128)S(1)} %copy-done.25), channel_id=1, source_target_pairs={{0,2},{1,3},{2,0},{3,1},{4,6},{5,7},{6,4},{7,5},{8,10},{9,11},{10,... | collective-permute-start | bytes 393224 | tf_op jit(solution)/shard_map/ppermute | solution.py:57
  193.8 1.2 collective-permute-start.26
  195.0 6.9 %collective-permute-done.24.r1 = f32[256,128]{1,0:T(8,128)S(1)} collective-permute-done((f32[256,128]{1,0:T(8,128)S(1)}, f32[256,128]{1,0:T(8,128)S(1)}, u32[]{:S(2)}, u32[]{:S(2)}) %collective-permute-start.24) | collective-permute-done | bytes 131104 | tf_op jit(solution)/shard_map/ppermute | solution.py:57
  201.9 3.1 %collective-permute-done.25.r2 = f32[256,128]{1,0:T(8,128)S(1)} collective-permute-done((f32[256,128]{1,0:T(8,128)S(1)}, f32[256,128]{1,0:T(8,128)S(1)}, u32[]{:S(2)}, u32[]{:S(2)}) %collective-permute-start.25) | collective-permute-done | bytes 131104 | tf_op jit(solution)/shard_map/ppermute | solution.py:57
  205.0 1.6 outputs.1
  (72 shorter events, 0.2 us)
Async XLA Ops:
  0.6 14.8 %copy-start.21 = (f32[256,128]{1,0:T(8,128)S(1)}, f32[256,128]{1,0:T(8,128)}, u32[]{:S(2)}) copy-start(f32[256,128]{1,0:T(8,128)} %x0.1) | copy-start | bytes 393220
  2.7 40.4 %collective-permute-start.3 = (f32[256,640]{1,0:T(8,128)}, f32[256,640]{1,0:T(8,128)}, u32[]{:S(2)}, u32[]{:S(2)}) collective-permute-start(f32[256,640]{1,0:T(8,128)} %shard_map.122.p0), channel_id=1, source_target_pairs={{0,4},{4,0},{8,12},{12,8},{16,20},{20,16},{24,28},{28,24},{32,36},... | collective-permute-start | bytes 1966088 | tf_op jit(solution)/shard_map/ppermute | solution.py:31
  5.9 37.1 %copy-start.19 = (s32[1,5]{1,0:T(1,128)S(1)}, s32[1,5]{1,0:T(1,128)}, u32[]{:S(2)}) copy-start(s32[1,5]{1,0:T(1,128)} %mask.3) | copy-start | bytes 64
  7.5 35.6 %copy-start.4 = (f32[256,640]{1,0:T(8,128)S(1)}, f32[256,640]{1,0:T(8,128)}, u32[]{:S(2)}) copy-start(f32[256,640]{1,0:T(8,128)} %shard_map.122.p0) | copy-start | bytes 1966084
  7.5 6.9 %collective-permute-start.7 = (f32[128,256]{1,0:T(8,128)}, f32[128,256]{1,0:T(8,128)S(1)}, u32[]{:S(2)}, u32[]{:S(2)}) collective-permute-start(f32[128,256]{1,0:T(8,128)} %shard_map.124.slices), channel_id=1, source_target_pairs={{0,32},{4,36},{8,40},{12,44},{16,48},{20,52},{24,56},{28,60},{32,0... | collective-permute-start | bytes 393224 | tf_op jit(solution)/shard_map/ppermute | solution.py:31
  7.6 43.1 %collective-permute-start.1 = (f32[256,640]{1,0:T(8,128)}, f32[256,640]{1,0:T(8,128)S(1)}, u32[]{:S(2)}, u32[]{:S(2)}) collective-permute-start(f32[256,640]{1,0:T(8,128)} %shard_map.122.p0), channel_id=1, source_target_pairs={{0,248},{4,252},{8,0},{12,4},{16,8},{20,12},{24,16},{28,20},{32,24... | collective-permute-start | bytes 1966088 | tf_op jit(solution)/shard_map/ppermute | solution.py:31
  14.4 36.4 %collective-permute-start = (f32[256,640]{1,0:T(8,128)}, f32[256,640]{1,0:T(8,128)S(1)}, u32[]{:S(2)}, u32[]{:S(2)}) collective-permute-start(f32[256,640]{1,0:T(8,128)} %shard_map.122.p0), channel_id=1, source_target_pairs={{0,8},{4,12},{8,16},{12,20},{16,24},{20,28},{24,32},{28,36},{32,40... | collective-permute-start | bytes 1966088 | tf_op jit(solution)/shard_map/ppermute | solution.py:31
  14.4 0.9 copy-start.9
  15.3 25.5 %copy-start.7 = (f32[256,256]{1,0:T(8,128)}, f32[256,256]{1,0:T(8,128)S(1)}, u32[]{:S(2)}) copy-start(f32[256,256]{1,0:T(8,128)S(1)} %shard_map.125.pair) | copy-start | bytes 786436
  15.3 22.6 %collective-permute-start.8 = (f32[256,256]{1,0:T(8,128)S(1)}, f32[256,256]{1,0:T(8,128)S(1)}, u32[]{:S(2)}, u32[]{:S(2)}) collective-permute-start(f32[256,256]{1,0:T(8,128)S(1)} %shard_map.125.pair), channel_id=1, source_target_pairs={{0,24},{4,28},{8,16},{12,20},{16,8},{20,12},{24,0},{28,4},{32,56},... | collective-permute-start | bytes 786440 | tf_op jit(solution)/shard_map/ppermute | solution.py:31
  15.5 6.1 %collective-permute-start.5 = (f32[256,128]{1,0:T(8,128)S(1)}, f32[256,128]{1,0:T(8,128)S(1)}, u32[]{:S(2)}, u32[]{:S(2)}) collective-permute-start(f32[256,128]{1,0:T(8,128)S(1)} %copy-done.21), channel_id=1, source_target_pairs={{0,2},{1,3},{2,0},{3,1},{4,6},{5,7},{6,4},{7,5},{8,10},{9,11},{10,... | collective-permute-start | bytes 393224 | tf_op jit(solution)/shard_map/ppermute | solution.py:57
  21.5 21.5 %copy-start.23 = (f32[256,128]{1,0:T(8,128)}, f32[256,128]{1,0:T(8,128)S(1)}, u32[]{:S(2)}) copy-start(f32[256,128]{1,0:T(8,128)S(1)} %collective-permute-done.5.x2) | copy-start | bytes 393220
  21.5 21.5 %collective-permute-start.4 = (f32[256,128]{1,0:T(8,128)S(1)}, f32[256,128]{1,0:T(8,128)}, u32[]{:S(2)}, u32[]{:S(2)}) collective-permute-start(f32[256,128]{1,0:T(8,128)S(1)} %copy-done.21), channel_id=1, source_target_pairs={{0,1},{1,2},{2,3},{3,0},{4,5},{5,6},{6,7},{7,4},{8,9},{9,10},{10,1... | collective-permute-start | bytes 393224 | tf_op jit(solution)/shard_map/ppermute | solution.py:57
  38.0 2.8 %copy-start.22 = (f32[256,256]{1,0:T(8,128)}, f32[256,256]{1,0:T(8,128)S(1)}, u32[]{:S(2)}) copy-start(f32[256,256]{1,0:T(8,128)S(1)} %collective-permute-done.8.mirrored) | copy-start | bytes 786436
  38.0 5.1 %collective-permute-start.6 = (f32[256,128]{1,0:T(8,128)S(1)}, f32[256,128]{1,0:T(8,128)}, u32[]{:S(2)}, u32[]{:S(2)}) collective-permute-start(f32[256,128]{1,0:T(8,128)S(1)} %copy-done.21), channel_id=1, source_target_pairs={{0,3},{1,0},{2,1},{3,2},{4,7},{5,4},{6,5},{7,6},{8,11},{9,8},{10,9... | collective-permute-start | bytes 393224 | tf_op jit(solution)/shard_map/ppermute | solution.py:57
  43.0 9.8 %copy-start.2 = (f32[1024,256]{1,0:T(8,128)S(1)}, f32[1024,256]{1,0:T(8,128)}, u32[]{:S(2)}) copy-start(f32[1024,256]{1,0:T(8,128)} %shard_map.126.b0) | copy-start | bytes 3145732
  43.0 34.3 %copy-start.18 = (s32[1,1024]{1,0:T(1,128)S(1)}, s32[1,1024]{1,0:T(1,128)}, u32[]{:S(2)}) copy-start(s32[1,1024]{1,0:T(1,128)} %order.5) | copy-start | bytes 12292
  49.4 1.4 copy-start.5
  50.8 23.1 %collective-permute-start.16 = (f32[1024,256]{1,0:T(8,128)}, f32[1024,256]{1,0:T(8,128)}, u32[]{:S(2)}, u32[]{:S(2)}) collective-permute-start(f32[1024,256]{1,0:T(8,128)} %shard_map.126.b0), channel_id=1, source_target_pairs={{0,8},{4,12},{8,0},{12,4},{16,24},{20,28},{24,16},{28,20},{32,40},... | collective-permute-start | bytes 3145736 | tf_op jit(solution)/shard_map/ppermute | solution.py:31
  50.9 31.4 %collective-permute-start.2 = (f32[256,640]{1,0:T(8,128)S(1)}, f32[256,640]{1,0:T(8,128)S(1)}, u32[]{:S(2)}, u32[]{:S(2)}) collective-permute-start(f32[256,640]{1,0:T(8,128)S(1)} %broadcast_select_fusion), channel_id=1, source_target_pairs={{0,4},{4,0},{8,12},{12,8},{16,20},{20,16},{24,28},{28,24},{32,36},... | collective-permute-start | bytes 1966088 | tf_op jit(solution)/shard_map/ppermute | solution.py:31
  52.8 68.6 %collective-permute-start.15 = (f32[1024,256]{1,0:T(8,128)S(1)}, f32[1024,256]{1,0:T(8,128)}, u32[]{:S(2)}, u32[]{:S(2)}) collective-permute-start(f32[1024,256]{1,0:T(8,128)S(1)} %copy-done.2), channel_id=1, source_target_pairs={{0,4},{4,0},{8,12},{12,8},{16,20},{20,16},{24,28},{28,24},{32,36},... | collective-permute-start | bytes 3145736 | tf_op jit(solution)/shard_map/ppermute | solution.py:31
  73.9 52.5 %collective-permute-start.17 = (f32[1024,256]{1,0:T(8,128)}, f32[1024,256]{1,0:T(8,128)}, u32[]{:S(2)}, u32[]{:S(2)}) collective-permute-start(f32[1024,256]{1,0:T(8,128)} %collective-permute-done.16.b2), channel_id=1, source_target_pairs={{0,4},{4,0},{8,12},{12,8},{16,20},{20,16},{24,28},{28,24},{32,36},... | collective-permute-start | bytes 3145736 | tf_op jit(solution)/shard_map/ppermute | solution.py:31
  77.3 4.9 %copy-start.1 = (f32[256,512]{1,0:T(8,128)S(1)}, f32[256,512]{1,0:T(8,128)}, u32[]{:S(2)}) copy-start(f32[256,512]{1,0:T(8,128)} %coefs.1) | copy-start | bytes 1572868
  77.3 4.9 %copy-start.6 = (f32[1024,512]{1,0:T(8,128)S(1)}, f32[1024,512]{1,0:T(8,128)}, u32[]{:S(2)}) copy-start(f32[1024,512]{1,0:T(8,128)} %copy-done.5) | copy-start | bytes 6291460
  77.3 4.9 %copy-start.12 = (f32[256,512]{1,0:T(8,128)S(1)}, f32[256,512]{1,0:T(8,128)}, u32[]{:S(2)}) copy-start(f32[256,512]{1,0:T(8,128)} %own_y.1) | copy-start | bytes 1572868
  77.3 4.9 %copy-start.13 = (bf16[4,256,256]{2,1,0:T(8,128)(2,1)S(1)}, bf16[4,256,256]{2,1,0:T(8,128)(2,1)}, u32[]{:S(2)}) copy-start(bf16[4,256,256]{2,1,0:T(8,128)(2,1)} %get-tuple-element.37.split_rows) | copy-start | bytes 1572868
  77.4 4.9 %copy-start.14 = (f32[4,256,1]{2,1,0:T(8,128)S(1)}, f32[4,256,1]{2,1,0:T(8,128)}, u32[]{:S(2)}) copy-start(f32[4,256,1]{2,1,0:T(8,128)} %get-tuple-element.38.norms) | copy-start | bytes 12292
  90.4 21.9 %copy-start = (f32[1,336,1024]{2,1,0:T(8,128)S(1)}, f32[1,336,1024]{2,1,0:T(8,128)}, u32[]{:S(2)}) copy-start(f32[1,336,1024]{2,1,0:T(8,128)} %m1.3) | copy-start | bytes 4128772
  90.4 21.9 %copy-start.3 = (f32[1,336,256]{2,1,0:T(8,128)S(1)}, f32[1,336,256]{2,1,0:T(8,128)}, u32[]{:S(2)}) copy-start(f32[1,336,256]{2,1,0:T(8,128)} %e1.1) | copy-start | bytes 1032196
  90.5 21.9 %copy-start.20 = (s32[64]{0:T(128)S(1)}, s32[64]{0:T(128)}, u32[]{:S(2)}) copy-start(s32[64]{0:T(128)} %leaf_map.3) | copy-start | bytes 772
  113.8 0.7 copy-start.17
  113.8 15.7 %copy-start.15 = (f32[256,128]{1,0:T(8,128)}, f32[256,128]{1,0:T(8,128)S(1)}, u32[]{:S(2)}) copy-start(f32[256,128]{1,0:T(8,128)S(1)} %get-tuple-element.62.w1) | copy-start | bytes 393220
  114.4 7.0 %all-to-all-start.1 = ((f32[4,32,256]{2,1,0:T(8,128)}), f32[4,32,256]{2,1,0:T(8,128)S(1)}, u32[]{:S(2)}, u32[]{:S(2)}) async-start(f32[4,32,256]{2,1,0:T(8,128)} %bitcast.14), calls=%async_computation.1 | async-start | bytes 262144 | tf_op jit(solution)/shard_map/all_to_all | solution.py:635
  117.9 35.3 %collective-permute-start.9 = (f32[1024,128]{1,0:T(8,128)}, f32[1024,128]{1,0:T(8,128)}, u32[]{:S(2)}, u32[]{:S(2)}) collective-permute-start(f32[1024,128]{1,0:T(8,128)} %get-tuple-element.40), channel_id=1, source_target_pairs={{0,1},{1,2},{2,3},{3,0},{4,5},{5,6},{6,7},{7,4},{8,9},{9,10},{10,1... | collective-permute-start | bytes 1572872 | tf_op jit(solution)/shard_map/ppermute | solution.py:57
  118.2 35.0 %collective-permute-start.10 = (f32[1024,128]{1,0:T(8,128)}, f32[1024,128]{1,0:T(8,128)}, u32[]{:S(2)}, u32[]{:S(2)}) collective-permute-start(f32[1024,128]{1,0:T(8,128)} %get-tuple-element.41), channel_id=1, source_target_pairs={{0,2},{1,3},{2,0},{3,1},{4,6},{5,7},{6,4},{7,5},{8,10},{9,11},{10,... | collective-permute-start | bytes 1572872 | tf_op jit(solution)/shard_map/ppermute | solution.py:57
  120.0 33.2 %collective-permute-start.11 = (f32[1024,128]{1,0:T(8,128)}, f32[1024,128]{1,0:T(8,128)}, u32[]{:S(2)}, u32[]{:S(2)}) collective-permute-start(f32[1024,128]{1,0:T(8,128)} %get-tuple-element.42), channel_id=1, source_target_pairs={{0,3},{1,0},{2,1},{3,2},{4,7},{5,4},{6,5},{7,6},{8,11},{9,8},{10,9... | collective-permute-start | bytes 1572872 | tf_op jit(solution)/shard_map/ppermute | solution.py:57
  121.5 5.0 %collective-permute-start.14 = (f32[32,256]{1,0:T(8,128)S(1)}, f32[32,256]{1,0:T(8,128)S(1)}, u32[]{:S(2)}, u32[]{:S(2)}) collective-permute-start(f32[32,256]{1,0:T(8,128)S(1)} %fusion.1.r0), channel_id=1, source_target_pairs={{0,56},{4,60},{8,48},{12,52},{16,40},{20,44},{24,32},{28,36},{32,2... | collective-permute-start | bytes 98312 | tf_op jit(solution)/shard_map/ppermute | solution.py:31
  126.4 3.2 %collective-permute-start.13 = (f32[32,256]{1,0:T(8,128)S(1)}, f32[32,256]{1,0:T(8,128)S(1)}, u32[]{:S(2)}, u32[]{:S(2)}) collective-permute-start(f32[32,256]{1,0:T(8,128)S(1)} %fusion.1.r0), channel_id=1, source_target_pairs={{0,32},{4,36},{8,40},{12,44},{16,48},{20,52},{24,56},{28,60},{32,0... | collective-permute-start | bytes 98312 | tf_op jit(solution)/shard_map/ppermute | solution.py:31
  126.4 4.4 %collective-permute-start.12 = (f32[32,256]{1,0:T(8,128)S(1)}, f32[32,256]{1,0:T(8,128)S(1)}, u32[]{:S(2)}, u32[]{:S(2)}) collective-permute-start(f32[32,256]{1,0:T(8,128)S(1)} %fusion.1.r0), channel_id=1, source_target_pairs={{0,24},{4,28},{8,16},{12,20},{16,8},{20,12},{24,0},{28,4},{32,56},... | collective-permute-start | bytes 98312 | tf_op jit(solution)/shard_map/ppermute | solution.py:31
  129.5 35.3 %copy-start.8 = (f32[1024,256]{1,0:T(8,128)}, f32[1024,256]{1,0:T(8,128)S(1)}, u32[]{:S(2)}) copy-start(f32[1024,256]{1,0:T(8,128)S(1)} %get-tuple-element.61.e1) | copy-start | bytes 3145732
  131.6 5.3 %collective-permute-start.20 = (f32[32,256]{1,0:T(8,128)S(1)}, f32[32,256]{1,0:T(8,128)S(1)}, u32[]{:S(2)}, u32[]{:S(2)}) collective-permute-start(f32[32,256]{1,0:T(8,128)S(1)} %get-tuple-element.48), channel_id=1, source_target_pairs={{0,56},{4,60},{8,48},{12,52},{16,40},{20,44},{24,32},{28,36},{32,2... | collective-permute-start | bytes 98312 | tf_op jit(solution)/shard_map/ppermute | solution.py:31
  133.9 4.1 %collective-permute-start.19 = (f32[32,256]{1,0:T(8,128)S(1)}, f32[32,256]{1,0:T(8,128)S(1)}, u32[]{:S(2)}, u32[]{:S(2)}) collective-permute-start(f32[32,256]{1,0:T(8,128)S(1)} %get-tuple-element.48), channel_id=1, source_target_pairs={{0,32},{4,36},{8,40},{12,44},{16,48},{20,52},{24,56},{28,60},{32,0... | collective-permute-start | bytes 98312 | tf_op jit(solution)/shard_map/ppermute | solution.py:31
  136.9 4.4 %collective-permute-start.18 = (f32[32,256]{1,0:T(8,128)S(1)}, f32[32,256]{1,0:T(8,128)S(1)}, u32[]{:S(2)}, u32[]{:S(2)}) collective-permute-start(f32[32,256]{1,0:T(8,128)S(1)} %get-tuple-element.48), channel_id=1, source_target_pairs={{0,24},{4,28},{8,16},{12,20},{16,8},{20,12},{24,0},{28,4},{32,56},... | collective-permute-start | bytes 98312 | tf_op jit(solution)/shard_map/ppermute | solution.py:31
  141.3 5.9 %collective-permute-start.23 = (f32[32,256]{1,0:T(8,128)S(1)}, f32[32,256]{1,0:T(8,128)S(1)}, u32[]{:S(2)}, u32[]{:S(2)}) collective-permute-start(f32[32,256]{1,0:T(8,128)S(1)} %add_add_fusion.r0), channel_id=1, source_target_pairs={{160,0},{164,4},{168,8},{172,12},{176,16},{180,20},{184,24},{188,2... | collective-permute-start | bytes 98312 | tf_op jit(solution)/shard_map/ppermute | solution.py:53
  145.2 5.2 %collective-permute-start.22 = (f32[32,256]{1,0:T(8,128)S(1)}, f32[32,256]{1,0:T(8,128)S(1)}, u32[]{:S(2)}, u32[]{:S(2)}) collective-permute-start(f32[32,256]{1,0:T(8,128)S(1)} %add_add_fusion.r0), channel_id=1, source_target_pairs={{64,0},{68,4},{72,8},{76,12},{80,16},{84,20},{88,24},{92,28},{224,... | collective-permute-start | bytes 98312 | tf_op jit(solution)/shard_map/ppermute | solution.py:53
  147.2 5.1 %collective-permute-start.21 = (f32[32,256]{1,0:T(8,128)S(1)}, f32[32,256]{1,0:T(8,128)S(1)}, u32[]{:S(2)}, u32[]{:S(2)}) collective-permute-start(f32[32,256]{1,0:T(8,128)S(1)} %add_add_fusion.r0), channel_id=1, source_target_pairs={{224,0},{228,4},{232,8},{236,12},{240,16},{244,20},{248,24},{252,2... | collective-permute-start | bytes 98312 | tf_op jit(solution)/shard_map/ppermute | solution.py:53
  153.1 22.1 %copy-start.10 = (f32[1024,128]{1,0:T(8,128)S(1)}, f32[1024,128]{1,0:T(8,128)}, u32[]{:S(2)}) copy-start(f32[1024,128]{1,0:T(8,128)} %get-tuple-element.52.p0) | copy-start | bytes 1572868
  178.8 1.0 copy-start.11
  179.9 10.1 %copy-start.26 = (f32[256,128]{1,0:T(8,128)S(1)}, f32[256,128]{1,0:T(8,128)}, u32[]{:S(2)}) copy-start(f32[256,128]{1,0:T(8,128)} %get-tuple-element.57) | copy-start | bytes 393220
  179.9 11.5 %copy-start.25 = (f32[256,128]{1,0:T(8,128)S(1)}, f32[256,128]{1,0:T(8,128)}, u32[]{:S(2)}) copy-start(f32[256,128]{1,0:T(8,128)} %get-tuple-element.58) | copy-start | bytes 393220
  179.9 13.9 %copy-start.24 = (f32[256,128]{1,0:T(8,128)S(1)}, f32[256,128]{1,0:T(8,128)}, u32[]{:S(2)}) copy-start(f32[256,128]{1,0:T(8,128)} %get-tuple-element.59) | copy-start | bytes 393220
  179.9 25.1 %copy-start.16 = (f32[256,128]{1,0:T(8,128)S(1)}, f32[256,128]{1,0:T(8,128)}, u32[]{:S(2)}) copy-start(f32[256,128]{1,0:T(8,128)} %get-tuple-element.56.r0) | copy-start | bytes 393220
  186.5 18.5 %all-to-all-start.2 = ((f32[4,256,128]{2,1,0:T(8,128)}), f32[4,256,128]{2,1,0:T(8,128)S(1)}, u32[]{:S(2)}, u32[]{:S(2)}) async-start(f32[4,256,128]{2,1,0:T(8,128)} %bitcast.9), calls=%async_computation.2 | async-start | bytes 1048576 | tf_op jit(solution)/shard_map/all_to_all | solution.py:584
  190.0 11.9 %collective-permute-start.24 = (f32[256,128]{1,0:T(8,128)S(1)}, f32[256,128]{1,0:T(8,128)S(1)}, u32[]{:S(2)}, u32[]{:S(2)}) collective-permute-start(f32[256,128]{1,0:T(8,128)S(1)} %copy-done.26), channel_id=1, source_target_pairs={{0,1},{1,2},{2,3},{3,0},{4,5},{5,6},{6,7},{7,4},{8,9},{9,10},{10,1... | collective-permute-start | bytes 393224 | tf_op jit(solution)/shard_map/ppermute | solution.py:57
  191.4 13.6 %collective-permute-start.25 = (f32[256,128]{1,0:T(8,128)S(1)}, f32[256,128]{1,0:T(8,128)S(1)}, u32[]{:S(2)}, u32[]{:S(2)}) collective-permute-start(f32[256,128]{1,0:T(8,128)S(1)} %copy-done.25), channel_id=1, source_target_pairs={{0,2},{1,3},{2,0},{3,1},{4,6},{5,7},{6,4},{7,5},{8,10},{9,11},{10,... | collective-permute-start | bytes 393224 | tf_op jit(solution)/shard_map/ppermute | solution.py:57
  193.8 11.2 %collective-permute-start.26 = (f32[256,128]{1,0:T(8,128)S(1)}, f32[256,128]{1,0:T(8,128)S(1)}, u32[]{:S(2)}, u32[]{:S(2)}) collective-permute-start(f32[256,128]{1,0:T(8,128)S(1)} %copy-done.24), channel_id=1, source_target_pairs={{0,3},{1,0},{2,1},{3,2},{4,7},{5,4},{6,5},{7,6},{8,11},{9,8},{10,9... | collective-permute-start | bytes 393224 | tf_op jit(solution)/shard_map/ppermute | solution.py:57

commit v6 on v5

--- a/solution.py
+++ b/solution.py
@@ -341,6 +341,10 @@
     run_copies(sems, [(buffer, out)])
 
 
+def sum_kernel(parts, out):
+    out[...] = parts[0] + parts[1] + (parts[2] + parts[3])
+
+
 def assemble(body, shape, count, *parts):
     return kernel(
         body,
@@ -357,17 +361,33 @@
     out[128:, :] = lower[...]
 
 
-def held_kernel(transfer, inverse, pair, mirrored, out, buffer, sems):
-    moves = [
-        (transfer.at[0, pl.ds(0, 256), :], buffer.at[pl.ds(0, 256), :]),
-        (pair, buffer.at[pl.ds(512, 256), :]),
-        (mirrored, buffer.at[pl.ds(768, 256), :]),
-    ]
+def held_kernel(pair, mirrored, transfer, inverse, out, buffer, sems):
+    moves = [(transfer.at[0, pl.ds(0, 256), :], buffer.at[pl.ds(0, 256), :])]
     for k in range(4):
         source = inverse.at[0, pl.ds(256, 64), pl.ds(k * 256, 256)]
         moves.append((source, buffer.at[pl.ds(256 + k * 64, 64), :]))
-    run_copies(sems, moves)
+    copies = [
+        pltpu.make_async_copy(source, target, sems.at[k])
+        for k, (source, target) in enumerate(moves)
+    ]
+    for copy in copies:
+        copy.start()
+    buffer[512:768, :] = pair[...]
+    buffer[768:, :] = mirrored[...]
+    for copy in copies:
+        copy.wait()
     run_copies(sems, [(buffer, out)])
+
+
+def held_call(pair, mirrored, transfer, inverse):
+    return kernel(
+        held_kernel,
+        [],
+        [pair, mirrored],
+        scratch=[pltpu.VMEM((1024, 256), F32), pltpu.SemaphoreType.DMA((5,))],
+        far_values=[transfer, inverse],
+        far_outs=[(1024, 256)],
+    )
 
 
 def nodes_kernel(place, b0, b1, b2, b3, e1, m2, f2, m3, own_e2, e2):
@@ -613,12 +633,11 @@
     lower = leaf_route(slices, lambda i: facing(i, 0, 1))
     pair = kernel(pair_kernel, [(256, 256)], [slices, lower])
     mirrored = leaf_route(pair, lambda i: facing(i, 1, 0))
-    held = assemble(held_kernel, (1024, 256), 7, *nodes, pair, mirrored)
+    held = held_call(pair, mirrored, *nodes)
 
     lead = lead_call(cluster_perm, leaf_basis, leaf_inverse)
 
     near = near_call(place, tile_mask, xs, (packed, partner))
-    near, held = lax.optimization_barrier((near, held))
     across = leaf_xor(held, 2)
     own_core = leaf_xor(held, 1)
     both_ways = leaf_xor(across, 1)
@@ -626,7 +645,7 @@
         place, tile_mask, ridge, (left, right, relay), near, targets, coefs, lead
     )
     led = swap_cols(led)
-    reduced = led.sum(0)
+    reduced = kernel(sum_kernel, [(RANK, 128)], [led])
     e1, m2, f2, m3, e2 = nodes_call(place, (held, own_core, across, both_ways))
 
     columns = [partial[0]] + [col_shift(partial[d], d) for d in (1, 2, 3)]

time: 207 us -> 198 us (0.957)
  waiting for transfers between devices: 66.4 us -> 50.2 us
  starting transfers between devices: 47.6 us -> 51.6 us
    ppermute x15, waiting for transfers between devices: 48.7 us -> 30.6 us  [leaf_route(): return lax.ppermute(value, 'leaf', [(i, target(i)) for i in range(LEAVES)])]
    ppermute x15, starting transfers between devices: 18.8 us -> 24.4 us  [leaf_route(): return lax.ppermute(value, 'leaf', [(i, target(i)) for i in range(LEAVES)])]
    ppermute x9, starting transfers between devices: 14.8 us -> 11.6 us  [col_shift(): return lax.ppermute(value, 'col', [(i, (i + step) % 4) for i in range(4)])]
    unnamed x54 -> x44, local copies, waits for them, and re-layouts: 4.05 us -> 5.77 us
    pallas_call x14 -> x15, Pallas kernels: 44.3 us -> 44.9 us  [kernel(): pl.pallas_call(body, in_specs=[SMEM] * len(scalars) + [VMEM] * len(values...]
  transfers between devices with their start and end apart: 29 -> 29, of which waited for: 13 -> 13; matrix products, arithmetic and copies ran while one was open for 1% -> 1% of each run, Pallas kernels for 14% -> 15%
where the time goes in v6:
time: 198 us; the launch traced here: 197 us
  starting transfers between devices  51.6 us (26%)
  waiting for transfers between devices  50.2 us (25%)
  Pallas kernels  46.6 us (24%)
  blocking collectives  40.3 us (20%)
  local copies, waits for them, and re-layouts  5.77 us (3%)
    pallas_call x15, Pallas kernels, kernel(): pl.pallas_call(body, in_specs=[SMEM] * len(scalars) + [VMEM] * len(values...  44.9 us
    ppermute x15, waiting for transfers between devices, leaf_route(): return lax.ppermute(value, 'leaf', [(i, target(i)) for i in range(LEAVES)])  30.6 us
    all_gather x3, blocking collectives, gather4(): return lax.all_gather(value, 'leaf', axis=0, axis_index_groups=groups)  26.9 us
    ppermute x15, starting transfers between devices, leaf_route(): return lax.ppermute(value, 'leaf', [(i, target(i)) for i in range(LEAVES)])  24.4 us
    ppermute x9, waiting for transfers between devices, col_shift(): return lax.ppermute(value, 'col', [(i, (i + step) % 4) for i in range(4)])  14.9 us
    all_to_all x1, blocking collectives, swap_cols(): return lax.all_to_all(value, 'col', 0, 0, tiled=True)  13.4 us
    ppermute x9, starting transfers between devices, col_shift(): return lax.ppermute(value, 'col', [(i, (i + step) % 4) for i in range(4)])  11.6 us
    ppermute x3, starting transfers between devices, z_from(): return lax.ppermute(value, 'leaf', route)  8.59 us
  transfers between devices with their start and end apart: 29, of which 13 were waited for; matrix products, arithmetic and copies ran while one was open for 1% of the time, Pallas kernels for 15%

profile of v6, /device:TPU:1, one launch (start us, length us, event | category | flops | bytes accessed | tf_op | source)
XLA Modules:
  0.0 197.1 jit_solution(15789315938032913152)
XLA Ops:
  0.6 2.0 shard_map.122.p0
  2.6 2.1 %collective-permute-start = (f32[256,640]{1,0:T(8,128)}, f32[256,640]{1,0:T(8,128)S(1)}, u32[]{:S(2)}, u32[]{:S(2)}) collective-permute-start(f32[256,640]{1,0:T(8,128)} %shard_map.122.p0), channel_id=1, source_target_pairs={{0,8},{4,12},{8,16},{12,20},{16,24},{20,28},{24,32},{28,36},{32,40... | collective-permute-start | bytes 1966088 | tf_op jit(solution)/shard_map/ppermute | solution.py:31
  4.7 6.6 %collective-permute-start.1 = (f32[256,640]{1,0:T(8,128)}, f32[256,640]{1,0:T(8,128)S(1)}, u32[]{:S(2)}, u32[]{:S(2)}) collective-permute-start(f32[256,640]{1,0:T(8,128)} %shard_map.122.p0), channel_id=1, source_target_pairs={{0,248},{4,252},{8,0},{12,4},{16,8},{20,12},{24,16},{28,20},{32,24... | collective-permute-start | bytes 1966088 | tf_op jit(solution)/shard_map/ppermute | solution.py:31
  11.4 1.5 shard_map.128.slices
  12.9 0.1 collective-permute-start.13
  13.0 12.6 %collective-permute-done.13.lower = f32[128,256]{1,0:T(8,128)S(1)} collective-permute-done((f32[128,256]{1,0:T(8,128)}, f32[128,256]{1,0:T(8,128)S(1)}, u32[]{:S(2)}, u32[]{:S(2)}) %collective-permute-start.13) | collective-permute-done | bytes 131104 | tf_op jit(solution)/shard_map/ppermute | solution.py:31
  25.6 0.9 copy-done.6
  26.5 0.1 collective-permute-start.14
  26.6 7.3 %collective-permute-done.14.mirrored = f32[256,256]{1,0:T(8,128)S(1)} collective-permute-done((f32[256,256]{1,0:T(8,128)S(1)}, f32[256,256]{1,0:T(8,128)S(1)}, u32[]{:S(2)}, u32[]{:S(2)}) %collective-permute-start.14) | collective-permute-done | bytes 262176 | tf_op jit(solution)/shard_map/ppermute | solution.py:31
  33.9 2.1 %shard_map.130.b0 = f32[1024,256]{1,0:T(8,128)} custom-call(f32[256,256]{1,0:T(8,128)S(1)} %shard_map.129.pair, f32[256,256]{1,0:T(8,128)S(1)} %collective-permute-done.14.mirrored, f32[1,336,256]{2,1,0:T(8,128)} %transfer.3, f32[1,336,1024]{2,1,0:T(8,128)} %m1.3), custom_call_target="tpu_custom_call" | custom-call | tf_op jit(solution)/shard_map/pallas_call | solution.py:97
  36.0 0.1 collective-permute-start.16
  36.1 2.8 %collective-permute-start.3 = (f32[256,640]{1,0:T(8,128)S(1)}, f32[256,640]{1,0:T(8,128)}, u32[]{:S(2)}, u32[]{:S(2)}) collective-permute-start(f32[256,640]{1,0:T(8,128)S(1)} %copy-done.4), channel_id=1, source_target_pairs={{0,4},{4,0},{8,12},{12,8},{16,20},{20,16},{24,28},{28,24},{32,36},... | collective-permute-start | bytes 1966088 | tf_op jit(solution)/shard_map/ppermute | solution.py:31
  38.9 0.9 broadcast_select_fusion
  39.8 1.3 collective-permute-start.4
  41.1 2.6 %collective-permute-start.5 = (f32[256,128]{1,0:T(8,128)}, f32[256,128]{1,0:T(8,128)S(1)}, u32[]{:S(2)}, u32[]{:S(2)}) collective-permute-start(f32[256,128]{1,0:T(8,128)} %x0.1), channel_id=1, source_target_pairs={{0,2},{1,3},{2,0},{3,1},{4,6},{5,7},{6,4},{7,5},{8,10},{9,11},{10,... | collective-permute-start | bytes 393224 | tf_op jit(solution)/shard_map/ppermute | solution.py:57
  43.7 2.2 %collective-permute-done.4.x1 = f32[256,128]{1,0:T(8,128)S(1)} collective-permute-done((f32[256,128]{1,0:T(8,128)}, f32[256,128]{1,0:T(8,128)S(1)}, u32[]{:S(2)}, u32[]{:S(2)}) %collective-permute-start.4) | collective-permute-done | bytes 131104 | tf_op jit(solution)/shard_map/ppermute | solution.py:57
  45.9 1.3 collective-permute-start.15
  47.2 2.7 %collective-permute-done.5.x2 = f32[256,128]{1,0:T(8,128)S(1)} collective-permute-done((f32[256,128]{1,0:T(8,128)}, f32[256,128]{1,0:T(8,128)S(1)}, u32[]{:S(2)}, u32[]{:S(2)}) %collective-permute-start.5) | collective-permute-done | bytes 131104 | tf_op jit(solution)/shard_map/ppermute | solution.py:57
  50.6 4.7 %shard_map.124.lead = f32[256,1024]{1,0:T(8,128)S(1)} custom-call(s32[1,1024]{1,0:T(1,128)S(1)} %copy-done.14, f32[1,1024,256]{2,1,0:T(8,128)} %basis.3, f32[1,1024,1024]{2,1,0:T(8,128)} %solve.3), custom_call_target="tpu_custom_call" | custom-call | tf_op jit(solution)/shard_map/pallas_call | solution.py:97
  55.3 3.0 %collective-permute-done.16.b2 = f32[1024,256]{1,0:T(8,128)S(1)} collective-permute-done((f32[1024,256]{1,0:T(8,128)}, f32[1024,256]{1,0:T(8,128)S(1)}, u32[]{:S(2)}, u32[]{:S(2)}) %collective-permute-start.16) | collective-permute-done | bytes 1048608 | tf_op jit(solution)/shard_map/ppermute | solution.py:31
  58.3 3.5 %collective-permute-start.17 = (f32[1024,256]{1,0:T(8,128)S(1)}, f32[1024,256]{1,0:T(8,128)}, u32[]{:S(2)}, u32[]{:S(2)}) collective-permute-start(f32[1024,256]{1,0:T(8,128)S(1)} %collective-permute-done.16.b2), channel_id=1, source_target_pairs={{0,4},{4,0},{8,12},{12,8},{16,20},{20,16},{24,28},{28,24},{32,36},... | collective-permute-start | bytes 3145736 | tf_op jit(solution)/shard_map/ppermute | solution.py:31
  61.9 6.3 %shard_map.123 = (f32[1024,512]{1,0:T(8,128)S(1)}, bf16[4,256,256]{2,1,0:T(8,128)(2,1)}, f32[4,256,1]{2,1,0:T(8,128)}) custom-call(s32[4]{0:T(128)S(1)} %pad_add_fusion.place, s32[1,5]{1,0:T(1,128)S(1)} %copy-done.15, f32[256,640]{1,0:T(8,128)S(1)} %copy-done.4, f32[256,640]{1,0:T(8,128)} %collective-permute-done.3.p1, f32[256,128]{1,0:T(8,128)} %x0.1, ...), custom_call_target="tpu_custom_call" | custom-call | tf_op jit(solution)/shard_map/pallas_call | solution.py:97
  68.2 1.0 copy-done.10
  69.3 1.0 copy-done.11
  70.3 8.8 %shard_map.125 = (f32[4,256,128]{2,1,0:T(8,128)S(1)}, f32[1024,128]{1,0:T(8,128)}, f32[1024,128]{1,0:T(8,128)}, f32[1024,128]{1,0:T(8,128)}, f32[1024,128]{1,0:T(8,128)}) custom-call(s32[4]{0:T(128)S(1)} %pad_add_fusion.place, s32[1,5]{1,0:T(1,128)S(1)} %copy-done.15, f32[1]{0:T(128)S(6)} %copy.13.ridge, f32[256,640]{1,0:T(8,128)S(1)} %collective-permute-done.p0, ...), custom_call_target="tpu_custom_call" | custom-call | tf_op jit(solution)/shard_map/pallas_call | solution.py:97
  79.2 13.4 %all_to_all.19.parts = f32[4,256,128]{2,1,0:T(8,128)S(1)} all-to-all(f32[4,256,128]{2,1,0:T(8,128)S(1)} %get-tuple-element.36), channel_id=1, replica_groups=mesh['leaf'=64,'col'=4] {'col'}, dimensions={0} | all-to-all | bytes 1048576 | tf_op jit(solution)/shard_map/all_to_all | solution.py:604
  92.6 7.6 %all-gather = f32[1024,128]{1,0:T(8,128)S(1)} all-gather(f32[256,128]{1,0:T(8,128)S(1)} %shard_map.126), channel_id=2, replica_groups={{0,4,8,12},{16,20,24,28},{32,36,40,44},{48,52,56,60},{64,68,72,76},{80,..., dimensions={0}, use_global_device_ids=true | all-gather | bytes 655360 | tf_op jit(solution)/shard_map/all_gather | solution.py:61
  100.3 2.1 %shard_map.127 = (f32[256,128]{1,0:T(8,128)S(1)}, f32[128,256]{1,0:T(8,128)}) custom-call(s32[4]{0:T(128)S(1)} %pad_add_fusion.place, s32[64]{0:T(128)S(1)} %copy-done.16, f32[4,256,128]{2,1,0:T(8,128)S(1)} %bitcast.12, f32[1,336,1024]{2,1,0:T(8,128)S(1)} %copy-done, f32[1,336,256]{2,1,0:T(8,128)S(1)} %copy-done.3), custom_call_target="tpu_custom_call" | custom-call | tf_op jit(solution)/shard_map/pallas_call | solution.py:97
  102.4 0.7 copy-done.12
  103.0 3.4 %all-to-all-start.1 = ((f32[4,32,256]{2,1,0:T(8,128)}), f32[4,32,256]{2,1,0:T(8,128)S(1)}, u32[]{:S(2)}, u32[]{:S(2)}) async-start(f32[4,32,256]{2,1,0:T(8,128)} %bitcast.5), calls=%async_computation.1 | async-start | bytes 262144 | tf_op jit(solution)/shard_map/all_to_all | solution.py:654
  106.5 0.3 collective-permute-start.7
  106.8 1.8 collective-permute-start.8
  108.5 0.7 collective-permute-start.9
  109.2 0.8 all-to-all-done.1
  110.1 0.4 collective-permute-start.10
  110.4 4.0 %collective-permute-done.10.r1 = f32[32,256]{1,0:T(8,128)S(1)} collective-permute-done((f32[32,256]{1,0:T(8,128)S(1)}, f32[32,256]{1,0:T(8,128)S(1)}, u32[]{:S(2)}, u32[]{:S(2)}) %collective-permute-start.10) | collective-permute-done | bytes 32800 | tf_op jit(solution)/shard_map/ppermute | solution.py:31
  114.4 1.5 collective-permute-start.12
  115.9 2.4 %shard_map.131 = (f32[1024,256]{1,0:T(8,128)S(1)}, f32[256,1024]{1,0:T(8,128)S(1)}, f32[256,256]{1,0:T(8,128)S(1)}, f32[256,1024]{1,0:T(8,128)S(1)}, f32[256,256]{1,0:T(8,128)S(1)}) custom-call(s32[4]{0:T(128)S(1)} %pad_add_fusion.place, f32[1024,256]{1,0:T(8,128)S(1)} %copy-done.2, f32[1024,256]{1,0:T(8,128)} %collective-permute-done.15.b1, ...), custom_call_target="tpu_custom_call" | custom-call | tf_op jit(solution)/shard_map/pallas_call | solution.py:97
  118.4 1.0 copy-done.5
  119.4 0.8 shard_map.132
  120.2 2.1 %collective-permute-start.20 = (f32[32,256]{1,0:T(8,128)S(1)}, f32[32,256]{1,0:T(8,128)S(1)}, u32[]{:S(2)}, u32[]{:S(2)}) collective-permute-start(f32[32,256]{1,0:T(8,128)S(1)} %get-tuple-element.40), channel_id=1, source_target_pairs={{0,56},{4,60},{8,48},{12,52},{16,40},{20,44},{24,32},{28,36},{32,2... | collective-permute-start | bytes 98312 | tf_op jit(solution)/shard_map/ppermute | solution.py:31
  122.3 1.5 collective-permute-start.19
  123.8 1.7 collective-permute-done.20
  125.5 2.4 %collective-permute-start.18 = (f32[32,256]{1,0:T(8,128)S(1)}, f32[32,256]{1,0:T(8,128)S(1)}, u32[]{:S(2)}, u32[]{:S(2)}) collective-permute-start(f32[32,256]{1,0:T(8,128)S(1)} %get-tuple-element.40), channel_id=1, source_target_pairs={{0,24},{4,28},{8,16},{12,20},{16,8},{20,12},{24,0},{28,4},{32,56},... | collective-permute-start | bytes 98312 | tf_op jit(solution)/shard_map/ppermute | solution.py:31
  127.9 2.0 %collective-permute-done.18 = f32[32,256]{1,0:T(8,128)S(1)} collective-permute-done((f32[32,256]{1,0:T(8,128)S(1)}, f32[32,256]{1,0:T(8,128)S(1)}, u32[]{:S(2)}, u32[]{:S(2)}) %collective-permute-start.18) | collective-permute-done | bytes 32800 | tf_op jit(solution)/shard_map/ppermute | solution.py:31
  129.9 5.1 %collective-permute-start.21 = (f32[32,256]{1,0:T(8,128)S(1)}, f32[32,256]{1,0:T(8,128)S(1)}, u32[]{:S(2)}, u32[]{:S(2)}) collective-permute-start(f32[32,256]{1,0:T(8,128)S(1)} %add_add_fusion.r0), channel_id=1, source_target_pairs={{224,0},{228,4},{232,8},{236,12},{240,16},{244,20},{248,24},{252,2... | collective-permute-start | bytes 98312 | tf_op jit(solution)/shard_map/ppermute | solution.py:53
  135.0 1.2 collective-permute-start.22
  136.2 0.1 collective-permute-done.21.r1
  136.3 2.3 %collective-permute-start.23 = (f32[32,256]{1,0:T(8,128)S(1)}, f32[32,256]{1,0:T(8,128)S(1)}, u32[]{:S(2)}, u32[]{:S(2)}) collective-permute-start(f32[32,256]{1,0:T(8,128)S(1)} %add_add_fusion.r0), channel_id=1, source_target_pairs={{160,0},{164,4},{168,8},{172,12},{176,16},{180,20},{184,24},{188,2... | collective-permute-start | bytes 98312 | tf_op jit(solution)/shard_map/ppermute | solution.py:53
  138.6 3.7 %collective-permute-done.23.r3 = f32[32,256]{1,0:T(8,128)S(1)} collective-permute-done((f32[32,256]{1,0:T(8,128)S(1)}, f32[32,256]{1,0:T(8,128)S(1)}, u32[]{:S(2)}, u32[]{:S(2)}) %collective-permute-start.23) | collective-permute-done | bytes 32800 | tf_op jit(solution)/shard_map/ppermute | solution.py:53
  142.3 0.9 shard_map.133
  143.3 12.0 %all-gather.1 = f32[128,256]{1,0:T(8,128)S(1)} all-gather(f32[32,256]{1,0:T(8,128)S(1)} %shard_map.133), channel_id=3, replica_groups={{0,4,8,12},{24,28,16,20},{32,36,40,44},{56,60,48,52},{64,68,72,76},{88,..., dimensions={0}, use_global_device_ids=true | all-gather | bytes 163840 | tf_op jit(solution)/shard_map/all_gather | solution.py:61
  155.3 3.2 %shard_map.135 = f32[256,128]{1,0:T(8,128)S(1)} custom-call(f32[4,32,256]{2,1,0:T(8,128)S(1)} %bitcast.13, f32[1024,256]{1,0:T(8,128)} %copy-done.5, f32[1,336,1024]{2,1,0:T(8,128)} %m1.3, f32[256,128]{1,0:T(8,128)} %copy-done.12), custom_call_target="tpu_custom_call" | custom-call | tf_op jit(solution)/shard_map/pallas_call | solution.py:97
  158.5 7.3 %all-gather.2 = f32[1024,128]{1,0:T(8,128)S(1)} all-gather(f32[256,128]{1,0:T(8,128)S(1)} %shard_map.135), channel_id=4, replica_groups={{0,4,8,12},{16,20,24,28},{32,36,40,44},{48,52,56,60},{64,68,72,76},{80,..., dimensions={0}, use_global_device_ids=true | all-gather | bytes 655360 | tf_op jit(solution)/shard_map/all_gather | solution.py:61
  165.8 3.4 %shard_map.134 = (f32[1024,128]{1,0:T(8,128)}, f32[256,128]{1,0:T(8,128)}, f32[256,128]{1,0:T(8,128)}, f32[256,128]{1,0:T(8,128)}, f32[256,128]{1,0:T(8,128)}) custom-call(s32[4]{0:T(128)S(1)} %pad_add_fusion.place, s32[1,1024]{1,0:T(1,128)S(1)} %copy-done.14, f32[1024,128]{1,0:T(8,128)S(1)} %copy-done.7, f32[1024,128]{1,0:T(8,128)S(1)} %collective-permute-done.7.p1, ...), custom_call_target="tpu_custom_call" | custom-call | tf_op jit(solution)/shard_map/pallas_call | solution.py:97
  169.2 1.0 copy-done.8
  170.3 6.6 %shard_map.136 = f32[1024,128]{1,0:T(8,128)} custom-call(s32[4]{0:T(128)S(1)} %pad_add_fusion.place, s32[64]{0:T(128)S(1)} %copy-done.16, s32[1,1024]{1,0:T(1,128)S(1)} %copy-done.14, f32[4,256,128]{2,1,0:T(8,128)S(1)} %bitcast.11, f32[1024,128]{1,0:T(8,128)S(1)} %copy-done.8, f32[1,1024,256]{2,1,0:T(8,128)} %basis.3, f32[1,1024,1024]{2,1,0:T(8,128)} %solve.3), custom_call_target="tpu_custom_call" | custom-call | tf_op jit(solution)/shard_map/pallas_call | solution.py:97
  176.9 3.5 %all-to-all-start.2 = ((f32[4,256,128]{2,1,0:T(8,128)}), f32[4,256,128]{2,1,0:T(8,128)S(1)}, u32[]{:S(2)}, u32[]{:S(2)}) async-start(f32[4,256,128]{2,1,0:T(8,128)} %bitcast.9), calls=%async_computation.2 | async-start | bytes 1048576 | tf_op jit(solution)/shard_map/all_to_all | solution.py:604
  180.4 1.4 collective-permute-start.24
  181.8 2.4 %collective-permute-start.25 = (f32[256,128]{1,0:T(8,128)S(1)}, f32[256,128]{1,0:T(8,128)S(1)}, u32[]{:S(2)}, u32[]{:S(2)}) collective-permute-start(f32[256,128]{1,0:T(8,128)S(1)} %copy-done.20), channel_id=1, source_target_pairs={{0,2},{1,3},{2,0},{3,1},{4,6},{5,7},{6,4},{7,5},{8,10},{9,11},{10,... | collective-permute-start | bytes 393224 | tf_op jit(solution)/shard_map/ppermute | solution.py:57
  184.2 1.2 collective-permute-start.26
  185.4 6.9 %collective-permute-done.24.r1 = f32[256,128]{1,0:T(8,128)S(1)} collective-permute-done((f32[256,128]{1,0:T(8,128)S(1)}, f32[256,128]{1,0:T(8,128)S(1)}, u32[]{:S(2)}, u32[]{:S(2)}) %collective-permute-start.24) | collective-permute-done | bytes 131104 | tf_op jit(solution)/shard_map/ppermute | solution.py:57
  192.3 3.1 %collective-permute-done.25.r2 = f32[256,128]{1,0:T(8,128)S(1)} collective-permute-done((f32[256,128]{1,0:T(8,128)S(1)}, f32[256,128]{1,0:T(8,128)S(1)}, u32[]{:S(2)}, u32[]{:S(2)}) %collective-permute-start.25) | collective-permute-done | bytes 131104 | tf_op jit(solution)/shard_map/ppermute | solution.py:57
  195.4 1.6 outputs.1
  (62 shorter events, 0.4 us)
Async XLA Ops:
  2.6 36.2 %collective-permute-start = (f32[256,640]{1,0:T(8,128)}, f32[256,640]{1,0:T(8,128)S(1)}, u32[]{:S(2)}, u32[]{:S(2)}) collective-permute-start(f32[256,640]{1,0:T(8,128)} %shard_map.122.p0), channel_id=1, source_target_pairs={{0,8},{4,12},{8,16},{12,20},{16,24},{20,28},{24,32},{28,36},{32,40... | collective-permute-start | bytes 1966088 | tf_op jit(solution)/shard_map/ppermute | solution.py:31
  4.7 34.1 %collective-permute-start.1 = (f32[256,640]{1,0:T(8,128)}, f32[256,640]{1,0:T(8,128)S(1)}, u32[]{:S(2)}, u32[]{:S(2)}) collective-permute-start(f32[256,640]{1,0:T(8,128)} %shard_map.122.p0), channel_id=1, source_target_pairs={{0,248},{4,252},{8,0},{12,4},{16,8},{20,12},{24,16},{28,20},{32,24... | collective-permute-start | bytes 1966088 | tf_op jit(solution)/shard_map/ppermute | solution.py:31
  12.9 23.2 %copy-start.4 = (f32[256,640]{1,0:T(8,128)S(1)}, f32[256,640]{1,0:T(8,128)}, u32[]{:S(2)}) copy-start(f32[256,640]{1,0:T(8,128)} %shard_map.122.p0) | copy-start | bytes 1966084
  12.9 12.7 %collective-permute-start.13 = (f32[128,256]{1,0:T(8,128)}, f32[128,256]{1,0:T(8,128)S(1)}, u32[]{:S(2)}, u32[]{:S(2)}) collective-permute-start(f32[128,256]{1,0:T(8,128)} %shard_map.128.slices), channel_id=1, source_target_pairs={{0,32},{4,36},{8,40},{12,44},{16,48},{20,52},{24,56},{28,60},{32,0... | collective-permute-start | bytes 393224 | tf_op jit(solution)/shard_map/ppermute | solution.py:31
  25.6 0.9 copy-start.6
  26.5 24.0 %copy-start.14 = (s32[1,1024]{1,0:T(1,128)S(1)}, s32[1,1024]{1,0:T(1,128)}, u32[]{:S(2)}) copy-start(s32[1,1024]{1,0:T(1,128)} %order.5) | copy-start | bytes 12292
  26.5 7.4 %collective-permute-start.14 = (f32[256,256]{1,0:T(8,128)S(1)}, f32[256,256]{1,0:T(8,128)S(1)}, u32[]{:S(2)}, u32[]{:S(2)}) collective-permute-start(f32[256,256]{1,0:T(8,128)S(1)} %shard_map.129.pair), channel_id=1, source_target_pairs={{0,24},{4,28},{8,16},{12,20},{16,8},{20,12},{24,0},{28,4},{32,56},... | collective-permute-start | bytes 786440 | tf_op jit(solution)/shard_map/ppermute | solution.py:31
  36.0 22.4 %collective-permute-start.16 = (f32[1024,256]{1,0:T(8,128)}, f32[1024,256]{1,0:T(8,128)S(1)}, u32[]{:S(2)}, u32[]{:S(2)}) collective-permute-start(f32[1024,256]{1,0:T(8,128)} %shard_map.130.b0), channel_id=1, source_target_pairs={{0,8},{4,12},{8,0},{12,4},{16,24},{20,28},{24,16},{28,20},{32,40},... | collective-permute-start | bytes 3145736 | tf_op jit(solution)/shard_map/ppermute | solution.py:31
  36.1 25.8 %collective-permute-start.3 = (f32[256,640]{1,0:T(8,128)S(1)}, f32[256,640]{1,0:T(8,128)}, u32[]{:S(2)}, u32[]{:S(2)}) collective-permute-start(f32[256,640]{1,0:T(8,128)S(1)} %copy-done.4), channel_id=1, source_target_pairs={{0,4},{4,0},{8,12},{12,8},{16,20},{20,16},{24,28},{28,24},{32,36},... | collective-permute-start | bytes 1966088 | tf_op jit(solution)/shard_map/ppermute | solution.py:31
  39.8 28.4 %collective-permute-start.2 = (f32[256,640]{1,0:T(8,128)}, f32[256,640]{1,0:T(8,128)}, u32[]{:S(2)}, u32[]{:S(2)}) collective-permute-start(f32[256,640]{1,0:T(8,128)} %broadcast_select_fusion), channel_id=1, source_target_pairs={{0,4},{4,0},{8,12},{12,8},{16,20},{20,16},{24,28},{28,24},{32,36},... | collective-permute-start | bytes 1966088 | tf_op jit(solution)/shard_map/ppermute | solution.py:31
  39.8 6.1 %collective-permute-start.4 = (f32[256,128]{1,0:T(8,128)}, f32[256,128]{1,0:T(8,128)S(1)}, u32[]{:S(2)}, u32[]{:S(2)}) collective-permute-start(f32[256,128]{1,0:T(8,128)} %x0.1), channel_id=1, source_target_pairs={{0,1},{1,2},{2,3},{3,0},{4,5},{5,6},{6,7},{7,4},{8,9},{9,10},{10,1... | collective-permute-start | bytes 393224 | tf_op jit(solution)/shard_map/ppermute | solution.py:57
  41.1 8.8 %collective-permute-start.5 = (f32[256,128]{1,0:T(8,128)}, f32[256,128]{1,0:T(8,128)S(1)}, u32[]{:S(2)}, u32[]{:S(2)}) collective-permute-start(f32[256,128]{1,0:T(8,128)} %x0.1), channel_id=1, source_target_pairs={{0,2},{1,3},{2,0},{3,1},{4,6},{5,7},{6,4},{7,5},{8,10},{9,11},{10,... | collective-permute-start | bytes 393224 | tf_op jit(solution)/shard_map/ppermute | solution.py:57
  45.9 4.6 %copy-start.17 = (f32[256,128]{1,0:T(8,128)}, f32[256,128]{1,0:T(8,128)S(1)}, u32[]{:S(2)}) copy-start(f32[256,128]{1,0:T(8,128)S(1)} %collective-permute-done.4.x1) | copy-start | bytes 393220
  45.9 64.1 %collective-permute-start.15 = (f32[1024,256]{1,0:T(8,128)}, f32[1024,256]{1,0:T(8,128)}, u32[]{:S(2)}, u32[]{:S(2)}) collective-permute-start(f32[1024,256]{1,0:T(8,128)} %shard_map.130.b0), channel_id=1, source_target_pairs={{0,4},{4,0},{8,12},{12,8},{16,20},{20,16},{24,28},{28,24},{32,36},... | collective-permute-start | bytes 3145736 | tf_op jit(solution)/shard_map/ppermute | solution.py:31
  49.9 0.7 copy-start.18
  49.9 12.1 %collective-permute-start.6 = (f32[256,128]{1,0:T(8,128)}, f32[256,128]{1,0:T(8,128)}, u32[]{:S(2)}, u32[]{:S(2)}) collective-permute-start(f32[256,128]{1,0:T(8,128)} %x0.1), channel_id=1, source_target_pairs={{0,3},{1,0},{2,1},{3,2},{4,7},{5,4},{6,5},{7,6},{8,11},{9,8},{10,9... | collective-permute-start | bytes 393224 | tf_op jit(solution)/shard_map/ppermute | solution.py:57
  50.6 11.4 %copy-start.15 = (s32[1,5]{1,0:T(1,128)S(1)}, s32[1,5]{1,0:T(1,128)}, u32[]{:S(2)}) copy-start(s32[1,5]{1,0:T(1,128)} %mask.3) | copy-start | bytes 64
  55.3 12.9 %copy-start.1 = (f32[256,512]{1,0:T(8,128)S(1)}, f32[256,512]{1,0:T(8,128)}, u32[]{:S(2)}) copy-start(f32[256,512]{1,0:T(8,128)} %coefs.1) | copy-start | bytes 1572868
  55.3 12.9 %copy-start.9 = (f32[256,512]{1,0:T(8,128)S(1)}, f32[256,512]{1,0:T(8,128)}, u32[]{:S(2)}) copy-start(f32[256,512]{1,0:T(8,128)} %own_y.1) | copy-start | bytes 1572868
  58.3 56.1 %collective-permute-start.17 = (f32[1024,256]{1,0:T(8,128)S(1)}, f32[1024,256]{1,0:T(8,128)}, u32[]{:S(2)}, u32[]{:S(2)}) collective-permute-start(f32[1024,256]{1,0:T(8,128)S(1)} %collective-permute-done.16.b2), channel_id=1, source_target_pairs={{0,4},{4,0},{8,12},{12,8},{16,20},{20,16},{24,28},{28,24},{32,36},... | collective-permute-start | bytes 3145736 | tf_op jit(solution)/shard_map/ppermute | solution.py:31
  68.2 1.0 copy-start.10
  69.3 1.0 copy-start.11
  79.2 21.1 %copy-start = (f32[1,336,1024]{2,1,0:T(8,128)S(1)}, f32[1,336,1024]{2,1,0:T(8,128)}, u32[]{:S(2)}) copy-start(f32[1,336,1024]{2,1,0:T(8,128)} %m1.3) | copy-start | bytes 4128772
  79.2 21.1 %copy-start.3 = (f32[1,336,256]{2,1,0:T(8,128)S(1)}, f32[1,336,256]{2,1,0:T(8,128)}, u32[]{:S(2)}) copy-start(f32[1,336,256]{2,1,0:T(8,128)} %transfer.3) | copy-start | bytes 1032196
  79.2 21.1 %copy-start.16 = (s32[64]{0:T(128)S(1)}, s32[64]{0:T(128)}, u32[]{:S(2)}) copy-start(s32[64]{0:T(128)} %leaf_map.3) | copy-start | bytes 772
  92.6 23.3 %copy-start.2 = (f32[1024,256]{1,0:T(8,128)S(1)}, f32[1024,256]{1,0:T(8,128)}, u32[]{:S(2)}) copy-start(f32[1024,256]{1,0:T(8,128)} %shard_map.130.b0) | copy-start | bytes 3145732
  102.4 0.7 copy-start.12
  103.0 7.0 %all-to-all-start.1 = ((f32[4,32,256]{2,1,0:T(8,128)}), f32[4,32,256]{2,1,0:T(8,128)S(1)}, u32[]{:S(2)}, u32[]{:S(2)}) async-start(f32[4,32,256]{2,1,0:T(8,128)} %bitcast.5), calls=%async_computation.1 | async-start | bytes 262144 | tf_op jit(solution)/shard_map/all_to_all | solution.py:654
  106.5 36.8 %collective-permute-start.7 = (f32[1024,128]{1,0:T(8,128)}, f32[1024,128]{1,0:T(8,128)S(1)}, u32[]{:S(2)}, u32[]{:S(2)}) collective-permute-start(f32[1024,128]{1,0:T(8,128)} %get-tuple-element.33), channel_id=1, source_target_pairs={{0,1},{1,2},{2,3},{3,0},{4,5},{5,6},{6,7},{7,4},{8,9},{9,10},{10,1... | collective-permute-start | bytes 1572872 | tf_op jit(solution)/shard_map/ppermute | solution.py:57
  106.8 36.5 %collective-permute-start.8 = (f32[1024,128]{1,0:T(8,128)}, f32[1024,128]{1,0:T(8,128)}, u32[]{:S(2)}, u32[]{:S(2)}) collective-permute-start(f32[1024,128]{1,0:T(8,128)} %get-tuple-element.34), channel_id=1, source_target_pairs={{0,2},{1,3},{2,0},{3,1},{4,6},{5,7},{6,4},{7,5},{8,10},{9,11},{10,... | collective-permute-start | bytes 1572872 | tf_op jit(solution)/shard_map/ppermute | solution.py:57
  108.5 34.7 %collective-permute-start.9 = (f32[1024,128]{1,0:T(8,128)}, f32[1024,128]{1,0:T(8,128)}, u32[]{:S(2)}, u32[]{:S(2)}) collective-permute-start(f32[1024,128]{1,0:T(8,128)} %get-tuple-element.35), channel_id=1, source_target_pairs={{0,3},{1,0},{2,1},{3,2},{4,7},{5,4},{6,5},{7,6},{8,11},{9,8},{10,9... | collective-permute-start | bytes 1572872 | tf_op jit(solution)/shard_map/ppermute | solution.py:57
  110.1 4.4 %collective-permute-start.10 = (f32[32,256]{1,0:T(8,128)S(1)}, f32[32,256]{1,0:T(8,128)S(1)}, u32[]{:S(2)}, u32[]{:S(2)}) collective-permute-start(f32[32,256]{1,0:T(8,128)S(1)} %fusion.1.r0), channel_id=1, source_target_pairs={{0,24},{4,28},{8,16},{12,20},{16,8},{20,12},{24,0},{28,4},{32,56},... | collective-permute-start | bytes 98312 | tf_op jit(solution)/shard_map/ppermute | solution.py:31
  114.4 5.0 %collective-permute-start.11 = (f32[32,256]{1,0:T(8,128)S(1)}, f32[32,256]{1,0:T(8,128)S(1)}, u32[]{:S(2)}, u32[]{:S(2)}) collective-permute-start(f32[32,256]{1,0:T(8,128)S(1)} %fusion.1.r0), channel_id=1, source_target_pairs={{0,32},{4,36},{8,40},{12,44},{16,48},{20,52},{24,56},{28,60},{32,0... | collective-permute-start | bytes 98312 | tf_op jit(solution)/shard_map/ppermute | solution.py:31
  114.4 5.0 %collective-permute-start.12 = (f32[32,256]{1,0:T(8,128)S(1)}, f32[32,256]{1,0:T(8,128)S(1)}, u32[]{:S(2)}, u32[]{:S(2)}) collective-permute-start(f32[32,256]{1,0:T(8,128)S(1)} %fusion.1.r0), channel_id=1, source_target_pairs={{0,56},{4,60},{8,48},{12,52},{16,40},{20,44},{24,32},{28,36},{32,2... | collective-permute-start | bytes 98312 | tf_op jit(solution)/shard_map/ppermute | solution.py:31
  118.4 1.0 copy-start.5
  120.2 5.3 %collective-permute-start.20 = (f32[32,256]{1,0:T(8,128)S(1)}, f32[32,256]{1,0:T(8,128)S(1)}, u32[]{:S(2)}, u32[]{:S(2)}) collective-permute-start(f32[32,256]{1,0:T(8,128)S(1)} %get-tuple-element.40), channel_id=1, source_target_pairs={{0,56},{4,60},{8,48},{12,52},{16,40},{20,44},{24,32},{28,36},{32,2... | collective-permute-start | bytes 98312 | tf_op jit(solution)/shard_map/ppermute | solution.py:31
  122.3 5.6 %collective-permute-start.19 = (f32[32,256]{1,0:T(8,128)S(1)}, f32[32,256]{1,0:T(8,128)S(1)}, u32[]{:S(2)}, u32[]{:S(2)}) collective-permute-start(f32[32,256]{1,0:T(8,128)S(1)} %get-tuple-element.40), channel_id=1, source_target_pairs={{0,32},{4,36},{8,40},{12,44},{16,48},{20,52},{24,56},{28,60},{32,0... | collective-permute-start | bytes 98312 | tf_op jit(solution)/shard_map/ppermute | solution.py:31
  125.5 4.4 %collective-permute-start.18 = (f32[32,256]{1,0:T(8,128)S(1)}, f32[32,256]{1,0:T(8,128)S(1)}, u32[]{:S(2)}, u32[]{:S(2)}) collective-permute-start(f32[32,256]{1,0:T(8,128)S(1)} %get-tuple-element.40), channel_id=1, source_target_pairs={{0,24},{4,28},{8,16},{12,20},{16,8},{20,12},{24,0},{28,4},{32,56},... | collective-permute-start | bytes 98312 | tf_op jit(solution)/shard_map/ppermute | solution.py:31
  129.9 6.4 %collective-permute-start.21 = (f32[32,256]{1,0:T(8,128)S(1)}, f32[32,256]{1,0:T(8,128)S(1)}, u32[]{:S(2)}, u32[]{:S(2)}) collective-permute-start(f32[32,256]{1,0:T(8,128)S(1)} %add_add_fusion.r0), channel_id=1, source_target_pairs={{224,0},{228,4},{232,8},{236,12},{240,16},{244,20},{248,24},{252,2... | collective-permute-start | bytes 98312 | tf_op jit(solution)/shard_map/ppermute | solution.py:53
  135.0 3.7 %collective-permute-start.22 = (f32[32,256]{1,0:T(8,128)S(1)}, f32[32,256]{1,0:T(8,128)S(1)}, u32[]{:S(2)}, u32[]{:S(2)}) collective-permute-start(f32[32,256]{1,0:T(8,128)S(1)} %add_add_fusion.r0), channel_id=1, source_target_pairs={{64,0},{68,4},{72,8},{76,12},{80,16},{84,20},{88,24},{92,28},{224,... | collective-permute-start | bytes 98312 | tf_op jit(solution)/shard_map/ppermute | solution.py:53
  136.3 6.0 %collective-permute-start.23 = (f32[32,256]{1,0:T(8,128)S(1)}, f32[32,256]{1,0:T(8,128)S(1)}, u32[]{:S(2)}, u32[]{:S(2)}) collective-permute-start(f32[32,256]{1,0:T(8,128)S(1)} %add_add_fusion.r0), channel_id=1, source_target_pairs={{160,0},{164,4},{168,8},{172,12},{176,16},{180,20},{184,24},{188,2... | collective-permute-start | bytes 98312 | tf_op jit(solution)/shard_map/ppermute | solution.py:53
  143.2 22.6 %copy-start.7 = (f32[1024,128]{1,0:T(8,128)S(1)}, f32[1024,128]{1,0:T(8,128)}, u32[]{:S(2)}) copy-start(f32[1024,128]{1,0:T(8,128)} %get-tuple-element.44.p0) | copy-start | bytes 1572868
  169.2 1.0 copy-start.8
  170.3 10.1 %copy-start.21 = (f32[256,128]{1,0:T(8,128)S(1)}, f32[256,128]{1,0:T(8,128)}, u32[]{:S(2)}) copy-start(f32[256,128]{1,0:T(8,128)} %get-tuple-element.49) | copy-start | bytes 393220
  170.3 11.5 %copy-start.20 = (f32[256,128]{1,0:T(8,128)S(1)}, f32[256,128]{1,0:T(8,128)}, u32[]{:S(2)}) copy-start(f32[256,128]{1,0:T(8,128)} %get-tuple-element.50) | copy-start | bytes 393220
  170.3 13.9 %copy-start.19 = (f32[256,128]{1,0:T(8,128)S(1)}, f32[256,128]{1,0:T(8,128)}, u32[]{:S(2)}) copy-start(f32[256,128]{1,0:T(8,128)} %get-tuple-element.51) | copy-start | bytes 393220
  170.3 25.2 %copy-start.13 = (f32[256,128]{1,0:T(8,128)S(1)}, f32[256,128]{1,0:T(8,128)}, u32[]{:S(2)}) copy-start(f32[256,128]{1,0:T(8,128)} %get-tuple-element.48.r0) | copy-start | bytes 393220
  176.9 18.5 %all-to-all-start.2 = ((f32[4,256,128]{2,1,0:T(8,128)}), f32[4,256,128]{2,1,0:T(8,128)S(1)}, u32[]{:S(2)}, u32[]{:S(2)}) async-start(f32[4,256,128]{2,1,0:T(8,128)} %bitcast.9), calls=%async_computation.2 | async-start | bytes 1048576 | tf_op jit(solution)/shard_map/all_to_all | solution.py:604
  180.4 11.9 %collective-permute-start.24 = (f32[256,128]{1,0:T(8,128)S(1)}, f32[256,128]{1,0:T(8,128)S(1)}, u32[]{:S(2)}, u32[]{:S(2)}) collective-permute-start(f32[256,128]{1,0:T(8,128)S(1)} %copy-done.21), channel_id=1, source_target_pairs={{0,1},{1,2},{2,3},{3,0},{4,5},{5,6},{6,7},{7,4},{8,9},{9,10},{10,1... | collective-permute-start | bytes 393224 | tf_op jit(solution)/shard_map/ppermute | solution.py:57
  181.8 13.6 %collective-permute-start.25 = (f32[256,128]{1,0:T(8,128)S(1)}, f32[256,128]{1,0:T(8,128)S(1)}, u32[]{:S(2)}, u32[]{:S(2)}) collective-permute-start(f32[256,128]{1,0:T(8,128)S(1)} %copy-done.20), channel_id=1, source_target_pairs={{0,2},{1,3},{2,0},{3,1},{4,6},{5,7},{6,4},{7,5},{8,10},{9,11},{10,... | collective-permute-start | bytes 393224 | tf_op jit(solution)/shard_map/ppermute | solution.py:57
  184.2 11.2 %collective-permute-start.26 = (f32[256,128]{1,0:T(8,128)S(1)}, f32[256,128]{1,0:T(8,128)S(1)}, u32[]{:S(2)}, u32[]{:S(2)}) collective-permute-start(f32[256,128]{1,0:T(8,128)S(1)} %copy-done.19), channel_id=1, source_target_pairs={{0,3},{1,0},{2,1},{3,2},{4,7},{5,4},{6,5},{7,6},{8,11},{9,8},{10,9... | collective-permute-start | bytes 393224 | tf_op jit(solution)/shard_map/ppermute | solution.py:57

commit v7 on v6

--- a/solution.py
+++ b/solution.py
@@ -339,10 +339,6 @@
         moves.append((source, buffer.at[pl.ds(64 + k * 16, 16), :]))
     run_copies(sems, moves)
     run_copies(sems, [(buffer, out)])
-
-
-def sum_kernel(parts, out):
-    out[...] = parts[0] + parts[1] + (parts[2] + parts[3])
 
 
 def assemble(body, shape, count, *parts):
@@ -638,6 +634,7 @@
     lead = lead_call(cluster_perm, leaf_basis, leaf_inverse)
 
     near = near_call(place, tile_mask, xs, (packed, partner))
+    near, held = lax.optimization_barrier((near, held))
     across = leaf_xor(held, 2)
     own_core = leaf_xor(held, 1)
     both_ways = leaf_xor(across, 1)
@@ -645,7 +642,7 @@
         place, tile_mask, ridge, (left, right, relay), near, targets, coefs, lead
     )
     led = swap_cols(led)
-    reduced = kernel(sum_kernel, [(RANK, 128)], [led])
+    reduced = led.sum(0)
     e1, m2, f2, m3, e2 = nodes_call(place, (held, own_core, across, both_ways))
 
     columns = [partial[0]] + [col_shift(partial[d], d) for d in (1, 2, 3)]

time: 198 us -> 207 us (1.045)
  waiting for transfers between devices: 50.2 us -> 66.4 us
  starting transfers between devices: 51.6 us -> 47.8 us
    ppermute x15, waiting for transfers between devices: 30.6 us -> 48.4 us  [leaf_route(): return lax.ppermute(value, 'leaf', [(i, target(i)) for i in range(LEAVES)])]
    ppermute x15, starting transfers between devices: 24.4 us -> 19 us  [leaf_route(): return lax.ppermute(value, 'leaf', [(i, target(i)) for i in range(LEAVES)])]
    ppermute x9, starting transfers between devices: 11.6 us -> 14.8 us  [col_shift(): return lax.ppermute(value, 'col', [(i, (i + step) % 4) for i in range(4)])]
    unnamed x44 -> x50, local copies, waits for them, and re-layouts: 5.77 us -> 4 us
    pallas_call x15 -> x14, Pallas kernels: 44.9 us -> 44.1 us  [kernel(): pl.pallas_call(body, in_specs=[SMEM] * len(scalars) + [VMEM] * len(values...]
  transfers between devices with their start and end apart: 29 -> 29, of which waited for: 13 -> 13; matrix products, arithmetic and copies ran while one was open for 1% -> 1% of each run, Pallas kernels for 15% -> 14%
where the time goes in v7:
time: 207 us
  waiting for transfers between devices  66.4 us (32%)
  starting transfers between devices  47.8 us (23%)
  Pallas kernels  45.7 us (22%)
  blocking collectives  39.6 us (19%)
  local copies, waits for them, and re-layouts  4 us (2%)
    ppermute x15, waiting for transfers between devices, leaf_route(): return lax.ppermute(value, 'leaf', [(i, target(i)) for i in range(LEAVES)])  48.4 us
    pallas_call x14, Pallas kernels, kernel(): pl.pallas_call(body, in_specs=[SMEM] * len(scalars) + [VMEM] * len(values...  44.1 us
    all_gather x3, blocking collectives, gather4(): return lax.all_gather(value, 'leaf', axis=0, axis_index_groups=groups)  26.1 us
    ppermute x15, starting transfers between devices, leaf_route(): return lax.ppermute(value, 'leaf', [(i, target(i)) for i in range(LEAVES)])  19 us
    ppermute x9, starting transfers between devices, col_shift(): return lax.ppermute(value, 'col', [(i, (i + step) % 4) for i in range(4)])  14.8 us
    all_to_all x1, blocking collectives, swap_cols(): return lax.all_to_all(value, 'col', 0, 0, tiled=True)  13.5 us
    ppermute x9, waiting for transfers between devices, col_shift(): return lax.ppermute(value, 'col', [(i, (i + step) % 4) for i in range(4)])  13.1 us
    ppermute x3, starting transfers between devices, z_from(): return lax.ppermute(value, 'leaf', route)  7.12 us
  transfers between devices with their start and end apart: 29, of which 13 were waited for; matrix products, arithmetic and copies ran while one was open for 1% of the time, Pallas kernels for 14%

profile of v7, /device:TPU:1, one launch (start us, length us, event | category | flops | bytes accessed | tf_op | source)
XLA Modules:
  0.0 206.6 jit_solution(3410016331089453165)
XLA Ops:
  0.6 0.0 copy-start.20
  0.6 2.0 shard_map.122.p0
  2.6 3.3 %collective-permute-start.3 = (f32[256,640]{1,0:T(8,128)}, f32[256,640]{1,0:T(8,128)}, u32[]{:S(2)}, u32[]{:S(2)}) collective-permute-start(f32[256,640]{1,0:T(8,128)} %shard_map.122.p0), channel_id=1, source_target_pairs={{0,4},{4,0},{8,12},{12,8},{16,20},{20,16},{24,28},{28,24},{32,36},... | collective-permute-start | bytes 1966088 | tf_op jit(solution)/shard_map/ppermute | solution.py:31
  5.9 1.6 shard_map.124.slices
  7.5 0.1 collective-permute-start.7
  7.6 6.8 %collective-permute-start.1 = (f32[256,640]{1,0:T(8,128)}, f32[256,640]{1,0:T(8,128)S(1)}, u32[]{:S(2)}, u32[]{:S(2)}) collective-permute-start(f32[256,640]{1,0:T(8,128)} %shard_map.122.p0), channel_id=1, source_target_pairs={{0,248},{4,252},{8,0},{12,4},{16,8},{20,12},{24,16},{28,20},{32,24... | collective-permute-start | bytes 1966088 | tf_op jit(solution)/shard_map/ppermute | solution.py:31
  14.4 0.9 copy-done.8
  15.3 0.1 collective-permute-start.8
  15.4 3.0 %collective-permute-start.5 = (f32[256,128]{1,0:T(8,128)S(1)}, f32[256,128]{1,0:T(8,128)S(1)}, u32[]{:S(2)}, u32[]{:S(2)}) collective-permute-start(f32[256,128]{1,0:T(8,128)S(1)} %copy-done.20), channel_id=1, source_target_pairs={{0,2},{1,3},{2,0},{3,1},{4,6},{5,7},{6,4},{7,5},{8,10},{9,11},{10,... | collective-permute-start | bytes 393224 | tf_op jit(solution)/shard_map/ppermute | solution.py:57
  18.4 3.1 %collective-permute-done.5.x2 = f32[256,128]{1,0:T(8,128)S(1)} collective-permute-done((f32[256,128]{1,0:T(8,128)S(1)}, f32[256,128]{1,0:T(8,128)S(1)}, u32[]{:S(2)}, u32[]{:S(2)}) %collective-permute-start.5) | collective-permute-done | bytes 131104 | tf_op jit(solution)/shard_map/ppermute | solution.py:57
  21.5 1.3 collective-permute-start.4
  22.8 15.1 %collective-permute-done.8.mirrored = f32[256,256]{1,0:T(8,128)S(1)} collective-permute-done((f32[256,256]{1,0:T(8,128)S(1)}, f32[256,256]{1,0:T(8,128)S(1)}, u32[]{:S(2)}, u32[]{:S(2)}) %collective-permute-start.8) | collective-permute-done | bytes 262176 | tf_op jit(solution)/shard_map/ppermute | solution.py:31
  37.9 2.7 %collective-permute-start.6 = (f32[256,128]{1,0:T(8,128)S(1)}, f32[256,128]{1,0:T(8,128)}, u32[]{:S(2)}, u32[]{:S(2)}) collective-permute-start(f32[256,128]{1,0:T(8,128)S(1)} %copy-done.20), channel_id=1, source_target_pairs={{0,3},{1,0},{2,1},{3,2},{4,7},{5,4},{6,5},{7,6},{8,11},{9,8},{10,9... | collective-permute-start | bytes 393224 | tf_op jit(solution)/shard_map/ppermute | solution.py:57
  40.7 0.1 pad_add_fusion.place
  40.8 2.0 shard_map.126.b0
  42.9 6.3 %shard_map.123 = (f32[1024,512]{1,0:T(8,128)S(1)}, bf16[4,256,256]{2,1,0:T(8,128)(2,1)}, f32[4,256,1]{2,1,0:T(8,128)}) custom-call(s32[4]{0:T(128)S(1)} %pad_add_fusion.place, s32[1,5]{1,0:T(1,128)S(1)} %copy-done.18, f32[256,640]{1,0:T(8,128)S(1)} %copy-done.4, f32[256,640]{1,0:T(8,128)} %collective-permute-done.3.p1, f32[256,128]{1,0:T(8,128)} %x0.1, ...), custom_call_target="tpu_custom_call" | custom-call | tf_op jit(solution)/shard_map/pallas_call | solution.py:97
  49.2 1.3 copy-done.5
  50.5 0.1 broadcast_select_fusion
  50.6 2.1 %collective-permute-start.2 = (f32[256,640]{1,0:T(8,128)S(1)}, f32[256,640]{1,0:T(8,128)S(1)}, u32[]{:S(2)}, u32[]{:S(2)}) collective-permute-start(f32[256,640]{1,0:T(8,128)S(1)} %broadcast_select_fusion), channel_id=1, source_target_pairs={{0,4},{4,0},{8,12},{12,8},{16,20},{20,16},{24,28},{28,24},{32,36},... | collective-permute-start | bytes 1966088 | tf_op jit(solution)/shard_map/ppermute | solution.py:31
  52.7 0.1 collective-permute-start.15
  52.8 20.8 %collective-permute-done.16.b2 = f32[1024,256]{1,0:T(8,128)} collective-permute-done((f32[1024,256]{1,0:T(8,128)}, f32[1024,256]{1,0:T(8,128)}, u32[]{:S(2)}, u32[]{:S(2)}) %collective-permute-start.16) | collective-permute-done | bytes 1048608 | tf_op jit(solution)/shard_map/ppermute | solution.py:31
  73.6 2.8 %collective-permute-start.17 = (f32[1024,256]{1,0:T(8,128)}, f32[1024,256]{1,0:T(8,128)}, u32[]{:S(2)}, u32[]{:S(2)}) collective-permute-start(f32[1024,256]{1,0:T(8,128)} %collective-permute-done.16.b2), channel_id=1, source_target_pairs={{0,4},{4,0},{8,12},{12,8},{16,20},{20,16},{24,28},{28,24},{32,36},... | collective-permute-start | bytes 3145736 | tf_op jit(solution)/shard_map/ppermute | solution.py:31
  77.1 4.8 %shard_map.127.lead = f32[256,1024]{1,0:T(8,128)S(1)} custom-call(s32[1,1024]{1,0:T(1,128)S(1)} %copy-done.17, f32[1,1024,256]{2,1,0:T(8,128)} %basis.3, f32[1,1024,1024]{2,1,0:T(8,128)} %solve.3), custom_call_target="tpu_custom_call" | custom-call | tf_op jit(solution)/shard_map/pallas_call | solution.py:97
  82.0 8.2 %shard_map.128 = (f32[4,256,128]{2,1,0:T(8,128)S(1)}, f32[1024,128]{1,0:T(8,128)}, f32[1024,128]{1,0:T(8,128)}, f32[1024,128]{1,0:T(8,128)}, f32[1024,128]{1,0:T(8,128)}) custom-call(s32[4]{0:T(128)S(1)} %pad_add_fusion.place, s32[1,5]{1,0:T(1,128)S(1)} %copy-done.18, f32[1]{0:T(128)S(6)} %copy.13.ridge, f32[256,640]{1,0:T(8,128)S(1)} %collective-permute-done.p0, ...), custom_call_target="tpu_custom_call" | custom-call | tf_op jit(solution)/shard_map/pallas_call | solution.py:97
  90.2 13.5 %all_to_all.19 = f32[4,256,128]{2,1,0:T(8,128)} all-to-all(f32[4,256,128]{2,1,0:T(8,128)S(1)} %get-tuple-element.43), channel_id=1, replica_groups=mesh['leaf'=64,'col'=4] {'col'}, dimensions={0} | all-to-all | bytes 1048576 | tf_op jit(solution)/shard_map/all_to_all | solution.py:600
  103.7 1.1 reduce_sum.9
  104.8 7.5 %all-gather = f32[1024,128]{1,0:T(8,128)S(1)} all-gather(f32[256,128]{1,0:T(8,128)S(1)} %reduce_sum.9), channel_id=2, replica_groups={{0,4,8,12},{16,20,24,28},{32,36,40,44},{48,52,56,60},{64,68,72,76},{80,..., dimensions={0}, use_global_device_ids=true | all-gather | bytes 655360 | tf_op jit(solution)/shard_map/all_gather | solution.py:61
  112.3 1.4 shard_map.129
  113.7 0.6 copy-done.16
  114.4 3.5 %all-to-all-start.1 = ((f32[4,32,256]{2,1,0:T(8,128)}), f32[4,32,256]{2,1,0:T(8,128)S(1)}, u32[]{:S(2)}, u32[]{:S(2)}) async-start(f32[4,32,256]{2,1,0:T(8,128)} %bitcast.14), calls=%async_computation.1 | async-start | bytes 262144 | tf_op jit(solution)/shard_map/all_to_all | solution.py:651
  117.8 0.3 collective-permute-start.9
  118.1 1.8 collective-permute-start.10
  119.9 0.7 collective-permute-start.11
  120.6 0.8 all-to-all-done.1
  121.4 0.1 collective-permute-start.14
  121.5 4.9 %collective-permute-done.14.r3 = f32[32,256]{1,0:T(8,128)S(1)} collective-permute-done((f32[32,256]{1,0:T(8,128)S(1)}, f32[32,256]{1,0:T(8,128)S(1)}, u32[]{:S(2)}, u32[]{:S(2)}) %collective-permute-start.14) | collective-permute-done | bytes 32800 | tf_op jit(solution)/shard_map/ppermute | solution.py:31
  126.4 0.3 collective-permute-start.12
  126.7 2.7 %shard_map.130 = (f32[1024,256]{1,0:T(8,128)S(1)}, f32[256,1024]{1,0:T(8,128)S(1)}, f32[256,256]{1,0:T(8,128)S(1)}, f32[256,1024]{1,0:T(8,128)S(1)}, f32[256,256]{1,0:T(8,128)S(1)}) custom-call(s32[4]{0:T(128)S(1)} %pad_add_fusion.place, f32[1024,256]{1,0:T(8,128)S(1)} %copy-done.2, f32[1024,256]{1,0:T(8,128)} %collective-permute-done.15.b1, ...), custom_call_target="tpu_custom_call" | custom-call | tf_op jit(solution)/shard_map/pallas_call | solution.py:97
  129.4 0.1 collective-permute-done.13.r2
  129.5 1.2 collective-permute-done.12.r1
  130.8 0.8 shard_map.131
  131.6 2.3 %collective-permute-start.20 = (f32[32,256]{1,0:T(8,128)S(1)}, f32[32,256]{1,0:T(8,128)S(1)}, u32[]{:S(2)}, u32[]{:S(2)}) collective-permute-start(f32[32,256]{1,0:T(8,128)S(1)} %get-tuple-element.48), channel_id=1, source_target_pairs={{0,56},{4,60},{8,48},{12,52},{16,40},{20,44},{24,32},{28,36},{32,2... | collective-permute-start | bytes 98312 | tf_op jit(solution)/shard_map/ppermute | solution.py:31
  133.9 0.0 collective-permute-start.19
  133.9 3.0 %collective-permute-done.20 = f32[32,256]{1,0:T(8,128)S(1)} collective-permute-done((f32[32,256]{1,0:T(8,128)S(1)}, f32[32,256]{1,0:T(8,128)S(1)}, u32[]{:S(2)}, u32[]{:S(2)}) %collective-permute-start.20) | collective-permute-done | bytes 32800 | tf_op jit(solution)/shard_map/ppermute | solution.py:31
  136.9 1.1 collective-permute-start.18
  138.0 3.3 %collective-permute-done.18 = f32[32,256]{1,0:T(8,128)S(1)} collective-permute-done((f32[32,256]{1,0:T(8,128)S(1)}, f32[32,256]{1,0:T(8,128)S(1)}, u32[]{:S(2)}, u32[]{:S(2)}) %collective-permute-start.18) | collective-permute-done | bytes 32800 | tf_op jit(solution)/shard_map/ppermute | solution.py:31
  141.3 3.9 %collective-permute-start.23 = (f32[32,256]{1,0:T(8,128)S(1)}, f32[32,256]{1,0:T(8,128)S(1)}, u32[]{:S(2)}, u32[]{:S(2)}) collective-permute-start(f32[32,256]{1,0:T(8,128)S(1)} %add_add_fusion.r0), channel_id=1, source_target_pairs={{160,0},{164,4},{168,8},{172,12},{176,16},{180,20},{184,24},{188,2... | collective-permute-start | bytes 98312 | tf_op jit(solution)/shard_map/ppermute | solution.py:53
  145.1 2.0 collective-permute-done.23.r3
  147.1 3.2 %collective-permute-start.21 = (f32[32,256]{1,0:T(8,128)S(1)}, f32[32,256]{1,0:T(8,128)S(1)}, u32[]{:S(2)}, u32[]{:S(2)}) collective-permute-start(f32[32,256]{1,0:T(8,128)S(1)} %add_add_fusion.r0), channel_id=1, source_target_pairs={{224,0},{228,4},{232,8},{236,12},{240,16},{244,20},{248,24},{252,2... | collective-permute-start | bytes 98312 | tf_op jit(solution)/shard_map/ppermute | solution.py:53
  150.4 2.1 collective-permute-done.21.r1
  152.4 0.9 shard_map.132
  153.4 11.4 %all-gather.1 = f32[128,256]{1,0:T(8,128)S(1)} all-gather(f32[32,256]{1,0:T(8,128)S(1)} %shard_map.132), channel_id=3, replica_groups={{0,4,8,12},{24,28,16,20},{32,36,40,44},{56,60,48,52},{64,68,72,76},{88,..., dimensions={0}, use_global_device_ids=true | all-gather | bytes 163840 | tf_op jit(solution)/shard_map/all_gather | solution.py:61
  164.7 3.2 %shard_map.134 = f32[256,128]{1,0:T(8,128)S(1)} custom-call(f32[4,32,256]{2,1,0:T(8,128)S(1)} %bitcast.13, f32[1024,256]{1,0:T(8,128)} %copy-done.7, f32[1,336,1024]{2,1,0:T(8,128)} %m1.3, f32[256,128]{1,0:T(8,128)} %copy-done.14), custom_call_target="tpu_custom_call" | custom-call | tf_op jit(solution)/shard_map/pallas_call | solution.py:97
  167.9 7.3 %all-gather.2 = f32[1024,128]{1,0:T(8,128)S(1)} all-gather(f32[256,128]{1,0:T(8,128)S(1)} %shard_map.134), channel_id=4, replica_groups={{0,4,8,12},{16,20,24,28},{32,36,40,44},{48,52,56,60},{64,68,72,76},{80,..., dimensions={0}, use_global_device_ids=true | all-gather | bytes 655360 | tf_op jit(solution)/shard_map/all_gather | solution.py:61
  175.2 3.5 %shard_map.133 = (f32[1024,128]{1,0:T(8,128)}, f32[256,128]{1,0:T(8,128)}, f32[256,128]{1,0:T(8,128)}, f32[256,128]{1,0:T(8,128)}, f32[256,128]{1,0:T(8,128)}) custom-call(s32[4]{0:T(128)S(1)} %pad_add_fusion.place, s32[1,1024]{1,0:T(1,128)S(1)} %copy-done.17, f32[1024,128]{1,0:T(8,128)S(1)} %copy-done.9, f32[1024,128]{1,0:T(8,128)} %collective-permute-done.9.p1, ...), custom_call_target="tpu_custom_call" | custom-call | tf_op jit(solution)/shard_map/pallas_call | solution.py:97
  178.8 1.0 copy-done.10
  179.8 6.6 %shard_map.135 = f32[1024,128]{1,0:T(8,128)} custom-call(s32[4]{0:T(128)S(1)} %pad_add_fusion.place, s32[64]{0:T(128)S(1)} %copy-done.19, s32[1,1024]{1,0:T(1,128)S(1)} %copy-done.17, f32[4,256,128]{2,1,0:T(8,128)S(1)} %bitcast.11, f32[1024,128]{1,0:T(8,128)S(1)} %copy-done.10, f32[1,1024,256]{2,1,0:T(8,128)} %basis.3, f32[1,1024,1024]{2,1,0:T(8,128)} %solve.3), custom_call_target="tpu_custom_call" | custom-call | tf_op jit(solution)/shard_map/pallas_call | solution.py:97
  186.4 3.5 %all-to-all-start.2 = ((f32[4,256,128]{2,1,0:T(8,128)}), f32[4,256,128]{2,1,0:T(8,128)S(1)}, u32[]{:S(2)}, u32[]{:S(2)}) async-start(f32[4,256,128]{2,1,0:T(8,128)} %bitcast.9), calls=%async_computation.2 | async-start | bytes 1048576 | tf_op jit(solution)/shard_map/all_to_all | solution.py:600
  189.9 1.4 collective-permute-start.24
  191.3 2.4 %collective-permute-start.25 = (f32[256,128]{1,0:T(8,128)S(1)}, f32[256,128]{1,0:T(8,128)S(1)}, u32[]{:S(2)}, u32[]{:S(2)}) collective-permute-start(f32[256,128]{1,0:T(8,128)S(1)} %copy-done.23), channel_id=1, source_target_pairs={{0,2},{1,3},{2,0},{3,1},{4,6},{5,7},{6,4},{7,5},{8,10},{9,11},{10,... | collective-permute-start | bytes 393224 | tf_op jit(solution)/shard_map/ppermute | solution.py:57
  193.8 1.2 collective-permute-start.26
  194.9 6.9 %collective-permute-done.24.r1 = f32[256,128]{1,0:T(8,128)S(1)} collective-permute-done((f32[256,128]{1,0:T(8,128)S(1)}, f32[256,128]{1,0:T(8,128)S(1)}, u32[]{:S(2)}, u32[]{:S(2)}) %collective-permute-start.24) | collective-permute-done | bytes 131104 | tf_op jit(solution)/shard_map/ppermute | solution.py:57
  201.8 3.1 %collective-permute-done.25.r2 = f32[256,128]{1,0:T(8,128)S(1)} collective-permute-done((f32[256,128]{1,0:T(8,128)S(1)}, f32[256,128]{1,0:T(8,128)S(1)}, u32[]{:S(2)}, u32[]{:S(2)}) %collective-permute-start.25) | collective-permute-done | bytes 131104 | tf_op jit(solution)/shard_map/ppermute | solution.py:57
  205.0 1.6 outputs.1
  (68 shorter events, 0.2 us)
Async XLA Ops:
  0.6 14.8 %copy-start.20 = (f32[256,128]{1,0:T(8,128)S(1)}, f32[256,128]{1,0:T(8,128)}, u32[]{:S(2)}) copy-start(f32[256,128]{1,0:T(8,128)} %x0.1) | copy-start | bytes 393220
  2.6 40.2 %collective-permute-start.3 = (f32[256,640]{1,0:T(8,128)}, f32[256,640]{1,0:T(8,128)}, u32[]{:S(2)}, u32[]{:S(2)}) collective-permute-start(f32[256,640]{1,0:T(8,128)} %shard_map.122.p0), channel_id=1, source_target_pairs={{0,4},{4,0},{8,12},{12,8},{16,20},{20,16},{24,28},{28,24},{32,36},... | collective-permute-start | bytes 1966088 | tf_op jit(solution)/shard_map/ppermute | solution.py:31
  5.9 36.9 %copy-start.18 = (s32[1,5]{1,0:T(1,128)S(1)}, s32[1,5]{1,0:T(1,128)}, u32[]{:S(2)}) copy-start(s32[1,5]{1,0:T(1,128)} %mask.3) | copy-start | bytes 64
  7.5 35.4 %copy-start.4 = (f32[256,640]{1,0:T(8,128)S(1)}, f32[256,640]{1,0:T(8,128)}, u32[]{:S(2)}) copy-start(f32[256,640]{1,0:T(8,128)} %shard_map.122.p0) | copy-start | bytes 1966084
  7.5 6.9 %collective-permute-start.7 = (f32[128,256]{1,0:T(8,128)}, f32[128,256]{1,0:T(8,128)S(1)}, u32[]{:S(2)}, u32[]{:S(2)}) collective-permute-start(f32[128,256]{1,0:T(8,128)} %shard_map.124.slices), channel_id=1, source_target_pairs={{0,32},{4,36},{8,40},{12,44},{16,48},{20,52},{24,56},{28,60},{32,0... | collective-permute-start | bytes 393224 | tf_op jit(solution)/shard_map/ppermute | solution.py:31
  7.6 42.9 %collective-permute-start.1 = (f32[256,640]{1,0:T(8,128)}, f32[256,640]{1,0:T(8,128)S(1)}, u32[]{:S(2)}, u32[]{:S(2)}) collective-permute-start(f32[256,640]{1,0:T(8,128)} %shard_map.122.p0), channel_id=1, source_target_pairs={{0,248},{4,252},{8,0},{12,4},{16,8},{20,12},{24,16},{28,20},{32,24... | collective-permute-start | bytes 1966088 | tf_op jit(solution)/shard_map/ppermute | solution.py:31
  14.4 36.1 %collective-permute-start = (f32[256,640]{1,0:T(8,128)}, f32[256,640]{1,0:T(8,128)S(1)}, u32[]{:S(2)}, u32[]{:S(2)}) collective-permute-start(f32[256,640]{1,0:T(8,128)} %shard_map.122.p0), channel_id=1, source_target_pairs={{0,8},{4,12},{8,16},{12,20},{16,24},{20,28},{24,32},{28,36},{32,40... | collective-permute-start | bytes 1966088 | tf_op jit(solution)/shard_map/ppermute | solution.py:31
  14.4 0.9 copy-start.8
  15.3 22.6 %collective-permute-start.8 = (f32[256,256]{1,0:T(8,128)S(1)}, f32[256,256]{1,0:T(8,128)S(1)}, u32[]{:S(2)}, u32[]{:S(2)}) collective-permute-start(f32[256,256]{1,0:T(8,128)S(1)} %shard_map.125.pair), channel_id=1, source_target_pairs={{0,24},{4,28},{8,16},{12,20},{16,8},{20,12},{24,0},{28,4},{32,56},... | collective-permute-start | bytes 786440 | tf_op jit(solution)/shard_map/ppermute | solution.py:31
  15.4 6.1 %collective-permute-start.5 = (f32[256,128]{1,0:T(8,128)S(1)}, f32[256,128]{1,0:T(8,128)S(1)}, u32[]{:S(2)}, u32[]{:S(2)}) collective-permute-start(f32[256,128]{1,0:T(8,128)S(1)} %copy-done.20), channel_id=1, source_target_pairs={{0,2},{1,3},{2,0},{3,1},{4,6},{5,7},{6,4},{7,5},{8,10},{9,11},{10,... | collective-permute-start | bytes 393224 | tf_op jit(solution)/shard_map/ppermute | solution.py:57
  21.5 21.4 %copy-start.21 = (f32[256,128]{1,0:T(8,128)}, f32[256,128]{1,0:T(8,128)S(1)}, u32[]{:S(2)}) copy-start(f32[256,128]{1,0:T(8,128)S(1)} %collective-permute-done.5.x2) | copy-start | bytes 393220
  21.5 21.3 %collective-permute-start.4 = (f32[256,128]{1,0:T(8,128)S(1)}, f32[256,128]{1,0:T(8,128)}, u32[]{:S(2)}, u32[]{:S(2)}) collective-permute-start(f32[256,128]{1,0:T(8,128)S(1)} %copy-done.20), channel_id=1, source_target_pairs={{0,1},{1,2},{2,3},{3,0},{4,5},{5,6},{6,7},{7,4},{8,9},{9,10},{10,1... | collective-permute-start | bytes 393224 | tf_op jit(solution)/shard_map/ppermute | solution.py:57
  37.9 4.9 %collective-permute-start.6 = (f32[256,128]{1,0:T(8,128)S(1)}, f32[256,128]{1,0:T(8,128)}, u32[]{:S(2)}, u32[]{:S(2)}) collective-permute-start(f32[256,128]{1,0:T(8,128)S(1)} %copy-done.20), channel_id=1, source_target_pairs={{0,3},{1,0},{2,1},{3,2},{4,7},{5,4},{6,5},{7,6},{8,11},{9,8},{10,9... | collective-permute-start | bytes 393224 | tf_op jit(solution)/shard_map/ppermute | solution.py:57
  42.8 9.9 %copy-start.2 = (f32[1024,256]{1,0:T(8,128)S(1)}, f32[1024,256]{1,0:T(8,128)}, u32[]{:S(2)}) copy-start(f32[1024,256]{1,0:T(8,128)} %shard_map.126.b0) | copy-start | bytes 3145732
  42.8 34.3 %copy-start.17 = (s32[1,1024]{1,0:T(1,128)S(1)}, s32[1,1024]{1,0:T(1,128)}, u32[]{:S(2)}) copy-start(s32[1,1024]{1,0:T(1,128)} %order.5) | copy-start | bytes 12292
  49.2 1.3 copy-start.5
  50.5 23.0 %collective-permute-start.16 = (f32[1024,256]{1,0:T(8,128)}, f32[1024,256]{1,0:T(8,128)}, u32[]{:S(2)}, u32[]{:S(2)}) collective-permute-start(f32[1024,256]{1,0:T(8,128)} %shard_map.126.b0), channel_id=1, source_target_pairs={{0,8},{4,12},{8,0},{12,4},{16,24},{20,28},{24,16},{28,20},{32,40},... | collective-permute-start | bytes 3145736 | tf_op jit(solution)/shard_map/ppermute | solution.py:31
  50.6 31.4 %collective-permute-start.2 = (f32[256,640]{1,0:T(8,128)S(1)}, f32[256,640]{1,0:T(8,128)S(1)}, u32[]{:S(2)}, u32[]{:S(2)}) collective-permute-start(f32[256,640]{1,0:T(8,128)S(1)} %broadcast_select_fusion), channel_id=1, source_target_pairs={{0,4},{4,0},{8,12},{12,8},{16,20},{20,16},{24,28},{28,24},{32,36},... | collective-permute-start | bytes 1966088 | tf_op jit(solution)/shard_map/ppermute | solution.py:31
  52.7 68.7 %collective-permute-start.15 = (f32[1024,256]{1,0:T(8,128)S(1)}, f32[1024,256]{1,0:T(8,128)}, u32[]{:S(2)}, u32[]{:S(2)}) collective-permute-start(f32[1024,256]{1,0:T(8,128)S(1)} %copy-done.2), channel_id=1, source_target_pairs={{0,4},{4,0},{8,12},{12,8},{16,20},{20,16},{24,28},{28,24},{32,36},... | collective-permute-start | bytes 3145736 | tf_op jit(solution)/shard_map/ppermute | solution.py:31
  73.6 52.8 %collective-permute-start.17 = (f32[1024,256]{1,0:T(8,128)}, f32[1024,256]{1,0:T(8,128)}, u32[]{:S(2)}, u32[]{:S(2)}) collective-permute-start(f32[1024,256]{1,0:T(8,128)} %collective-permute-done.16.b2), channel_id=1, source_target_pairs={{0,4},{4,0},{8,12},{12,8},{16,20},{20,16},{24,28},{28,24},{32,36},... | collective-permute-start | bytes 3145736 | tf_op jit(solution)/shard_map/ppermute | solution.py:31
  77.1 4.9 %copy-start.1 = (f32[256,512]{1,0:T(8,128)S(1)}, f32[256,512]{1,0:T(8,128)}, u32[]{:S(2)}) copy-start(f32[256,512]{1,0:T(8,128)} %coefs.1) | copy-start | bytes 1572868
  77.1 4.9 %copy-start.6 = (f32[1024,512]{1,0:T(8,128)S(1)}, f32[1024,512]{1,0:T(8,128)}, u32[]{:S(2)}) copy-start(f32[1024,512]{1,0:T(8,128)} %copy-done.5) | copy-start | bytes 6291460
  77.1 4.9 %copy-start.11 = (f32[256,512]{1,0:T(8,128)S(1)}, f32[256,512]{1,0:T(8,128)}, u32[]{:S(2)}) copy-start(f32[256,512]{1,0:T(8,128)} %own_y.1) | copy-start | bytes 1572868
  77.1 4.9 %copy-start.12 = (bf16[4,256,256]{2,1,0:T(8,128)(2,1)S(1)}, bf16[4,256,256]{2,1,0:T(8,128)(2,1)}, u32[]{:S(2)}) copy-start(bf16[4,256,256]{2,1,0:T(8,128)(2,1)} %get-tuple-element.37.split_rows) | copy-start | bytes 1572868
  77.1 4.9 %copy-start.13 = (f32[4,256,1]{2,1,0:T(8,128)S(1)}, f32[4,256,1]{2,1,0:T(8,128)}, u32[]{:S(2)}) copy-start(f32[4,256,1]{2,1,0:T(8,128)} %get-tuple-element.38.norms) | copy-start | bytes 12292
  90.2 22.1 %copy-start = (f32[1,336,1024]{2,1,0:T(8,128)S(1)}, f32[1,336,1024]{2,1,0:T(8,128)}, u32[]{:S(2)}) copy-start(f32[1,336,1024]{2,1,0:T(8,128)} %m1.3) | copy-start | bytes 4128772
  90.2 22.1 %copy-start.3 = (f32[1,336,256]{2,1,0:T(8,128)S(1)}, f32[1,336,256]{2,1,0:T(8,128)}, u32[]{:S(2)}) copy-start(f32[1,336,256]{2,1,0:T(8,128)} %e1.1) | copy-start | bytes 1032196
  90.2 22.1 %copy-start.19 = (s32[64]{0:T(128)S(1)}, s32[64]{0:T(128)}, u32[]{:S(2)}) copy-start(s32[64]{0:T(128)} %leaf_map.3) | copy-start | bytes 772
  113.7 0.7 copy-start.16
  113.7 15.7 %copy-start.14 = (f32[256,128]{1,0:T(8,128)}, f32[256,128]{1,0:T(8,128)S(1)}, u32[]{:S(2)}) copy-start(f32[256,128]{1,0:T(8,128)S(1)} %get-tuple-element.62.w1) | copy-start | bytes 393220
  114.4 7.0 %all-to-all-start.1 = ((f32[4,32,256]{2,1,0:T(8,128)}), f32[4,32,256]{2,1,0:T(8,128)S(1)}, u32[]{:S(2)}, u32[]{:S(2)}) async-start(f32[4,32,256]{2,1,0:T(8,128)} %bitcast.14), calls=%async_computation.1 | async-start | bytes 262144 | tf_op jit(solution)/shard_map/all_to_all | solution.py:651
  117.8 35.5 %collective-permute-start.9 = (f32[1024,128]{1,0:T(8,128)}, f32[1024,128]{1,0:T(8,128)}, u32[]{:S(2)}, u32[]{:S(2)}) collective-permute-start(f32[1024,128]{1,0:T(8,128)} %get-tuple-element.40), channel_id=1, source_target_pairs={{0,1},{1,2},{2,3},{3,0},{4,5},{5,6},{6,7},{7,4},{8,9},{9,10},{10,1... | collective-permute-start | bytes 1572872 | tf_op jit(solution)/shard_map/ppermute | solution.py:57
  118.1 35.2 %collective-permute-start.10 = (f32[1024,128]{1,0:T(8,128)}, f32[1024,128]{1,0:T(8,128)}, u32[]{:S(2)}, u32[]{:S(2)}) collective-permute-start(f32[1024,128]{1,0:T(8,128)} %get-tuple-element.41), channel_id=1, source_target_pairs={{0,2},{1,3},{2,0},{3,1},{4,6},{5,7},{6,4},{7,5},{8,10},{9,11},{10,... | collective-permute-start | bytes 1572872 | tf_op jit(solution)/shard_map/ppermute | solution.py:57
  119.9 33.5 %collective-permute-start.11 = (f32[1024,128]{1,0:T(8,128)}, f32[1024,128]{1,0:T(8,128)}, u32[]{:S(2)}, u32[]{:S(2)}) collective-permute-start(f32[1024,128]{1,0:T(8,128)} %get-tuple-element.42), channel_id=1, source_target_pairs={{0,3},{1,0},{2,1},{3,2},{4,7},{5,4},{6,5},{7,6},{8,11},{9,8},{10,9... | collective-permute-start | bytes 1572872 | tf_op jit(solution)/shard_map/ppermute | solution.py:57
  121.4 5.0 %collective-permute-start.14 = (f32[32,256]{1,0:T(8,128)S(1)}, f32[32,256]{1,0:T(8,128)S(1)}, u32[]{:S(2)}, u32[]{:S(2)}) collective-permute-start(f32[32,256]{1,0:T(8,128)S(1)} %fusion.1.r0), channel_id=1, source_target_pairs={{0,56},{4,60},{8,48},{12,52},{16,40},{20,44},{24,32},{28,36},{32,2... | collective-permute-start | bytes 98312 | tf_op jit(solution)/shard_map/ppermute | solution.py:31
  126.4 3.2 %collective-permute-start.13 = (f32[32,256]{1,0:T(8,128)S(1)}, f32[32,256]{1,0:T(8,128)S(1)}, u32[]{:S(2)}, u32[]{:S(2)}) collective-permute-start(f32[32,256]{1,0:T(8,128)S(1)} %fusion.1.r0), channel_id=1, source_target_pairs={{0,32},{4,36},{8,40},{12,44},{16,48},{20,52},{24,56},{28,60},{32,0... | collective-permute-start | bytes 98312 | tf_op jit(solution)/shard_map/ppermute | solution.py:31
  126.4 4.4 %collective-permute-start.12 = (f32[32,256]{1,0:T(8,128)S(1)}, f32[32,256]{1,0:T(8,128)S(1)}, u32[]{:S(2)}, u32[]{:S(2)}) collective-permute-start(f32[32,256]{1,0:T(8,128)S(1)} %fusion.1.r0), channel_id=1, source_target_pairs={{0,24},{4,28},{8,16},{12,20},{16,8},{20,12},{24,0},{28,4},{32,56},... | collective-permute-start | bytes 98312 | tf_op jit(solution)/shard_map/ppermute | solution.py:31
  129.4 35.3 %copy-start.7 = (f32[1024,256]{1,0:T(8,128)}, f32[1024,256]{1,0:T(8,128)S(1)}, u32[]{:S(2)}) copy-start(f32[1024,256]{1,0:T(8,128)S(1)} %get-tuple-element.61.e1) | copy-start | bytes 3145732
  131.6 5.3 %collective-permute-start.20 = (f32[32,256]{1,0:T(8,128)S(1)}, f32[32,256]{1,0:T(8,128)S(1)}, u32[]{:S(2)}, u32[]{:S(2)}) collective-permute-start(f32[32,256]{1,0:T(8,128)S(1)} %get-tuple-element.48), channel_id=1, source_target_pairs={{0,56},{4,60},{8,48},{12,52},{16,40},{20,44},{24,32},{28,36},{32,2... | collective-permute-start | bytes 98312 | tf_op jit(solution)/shard_map/ppermute | solution.py:31
  133.9 4.1 %collective-permute-start.19 = (f32[32,256]{1,0:T(8,128)S(1)}, f32[32,256]{1,0:T(8,128)S(1)}, u32[]{:S(2)}, u32[]{:S(2)}) collective-permute-start(f32[32,256]{1,0:T(8,128)S(1)} %get-tuple-element.48), channel_id=1, source_target_pairs={{0,32},{4,36},{8,40},{12,44},{16,48},{20,52},{24,56},{28,60},{32,0... | collective-permute-start | bytes 98312 | tf_op jit(solution)/shard_map/ppermute | solution.py:31
  136.9 4.4 %collective-permute-start.18 = (f32[32,256]{1,0:T(8,128)S(1)}, f32[32,256]{1,0:T(8,128)S(1)}, u32[]{:S(2)}, u32[]{:S(2)}) collective-permute-start(f32[32,256]{1,0:T(8,128)S(1)} %get-tuple-element.48), channel_id=1, source_target_pairs={{0,24},{4,28},{8,16},{12,20},{16,8},{20,12},{24,0},{28,4},{32,56},... | collective-permute-start | bytes 98312 | tf_op jit(solution)/shard_map/ppermute | solution.py:31
  141.3 5.9 %collective-permute-start.23 = (f32[32,256]{1,0:T(8,128)S(1)}, f32[32,256]{1,0:T(8,128)S(1)}, u32[]{:S(2)}, u32[]{:S(2)}) collective-permute-start(f32[32,256]{1,0:T(8,128)S(1)} %add_add_fusion.r0), channel_id=1, source_target_pairs={{160,0},{164,4},{168,8},{172,12},{176,16},{180,20},{184,24},{188,2... | collective-permute-start | bytes 98312 | tf_op jit(solution)/shard_map/ppermute | solution.py:53
  145.1 5.2 %collective-permute-start.22 = (f32[32,256]{1,0:T(8,128)S(1)}, f32[32,256]{1,0:T(8,128)S(1)}, u32[]{:S(2)}, u32[]{:S(2)}) collective-permute-start(f32[32,256]{1,0:T(8,128)S(1)} %add_add_fusion.r0), channel_id=1, source_target_pairs={{64,0},{68,4},{72,8},{76,12},{80,16},{84,20},{88,24},{92,28},{224,... | collective-permute-start | bytes 98312 | tf_op jit(solution)/shard_map/ppermute | solution.py:53
  147.1 5.3 %collective-permute-start.21 = (f32[32,256]{1,0:T(8,128)S(1)}, f32[32,256]{1,0:T(8,128)S(1)}, u32[]{:S(2)}, u32[]{:S(2)}) collective-permute-start(f32[32,256]{1,0:T(8,128)S(1)} %add_add_fusion.r0), channel_id=1, source_target_pairs={{224,0},{228,4},{232,8},{236,12},{240,16},{244,20},{248,24},{252,2... | collective-permute-start | bytes 98312 | tf_op jit(solution)/shard_map/ppermute | solution.py:53
  153.3 21.9 %copy-start.9 = (f32[1024,128]{1,0:T(8,128)S(1)}, f32[1024,128]{1,0:T(8,128)}, u32[]{:S(2)}) copy-start(f32[1024,128]{1,0:T(8,128)} %get-tuple-element.52.p0) | copy-start | bytes 1572868
  178.8 1.0 copy-start.10
  179.8 10.1 %copy-start.24 = (f32[256,128]{1,0:T(8,128)S(1)}, f32[256,128]{1,0:T(8,128)}, u32[]{:S(2)}) copy-start(f32[256,128]{1,0:T(8,128)} %get-tuple-element.57) | copy-start | bytes 393220
  179.8 11.5 %copy-start.23 = (f32[256,128]{1,0:T(8,128)S(1)}, f32[256,128]{1,0:T(8,128)}, u32[]{:S(2)}) copy-start(f32[256,128]{1,0:T(8,128)} %get-tuple-element.58) | copy-start | bytes 393220
  179.8 13.9 %copy-start.22 = (f32[256,128]{1,0:T(8,128)S(1)}, f32[256,128]{1,0:T(8,128)}, u32[]{:S(2)}) copy-start(f32[256,128]{1,0:T(8,128)} %get-tuple-element.59) | copy-start | bytes 393220
  179.8 25.1 %copy-start.15 = (f32[256,128]{1,0:T(8,128)S(1)}, f32[256,128]{1,0:T(8,128)}, u32[]{:S(2)}) copy-start(f32[256,128]{1,0:T(8,128)} %get-tuple-element.56.r0) | copy-start | bytes 393220
  186.4 18.5 %all-to-all-start.2 = ((f32[4,256,128]{2,1,0:T(8,128)}), f32[4,256,128]{2,1,0:T(8,128)S(1)}, u32[]{:S(2)}, u32[]{:S(2)}) async-start(f32[4,256,128]{2,1,0:T(8,128)} %bitcast.9), calls=%async_computation.2 | async-start | bytes 1048576 | tf_op jit(solution)/shard_map/all_to_all | solution.py:600
  189.9 11.9 %collective-permute-start.24 = (f32[256,128]{1,0:T(8,128)S(1)}, f32[256,128]{1,0:T(8,128)S(1)}, u32[]{:S(2)}, u32[]{:S(2)}) collective-permute-start(f32[256,128]{1,0:T(8,128)S(1)} %copy-done.24), channel_id=1, source_target_pairs={{0,1},{1,2},{2,3},{3,0},{4,5},{5,6},{6,7},{7,4},{8,9},{9,10},{10,1... | collective-permute-start | bytes 393224 | tf_op jit(solution)/shard_map/ppermute | solution.py:57
  191.3 13.6 %collective-permute-start.25 = (f32[256,128]{1,0:T(8,128)S(1)}, f32[256,128]{1,0:T(8,128)S(1)}, u32[]{:S(2)}, u32[]{:S(2)}) collective-permute-start(f32[256,128]{1,0:T(8,128)S(1)} %copy-done.23), channel_id=1, source_target_pairs={{0,2},{1,3},{2,0},{3,1},{4,6},{5,7},{6,4},{7,5},{8,10},{9,11},{10,... | collective-permute-start | bytes 393224 | tf_op jit(solution)/shard_map/ppermute | solution.py:57
  193.8 11.2 %collective-permute-start.26 = (f32[256,128]{1,0:T(8,128)S(1)}, f32[256,128]{1,0:T(8,128)S(1)}, u32[]{:S(2)}, u32[]{:S(2)}) collective-permute-start(f32[256,128]{1,0:T(8,128)S(1)} %copy-done.22), channel_id=1, source_target_pairs={{0,3},{1,0},{2,1},{3,2},{4,7},{5,4},{6,5},{7,6},{8,11},{9,8},{10,9... | collective-permute-start | bytes 393224 | tf_op jit(solution)/shard_map/ppermute | solution.py:57

commit v8 on v7

--- a/solution.py
+++ b/solution.py
@@ -534,19 +534,20 @@
 
 
 def finish_kernel(
-    place, leaf_map, order, pieces, ordered, basis, solve, delta,
-    basis_in, solve_in, sems, picks, rhs, sides,
+    place, leaf_map, order, pieces, ordered, basis, solve, delta, solve_in, sems, picks, rhs, sides
 ):
-    first, *rest = load_solve(basis, solve, basis_in, solve_in, sems)
+    rest = []
+    for k in range(4):
+        rows = pl.ds(k * Q, Q)
+        rest.append(pltpu.make_async_copy(solve.at[0, rows, :], solve_in.at[rows, :], sems.at[k]))
+    for copy in rest:
+        copy.start()
     base = place[3] // 4 * 4
     slot = jnp.int32(3)
     for k in range(3):
         slot = jnp.where(leaf_map[base + k] == place[3], k, slot)
     picks_by_row(order[...], picks)
-    first.wait()
-    rhs[...] = jnp.concatenate(
-        split(ordered[...] - dot3(basis_in[...], pieces[slot])), axis=1
-    )
+    rhs[...] = jnp.concatenate(split(ordered[...] - dot3(basis[0], pieces[slot])), axis=1)
     for k in range(4):
         rest[k].wait()
         rows = slice(k * Q, (k + 1) * Q)
@@ -566,15 +567,15 @@
     return kernel(
         finish_kernel,
         [(1024, 128)],
-        [order, pieces, ordered],
+        [order, pieces, ordered, leaf_basis],
         (place, leaf_map),
-        SOLVE_SCRATCH
+        SOLVE_SCRATCH[1:]
         + [
             pltpu.VMEM((1024, 1024), BF16),
             pltpu.VMEM((1024, 256), BF16),
             pltpu.VMEM((1024, 256), BF16),
         ],
-        [leaf_basis, leaf_inverse],
+        [leaf_inverse],
     )
 
 

time: 207 us -> 208 us (level)
  no operation moved by 1% of the time
where the time goes in v8:
time: 208 us; the launch traced here: 207 us
  waiting for transfers between devices  66.2 us (32%)
  starting transfers between devices  47.8 us (23%)
  Pallas kernels  46 us (22%)
  blocking collectives  39.8 us (19%)
  local copies, waits for them, and re-layouts  4.01 us (2%)
    ppermute x15, waiting for transfers between devices, leaf_route(): return lax.ppermute(value, 'leaf', [(i, target(i)) for i in range(LEAVES)])  48.5 us
    pallas_call x14, Pallas kernels, kernel(): pl.pallas_call(body, in_specs=[SMEM] * len(scalars) + [VMEM] * len(values...  44.4 us
    all_gather x3, blocking collectives, gather4(): return lax.all_gather(value, 'leaf', axis=0, axis_index_groups=groups)  26.4 us
    ppermute x15, starting transfers between devices, leaf_route(): return lax.ppermute(value, 'leaf', [(i, target(i)) for i in range(LEAVES)])  19 us
    ppermute x9, starting transfers between devices, col_shift(): return lax.ppermute(value, 'col', [(i, (i + step) % 4) for i in range(4)])  14.8 us
    all_to_all x1, blocking collectives, swap_cols(): return lax.all_to_all(value, 'col', 0, 0, tiled=True)  13.5 us
    ppermute x9, waiting for transfers between devices, col_shift(): return lax.ppermute(value, 'col', [(i, (i + step) % 4) for i in range(4)])  13.1 us
    ppermute x3, starting transfers between devices, z_from(): return lax.ppermute(value, 'leaf', route)  7.1 us
  transfers between devices with their start and end apart: 29, of which 13 were waited for; matrix products, arithmetic and copies ran while one was open for 1% of the time, Pallas kernels for 14%

profile of v8, /device:TPU:1, one launch (start us, length us, event | category | flops | bytes accessed | tf_op | source)
XLA Modules:
  0.0 206.9 jit_solution(6852973782429883289)
XLA Ops:
  0.6 0.0 copy-start.21
  0.6 2.0 shard_map.122.p0
  2.6 3.3 %collective-permute-start.3 = (f32[256,640]{1,0:T(8,128)}, f32[256,640]{1,0:T(8,128)}, u32[]{:S(2)}, u32[]{:S(2)}) collective-permute-start(f32[256,640]{1,0:T(8,128)} %shard_map.122.p0), channel_id=1, source_target_pairs={{0,4},{4,0},{8,12},{12,8},{16,20},{20,16},{24,28},{28,24},{32,36},... | collective-permute-start | bytes 1966088 | tf_op jit(solution)/shard_map/ppermute | solution.py:31
  5.9 1.6 shard_map.124.slices
  7.5 0.1 collective-permute-start.7
  7.6 6.8 %collective-permute-start.1 = (f32[256,640]{1,0:T(8,128)}, f32[256,640]{1,0:T(8,128)S(1)}, u32[]{:S(2)}, u32[]{:S(2)}) collective-permute-start(f32[256,640]{1,0:T(8,128)} %shard_map.122.p0), channel_id=1, source_target_pairs={{0,248},{4,252},{8,0},{12,4},{16,8},{20,12},{24,16},{28,20},{32,24... | collective-permute-start | bytes 1966088 | tf_op jit(solution)/shard_map/ppermute | solution.py:31
  14.4 0.9 copy-done.9
  15.3 0.1 collective-permute-start.8
  15.4 3.0 %collective-permute-start.5 = (f32[256,128]{1,0:T(8,128)S(1)}, f32[256,128]{1,0:T(8,128)S(1)}, u32[]{:S(2)}, u32[]{:S(2)}) collective-permute-start(f32[256,128]{1,0:T(8,128)S(1)} %copy-done.21), channel_id=1, source_target_pairs={{0,2},{1,3},{2,0},{3,1},{4,6},{5,7},{6,4},{7,5},{8,10},{9,11},{10,... | collective-permute-start | bytes 393224 | tf_op jit(solution)/shard_map/ppermute | solution.py:57
  18.4 3.1 %collective-permute-done.5.x2 = f32[256,128]{1,0:T(8,128)S(1)} collective-permute-done((f32[256,128]{1,0:T(8,128)S(1)}, f32[256,128]{1,0:T(8,128)S(1)}, u32[]{:S(2)}, u32[]{:S(2)}) %collective-permute-start.5) | collective-permute-done | bytes 131104 | tf_op jit(solution)/shard_map/ppermute | solution.py:57
  21.5 1.3 collective-permute-start.4
  22.8 15.1 %collective-permute-done.8.mirrored = f32[256,256]{1,0:T(8,128)S(1)} collective-permute-done((f32[256,256]{1,0:T(8,128)S(1)}, f32[256,256]{1,0:T(8,128)S(1)}, u32[]{:S(2)}, u32[]{:S(2)}) %collective-permute-start.8) | collective-permute-done | bytes 262176 | tf_op jit(solution)/shard_map/ppermute | solution.py:31
  37.9 2.7 %collective-permute-start.6 = (f32[256,128]{1,0:T(8,128)S(1)}, f32[256,128]{1,0:T(8,128)}, u32[]{:S(2)}, u32[]{:S(2)}) collective-permute-start(f32[256,128]{1,0:T(8,128)S(1)} %copy-done.21), channel_id=1, source_target_pairs={{0,3},{1,0},{2,1},{3,2},{4,7},{5,4},{6,5},{7,6},{8,11},{9,8},{10,9... | collective-permute-start | bytes 393224 | tf_op jit(solution)/shard_map/ppermute | solution.py:57
  40.7 0.1 pad_add_fusion.place
  40.8 2.0 shard_map.126.b0
  42.9 6.3 %shard_map.123 = (f32[1024,512]{1,0:T(8,128)S(1)}, bf16[4,256,256]{2,1,0:T(8,128)(2,1)}, f32[4,256,1]{2,1,0:T(8,128)}) custom-call(s32[4]{0:T(128)S(1)} %pad_add_fusion.place, s32[1,5]{1,0:T(1,128)S(1)} %copy-done.19, f32[256,640]{1,0:T(8,128)S(1)} %copy-done.5, f32[256,640]{1,0:T(8,128)} %collective-permute-done.3.p1, f32[256,128]{1,0:T(8,128)} %x0.1, ...), custom_call_target="tpu_custom_call" | custom-call | tf_op jit(solution)/shard_map/pallas_call | solution.py:97
  49.2 1.3 copy-done.6
  50.5 0.1 broadcast_select_fusion
  50.6 2.1 collective-permute-start.2
  52.7 0.1 collective-permute-start.15
  52.8 20.8 %collective-permute-done.16.b2 = f32[1024,256]{1,0:T(8,128)} collective-permute-done((f32[1024,256]{1,0:T(8,128)}, f32[1024,256]{1,0:T(8,128)}, u32[]{:S(2)}, u32[]{:S(2)}) %collective-permute-start.16) | collective-permute-done | bytes 1048608 | tf_op jit(solution)/shard_map/ppermute | solution.py:31
  73.6 2.8 %collective-permute-start.17 = (f32[1024,256]{1,0:T(8,128)}, f32[1024,256]{1,0:T(8,128)}, u32[]{:S(2)}, u32[]{:S(2)}) collective-permute-start(f32[1024,256]{1,0:T(8,128)} %collective-permute-done.16.b2), channel_id=1, source_target_pairs={{0,4},{4,0},{8,12},{12,8},{16,20},{20,16},{24,28},{28,24},{32,36},... | collective-permute-start | bytes 3145736 | tf_op jit(solution)/shard_map/ppermute | solution.py:31
  77.1 0.0 copy-start.1
  77.1 4.8 %shard_map.127.lead = f32[256,1024]{1,0:T(8,128)S(1)} custom-call(s32[1,1024]{1,0:T(1,128)S(1)} %copy-done.18, f32[1,1024,256]{2,1,0:T(8,128)} %basis.3, f32[1,1024,1024]{2,1,0:T(8,128)} %solve.3), custom_call_target="tpu_custom_call" | custom-call | tf_op jit(solution)/shard_map/pallas_call | solution.py:97
  82.0 8.2 %shard_map.128 = (f32[4,256,128]{2,1,0:T(8,128)S(1)}, f32[1024,128]{1,0:T(8,128)}, f32[1024,128]{1,0:T(8,128)}, f32[1024,128]{1,0:T(8,128)}, f32[1024,128]{1,0:T(8,128)}) custom-call(s32[4]{0:T(128)S(1)} %pad_add_fusion.place, s32[1,5]{1,0:T(1,128)S(1)} %copy-done.19, f32[1]{0:T(128)S(6)} %copy.13.ridge, f32[256,640]{1,0:T(8,128)S(1)} %collective-permute-done.p0, ...), custom_call_target="tpu_custom_call" | custom-call | tf_op jit(solution)/shard_map/pallas_call | solution.py:97
  90.3 13.5 %all_to_all.19 = f32[4,256,128]{2,1,0:T(8,128)} all-to-all(f32[4,256,128]{2,1,0:T(8,128)S(1)} %get-tuple-element.43), channel_id=1, replica_groups=mesh['leaf'=64,'col'=4] {'col'}, dimensions={0} | all-to-all | bytes 1048576 | tf_op jit(solution)/shard_map/all_to_all | solution.py:601
  103.7 1.1 reduce_sum.9
  104.8 7.5 %all-gather = f32[1024,128]{1,0:T(8,128)S(1)} all-gather(f32[256,128]{1,0:T(8,128)S(1)} %reduce_sum.9), channel_id=2, replica_groups={{0,4,8,12},{16,20,24,28},{32,36,40,44},{48,52,56,60},{64,68,72,76},{80,..., dimensions={0}, use_global_device_ids=true | all-gather | bytes 655360 | tf_op jit(solution)/shard_map/all_gather | solution.py:61
  112.3 1.4 shard_map.129
  113.8 0.6 copy-done.17
  114.4 3.4 %all-to-all-start.1 = ((f32[4,32,256]{2,1,0:T(8,128)}), f32[4,32,256]{2,1,0:T(8,128)S(1)}, u32[]{:S(2)}, u32[]{:S(2)}) async-start(f32[4,32,256]{2,1,0:T(8,128)} %bitcast.14), calls=%async_computation.1 | async-start | bytes 262144 | tf_op jit(solution)/shard_map/all_to_all | solution.py:652
  117.8 0.3 collective-permute-start.9
  118.1 1.8 collective-permute-start.10
  119.9 0.7 collective-permute-start.11
  120.6 0.8 all-to-all-done.1
  121.4 0.1 collective-permute-start.14
  121.5 4.9 %collective-permute-done.14.r3 = f32[32,256]{1,0:T(8,128)S(1)} collective-permute-done((f32[32,256]{1,0:T(8,128)S(1)}, f32[32,256]{1,0:T(8,128)S(1)}, u32[]{:S(2)}, u32[]{:S(2)}) %collective-permute-start.14) | collective-permute-done | bytes 32800 | tf_op jit(solution)/shard_map/ppermute | solution.py:31
  126.4 0.3 collective-permute-start.12
  126.7 2.7 %shard_map.130 = (f32[1024,256]{1,0:T(8,128)S(1)}, f32[256,1024]{1,0:T(8,128)S(1)}, f32[256,256]{1,0:T(8,128)S(1)}, f32[256,1024]{1,0:T(8,128)S(1)}, f32[256,256]{1,0:T(8,128)S(1)}) custom-call(s32[4]{0:T(128)S(1)} %pad_add_fusion.place, f32[1024,256]{1,0:T(8,128)S(1)} %copy-done.2, f32[1024,256]{1,0:T(8,128)} %collective-permute-done.15.b1, ...), custom_call_target="tpu_custom_call" | custom-call | tf_op jit(solution)/shard_map/pallas_call | solution.py:97
  129.4 0.1 collective-permute-done.13.r2
  129.6 1.2 collective-permute-done.12.r1
  130.8 0.8 shard_map.131
  131.6 2.3 %collective-permute-start.20 = (f32[32,256]{1,0:T(8,128)S(1)}, f32[32,256]{1,0:T(8,128)S(1)}, u32[]{:S(2)}, u32[]{:S(2)}) collective-permute-start(f32[32,256]{1,0:T(8,128)S(1)} %get-tuple-element.48), channel_id=1, source_target_pairs={{0,56},{4,60},{8,48},{12,52},{16,40},{20,44},{24,32},{28,36},{32,2... | collective-permute-start | bytes 98312 | tf_op jit(solution)/shard_map/ppermute | solution.py:31
  133.9 3.0 %collective-permute-done.20 = f32[32,256]{1,0:T(8,128)S(1)} collective-permute-done((f32[32,256]{1,0:T(8,128)S(1)}, f32[32,256]{1,0:T(8,128)S(1)}, u32[]{:S(2)}, u32[]{:S(2)}) %collective-permute-start.20) | collective-permute-done | bytes 32800 | tf_op jit(solution)/shard_map/ppermute | solution.py:31
  136.9 1.1 collective-permute-start.18
  138.0 3.3 %collective-permute-done.18 = f32[32,256]{1,0:T(8,128)S(1)} collective-permute-done((f32[32,256]{1,0:T(8,128)S(1)}, f32[32,256]{1,0:T(8,128)S(1)}, u32[]{:S(2)}, u32[]{:S(2)}) %collective-permute-start.18) | collective-permute-done | bytes 32800 | tf_op jit(solution)/shard_map/ppermute | solution.py:31
  141.3 3.9 %collective-permute-start.23 = (f32[32,256]{1,0:T(8,128)S(1)}, f32[32,256]{1,0:T(8,128)S(1)}, u32[]{:S(2)}, u32[]{:S(2)}) collective-permute-start(f32[32,256]{1,0:T(8,128)S(1)} %add_add_fusion.r0), channel_id=1, source_target_pairs={{160,0},{164,4},{168,8},{172,12},{176,16},{180,20},{184,24},{188,2... | collective-permute-start | bytes 98312 | tf_op jit(solution)/shard_map/ppermute | solution.py:53
  145.2 2.0 collective-permute-done.23.r3
  147.1 3.2 %collective-permute-start.21 = (f32[32,256]{1,0:T(8,128)S(1)}, f32[32,256]{1,0:T(8,128)S(1)}, u32[]{:S(2)}, u32[]{:S(2)}) collective-permute-start(f32[32,256]{1,0:T(8,128)S(1)} %add_add_fusion.r0), channel_id=1, source_target_pairs={{224,0},{228,4},{232,8},{236,12},{240,16},{244,20},{248,24},{252,2... | collective-permute-start | bytes 98312 | tf_op jit(solution)/shard_map/ppermute | solution.py:53
  150.4 1.8 collective-permute-done.21.r1
  152.2 0.9 shard_map.132
  153.1 11.6 %all-gather.1 = f32[128,256]{1,0:T(8,128)S(1)} all-gather(f32[32,256]{1,0:T(8,128)S(1)} %shard_map.132), channel_id=3, replica_groups={{0,4,8,12},{24,28,16,20},{32,36,40,44},{56,60,48,52},{64,68,72,76},{88,..., dimensions={0}, use_global_device_ids=true | all-gather | bytes 163840 | tf_op jit(solution)/shard_map/all_gather | solution.py:61
  164.7 3.3 %shard_map.134 = f32[256,128]{1,0:T(8,128)S(1)} custom-call(f32[4,32,256]{2,1,0:T(8,128)S(1)} %bitcast.13, f32[1024,256]{1,0:T(8,128)} %copy-done.8, f32[1,336,1024]{2,1,0:T(8,128)} %m1.3, f32[256,128]{1,0:T(8,128)} %copy-done.15), custom_call_target="tpu_custom_call" | custom-call | tf_op jit(solution)/shard_map/pallas_call | solution.py:97
  168.0 7.3 %all-gather.2 = f32[1024,128]{1,0:T(8,128)S(1)} all-gather(f32[256,128]{1,0:T(8,128)S(1)} %shard_map.134), channel_id=4, replica_groups={{0,4,8,12},{16,20,24,28},{32,36,40,44},{48,52,56,60},{64,68,72,76},{80,..., dimensions={0}, use_global_device_ids=true | all-gather | bytes 655360 | tf_op jit(solution)/shard_map/all_gather | solution.py:61
  175.3 3.6 %shard_map.133 = (f32[1024,128]{1,0:T(8,128)}, f32[256,128]{1,0:T(8,128)}, f32[256,128]{1,0:T(8,128)}, f32[256,128]{1,0:T(8,128)}, f32[256,128]{1,0:T(8,128)}) custom-call(s32[4]{0:T(128)S(1)} %pad_add_fusion.place, s32[1,1024]{1,0:T(1,128)S(1)} %copy-done.18, f32[1024,128]{1,0:T(8,128)S(1)} %copy-done.10, f32[1024,128]{1,0:T(8,128)} %collective-permute-done.9.p1, ...), custom_call_target="tpu_custom_call" | custom-call | tf_op jit(solution)/shard_map/pallas_call | solution.py:97
  178.9 1.0 copy-done.11
  179.9 6.8 %shard_map.135 = f32[1024,128]{1,0:T(8,128)} custom-call(s32[4]{0:T(128)S(1)} %pad_add_fusion.place, s32[64]{0:T(128)S(1)} %copy-done.20, s32[1,1024]{1,0:T(1,128)S(1)} %copy-done.18, f32[4,256,128]{2,1,0:T(8,128)S(1)} %bitcast.11, f32[1024,128]{1,0:T(8,128)S(1)} %copy-done.11, f32[1,1024,256]{2,1,0:T(8,128)S(1)} %copy-done.3, f32[1,1024,1024]{2,1,0:T(8,128)} %solve.3), custom_call_target="tpu_custom_call" | custom-call | tf_op jit(solution)/shard_map/pallas_call | solution.py:97
  186.8 3.5 %all-to-all-start.2 = ((f32[4,256,128]{2,1,0:T(8,128)}), f32[4,256,128]{2,1,0:T(8,128)S(1)}, u32[]{:S(2)}, u32[]{:S(2)}) async-start(f32[4,256,128]{2,1,0:T(8,128)} %bitcast.9), calls=%async_computation.2 | async-start | bytes 1048576 | tf_op jit(solution)/shard_map/all_to_all | solution.py:601
  190.3 1.4 collective-permute-start.24
  191.7 2.4 %collective-permute-start.25 = (f32[256,128]{1,0:T(8,128)S(1)}, f32[256,128]{1,0:T(8,128)S(1)}, u32[]{:S(2)}, u32[]{:S(2)}) collective-permute-start(f32[256,128]{1,0:T(8,128)S(1)} %copy-done.24), channel_id=1, source_target_pairs={{0,2},{1,3},{2,0},{3,1},{4,6},{5,7},{6,4},{7,5},{8,10},{9,11},{10,... | collective-permute-start | bytes 393224 | tf_op jit(solution)/shard_map/ppermute | solution.py:57
  194.1 1.2 collective-permute-start.26
  195.3 6.9 %collective-permute-done.24.r1 = f32[256,128]{1,0:T(8,128)S(1)} collective-permute-done((f32[256,128]{1,0:T(8,128)S(1)}, f32[256,128]{1,0:T(8,128)S(1)}, u32[]{:S(2)}, u32[]{:S(2)}) %collective-permute-start.24) | collective-permute-done | bytes 131104 | tf_op jit(solution)/shard_map/ppermute | solution.py:57
  202.1 3.1 %collective-permute-done.25.r2 = f32[256,128]{1,0:T(8,128)S(1)} collective-permute-done((f32[256,128]{1,0:T(8,128)S(1)}, f32[256,128]{1,0:T(8,128)S(1)}, u32[]{:S(2)}, u32[]{:S(2)}) %collective-permute-start.25) | collective-permute-done | bytes 131104 | tf_op jit(solution)/shard_map/ppermute | solution.py:57
  205.3 1.6 outputs.1
  (70 shorter events, 0.2 us)
Async XLA Ops:
  0.6 14.8 %copy-start.21 = (f32[256,128]{1,0:T(8,128)S(1)}, f32[256,128]{1,0:T(8,128)}, u32[]{:S(2)}) copy-start(f32[256,128]{1,0:T(8,128)} %x0.1) | copy-start | bytes 393220
  2.6 40.2 %collective-permute-start.3 = (f32[256,640]{1,0:T(8,128)}, f32[256,640]{1,0:T(8,128)}, u32[]{:S(2)}, u32[]{:S(2)}) collective-permute-start(f32[256,640]{1,0:T(8,128)} %shard_map.122.p0), channel_id=1, source_target_pairs={{0,4},{4,0},{8,12},{12,8},{16,20},{20,16},{24,28},{28,24},{32,36},... | collective-permute-start | bytes 1966088 | tf_op jit(solution)/shard_map/ppermute | solution.py:31
  5.9 36.9 %copy-start.19 = (s32[1,5]{1,0:T(1,128)S(1)}, s32[1,5]{1,0:T(1,128)}, u32[]{:S(2)}) copy-start(s32[1,5]{1,0:T(1,128)} %mask.3) | copy-start | bytes 64
  7.5 35.4 %copy-start.5 = (f32[256,640]{1,0:T(8,128)S(1)}, f32[256,640]{1,0:T(8,128)}, u32[]{:S(2)}) copy-start(f32[256,640]{1,0:T(8,128)} %shard_map.122.p0) | copy-start | bytes 1966084
  7.5 6.9 %collective-permute-start.7 = (f32[128,256]{1,0:T(8,128)}, f32[128,256]{1,0:T(8,128)S(1)}, u32[]{:S(2)}, u32[]{:S(2)}) collective-permute-start(f32[128,256]{1,0:T(8,128)} %shard_map.124.slices), channel_id=1, source_target_pairs={{0,32},{4,36},{8,40},{12,44},{16,48},{20,52},{24,56},{28,60},{32,0... | collective-permute-start | bytes 393224 | tf_op jit(solution)/shard_map/ppermute | solution.py:31
  7.6 42.9 %collective-permute-start.1 = (f32[256,640]{1,0:T(8,128)}, f32[256,640]{1,0:T(8,128)S(1)}, u32[]{:S(2)}, u32[]{:S(2)}) collective-permute-start(f32[256,640]{1,0:T(8,128)} %shard_map.122.p0), channel_id=1, source_target_pairs={{0,248},{4,252},{8,0},{12,4},{16,8},{20,12},{24,16},{28,20},{32,24... | collective-permute-start | bytes 1966088 | tf_op jit(solution)/shard_map/ppermute | solution.py:31
  14.4 36.2 %collective-permute-start = (f32[256,640]{1,0:T(8,128)}, f32[256,640]{1,0:T(8,128)S(1)}, u32[]{:S(2)}, u32[]{:S(2)}) collective-permute-start(f32[256,640]{1,0:T(8,128)} %shard_map.122.p0), channel_id=1, source_target_pairs={{0,8},{4,12},{8,16},{12,20},{16,24},{20,28},{24,32},{28,36},{32,40... | collective-permute-start | bytes 1966088 | tf_op jit(solution)/shard_map/ppermute | solution.py:31
  14.4 0.9 copy-start.9
  15.3 22.6 %collective-permute-start.8 = (f32[256,256]{1,0:T(8,128)S(1)}, f32[256,256]{1,0:T(8,128)S(1)}, u32[]{:S(2)}, u32[]{:S(2)}) collective-permute-start(f32[256,256]{1,0:T(8,128)S(1)} %shard_map.125.pair), channel_id=1, source_target_pairs={{0,24},{4,28},{8,16},{12,20},{16,8},{20,12},{24,0},{28,4},{32,56},... | collective-permute-start | bytes 786440 | tf_op jit(solution)/shard_map/ppermute | solution.py:31
  15.4 6.1 %collective-permute-start.5 = (f32[256,128]{1,0:T(8,128)S(1)}, f32[256,128]{1,0:T(8,128)S(1)}, u32[]{:S(2)}, u32[]{:S(2)}) collective-permute-start(f32[256,128]{1,0:T(8,128)S(1)} %copy-done.21), channel_id=1, source_target_pairs={{0,2},{1,3},{2,0},{3,1},{4,6},{5,7},{6,4},{7,5},{8,10},{9,11},{10,... | collective-permute-start | bytes 393224 | tf_op jit(solution)/shard_map/ppermute | solution.py:57
  21.5 21.4 %copy-start.22 = (f32[256,128]{1,0:T(8,128)}, f32[256,128]{1,0:T(8,128)S(1)}, u32[]{:S(2)}) copy-start(f32[256,128]{1,0:T(8,128)S(1)} %collective-permute-done.5.x2) | copy-start | bytes 393220
  21.5 21.3 %collective-permute-start.4 = (f32[256,128]{1,0:T(8,128)S(1)}, f32[256,128]{1,0:T(8,128)}, u32[]{:S(2)}, u32[]{:S(2)}) collective-permute-start(f32[256,128]{1,0:T(8,128)S(1)} %copy-done.21), channel_id=1, source_target_pairs={{0,1},{1,2},{2,3},{3,0},{4,5},{5,6},{6,7},{7,4},{8,9},{9,10},{10,1... | collective-permute-start | bytes 393224 | tf_op jit(solution)/shard_map/ppermute | solution.py:57
  37.9 4.9 %collective-permute-start.6 = (f32[256,128]{1,0:T(8,128)S(1)}, f32[256,128]{1,0:T(8,128)}, u32[]{:S(2)}, u32[]{:S(2)}) collective-permute-start(f32[256,128]{1,0:T(8,128)S(1)} %copy-done.21), channel_id=1, source_target_pairs={{0,3},{1,0},{2,1},{3,2},{4,7},{5,4},{6,5},{7,6},{8,11},{9,8},{10,9... | collective-permute-start | bytes 393224 | tf_op jit(solution)/shard_map/ppermute | solution.py:57
  42.8 9.9 %copy-start.2 = (f32[1024,256]{1,0:T(8,128)S(1)}, f32[1024,256]{1,0:T(8,128)}, u32[]{:S(2)}) copy-start(f32[1024,256]{1,0:T(8,128)} %shard_map.126.b0) | copy-start | bytes 3145732
  42.8 34.3 %copy-start.18 = (s32[1,1024]{1,0:T(1,128)S(1)}, s32[1,1024]{1,0:T(1,128)}, u32[]{:S(2)}) copy-start(s32[1,1024]{1,0:T(1,128)} %order.5) | copy-start | bytes 12292
  49.2 1.3 copy-start.6
  50.5 23.1 %collective-permute-start.16 = (f32[1024,256]{1,0:T(8,128)}, f32[1024,256]{1,0:T(8,128)}, u32[]{:S(2)}, u32[]{:S(2)}) collective-permute-start(f32[1024,256]{1,0:T(8,128)} %shard_map.126.b0), channel_id=1, source_target_pairs={{0,8},{4,12},{8,0},{12,4},{16,24},{20,28},{24,16},{28,20},{32,40},... | collective-permute-start | bytes 3145736 | tf_op jit(solution)/shard_map/ppermute | solution.py:31
  50.6 31.4 %collective-permute-start.2 = (f32[256,640]{1,0:T(8,128)S(1)}, f32[256,640]{1,0:T(8,128)S(1)}, u32[]{:S(2)}, u32[]{:S(2)}) collective-permute-start(f32[256,640]{1,0:T(8,128)S(1)} %broadcast_select_fusion), channel_id=1, source_target_pairs={{0,4},{4,0},{8,12},{12,8},{16,20},{20,16},{24,28},{28,24},{32,36},... | collective-permute-start | bytes 1966088 | tf_op jit(solution)/shard_map/ppermute | solution.py:31
  52.7 68.7 %collective-permute-start.15 = (f32[1024,256]{1,0:T(8,128)S(1)}, f32[1024,256]{1,0:T(8,128)}, u32[]{:S(2)}, u32[]{:S(2)}) collective-permute-start(f32[1024,256]{1,0:T(8,128)S(1)} %copy-done.2), channel_id=1, source_target_pairs={{0,4},{4,0},{8,12},{12,8},{16,20},{20,16},{24,28},{28,24},{32,36},... | collective-permute-start | bytes 3145736 | tf_op jit(solution)/shard_map/ppermute | solution.py:31
  73.6 52.8 %collective-permute-start.17 = (f32[1024,256]{1,0:T(8,128)}, f32[1024,256]{1,0:T(8,128)}, u32[]{:S(2)}, u32[]{:S(2)}) collective-permute-start(f32[1024,256]{1,0:T(8,128)} %collective-permute-done.16.b2), channel_id=1, source_target_pairs={{0,4},{4,0},{8,12},{12,8},{16,20},{20,16},{24,28},{28,24},{32,36},... | collective-permute-start | bytes 3145736 | tf_op jit(solution)/shard_map/ppermute | solution.py:31
  77.1 4.9 %copy-start.1 = (f32[256,512]{1,0:T(8,128)S(1)}, f32[256,512]{1,0:T(8,128)}, u32[]{:S(2)}) copy-start(f32[256,512]{1,0:T(8,128)} %coefs.1) | copy-start | bytes 1572868
  77.1 4.9 %copy-start.7 = (f32[1024,512]{1,0:T(8,128)S(1)}, f32[1024,512]{1,0:T(8,128)}, u32[]{:S(2)}) copy-start(f32[1024,512]{1,0:T(8,128)} %copy-done.6) | copy-start | bytes 6291460
  77.1 4.9 %copy-start.12 = (f32[256,512]{1,0:T(8,128)S(1)}, f32[256,512]{1,0:T(8,128)}, u32[]{:S(2)}) copy-start(f32[256,512]{1,0:T(8,128)} %own_y.1) | copy-start | bytes 1572868
  77.1 4.9 %copy-start.13 = (bf16[4,256,256]{2,1,0:T(8,128)(2,1)S(1)}, bf16[4,256,256]{2,1,0:T(8,128)(2,1)}, u32[]{:S(2)}) copy-start(bf16[4,256,256]{2,1,0:T(8,128)(2,1)} %get-tuple-element.37.split_rows) | copy-start | bytes 1572868
  77.1 4.9 %copy-start.14 = (f32[4,256,1]{2,1,0:T(8,128)S(1)}, f32[4,256,1]{2,1,0:T(8,128)}, u32[]{:S(2)}) copy-start(f32[4,256,1]{2,1,0:T(8,128)} %get-tuple-element.38.norms) | copy-start | bytes 12292
  90.2 22.1 %copy-start = (f32[1,336,1024]{2,1,0:T(8,128)S(1)}, f32[1,336,1024]{2,1,0:T(8,128)}, u32[]{:S(2)}) copy-start(f32[1,336,1024]{2,1,0:T(8,128)} %m1.3) | copy-start | bytes 4128772
  90.2 22.1 %copy-start.4 = (f32[1,336,256]{2,1,0:T(8,128)S(1)}, f32[1,336,256]{2,1,0:T(8,128)}, u32[]{:S(2)}) copy-start(f32[1,336,256]{2,1,0:T(8,128)} %e1.1) | copy-start | bytes 1032196
  90.2 22.1 %copy-start.20 = (s32[64]{0:T(128)S(1)}, s32[64]{0:T(128)}, u32[]{:S(2)}) copy-start(s32[64]{0:T(128)} %leaf_map.3) | copy-start | bytes 772
  113.7 0.7 copy-start.17
  113.8 15.7 %copy-start.15 = (f32[256,128]{1,0:T(8,128)}, f32[256,128]{1,0:T(8,128)S(1)}, u32[]{:S(2)}) copy-start(f32[256,128]{1,0:T(8,128)S(1)} %get-tuple-element.62.w1) | copy-start | bytes 393220
  114.4 7.0 %all-to-all-start.1 = ((f32[4,32,256]{2,1,0:T(8,128)}), f32[4,32,256]{2,1,0:T(8,128)S(1)}, u32[]{:S(2)}, u32[]{:S(2)}) async-start(f32[4,32,256]{2,1,0:T(8,128)} %bitcast.14), calls=%async_computation.1 | async-start | bytes 262144 | tf_op jit(solution)/shard_map/all_to_all | solution.py:652
  117.8 35.3 %collective-permute-start.9 = (f32[1024,128]{1,0:T(8,128)}, f32[1024,128]{1,0:T(8,128)}, u32[]{:S(2)}, u32[]{:S(2)}) collective-permute-start(f32[1024,128]{1,0:T(8,128)} %get-tuple-element.40), channel_id=1, source_target_pairs={{0,1},{1,2},{2,3},{3,0},{4,5},{5,6},{6,7},{7,4},{8,9},{9,10},{10,1... | collective-permute-start | bytes 1572872 | tf_op jit(solution)/shard_map/ppermute | solution.py:57
  118.1 35.0 %collective-permute-start.10 = (f32[1024,128]{1,0:T(8,128)}, f32[1024,128]{1,0:T(8,128)}, u32[]{:S(2)}, u32[]{:S(2)}) collective-permute-start(f32[1024,128]{1,0:T(8,128)} %get-tuple-element.41), channel_id=1, source_target_pairs={{0,2},{1,3},{2,0},{3,1},{4,6},{5,7},{6,4},{7,5},{8,10},{9,11},{10,... | collective-permute-start | bytes 1572872 | tf_op jit(solution)/shard_map/ppermute | solution.py:57
  119.9 33.2 %collective-permute-start.11 = (f32[1024,128]{1,0:T(8,128)}, f32[1024,128]{1,0:T(8,128)}, u32[]{:S(2)}, u32[]{:S(2)}) collective-permute-start(f32[1024,128]{1,0:T(8,128)} %get-tuple-element.42), channel_id=1, source_target_pairs={{0,3},{1,0},{2,1},{3,2},{4,7},{5,4},{6,5},{7,6},{8,11},{9,8},{10,9... | collective-permute-start | bytes 1572872 | tf_op jit(solution)/shard_map/ppermute | solution.py:57
  121.4 5.0 %collective-permute-start.14 = (f32[32,256]{1,0:T(8,128)S(1)}, f32[32,256]{1,0:T(8,128)S(1)}, u32[]{:S(2)}, u32[]{:S(2)}) collective-permute-start(f32[32,256]{1,0:T(8,128)S(1)} %fusion.1.r0), channel_id=1, source_target_pairs={{0,56},{4,60},{8,48},{12,52},{16,40},{20,44},{24,32},{28,36},{32,2... | collective-permute-start | bytes 98312 | tf_op jit(solution)/shard_map/ppermute | solution.py:31
  126.4 3.2 %collective-permute-start.13 = (f32[32,256]{1,0:T(8,128)S(1)}, f32[32,256]{1,0:T(8,128)S(1)}, u32[]{:S(2)}, u32[]{:S(2)}) collective-permute-start(f32[32,256]{1,0:T(8,128)S(1)} %fusion.1.r0), channel_id=1, source_target_pairs={{0,32},{4,36},{8,40},{12,44},{16,48},{20,52},{24,56},{28,60},{32,0... | collective-permute-start | bytes 98312 | tf_op jit(solution)/shard_map/ppermute | solution.py:31
  126.4 4.4 %collective-permute-start.12 = (f32[32,256]{1,0:T(8,128)S(1)}, f32[32,256]{1,0:T(8,128)S(1)}, u32[]{:S(2)}, u32[]{:S(2)}) collective-permute-start(f32[32,256]{1,0:T(8,128)S(1)} %fusion.1.r0), channel_id=1, source_target_pairs={{0,24},{4,28},{8,16},{12,20},{16,8},{20,12},{24,0},{28,4},{32,56},... | collective-permute-start | bytes 98312 | tf_op jit(solution)/shard_map/ppermute | solution.py:31
  129.4 35.3 %copy-start.8 = (f32[1024,256]{1,0:T(8,128)}, f32[1024,256]{1,0:T(8,128)S(1)}, u32[]{:S(2)}) copy-start(f32[1024,256]{1,0:T(8,128)S(1)} %get-tuple-element.61.e1) | copy-start | bytes 3145732
  131.6 5.3 %collective-permute-start.20 = (f32[32,256]{1,0:T(8,128)S(1)}, f32[32,256]{1,0:T(8,128)S(1)}, u32[]{:S(2)}, u32[]{:S(2)}) collective-permute-start(f32[32,256]{1,0:T(8,128)S(1)} %get-tuple-element.48), channel_id=1, source_target_pairs={{0,56},{4,60},{8,48},{12,52},{16,40},{20,44},{24,32},{28,36},{32,2... | collective-permute-start | bytes 98312 | tf_op jit(solution)/shard_map/ppermute | solution.py:31
  133.9 4.1 %collective-permute-start.19 = (f32[32,256]{1,0:T(8,128)S(1)}, f32[32,256]{1,0:T(8,128)S(1)}, u32[]{:S(2)}, u32[]{:S(2)}) collective-permute-start(f32[32,256]{1,0:T(8,128)S(1)} %get-tuple-element.48), channel_id=1, source_target_pairs={{0,32},{4,36},{8,40},{12,44},{16,48},{20,52},{24,56},{28,60},{32,0... | collective-permute-start | bytes 98312 | tf_op jit(solution)/shard_map/ppermute | solution.py:31
  136.9 4.4 %collective-permute-start.18 = (f32[32,256]{1,0:T(8,128)S(1)}, f32[32,256]{1,0:T(8,128)S(1)}, u32[]{:S(2)}, u32[]{:S(2)}) collective-permute-start(f32[32,256]{1,0:T(8,128)S(1)} %get-tuple-element.48), channel_id=1, source_target_pairs={{0,24},{4,28},{8,16},{12,20},{16,8},{20,12},{24,0},{28,4},{32,56},... | collective-permute-start | bytes 98312 | tf_op jit(solution)/shard_map/ppermute | solution.py:31
  141.3 5.9 %collective-permute-start.23 = (f32[32,256]{1,0:T(8,128)S(1)}, f32[32,256]{1,0:T(8,128)S(1)}, u32[]{:S(2)}, u32[]{:S(2)}) collective-permute-start(f32[32,256]{1,0:T(8,128)S(1)} %add_add_fusion.r0), channel_id=1, source_target_pairs={{160,0},{164,4},{168,8},{172,12},{176,16},{180,20},{184,24},{188,2... | collective-permute-start | bytes 98312 | tf_op jit(solution)/shard_map/ppermute | solution.py:53
  145.2 5.2 %collective-permute-start.22 = (f32[32,256]{1,0:T(8,128)S(1)}, f32[32,256]{1,0:T(8,128)S(1)}, u32[]{:S(2)}, u32[]{:S(2)}) collective-permute-start(f32[32,256]{1,0:T(8,128)S(1)} %add_add_fusion.r0), channel_id=1, source_target_pairs={{64,0},{68,4},{72,8},{76,12},{80,16},{84,20},{88,24},{92,28},{224,... | collective-permute-start | bytes 98312 | tf_op jit(solution)/shard_map/ppermute | solution.py:53
  147.1 5.0 %collective-permute-start.21 = (f32[32,256]{1,0:T(8,128)S(1)}, f32[32,256]{1,0:T(8,128)S(1)}, u32[]{:S(2)}, u32[]{:S(2)}) collective-permute-start(f32[32,256]{1,0:T(8,128)S(1)} %add_add_fusion.r0), channel_id=1, source_target_pairs={{224,0},{228,4},{232,8},{236,12},{240,16},{244,20},{248,24},{252,2... | collective-permute-start | bytes 98312 | tf_op jit(solution)/shard_map/ppermute | solution.py:53
  153.1 22.3 %copy-start.10 = (f32[1024,128]{1,0:T(8,128)S(1)}, f32[1024,128]{1,0:T(8,128)}, u32[]{:S(2)}) copy-start(f32[1024,128]{1,0:T(8,128)} %get-tuple-element.52.p0) | copy-start | bytes 1572868
  164.7 14.1 %copy-start.3 = (f32[1,1024,256]{2,1,0:T(8,128)S(1)}, f32[1,1024,256]{2,1,0:T(8,128)}, u32[]{:S(2)}) copy-start(f32[1,1024,256]{2,1,0:T(8,128)} %basis.3) | copy-start | bytes 3145732
  178.9 1.0 copy-start.11
  179.9 10.3 %copy-start.25 = (f32[256,128]{1,0:T(8,128)S(1)}, f32[256,128]{1,0:T(8,128)}, u32[]{:S(2)}) copy-start(f32[256,128]{1,0:T(8,128)} %get-tuple-element.57) | copy-start | bytes 393220
  179.9 11.7 %copy-start.24 = (f32[256,128]{1,0:T(8,128)S(1)}, f32[256,128]{1,0:T(8,128)}, u32[]{:S(2)}) copy-start(f32[256,128]{1,0:T(8,128)} %get-tuple-element.58) | copy-start | bytes 393220
  179.9 14.1 %copy-start.23 = (f32[256,128]{1,0:T(8,128)S(1)}, f32[256,128]{1,0:T(8,128)}, u32[]{:S(2)}) copy-start(f32[256,128]{1,0:T(8,128)} %get-tuple-element.59) | copy-start | bytes 393220
  179.9 25.4 %copy-start.16 = (f32[256,128]{1,0:T(8,128)S(1)}, f32[256,128]{1,0:T(8,128)}, u32[]{:S(2)}) copy-start(f32[256,128]{1,0:T(8,128)} %get-tuple-element.56.r0) | copy-start | bytes 393220
  186.8 18.5 %all-to-all-start.2 = ((f32[4,256,128]{2,1,0:T(8,128)}), f32[4,256,128]{2,1,0:T(8,128)S(1)}, u32[]{:S(2)}, u32[]{:S(2)}) async-start(f32[4,256,128]{2,1,0:T(8,128)} %bitcast.9), calls=%async_computation.2 | async-start | bytes 1048576 | tf_op jit(solution)/shard_map/all_to_all | solution.py:601
  190.3 11.9 %collective-permute-start.24 = (f32[256,128]{1,0:T(8,128)S(1)}, f32[256,128]{1,0:T(8,128)S(1)}, u32[]{:S(2)}, u32[]{:S(2)}) collective-permute-start(f32[256,128]{1,0:T(8,128)S(1)} %copy-done.25), channel_id=1, source_target_pairs={{0,1},{1,2},{2,3},{3,0},{4,5},{5,6},{6,7},{7,4},{8,9},{9,10},{10,1... | collective-permute-start | bytes 393224 | tf_op jit(solution)/shard_map/ppermute | solution.py:57
  191.7 13.6 %collective-permute-start.25 = (f32[256,128]{1,0:T(8,128)S(1)}, f32[256,128]{1,0:T(8,128)S(1)}, u32[]{:S(2)}, u32[]{:S(2)}) collective-permute-start(f32[256,128]{1,0:T(8,128)S(1)} %copy-done.24), channel_id=1, source_target_pairs={{0,2},{1,3},{2,0},{3,1},{4,6},{5,7},{6,4},{7,5},{8,10},{9,11},{10,... | collective-permute-start | bytes 393224 | tf_op jit(solution)/shard_map/ppermute | solution.py:57
  194.1 11.2 %collective-permute-start.26 = (f32[256,128]{1,0:T(8,128)S(1)}, f32[256,128]{1,0:T(8,128)S(1)}, u32[]{:S(2)}, u32[]{:S(2)}) collective-permute-start(f32[256,128]{1,0:T(8,128)S(1)} %copy-done.23), channel_id=1, source_target_pairs={{0,3},{1,0},{2,1},{3,2},{4,7},{5,4},{6,5},{7,6},{8,11},{9,8},{10,9... | collective-permute-start | bytes 393224 | tf_op jit(solution)/shard_map/ppermute | solution.py:57
